TPU v7x, 32 devices: a whole 2x2x4 slice. The times are simulated.
32 devices in a mesh: groups: 2 (over x), space: 16 (over z, y, core).
Axes of the slice: x: 2, y: 2, z: 4, core: 2. Of those that a mesh axis runs over, the one named last changes fastest.
Arguments:
- patches: bfloat16 [8192, 1024], P(('groups', 'space')), parts along dimension 0, may hold values from -6 to 6
- var_order: int32 [64], replicated, may hold values from 0 to 63, each once
- embed_weight: bfloat16 [64, 16, 1024], replicated, may hold values from -1.5 to 1.5
- var_embed: bfloat16 [64, 1024], replicated, may hold values from -2 to 2
- agg_keys: bfloat16 [16, 1024], replicated, may hold values from -9 to 9
- agg_value: bfloat16 [1024, 1024], replicated, may hold values from -0.1875 to 0.1875
- agg_out: bfloat16 [1024, 1024], replicated, may hold values from -0.1875 to 0.1875
- pos_embed: bfloat16 [4096, 1024], P('space'), may hold values from -3 to 3
- norm_gain: float32 [1024], replicated, may hold values from 0.25 to 1.75
- qkv_weight: bfloat16 [1024, 3072], P(None, 'space'), may hold values from -2.6 to 2.6
- attn_out: bfloat16 [1024, 1024], replicated, may hold values from -0.1875 to 0.1875
Outputs:
- encoded: bfloat16 [8192, 1024], P(('groups', 'space')), parts along dimension 0
There are 2 independent parts, one for each index of `groups`. A program takes and returns all parts, laid end to end along the dimension named above; an argument that names none is the same for every part. Nothing has to cross between parts.
Inputs may be any that keep to these rules, and one draw needn't show every extreme that they name: var_order is a permutation of the variables.
All inputs are finite; a program needn't handle non-finite values.
Results may differ from a plain program's by a relative error of at most 0.008.
Values may be sent and summed in bfloat16 or wider, within the bound.
No kernel may reach another device: no remote copies, remote signals or barrier semaphores. Data moves between devices by JAX's collectives and lax.ppermute only.
A program may use at most 128 MiB of HBM per device.

v0:
```python
import functools
import math

import jax
import jax.numpy as jnp
from jax import lax
from jax.experimental import pallas as pl
from jax.experimental.pallas import tpu as pltpu
from jax.sharding import PartitionSpec as P

BF16 = jnp.bfloat16
F32 = jnp.float32
LANES = 128
VMEM_LIMIT = 56 * 1024 * 1024


def dot(left, right):
    return jnp.dot(left, right, preferred_element_type=F32)


def dot_t(left, right):
    return lax.dot_general(left, right, (((1,), (1,)), ((), ())), preferred_element_type=F32)


def iota(shape, dim):
    return lax.broadcasted_iota(jnp.int32, shape, dim)


def aggregate_kernel(
    order_ref,
    order_col_ref,
    patches_ref,
    embed_ref,
    var_embed_ref,
    keys_ref,
    value_ref,
    out_w_ref,
    pos_ref,
    gain_ref,
    tokens_ref,
    normed_ref,
    table_ref,
):
    var_count, pixels, width = embed_ref.shape
    heads = keys_ref.shape[0]
    head_size = width // heads
    scale = 1.0 / math.sqrt(head_size)
    tokens = patches_ref.shape[0]
    spread = var_count * heads

    for j in range(var_count):
        table_ref[j] = embed_ref[order_ref[j]]
    table = table_ref[...].reshape(var_count * pixels, width)
    select = (order_col_ref[...] == iota((var_count, var_count), 1)).astype(F32).astype(BF16)
    offsets = dot(select, var_embed_ref[...]).astype(BF16)

    repeat = (iota((LANES, heads), 0) % heads == iota((LANES, heads), 1)).astype(F32).astype(BF16)
    keys = dot(repeat, keys_ref[...]).astype(BF16)
    table_keys = dot_t(table, keys)
    offset_keys = dot_t(offsets, keys)
    high = table_keys.astype(BF16)
    low = (table_keys - high.astype(F32)).astype(BF16)
    patches = patches_ref[...]
    copies = spread // LANES
    rows_of = iota((var_count * pixels, LANES), 0) // pixels
    scores = []
    for block in range(copies):
        cols_of = (iota((var_count * pixels, LANES), 1) + block * LANES) // heads
        here = rows_of == cols_of
        high_b = jnp.where(here, high, jnp.zeros_like(high))
        low_b = jnp.where(here, low, jnp.zeros_like(low))
        channel = (iota((var_count, LANES), 1) + block * LANES) // heads
        row = jnp.sum(
            jnp.where(channel == iota((var_count, LANES), 0), offset_keys, 0.0),
            axis=0,
            keepdims=True,
        )
        scores.append((dot(patches, high_b) + dot(patches, low_b) + row) * scale)

    top = functools.reduce(jnp.maximum, scores)
    step = heads
    while step < LANES:
        top = jnp.maximum(top, pltpu.roll(top, step, 1))
        step *= 2
    exps = [jnp.exp(s - top) for s in scores]
    total = functools.reduce(jnp.add, exps)
    step = heads
    while step < LANES:
        total = total + pltpu.roll(total, step, 1)
        step *= 2
    probs = jnp.concatenate([(e / total).astype(BF16) for e in exps], axis=1)

    table_values = dot(table, value_ref[...]).astype(BF16)
    offset_values = dot(offsets, value_ref[...]).astype(BF16)
    spread_rows = (iota((spread, var_count), 0) // heads == iota((spread, var_count), 1)).astype(F32)
    offset_rows = dot(spread_rows.astype(BF16), offset_values).astype(BF16)
    mine = iota((spread, width), 0) % heads == iota((spread, width), 1) // head_size
    offset_rows = jnp.where(mine, offset_rows, jnp.zeros_like(offset_rows))
    base = dot(probs, offset_rows)

    group = math.gcd(spread, 256)
    row_g, col_g = iota((group, group), 0), iota((group, group), 1)
    same = row_g // heads == col_g // pixels
    left_half = iota((tokens, 2 * head_size), 1) < head_size
    values = []
    for pair in range(heads // 2):
        halves = []
        cols = slice(pair * 2 * head_size, (pair + 1) * 2 * head_size)
        for head in (2 * pair, 2 * pair + 1):
            pick = jnp.where(same & (row_g % heads == head), 1.0, 0.0).astype(BF16)
            weights = jnp.concatenate(
                [
                    dot(probs[:, g * group : (g + 1) * group], pick).astype(BF16)
                    for g in range(spread // group)
                ],
                axis=1,
            )
            halves.append(dot(weights * patches, table_values[:, cols]))
        values.append((jnp.where(left_half, halves[0], halves[1]) + base[:, cols]).astype(BF16))
    values = jnp.concatenate(values, axis=1)

    tokens_zero = (dot(values, out_w_ref[...]) + pos_ref[...].astype(F32)).astype(BF16)
    tokens_ref[...] = tokens_zero
    full = tokens_zero.astype(F32)
    centred = full - jnp.mean(full, axis=-1, keepdims=True)
    variance = jnp.mean(centred * centred, axis=-1, keepdims=True)
    normed_ref[...] = (centred * lax.rsqrt(variance + 1e-05) * gain_ref[...]).astype(BF16)


def aggregate(patches, var_order, embed_weight, var_embed, keys, value, out_w, pos, gain):
    tokens, width = pos.shape
    var_count = embed_weight.shape[0]
    vmem = pl.BlockSpec(memory_space=pltpu.VMEM)
    return pl.pallas_call(
        aggregate_kernel,
        out_shape=[jax.ShapeDtypeStruct((tokens, width), BF16)] * 2,
        in_specs=[pl.BlockSpec(memory_space=pltpu.SMEM)] + [vmem] * 9,
        out_specs=[vmem, vmem],
        scratch_shapes=[pltpu.VMEM(embed_weight.shape, BF16)],
        compiler_params=pltpu.CompilerParams(vmem_limit_bytes=VMEM_LIMIT),
        cost_estimate=pl.CostEstimate(
            flops=12 * width * width * tokens * 4, bytes_accessed=9 << 20, transcendentals=1 << 18
        ),
        name="aggregate",
    )(
        var_order,
        var_order.reshape(var_count, 1),
        patches,
        embed_weight,
        var_embed,
        keys,
        value,
        out_w,
        pos,
        gain.reshape(1, width),
    )


def attend_kernel(
    side_ref,
    own_ref,
    sib_ref,
    left_own_ref,
    left_sib_ref,
    right_own_ref,
    right_sib_ref,
    weight_ref,
    context_ref,
    query_s,
    key_s,
    value_s,
):
    side = side_ref[0]
    tokens = own_ref.shape[0]
    kinds, cols, width = weight_ref.shape
    pairs = cols // LANES
    head_size = LANES // 2
    scale = 1.0 / math.sqrt(head_size)
    pieces = [
        (left_own_ref, side),
        (left_sib_ref, 1 - side),
        (own_ref, 2 + side),
        (sib_ref, 3 - side),
        (right_own_ref, 4 + side),
        (right_sib_ref, 5 - side),
    ]
    ones = jnp.ones((tokens, LANES), BF16)
    for number, (ref, place) in enumerate(pieces):
        rows = ref[...]
        key_s[place] = dot_t(weight_ref[1], rows).astype(BF16)
        value = dot_t(rows, weight_ref[2]).astype(BF16)
        for pair in range(pairs):
            value_s[place, pair] = jnp.concatenate(
                [value[:, pair * LANES : (pair + 1) * LANES], ones], axis=1
            )
        if number in (2, 3):
            query = (dot_t(rows, weight_ref[0]).astype(BF16).astype(F32) * scale).astype(BF16)
            for pair in range(pairs):
                query_s[place - 2, pair] = query[:, pair * LANES : (pair + 1) * LANES]

    left_half = iota((tokens, LANES), 1) < head_size

    def attend(pair, carry):
        row = pl.multiple_of(pair * LANES, LANES)
        for sector in range(2):
            query = query_s[sector, pair]
            halves = []
            for half in range(2):
                keep = left_half if half == 0 else jnp.logical_not(left_half)
                masked = jnp.where(keep, query, jnp.zeros_like(query))
                scores = [
                    dot(masked, key_s[sector + k, pl.ds(row, LANES), :]) for k in range(5)
                ]
                top = jnp.max(functools.reduce(jnp.maximum, scores), axis=-1, keepdims=True)
                acc = None
                for k in range(5):
                    part = dot(jnp.exp(scores[k] - top).astype(BF16), value_s[sector + k, pair])
                    acc = part if acc is None else acc + part
                halves.append(acc[:, :LANES] / acc[:, LANES:])
            context_ref[sector, pair] = jnp.where(left_half, halves[0], halves[1]).astype(BF16)
        return carry

    lax.fori_loop(0, pairs, attend, 0)


def attend(side, pieces, weight):
    tokens, width = pieces[0].shape
    cols = weight.shape[1]
    pairs = cols // LANES
    vmem = pl.BlockSpec(memory_space=pltpu.VMEM)
    return pl.pallas_call(
        attend_kernel,
        out_shape=jax.ShapeDtypeStruct((2, pairs, tokens, LANES), BF16),
        in_specs=[pl.BlockSpec(memory_space=pltpu.SMEM)] + [vmem] * 7,
        out_specs=vmem,
        scratch_shapes=[
            pltpu.VMEM((2, pairs, tokens, LANES), BF16),
            pltpu.VMEM((6, cols, tokens), BF16),
            pltpu.VMEM((6, pairs, tokens, 2 * LANES), BF16),
        ],
        compiler_params=pltpu.CompilerParams(vmem_limit_bytes=VMEM_LIMIT),
        cost_estimate=pl.CostEstimate(
            flops=40 * width * cols * tokens, bytes_accessed=8 << 20, transcendentals=5 << 20
        ),
        name="attend",
    )(side, *pieces, weight)


def finish_kernel(side_ref, tokens_ref, mine_ref, other_ref, weight_ref, out_ref):
    side = side_ref[0]
    pairs, tokens, lanes = mine_ref.shape
    width = tokens_ref.shape[1]

    def part(ref, parity):
        rows = jnp.concatenate([ref[pair] for pair in range(pairs)], axis=1)
        return dot(rows, weight_ref[:, parity].reshape(pairs * lanes, width))

    update = part(mine_ref, side) + part(other_ref, 1 - side)
    out_ref[...] = (tokens_ref[...].astype(F32) + update).astype(BF16)


def finish(side, tokens_zero, mine, other, attn_out):
    tokens, width = tokens_zero.shape
    head_size = LANES // 2
    vmem = pl.BlockSpec(memory_space=pltpu.VMEM)
    return pl.pallas_call(
        finish_kernel,
        out_shape=jax.ShapeDtypeStruct((tokens, width), BF16),
        in_specs=[pl.BlockSpec(memory_space=pltpu.SMEM)] + [vmem] * 4,
        out_specs=vmem,
        compiler_params=pltpu.CompilerParams(vmem_limit_bytes=VMEM_LIMIT),
        cost_estimate=pl.CostEstimate(
            flops=2 * width * width * tokens, bytes_accessed=4 << 20, transcendentals=0
        ),
        name="finish",
    )(side, tokens_zero, mine, other, attn_out.reshape(-1, 2, head_size, width))


def sibling(value):
    length = lax.axis_size("space")
    return lax.ppermute(value, "space", [(i, i ^ 1) for i in range(length)])


def from_chip(value, by):
    length = lax.axis_size("space")
    return lax.ppermute(value, "space", [((i + 2 * by) % length, i) for i in range(length)])


def parity_weight(qkv_weight, side, head_size):
    rows = qkv_weight.T
    gathered = lax.all_gather(rows, "space", axis=0, tiled=True)
    width = gathered.shape[1]
    blocks = gathered.reshape(-1, 2, head_size, width)
    return lax.dynamic_index_in_dim(blocks, side, 1, keepdims=False).reshape(3, -1, width)


def per_device(
    patches,
    var_order,
    embed_weight,
    var_embed,
    agg_keys,
    agg_value,
    agg_out,
    pos_embed,
    norm_gain,
    qkv_weight,
    attn_out,
):
    head_size = embed_weight.shape[2] // agg_keys.shape[0]
    side = lax.axis_index("space") % 2
    side_arg = side.reshape(1).astype(jnp.int32)
    weight = parity_weight(qkv_weight, side, head_size)
    tokens_zero, normed = aggregate(
        patches, var_order, embed_weight, var_embed, agg_keys, agg_value, agg_out, pos_embed, norm_gain
    )
    left = from_chip(normed, -1)
    right = from_chip(normed, 1)
    pieces = (normed, sibling(normed), left, sibling(left), right, sibling(right))
    context = attend(side_arg, pieces, weight)
    mine = lax.dynamic_index_in_dim(context, side, 0, keepdims=False)
    other = sibling(lax.dynamic_index_in_dim(context, 1 - side, 0, keepdims=False))
    return finish(side_arg, tokens_zero, mine, other, attn_out)


def solution(mesh):
    in_specs = (
        P(("groups", "space"), None),
        P(),
        P(),
        P(),
        P(),
        P(),
        P(),
        P("space", None),
        P(),
        P(None, "space"),
        P(),
    )
    out_specs = P(("groups", "space"), None)
    return jax.shard_map(
        per_device, mesh=mesh, in_specs=in_specs, out_specs=out_specs, check_vma=False
    )
```

profile of v0, /device:TPU:0, one launch (start us, length us, event | category | flops | bytes accessed | tf_op | source)
XLA Modules:
  0.0 120.0 jit_solution(4173782838957063956)
XLA Ops:
  6.5 0.0 all-gather.2.cloned.1.call-start
  6.5 0.7 all-gather.2.cloned.1.call-update
  7.3 1.4 %copy.12.order_col_ref = s32[64,1]{1,0:T(8,128)} copy(s32[64,1]{0,1:T(1,128)} %bitcast.17) | data formatting | bytes 512 | tf_op jit(solution)/shard_map/reshape | solution.py:147
  8.6 17.2 %aggregate.1 = (bf16[256,1024]{1,0:T(8,128)(2,1)}, bf16[256,1024]{1,0:T(8,128)(2,1)}) custom-call(s32[64]{0:T(128)} %order_ref.1, s32[64,1]{1,0:T(8,128)} %copy.12.order_col_ref, bf16[256,1024]{1,0:T(8,128)(2,1)} %patches_ref.1, bf16[64,16,1024]{2,1,0:T(8,128)(2,1)} %embed_ref.1, bf16[64,1024]{1,0:T(8,128)(2,1)} %var_embed_ref.1, bf16[16,1024]{1,0:T(8,128)(2,1)} %keys_ref.1, ...), custom_call_target="tpu_custom_call" | custom-call | flops 12884901888 | bytes 9437184 | tf_op jit(solution)/shard_map/aggregate/pallas_call | solution.py:134
  25.8 3.0 %collective-permute-start.1 = (bf16[256,1024]{1,0:T(8,128)(2,1)}, bf16[256,1024]{1,0:T(8,128)(2,1)S(1)}, u32[]{:S(2)}, u32[]{:S(2)}) collective-permute-start(bf16[256,1024]{1,0:T(8,128)(2,1)} %get-tuple-element.8.own_ref), channel_id=1, source_target_pairs={{14,0},{15,1},{0,2},{1,3},{2,4},{3,5},{4,6},{5,7},{6,8},{7,9},{8,1... | collective-permute-start | bytes 1572872 | tf_op jit(solution)/shard_map/ppermute | solution.py:286
  28.8 3.0 %collective-permute-start.3 = (bf16[256,1024]{1,0:T(8,128)(2,1)}, bf16[256,1024]{1,0:T(8,128)(2,1)S(1)}, u32[]{:S(2)}, u32[]{:S(2)}) collective-permute-start(bf16[256,1024]{1,0:T(8,128)(2,1)} %get-tuple-element.8.own_ref), channel_id=1, source_target_pairs={{2,0},{3,1},{4,2},{5,3},{6,4},{7,5},{8,6},{9,7},{10,8},{11,9},{12,... | collective-permute-start | bytes 1572872 | tf_op jit(solution)/shard_map/ppermute | solution.py:286
  31.8 0.0 collective-permute-start
  31.8 24.6 %collective-permute-done.1.left_own_ref = bf16[256,1024]{1,0:T(8,128)(2,1)S(1)} collective-permute-done((bf16[256,1024]{1,0:T(8,128)(2,1)}, bf16[256,1024]{1,0:T(8,128)(2,1)S(1)}, u32[]{:S(2)}, u32[]{:S(2)}) %collective-permute-start.1) | collective-permute-done | bytes 524320 | tf_op jit(solution)/shard_map/ppermute | solution.py:286
  56.5 0.0 copy-start.1
  56.5 0.0 collective-permute-start.2
  56.5 2.1 %collective-permute-done.3.right_own_ref = bf16[256,1024]{1,0:T(8,128)(2,1)S(1)} collective-permute-done((bf16[256,1024]{1,0:T(8,128)(2,1)}, bf16[256,1024]{1,0:T(8,128)(2,1)S(1)}, u32[]{:S(2)}, u32[]{:S(2)}) %collective-permute-start.3) | collective-permute-done | bytes 524320 | tf_op jit(solution)/shard_map/ppermute | solution.py:286
  58.6 0.0 copy-start.2
  58.6 0.0 collective-permute-start.4
  58.6 25.2 %all-gather.2.cloned.1.call-done = bf16[3072,1024]{1,0:T(8,128)(2,1)} async-done(((bf16[192,1024]{1,0:T(8,128)(2,1)}), bf16[3072,1024]{1,0:T(8,128)(2,1)}) %all-gather.2.cloned.1.call-update) | async-done | bytes 6291472 | tf_op jit(solution)/shard_map/all_gather | solution.py:291
  83.8 4.1 %constant_dynamic-slice_fusion = bf16[24,1,64,1024]{3,2,1,0:T(8,128)(2,1)} fusion(bf16[24,2,64,1024]{3,2,1,0:T(8,128)(2,1)} %bitcast.15, s32[]{:T(128)S(6)} %select_n.17), kind=kLoop, calls=%fused_computation.2 | loop fusion | bytes 6291460 | tf_op jit(solution)/shard_map/jit(dynamic_index_in_dim)/dynamic_slice | solution.py:294
  87.9 0.0 copy-done.1
  87.9 0.0 copy-done.2
  87.9 0.0 collective-permute-done.sib_ref
  87.9 0.0 copy-start.3
  87.9 0.0 collective-permute-done.2.left_sib_ref
  87.9 0.0 copy-start.4
  87.9 0.0 collective-permute-done.4.right_sib_ref
  87.9 0.0 copy-start.5
  87.9 0.7 copy-done.3
  88.7 0.2 copy-done.4
  88.9 0.2 copy-done.5
  89.1 16.7 %attend.1 = bf16[2,4,256,128]{3,2,1,0:T(8,128)(2,1)} custom-call(s32[1]{0:T(128)} %bitcast.side_ref, bf16[256,1024]{1,0:T(8,128)(2,1)} %get-tuple-element.8.own_ref, bf16[256,1024]{1,0:T(8,128)(2,1)} %copy-done.3, bf16[256,1024]{1,0:T(8,128)(2,1)} %copy-done.1, bf16[256,1024]{1,0:T(8,128)(2,1)} %copy-done.4, bf16[256,1024]{1,0:T(8,128)(2,1)} %copy-done.2, ...), custom_call_target="tpu_custom_call" | custom-call | flops 5368709120 | bytes 8388608 | tf_op jit(solution)/shard_map/attend/pallas_call | solution.py:231
  105.8 1.8 %dynamic-slice_bitcast_fusion = (bf16[4,256,128]{2,1,0:T(8,128)(2,1)S(1)}, bf16[4,256,128]{2,1,0:T(8,128)(2,1)}) fusion(bf16[2,4,256,128]{3,2,1,0:T(8,128)(2,1)} %attend.1, s32[]{:T(128)S(6)} %select_n.18, s32[]{:T(128)S(6)} %select_n.17), kind=kLoop, calls=%fused_computation | loop fusion | bytes 1048584 | tf_op jit(solution)/shard_map/jit(dynamic_index_in_dim)/squeeze | solution.py:322
  107.5 0.2 collective-permute-start.5
  107.8 1.3 %collective-permute-done.5.other_ref = bf16[4,256,128]{2,1,0:T(8,128)(2,1)S(1)} collective-permute-done((bf16[4,256,128]{2,1,0:T(8,128)(2,1)S(1)}, bf16[4,256,128]{2,1,0:T(8,128)(2,1)S(1)}, u32[]{:S(2)}, u32[]{:S(2)}) %collective-permute-start.5) | collective-permute-done | bytes 262176 | tf_op jit(solution)/shard_map/ppermute | solution.py:281
  109.1 0.0 copy-start
  109.1 0.7 copy-done
  109.8 3.4 %finish.1 = bf16[256,1024]{1,0:T(8,128)(2,1)} custom-call(s32[1]{0:T(128)} %bitcast.side_ref, bf16[256,1024]{1,0:T(8,128)(2,1)} %get-tuple-element.7.tokens_ref, bf16[4,256,128]{2,1,0:T(8,128)(2,1)} %get-tuple-element.10.mine_ref, bf16[4,256,128]{2,1,0:T(8,128)(2,1)} %copy-done, bf16[8,2,64,1024]{3,2,1,0:T(8,128)(2,1)} %bitcast.14), custom_call_target="tpu_custom_call" | custom-call | flops 536870912 | bytes 4194304 | tf_op jit(solution)/shard_map/finish/pallas_call | solution.py:266
Async XLA Ops:
  6.5 77.3 %all-gather.2.cloned.1.call-start = ((), (), s32[]{:S(2)}) async-start(), calls=%async_computation | async-start | bytes 6684672 | tf_op jit(solution)/shard_map/all_gather | solution.py:291
  25.8 30.6 %collective-permute-start.1 = (bf16[256,1024]{1,0:T(8,128)(2,1)}, bf16[256,1024]{1,0:T(8,128)(2,1)S(1)}, u32[]{:S(2)}, u32[]{:S(2)}) collective-permute-start(bf16[256,1024]{1,0:T(8,128)(2,1)} %get-tuple-element.8.own_ref), channel_id=1, source_target_pairs={{14,0},{15,1},{0,2},{1,3},{2,4},{3,5},{4,6},{5,7},{6,8},{7,9},{8,1... | collective-permute-start | bytes 1572872 | tf_op jit(solution)/shard_map/ppermute | solution.py:286
  28.8 29.8 %collective-permute-start.3 = (bf16[256,1024]{1,0:T(8,128)(2,1)}, bf16[256,1024]{1,0:T(8,128)(2,1)S(1)}, u32[]{:S(2)}, u32[]{:S(2)}) collective-permute-start(bf16[256,1024]{1,0:T(8,128)(2,1)} %get-tuple-element.8.own_ref), channel_id=1, source_target_pairs={{2,0},{3,1},{4,2},{5,3},{6,4},{7,5},{8,6},{9,7},{10,8},{11,9},{12,... | collective-permute-start | bytes 1572872 | tf_op jit(solution)/shard_map/ppermute | solution.py:286
  31.8 56.1 %collective-permute-start = (bf16[256,1024]{1,0:T(8,128)(2,1)}, bf16[256,1024]{1,0:T(8,128)(2,1)S(1)}, u32[]{:S(2)}, u32[]{:S(2)}) collective-permute-start(bf16[256,1024]{1,0:T(8,128)(2,1)} %get-tuple-element.8.own_ref), channel_id=1, source_target_pairs={{0,1},{1,0},{2,3},{3,2},{4,5},{5,4},{6,7},{7,6},{8,9},{9,8},{10,11... | collective-permute-start | bytes 1572872 | tf_op jit(solution)/shard_map/ppermute | solution.py:281
  56.5 31.4 %copy-start.1 = (bf16[256,1024]{1,0:T(8,128)(2,1)}, bf16[256,1024]{1,0:T(8,128)(2,1)S(1)}, u32[]{:S(2)}) copy-start(bf16[256,1024]{1,0:T(8,128)(2,1)S(1)} %collective-permute-done.1.left_own_ref) | copy-start | bytes 1572868
  56.5 31.4 %collective-permute-start.2 = (bf16[256,1024]{1,0:T(8,128)(2,1)S(1)}, bf16[256,1024]{1,0:T(8,128)(2,1)S(1)}, u32[]{:S(2)}, u32[]{:S(2)}) collective-permute-start(bf16[256,1024]{1,0:T(8,128)(2,1)S(1)} %collective-permute-done.1.left_own_ref), channel_id=1, source_target_pairs={{0,1},{1,0},{2,3},{3,2},{4,5},{5,4},{6,7},{7,6},{8,9},{9,8},{10,11... | collective-permute-start | bytes 1572872 | tf_op jit(solution)/shard_map/ppermute | solution.py:281
  58.6 29.3 %copy-start.2 = (bf16[256,1024]{1,0:T(8,128)(2,1)}, bf16[256,1024]{1,0:T(8,128)(2,1)S(1)}, u32[]{:S(2)}) copy-start(bf16[256,1024]{1,0:T(8,128)(2,1)S(1)} %collective-permute-done.3.right_own_ref) | copy-start | bytes 1572868
  58.6 29.3 %collective-permute-start.4 = (bf16[256,1024]{1,0:T(8,128)(2,1)S(1)}, bf16[256,1024]{1,0:T(8,128)(2,1)S(1)}, u32[]{:S(2)}, u32[]{:S(2)}) collective-permute-start(bf16[256,1024]{1,0:T(8,128)(2,1)S(1)} %collective-permute-done.3.right_own_ref), channel_id=1, source_target_pairs={{0,1},{1,0},{2,3},{3,2},{4,5},{5,4},{6,7},{7,6},{8,9},{9,8},{10,11... | collective-permute-start | bytes 1572872 | tf_op jit(solution)/shard_map/ppermute | solution.py:281
  87.9 0.8 copy-start.3
  87.9 1.0 copy-start.4
  87.9 1.1 copy-start.5
  107.5 1.5 %collective-permute-start.5 = (bf16[4,256,128]{2,1,0:T(8,128)(2,1)S(1)}, bf16[4,256,128]{2,1,0:T(8,128)(2,1)S(1)}, u32[]{:S(2)}, u32[]{:S(2)}) collective-permute-start(bf16[4,256,128]{2,1,0:T(8,128)(2,1)S(1)} %get-tuple-element.9), channel_id=1, source_target_pairs={{0,1},{1,0},{2,3},{3,2},{4,5},{5,4},{6,7},{7,6},{8,9},{9,8},{10,11... | collective-permute-start | bytes 786440 | tf_op jit(solution)/shard_map/ppermute | solution.py:281
  109.1 0.7 copy-start
Sparse Core Ops, SparseCore 0:
  9.6 74.1 all-gather.1
where the time goes:
time: 120 us
  waiting for transfers between devices  54 us (45%)
  Pallas kernels  37.3 us (31%)
  between operations  13.4 us (11%)
  local copies, waits for them, and re-layouts  9.02 us (8%)
  starting transfers between devices  6.26 us (5%)
    ppermute x2, waiting for transfers between devices, from_chip(): lax.ppermute(value, 'space', [((i + 2 * by) % length, i) for i in range(l...  26.7 us
    all_gather x1, waiting for transfers between devices, parity_weight(): gathered = lax.all_gather(rows, 'space', axis=0, tiled=True)  25.2 us
    pallas_call x1, Pallas kernels, aggregate(): pl.pallas_call(aggregate_kernel, out_shape=[jax.ShapeDtypeStruct((tokens,...  17.2 us
    pallas_call x1, Pallas kernels, attend(): pl.pallas_call(attend_kernel, out_shape=jax.ShapeDtypeStruct((2, pairs, t...  16.7 us
    ppermute x2, starting transfers between devices, from_chip(): lax.ppermute(value, 'space', [((i + 2 * by) % length, i) for i in range(l...  6.01 us
    dynamic_slice x1, local copies, waits for them, and re-layouts, parity_weight(): lax.dynamic_index_in_dim(blocks, side, 1, keepdims=False)  4.07 us
    pallas_call x1, Pallas kernels, finish(): pl.pallas_call(finish_kernel, out_shape=jax.ShapeDtypeStruct((tokens, wid...  3.43 us
  transfers between devices with their start and end apart: 7, of which 4 were waited for; matrix products, arithmetic and copies ran while one was open for 5% of the time, Pallas kernels for 14%

commit v1 on v0

v1 whole, which is shorter than its diff:
```python
import functools
import math

import jax
import jax.numpy as jnp
from jax import lax
from jax.experimental import pallas as pl
from jax.experimental.pallas import tpu as pltpu
from jax.sharding import PartitionSpec as P

BF16 = jnp.bfloat16
F32 = jnp.float32
LANES = 128
AGG_VMEM = 24 * 1024 * 1024
ATTEND_VMEM = 40 * 1024 * 1024


def dot(left, right):
    return jnp.dot(left, right, preferred_element_type=F32)


def dot_t(left, right):
    return lax.dot_general(left, right, (((1,), (1,)), ((), ())), preferred_element_type=F32)


def iota(shape, dim):
    return lax.broadcasted_iota(jnp.int32, shape, dim)


def table_kernel(
    order_ref,
    embed_ref,
    var_embed_ref,
    keys_ref,
    value_ref,
    high_ref,
    low_ref,
    row_ref,
    early_values_ref,
    late_values_ref,
    early_offset_ref,
    late_offset_ref,
    table_ref,
):
    var_count, pixels, width = embed_ref.shape
    heads = keys_ref.shape[0]
    head_size = width // heads
    spread = var_count * heads

    line = iota((var_count, var_count), 0)
    order = jnp.zeros((var_count, var_count), jnp.int32)
    for j in range(var_count):
        table_ref[j] = embed_ref[order_ref[j]]
        order = jnp.where(line == j, order_ref[j], order)
    table = table_ref[...].reshape(var_count * pixels, width)
    select = (order == iota((var_count, var_count), 1)).astype(F32).astype(BF16)
    offsets = dot(select, var_embed_ref[...]).astype(BF16)

    repeat = (iota((LANES, heads), 0) % heads == iota((LANES, heads), 1)).astype(F32).astype(BF16)
    keys = dot(repeat, keys_ref[...]).astype(BF16)
    table_keys = dot_t(table, keys)
    offset_keys = dot_t(offsets, keys)
    high = table_keys.astype(BF16)
    low = (table_keys - high.astype(F32)).astype(BF16)
    rows_of = iota((var_count * pixels, LANES), 0) // pixels
    for block in range(spread // LANES):
        cols = slice(block * LANES, (block + 1) * LANES)
        here = rows_of == (iota((var_count * pixels, LANES), 1) + block * LANES) // heads
        high_ref[:, cols] = jnp.where(here, high, jnp.zeros_like(high))
        low_ref[:, cols] = jnp.where(here, low, jnp.zeros_like(low))
        channel = (iota((var_count, LANES), 1) + block * LANES) // heads
        row_ref[:, cols] = jnp.sum(
            jnp.where(channel == iota((var_count, LANES), 0), offset_keys, 0.0),
            axis=0,
            keepdims=True,
        )

    half = width // 2
    early_values_ref[...] = dot(table, value_ref[:, :half]).astype(BF16)
    late_values_ref[...] = dot(table, value_ref[:, half:]).astype(BF16)
    offset_values = dot(offsets, value_ref[...]).astype(BF16)
    spread_rows = (iota((spread, var_count), 0) // heads == iota((spread, var_count), 1)).astype(F32)
    offset_rows = dot(spread_rows.astype(BF16), offset_values).astype(BF16)
    mine = iota((spread, width), 0) % heads == iota((spread, width), 1) // head_size
    offset_rows = jnp.where(mine, offset_rows, jnp.zeros_like(offset_rows))
    early_offset_ref[...] = offset_rows[:, :half]
    late_offset_ref[...] = offset_rows[:, half:]


def mix_heads(probs, patches, table_values, base, first, pairs, heads, head_size, pixels):
    tokens, spread = probs.shape
    group = math.gcd(spread, 256)
    row_g, col_g = iota((group, group), 0), iota((group, group), 1)
    same = row_g // heads == col_g // pixels
    left_half = iota((tokens, 2 * head_size), 1) < head_size
    values = []
    for pair in range(pairs):
        halves = []
        cols = slice(pair * 2 * head_size, (pair + 1) * 2 * head_size)
        for head in (first + 2 * pair, first + 2 * pair + 1):
            pick = jnp.where(same & (row_g % heads == head), 1.0, 0.0).astype(BF16)
            weights = jnp.concatenate(
                [
                    dot(probs[:, g * group : (g + 1) * group], pick).astype(BF16)
                    for g in range(spread // group)
                ],
                axis=1,
            )
            halves.append(dot(weights * patches, table_values[:, cols]))
        values.append((jnp.where(left_half, halves[0], halves[1]) + base[:, cols]).astype(BF16))
    return jnp.concatenate(values, axis=1)


def first_kernel(
    patches_ref, high_ref, low_ref, row_ref, values_ref, offset_ref, probs_ref, half_ref, *, heads
):
    tokens, spread = patches_ref.shape[0], high_ref.shape[1]
    width = patches_ref.shape[1]
    head_size = offset_ref.shape[1] * 2 // heads
    pixels = width * heads // spread
    scale = 1.0 / math.sqrt(head_size)
    patches = patches_ref[...]
    scores = []
    for block in range(spread // LANES):
        cols = slice(block * LANES, (block + 1) * LANES)
        scores.append(
            (dot(patches, high_ref[:, cols]) + dot(patches, low_ref[:, cols]) + row_ref[:, cols])
            * scale
        )
    top = functools.reduce(jnp.maximum, scores)
    step = heads
    while step < LANES:
        top = jnp.maximum(top, pltpu.roll(top, step, 1))
        step *= 2
    exps = [jnp.exp(s - top) for s in scores]
    total = functools.reduce(jnp.add, exps)
    step = heads
    while step < LANES:
        total = total + pltpu.roll(total, step, 1)
        step *= 2
    probs = jnp.concatenate([(e / total).astype(BF16) for e in exps], axis=1)
    probs_ref[...] = probs
    base = dot(probs, offset_ref[...])
    half_ref[...] = mix_heads(
        probs, patches, values_ref, base, 0, heads // 4, heads, head_size, pixels
    )


def second_kernel(
    patches_ref,
    probs_ref,
    half_ref,
    values_ref,
    offset_ref,
    out_w_ref,
    pos_ref,
    gain_ref,
    tokens_ref,
    normed_ref,
    *,
    heads,
):
    spread = probs_ref.shape[1]
    head_size = out_w_ref.shape[0] // heads
    pixels = patches_ref.shape[1] * heads // spread
    probs = probs_ref[...]
    base = dot(probs, offset_ref[...])
    late = mix_heads(
        probs,
        patches_ref[...],
        values_ref,
        base,
        heads // 2,
        heads // 4,
        heads,
        head_size,
        pixels,
    )
    values = jnp.concatenate([half_ref[...], late], axis=1)
    tokens_zero = (dot(values, out_w_ref[...]) + pos_ref[...].astype(F32)).astype(BF16)
    tokens_ref[...] = tokens_zero
    full = tokens_zero.astype(F32)
    centred = full - jnp.mean(full, axis=-1, keepdims=True)
    variance = jnp.mean(centred * centred, axis=-1, keepdims=True)
    normed_ref[...] = (centred * lax.rsqrt(variance + 1e-05) * gain_ref[...]).astype(BF16)


def cost(gflops, mib, exps=0):
    return pl.CostEstimate(
        flops=int(gflops * 1e9), bytes_accessed=int(mib * (1 << 20)), transcendentals=exps
    )


VMEM = pl.BlockSpec(memory_space=pltpu.VMEM)
SMEM = pl.BlockSpec(memory_space=pltpu.SMEM)


def aggregate(patches, var_order, embed_weight, var_embed, keys, value, out_w, pos, gain):
    tokens, width = pos.shape
    var_count, pixels, _ = embed_weight.shape
    heads = keys.shape[0]
    spread = var_count * heads
    half = width // 2
    params = pltpu.CompilerParams(vmem_limit_bytes=AGG_VMEM)
    high, low, row, early_values, late_values, early_offset, late_offset = pl.pallas_call(
        table_kernel,
        out_shape=[
            jax.ShapeDtypeStruct((var_count * pixels, spread), BF16),
            jax.ShapeDtypeStruct((var_count * pixels, spread), BF16),
            jax.ShapeDtypeStruct((1, spread), F32),
            jax.ShapeDtypeStruct((var_count * pixels, half), BF16),
            jax.ShapeDtypeStruct((var_count * pixels, half), BF16),
            jax.ShapeDtypeStruct((spread, half), BF16),
            jax.ShapeDtypeStruct((spread, half), BF16),
        ],
        in_specs=[SMEM] + [VMEM] * 4,
        out_specs=[VMEM] * 7,
        scratch_shapes=[pltpu.VMEM(embed_weight.shape, BF16)],
        compiler_params=params,
        cost_estimate=cost(6, 12),
        name="tables",
    )(var_order, embed_weight, var_embed, keys, value)
    probs, early = pl.pallas_call(
        functools.partial(first_kernel, heads=heads),
        out_shape=[
            jax.ShapeDtypeStruct((tokens, spread), BF16),
            jax.ShapeDtypeStruct((tokens, half), BF16),
        ],
        in_specs=[VMEM] * 6,
        out_specs=[VMEM] * 2,
        compiler_params=params,
        cost_estimate=cost(6, 8, 1 << 18),
        name="early_heads",
    )(patches, high, low, row, early_values, early_offset)
    return pl.pallas_call(
        functools.partial(second_kernel, heads=heads),
        out_shape=[jax.ShapeDtypeStruct((tokens, width), BF16)] * 2,
        in_specs=[VMEM] * 8,
        out_specs=[VMEM] * 2,
        compiler_params=params,
        cost_estimate=cost(6, 8),
        name="late_heads",
    )(patches, probs, early, late_values, late_offset, out_w, pos, gain.reshape(1, width))


def attend_kernel(places_ref, *refs):
    count = len(refs) - 13
    own_ref, sib_ref, left_own_ref, left_sib_ref, right_own_ref, right_sib_ref = refs[:6]
    weight_refs = refs[6 : 6 + count]
    mine_ref, other_ref, query_s, key_s, value_s, weight_s, sems = refs[6 + count :]
    side = places_ref[0]
    copies = [
        pltpu.make_async_copy(ref, weight_s.at[places_ref[1 + i]], sems.at[i])
        for i, ref in enumerate(weight_refs)
    ]
    for copy in copies:
        copy.start()
    for copy in copies:
        copy.wait()
    tokens, width = own_ref.shape
    pairs = mine_ref.shape[0]
    cols = pairs * LANES
    weight = weight_s[...].reshape(3, cols, width)
    head_size = LANES // 2
    scale = 1.0 / math.sqrt(head_size)
    pieces = [
        (left_own_ref, side),
        (left_sib_ref, 1 - side),
        (own_ref, 2 + side),
        (sib_ref, 3 - side),
        (right_own_ref, 4 + side),
        (right_sib_ref, 5 - side),
    ]
    ones = jnp.ones((tokens, LANES), BF16)
    for number, (ref, place) in enumerate(pieces):
        rows = ref[...]
        key_s[place] = dot_t(weight[1], rows).astype(BF16)
        value = dot_t(rows, weight[2]).astype(BF16)
        for pair in range(pairs):
            value_s[place, pair] = jnp.concatenate(
                [value[:, pair * LANES : (pair + 1) * LANES], ones], axis=1
            )
        if number in (2, 3):
            query = (dot_t(rows, weight[0]).astype(BF16).astype(F32) * scale).astype(BF16)
            for pair in range(pairs):
                query_s[number - 2, pair] = query[:, pair * LANES : (pair + 1) * LANES]

    left_half = iota((tokens, LANES), 1) < head_size

    def attend(pair, carry):
        row = pl.multiple_of(pair * LANES, LANES)
        for number, (out_ref, sector) in enumerate(((mine_ref, side), (other_ref, 1 - side))):
            query = query_s[number, pair]
            halves = []
            for half in range(2):
                keep = left_half if half == 0 else jnp.logical_not(left_half)
                masked = jnp.where(keep, query, jnp.zeros_like(query))
                scores = [
                    dot(masked, key_s[sector + k, pl.ds(row, LANES), :]) for k in range(5)
                ]
                top = jnp.max(functools.reduce(jnp.maximum, scores), axis=-1, keepdims=True)
                acc = None
                for k in range(5):
                    part = dot(jnp.exp(scores[k] - top).astype(BF16), value_s[sector + k, pair])
                    acc = part if acc is None else acc + part
                halves.append(acc[:, :LANES] / acc[:, LANES:])
            out_ref[pair] = jnp.where(left_half, halves[0], halves[1]).astype(BF16)
        return carry

    lax.fori_loop(0, pairs, attend, 0)


def attend(places, pieces, weights):
    tokens, width = pieces[0].shape
    rows = weights[0].shape[0]
    cols = rows * len(weights) // 3
    pairs = cols // LANES
    return pl.pallas_call(
        attend_kernel,
        out_shape=[jax.ShapeDtypeStruct((pairs, tokens, LANES), BF16)] * 2,
        in_specs=[SMEM] + [VMEM] * 6 + [pl.BlockSpec(memory_space=pl.ANY)] * len(weights),
        out_specs=[VMEM, VMEM],
        scratch_shapes=[
            pltpu.VMEM((2, pairs, tokens, LANES), BF16),
            pltpu.VMEM((6, cols, tokens), BF16),
            pltpu.VMEM((6, pairs, tokens, 2 * LANES), BF16),
            pltpu.VMEM((len(weights), rows, width), BF16),
            pltpu.SemaphoreType.DMA((len(weights),)),
        ],
        compiler_params=pltpu.CompilerParams(vmem_limit_bytes=ATTEND_VMEM),
        cost_estimate=cost(10, 8, 5 << 20),
        name="attend",
    )(places, *pieces, *weights)


def finish_kernel(side_ref, tokens_ref, mine_ref, other_ref, weight_ref, out_ref):
    side = side_ref[0]
    pairs, tokens, lanes = mine_ref.shape
    width = tokens_ref.shape[1]

    def part(ref, parity):
        rows = jnp.concatenate([ref[pair] for pair in range(pairs)], axis=1)
        return dot(rows, weight_ref[:, parity].reshape(pairs * lanes, width))

    update = part(mine_ref, side) + part(other_ref, 1 - side)
    out_ref[...] = (tokens_ref[...].astype(F32) + update).astype(BF16)


def finish(places, tokens_zero, mine, other, attn_out):
    tokens, width = tokens_zero.shape
    return pl.pallas_call(
        finish_kernel,
        out_shape=jax.ShapeDtypeStruct((tokens, width), BF16),
        in_specs=[SMEM] + [VMEM] * 4,
        out_specs=VMEM,
        compiler_params=pltpu.CompilerParams(vmem_limit_bytes=AGG_VMEM),
        cost_estimate=cost(1, 4),
        name="finish",
    )(places, tokens_zero, mine, other, attn_out.reshape(-1, 2, LANES // 2, width))


def sibling(value):
    length = lax.axis_size("space")
    return lax.ppermute(value, "space", [(i, i ^ 1) for i in range(length)])


def from_chip(value, by):
    length = lax.axis_size("space")
    return lax.ppermute(value, "space", [((i + 2 * by) % length, i) for i in range(length)])


RING = (0, 2, 4, 6, 7, 5, 3, 1)


def around(value, by):
    pairs = []
    for place, chip in enumerate(RING):
        for core in range(2):
            step = by if isinstance(by, int) else by[core]
            pairs.append((2 * chip + core, 2 * RING[(place + step) % len(RING)] + core))
    return lax.ppermute(value, "space", pairs)


def parity_weight(qkv_weight, side, head_size):
    rows = qkv_weight.T
    width = rows.shape[1]
    length = lax.axis_size("space")
    if length != 2 * len(RING) or rows.shape[0] != 3 * head_size:
        gathered = lax.all_gather(rows, "space", axis=0, tiled=True)
        blocks = gathered.reshape(-1, 2, head_size, width)
        picked = lax.dynamic_index_in_dim(blocks, side, 1, keepdims=False)
        return [picked.reshape(-1, width)], [jnp.int32(0)]
    low, middle, high = (rows[i * head_size : (i + 1) * head_size] for i in range(3))
    given = sibling(middle)
    block = jnp.where(
        side == 0,
        jnp.concatenate([low, high, given], axis=0),
        jnp.concatenate([given, low, high], axis=0),
    )
    chip = lax.axis_index("space") // 2
    here = jnp.where(chip % 2 == 0, chip // 2, 7 - chip // 2)

    def place(step):
        at = (here + step) % 8
        return jnp.where(at < 4, 2 * at, 2 * (7 - at) + 1).astype(jnp.int32)

    pieces, places = [block], [place(0)]
    up = down = block
    for step in (1, 2, 3):
        up, down = around(up, 1), around(down, -1)
        pieces += [up, down]
        places += [place(-step), place(step)]
    pieces.append(around(jnp.where(side == 0, up, down), (1, -1)))
    places.append(place(4))
    return pieces, places


def per_device(
    patches,
    var_order,
    embed_weight,
    var_embed,
    agg_keys,
    agg_value,
    agg_out,
    pos_embed,
    norm_gain,
    qkv_weight,
    attn_out,
):
    head_size = embed_weight.shape[2] // agg_keys.shape[0]
    side = (lax.axis_index("space") % 2).astype(jnp.int32)
    weights, spots = parity_weight(qkv_weight, side, head_size)
    places = jnp.stack([side] + spots)
    tokens_zero, normed = aggregate(
        patches, var_order, embed_weight, var_embed, agg_keys, agg_value, agg_out, pos_embed, norm_gain
    )
    left = from_chip(normed, -1)
    right = from_chip(normed, 1)
    pieces = (normed, sibling(normed), left, sibling(left), right, sibling(right))
    mine, other = attend(places, pieces, weights)
    return finish(places, tokens_zero, mine, sibling(other), attn_out)


def solution(mesh):
    in_specs = (
        P(("groups", "space"), None),
        P(),
        P(),
        P(),
        P(),
        P(),
        P(),
        P("space", None),
        P(),
        P(None, "space"),
        P(),
    )
    out_specs = P(("groups", "space"), None)
    return jax.shard_map(
        per_device, mesh=mesh, in_specs=in_specs, out_specs=out_specs, check_vma=False
    )
```

time: 120 us -> 106 us (0.88)
  waiting for transfers between devices: 54 us -> 35.9 us
  between operations: 13.4 us -> 0.18 us
  local copies, waits for them, and re-layouts: 9.02 us -> 22.2 us
  starting transfers between devices: 6.26 us -> 13.1 us
  Pallas kernels: 37.3 us -> 33.1 us
    all_gather x1 -> x0, waiting for transfers between devices: 25.2 us -> none  [parity_weight(): gathered = lax.all_gather(rows, 'space', axis=0, tiled=True)]
    unnamed x12 -> x60, local copies, waits for them, and re-layouts: 1.83 us -> 21.1 us
    ppermute x0 -> x7, waiting for transfers between devices: none -> 16.2 us  [around(): return lax.ppermute(value, 'space', pairs)]
    ppermute x2, waiting for transfers between devices: 26.7 us -> 18.2 us  [from_chip(): lax.ppermute(value, 'space', [((i + 2 * by) % length, i) for i in range(l...]
    ppermute x0 -> x7, starting transfers between devices: none -> 7.48 us  [around(): return lax.ppermute(value, 'space', pairs)]
    dynamic_slice x1 -> x0, local copies, waits for them, and re-layouts: 4.07 us -> none  [parity_weight(): lax.dynamic_index_in_dim(blocks, side, 1, keepdims=False)]
    pallas_call x2 -> x4, Pallas kernels: 33.9 us -> 31.1 us  [the longest x1 16.7 us: attend(): pl.pallas_call(attend_kernel, out_shape=[jax.ShapeDtypeStruct((pairs, tok...]
    squeeze x1 -> x0, local copies, waits for them, and re-layouts: 1.77 us -> none  [per_device(): lax.dynamic_index_in_dim(context, 1 - side, 0, keepdims=False)]
  transfers between devices with their start and end apart: 7 -> 14, of which waited for: 4 -> 7; matrix products, arithmetic and copies ran while one was open for 5% -> 1% of each run, Pallas kernels for 14% -> 14%
where the time goes in v1:
time: 106 us; the launch traced here: 105 us
  waiting for transfers between devices  35.9 us (34%)
  Pallas kernels  33.1 us (31%)
  local copies, waits for them, and re-layouts  22.2 us (21%)
  starting transfers between devices  13.1 us (12%)
    unnamed x60, local copies, waits for them, and re-layouts  21.1 us
    ppermute x2, waiting for transfers between devices, from_chip(): lax.ppermute(value, 'space', [((i + 2 * by) % length, i) for i in range(l...  18.2 us
    pallas_call x1, Pallas kernels, attend(): pl.pallas_call(attend_kernel, out_shape=[jax.ShapeDtypeStruct((pairs, tok...  16.7 us
    ppermute x7, waiting for transfers between devices, around(): return lax.ppermute(value, 'space', pairs)  16.2 us
    ppermute x7, starting transfers between devices, around(): return lax.ppermute(value, 'space', pairs)  7.48 us
    pallas_call x1, Pallas kernels, aggregate(): pl.pallas_call(functools.partial(first_kernel, heads=heads), out_shape=[j...  5.8 us
    pallas_call x1, Pallas kernels, aggregate(): pl.pallas_call(table_kernel, out_shape=[jax.ShapeDtypeStruct((var_count *...  4.99 us
    ppermute x2, starting transfers between devices, from_chip(): lax.ppermute(value, 'space', [((i + 2 * by) % length, i) for i in range(l...  4.79 us
  transfers between devices with their start and end apart: 14, of which 7 were waited for; matrix products, arithmetic and copies ran while one was open for 1% of the time, Pallas kernels for 14%

profile of v1, /device:TPU:0, one launch (start us, length us, event | category | flops | bytes accessed | tf_op | source)
XLA Modules:
  0.0 105.4 jit_solution(6181539123187257351)
XLA Ops:
  0.0 1.1 %fusion = (bf16[64,1024]{1,0:T(8,128)(2,1)S(1)}, bf16[64,1024]{1,0:T(8,128)(2,1)S(1)}, bf16[64,1024]{1,0:T(8,128)(2,1)S(1)}) fusion(bf16[192,1024]{1,0:T(8,128)(2,1)} %bitcast.14), kind=kLoop, calls=%fused_computation.2 | loop fusion | bytes 786432 | tf_op jit(solution)/shard_map/slice | solution.py:393
  1.1 0.5 collective-permute-start.5
  1.6 1.6 %copy-done = bf16[64,16,1024]{2,1,0:T(8,128)(2,1)S(1)} copy-done((bf16[64,16,1024]{2,1,0:T(8,128)(2,1)S(1)}, bf16[64,16,1024]{2,1,0:T(8,128)(2,1)}, u32[]{:S(2)}) %copy-start) | copy-done | bytes 2097176
  3.2 1.6 %copy-done.1 = bf16[1024,1024]{1,0:T(8,128)(2,1)S(1)} copy-done((bf16[1024,1024]{1,0:T(8,128)(2,1)S(1)}, bf16[1024,1024]{1,0:T(8,128)(2,1)}, u32[]{:S(2)}) %copy-start.1) | copy-done | bytes 2097176
  4.8 0.9 copy-done.14
  5.7 0.8 copy-done.15
  6.4 0.7 copy-done.17
  7.1 5.0 %tables.1 = (bf16[1024,1024]{1,0:T(8,128)(2,1)S(1)}, bf16[1024,1024]{1,0:T(8,128)(2,1)S(1)}, f32[1,1024]{1,0:T(1,128)S(1)}, bf16[1024,512]{1,0:T(8,128)(2,1)S(1)...) custom-call(s32[64]{0:T(128)S(1)} %copy-done.17, ...), custom_call_target="tpu_custom_call" | custom-call | flops 6000000000 | bytes 12582912 | tf_op jit(solution)/shard_map/tables/pallas_call | solution.py:205
  12.1 0.0 copy-start.20
  12.1 1.3 %copy-done.20 = bf16[1024,1024]{1,0:T(8,128)(2,1)} copy-done((bf16[1024,1024]{1,0:T(8,128)(2,1)}, bf16[1024,1024]{1,0:T(8,128)(2,1)S(1)}, u32[]{:S(2)}) %copy-start.20) | copy-done | bytes 2097176
  13.4 1.0 copy-done.22
  14.4 1.0 copy-done.24
  15.4 1.0 copy-done.26
  16.4 1.0 copy-done.28
  17.3 0.0 collective-permute-done.5
  17.3 0.1 maximum_select_fusion.refs_6_
  17.4 2.6 %collective-permute-start.6 = (bf16[192,1024]{1,0:T(8,128)(2,1)S(1)}, bf16[192,1024]{1,0:T(8,128)(2,1)S(1)}, u32[]{:S(2)}, u32[]{:S(2)}) collective-permute-start(bf16[192,1024]{1,0:T(8,128)(2,1)S(1)} %maximum_select_fusion.refs_6_), channel_id=1, source_target_pairs={{0,4},{1,5},{4,8},{5,9},{8,12},{9,13},{12,14},{13,15},{14,10},{15,... | collective-permute-start | bytes 1179656 | tf_op jit(solution)/shard_map/ppermute | solution.py:381
  20.0 0.0 collective-permute-start.7
  20.1 0.0 copy-done.4
  20.1 1.6 %copy-done.21 = bf16[1024,1024]{1,0:T(8,128)(2,1)S(1)} copy-done((bf16[1024,1024]{1,0:T(8,128)(2,1)S(1)}, bf16[1024,1024]{1,0:T(8,128)(2,1)}, u32[]{:S(2)}) %copy-start.21) | copy-done | bytes 2097176
  21.7 1.2 %copy-done.23 = bf16[1024,512]{1,0:T(8,128)(2,1)S(1)} copy-done((bf16[1024,512]{1,0:T(8,128)(2,1)S(1)}, bf16[1024,512]{1,0:T(8,128)(2,1)}, u32[]{:S(2)}) %copy-start.23) | copy-done | bytes 1048600
  22.9 1.2 %copy-done.25 = bf16[1024,512]{1,0:T(8,128)(2,1)S(1)} copy-done((bf16[1024,512]{1,0:T(8,128)(2,1)S(1)}, bf16[1024,512]{1,0:T(8,128)(2,1)}, u32[]{:S(2)}) %copy-start.25) | copy-done | bytes 1048600
  24.1 0.0 copy-start.29
  24.1 5.8 %early_heads.1 = (bf16[256,1024]{1,0:T(8,128)(2,1)S(1)}, bf16[256,512]{1,0:T(8,128)(2,1)S(1)}) custom-call(bf16[256,1024]{1,0:T(8,128)(2,1)S(1)} %copy-done.4, bf16[1024,1024]{1,0:T(8,128)(2,1)S(1)} %get-tuple-element.18.high_ref, bf16[1024,1024]{1,0:T(8,128)(2,1)S(1)} %copy-done.21, f32[1,1024]{1,0:T(1,128)S(1)} %get-tuple-element.20.row_ref, ...), custom_call_target="tpu_custom_call" | custom-call | flops 6000000000 | bytes 8388608 | tf_op jit(solution)/shard_map/early_heads/pallas_call | solution.py:223
  29.9 0.0 collective-permute-done.6.refs_7_
  30.0 2.1 %collective-permute-start.8 = (bf16[192,1024]{1,0:T(8,128)(2,1)S(1)}, bf16[192,1024]{1,0:T(8,128)(2,1)S(1)}, u32[]{:S(2)}, u32[]{:S(2)}) collective-permute-start(bf16[192,1024]{1,0:T(8,128)(2,1)S(1)} %collective-permute-done.6.refs_7_), channel_id=1, source_target_pairs={{0,4},{1,5},{4,8},{5,9},{8,12},{9,13},{12,14},{13,15},{14,10},{15,... | collective-permute-start | bytes 1179656 | tf_op jit(solution)/shard_map/ppermute | solution.py:381
  32.0 0.0 collective-permute-done.7.refs_8_
  32.0 0.2 collective-permute-start.9
  32.2 0.0 copy-done.27
  32.2 0.0 copy-done.29
  32.3 3.6 %late_heads.1 = (bf16[256,1024]{1,0:T(8,128)(2,1)S(1)}, bf16[256,1024]{1,0:T(8,128)(2,1)S(1)}) custom-call(bf16[256,1024]{1,0:T(8,128)(2,1)S(1)} %copy-done.4, bf16[256,1024]{1,0:T(8,128)(2,1)S(1)} %get-tuple-element.23.probs_ref, bf16[256,512]{1,0:T(8,128)(2,1)S(1)} %get-tuple-element.24.half_ref, bf16[1024,512]{1,0:T(8,128)(2,1)S(1)} %copy-done.27, ...), custom_call_target="tpu_custom_call" | custom-call | flops 6000000000 | bytes 8388608 | tf_op jit(solution)/shard_map/late_heads/pallas_call | solution.py:235
  35.9 0.0 copy-start.18
  35.9 0.8 copy-done.18
  36.7 1.8 %collective-permute-start.1 = (bf16[256,1024]{1,0:T(8,128)(2,1)S(1)}, bf16[256,1024]{1,0:T(8,128)(2,1)S(1)}, u32[]{:S(2)}, u32[]{:S(2)}) collective-permute-start(bf16[256,1024]{1,0:T(8,128)(2,1)S(1)} %get-tuple-element.28.refs_0_), channel_id=1, source_target_pairs={{14,0},{15,1},{0,2},{1,3},{2,4},{3,5},{4,6},{5,7},{6,8},{7,9},{8,1... | collective-permute-start | bytes 1572872 | tf_op jit(solution)/shard_map/ppermute | solution.py:369
  38.4 3.0 %collective-permute-start.3 = (bf16[256,1024]{1,0:T(8,128)(2,1)S(1)}, bf16[256,1024]{1,0:T(8,128)(2,1)S(1)}, u32[]{:S(2)}, u32[]{:S(2)}) collective-permute-start(bf16[256,1024]{1,0:T(8,128)(2,1)S(1)} %get-tuple-element.28.refs_0_), channel_id=1, source_target_pairs={{2,0},{3,1},{4,2},{5,3},{6,4},{7,5},{8,6},{9,7},{10,8},{11,9},{12,... | collective-permute-start | bytes 1572872 | tf_op jit(solution)/shard_map/ppermute | solution.py:369
  41.5 0.5 collective-permute-done.8.refs_9_
  42.0 1.0 collective-permute-start.10
  43.0 0.7 copy-done.10
  43.7 0.3 collective-permute-done.9.refs_10_
  44.0 1.5 %collective-permute-start.11 = (bf16[192,1024]{1,0:T(8,128)(2,1)S(1)}, bf16[192,1024]{1,0:T(8,128)(2,1)S(1)}, u32[]{:S(2)}, u32[]{:S(2)}) collective-permute-start(bf16[192,1024]{1,0:T(8,128)(2,1)S(1)} %collective-permute-done.9.refs_10_), channel_id=1, source_target_pairs={{0,2},{1,3},{4,0},{5,1},{8,4},{9,5},{12,8},{13,9},{14,12},{15,13},... | collective-permute-start | bytes 1179656 | tf_op jit(solution)/shard_map/ppermute | solution.py:381
  45.6 0.8 copy-done.12
  46.3 0.0 collective-permute-start
  46.4 17.9 %collective-permute-done.1.refs_2_ = bf16[256,1024]{1,0:T(8,128)(2,1)S(1)} collective-permute-done((bf16[256,1024]{1,0:T(8,128)(2,1)S(1)}, bf16[256,1024]{1,0:T(8,128)(2,1)S(1)}, u32[]{:S(2)}, u32[]{:S(2)}) %collective-permute-start.1) | collective-permute-done | bytes 524320 | tf_op jit(solution)/shard_map/ppermute | solution.py:369
  64.2 0.0 collective-permute-start.2
  64.2 0.3 collective-permute-done.3.refs_4_
  64.5 0.2 collective-permute-start.4
  64.7 7.4 %collective-permute-done.10.refs_11_ = bf16[192,1024]{1,0:T(8,128)(2,1)S(1)} collective-permute-done((bf16[192,1024]{1,0:T(8,128)(2,1)S(1)}, bf16[192,1024]{1,0:T(8,128)(2,1)S(1)}, u32[]{:S(2)}, u32[]{:S(2)}) %collective-permute-start.10) | collective-permute-done | bytes 393248 | tf_op jit(solution)/shard_map/ppermute | solution.py:381
  72.1 0.0 collective-permute-done.11.refs_12_
  72.1 0.8 broadcast_select_fusion
  72.9 0.0 collective-permute-start.12
  72.9 0.1 stack.39.places_ref.side_ref
  73.0 0.0 collective-permute-done.refs_1_
  73.0 0.0 collective-permute-done.2.refs_3_
  73.1 0.0 collective-permute-done.4.refs_5_
  73.1 8.0 %collective-permute-done.12.refs_13_ = bf16[192,1024]{1,0:T(8,128)(2,1)} collective-permute-done((bf16[192,1024]{1,0:T(8,128)(2,1)}, bf16[192,1024]{1,0:T(8,128)(2,1)}, u32[]{:S(2)}, u32[]{:S(2)}) %collective-permute-start.12) | collective-permute-done | bytes 393248 | tf_op jit(solution)/shard_map/ppermute | solution.py:381
  81.0 1.0 copy-done.7
  82.0 1.0 copy-done.9
  83.0 1.0 copy-done.11
  84.0 1.0 copy-done.13
  85.0 16.7 %attend.1 = (bf16[4,256,128]{2,1,0:T(8,128)(2,1)S(1)}, bf16[4,256,128]{2,1,0:T(8,128)(2,1)S(1)}) custom-call(s32[9]{0:T(128)S(1)} %stack.39.places_ref.side_ref, bf16[256,1024]{1,0:T(8,128)(2,1)S(1)} %get-tuple-element.28.refs_0_, bf16[256,1024]{1,0:T(8,128)(2,1)S(1)} %collective-permute-done.refs_1_, bf16[256,1024]{1,0:T(8,128)(2,1)S(1)} %collective-permute-done.1.refs_2_, ...), custom_call_target="tpu_custom_call" | custom-call | flops 10000000000 | bytes 8388608 | tf_op jit(solution)/shard_map/attend/pallas_call | solution.py:318
  101.7 0.1 collective-permute-start.13
  101.8 1.5 %collective-permute-done.13.other_ref = bf16[4,256,128]{2,1,0:T(8,128)(2,1)S(1)} collective-permute-done((bf16[4,256,128]{2,1,0:T(8,128)(2,1)S(1)}, bf16[4,256,128]{2,1,0:T(8,128)(2,1)S(1)}, u32[]{:S(2)}, u32[]{:S(2)}) %collective-permute-start.13) | collective-permute-done | bytes 262176 | tf_op jit(solution)/shard_map/ppermute | solution.py:364
  103.3 0.0 copy-done.3
  103.3 2.1 %finish.1 = bf16[256,1024]{1,0:T(8,128)(2,1)} custom-call(s32[9]{0:T(128)S(1)} %stack.39.places_ref.side_ref, bf16[256,1024]{1,0:T(8,128)(2,1)S(1)} %copy-done.19, bf16[4,256,128]{2,1,0:T(8,128)(2,1)S(1)} %get-tuple-element.29.mine_ref, bf16[4,256,128]{2,1,0:T(8,128)(2,1)S(1)} %collective-permute-done.13.other_ref, bf16[8,2,64,1024]{3,2,1,0:T(8,128)(2,1)S(1)} %bitcast.12), custom_call_target="tpu_custom_call" | custom-call | flops 1000000000 | bytes 4194304 | tf_op jit(solution)/shard_map/finish/pallas_call | solution.py:351
  (33 shorter events, 0.1 us)
Async XLA Ops:
  1.1 16.3 %collective-permute-start.5 = (bf16[64,1024]{1,0:T(8,128)(2,1)S(1)}, bf16[64,1024]{1,0:T(8,128)(2,1)S(1)}, u32[]{:S(2)}, u32[]{:S(2)}) collective-permute-start(bf16[64,1024]{1,0:T(8,128)(2,1)S(1)} %get-tuple-element.32), channel_id=1, source_target_pairs={{0,1},{1,0},{2,3},{3,2},{4,5},{5,4},{6,7},{7,6},{8,9},{9,8},{10,11... | collective-permute-start | bytes 393224 | tf_op jit(solution)/shard_map/ppermute | solution.py:364
  1.6 1.6 %copy-start = (bf16[64,16,1024]{2,1,0:T(8,128)(2,1)S(1)}, bf16[64,16,1024]{2,1,0:T(8,128)(2,1)}, u32[]{:S(2)}) copy-start(bf16[64,16,1024]{2,1,0:T(8,128)(2,1)} %embed_ref.1) | copy-start | bytes 6291460
  3.2 1.6 %copy-start.1 = (bf16[1024,1024]{1,0:T(8,128)(2,1)S(1)}, bf16[1024,1024]{1,0:T(8,128)(2,1)}, u32[]{:S(2)}) copy-start(bf16[1024,1024]{1,0:T(8,128)(2,1)} %value_ref.1) | copy-start | bytes 6291460
  4.8 0.9 copy-start.14
  5.7 0.8 copy-start.15
  6.4 0.7 copy-start.17
  7.1 13.0 %copy-start.4 = (bf16[256,1024]{1,0:T(8,128)(2,1)S(1)}, bf16[256,1024]{1,0:T(8,128)(2,1)}, u32[]{:S(2)}) copy-start(bf16[256,1024]{1,0:T(8,128)(2,1)} %patches_ref.3) | copy-start | bytes 1572868
  12.1 1.3 %copy-start.20 = (bf16[1024,1024]{1,0:T(8,128)(2,1)}, bf16[1024,1024]{1,0:T(8,128)(2,1)S(1)}, u32[]{:S(2)}) copy-start(bf16[1024,1024]{1,0:T(8,128)(2,1)S(1)} %get-tuple-element.19.low_ref) | copy-start | bytes 6291460
  13.4 1.0 copy-start.22
  14.4 1.0 copy-start.24
  15.4 1.0 copy-start.26
  16.4 1.0 copy-start.28
  17.4 12.5 %collective-permute-start.6 = (bf16[192,1024]{1,0:T(8,128)(2,1)S(1)}, bf16[192,1024]{1,0:T(8,128)(2,1)S(1)}, u32[]{:S(2)}, u32[]{:S(2)}) collective-permute-start(bf16[192,1024]{1,0:T(8,128)(2,1)S(1)} %maximum_select_fusion.refs_6_), channel_id=1, source_target_pairs={{0,4},{1,5},{4,8},{5,9},{8,12},{9,13},{12,14},{13,15},{14,10},{15,... | collective-permute-start | bytes 1179656 | tf_op jit(solution)/shard_map/ppermute | solution.py:381
  20.0 12.0 %collective-permute-start.7 = (bf16[192,1024]{1,0:T(8,128)(2,1)S(1)}, bf16[192,1024]{1,0:T(8,128)(2,1)S(1)}, u32[]{:S(2)}, u32[]{:S(2)}) collective-permute-start(bf16[192,1024]{1,0:T(8,128)(2,1)S(1)} %maximum_select_fusion.refs_6_), channel_id=1, source_target_pairs={{0,2},{1,3},{4,0},{5,1},{8,4},{9,5},{12,8},{13,9},{14,12},{15,13},... | collective-permute-start | bytes 1179656 | tf_op jit(solution)/shard_map/ppermute | solution.py:381
  20.1 1.6 %copy-start.21 = (bf16[1024,1024]{1,0:T(8,128)(2,1)S(1)}, bf16[1024,1024]{1,0:T(8,128)(2,1)}, u32[]{:S(2)}) copy-start(bf16[1024,1024]{1,0:T(8,128)(2,1)} %copy-done.20) | copy-start | bytes 6291460
  21.7 1.2 %copy-start.23 = (bf16[1024,512]{1,0:T(8,128)(2,1)S(1)}, bf16[1024,512]{1,0:T(8,128)(2,1)}, u32[]{:S(2)}) copy-start(bf16[1024,512]{1,0:T(8,128)(2,1)} %copy-done.22) | copy-start | bytes 3145732
  22.9 1.2 %copy-start.25 = (bf16[1024,512]{1,0:T(8,128)(2,1)S(1)}, bf16[1024,512]{1,0:T(8,128)(2,1)}, u32[]{:S(2)}) copy-start(bf16[1024,512]{1,0:T(8,128)(2,1)} %copy-done.24) | copy-start | bytes 3145732
  24.1 8.1 %copy-start.2 = (bf16[1024,1024]{1,0:T(8,128)(2,1)S(1)}, bf16[1024,1024]{1,0:T(8,128)(2,1)}, u32[]{:S(2)}) copy-start(bf16[1024,1024]{1,0:T(8,128)(2,1)} %out_w_ref.1) | copy-start | bytes 6291460
  24.1 8.1 %copy-start.5 = (bf16[256,1024]{1,0:T(8,128)(2,1)S(1)}, bf16[256,1024]{1,0:T(8,128)(2,1)}, u32[]{:S(2)}) copy-start(bf16[256,1024]{1,0:T(8,128)(2,1)} %pos_ref.1) | copy-start | bytes 1572868
  24.1 8.1 %copy-start.16 = (f32[1024]{0:T(1024)S(1)}, f32[1024]{0:T(1024)}, u32[]{:S(2)}) copy-start(f32[1024]{0:T(1024)} %param.19) | copy-start | bytes 12292
  24.1 8.1 %copy-start.27 = (bf16[1024,512]{1,0:T(8,128)(2,1)S(1)}, bf16[1024,512]{1,0:T(8,128)(2,1)}, u32[]{:S(2)}) copy-start(bf16[1024,512]{1,0:T(8,128)(2,1)} %copy-done.26) | copy-start | bytes 3145732
  24.1 8.1 %copy-start.29 = (bf16[1024,512]{1,0:T(8,128)(2,1)S(1)}, bf16[1024,512]{1,0:T(8,128)(2,1)}, u32[]{:S(2)}) copy-start(bf16[1024,512]{1,0:T(8,128)(2,1)} %copy-done.28) | copy-start | bytes 3145732
  29.9 5.9 %copy-start.6 = (bf16[192,1024]{1,0:T(8,128)(2,1)}, bf16[192,1024]{1,0:T(8,128)(2,1)S(1)}, u32[]{:S(2)}) copy-start(bf16[192,1024]{1,0:T(8,128)(2,1)S(1)} %collective-permute-done.6.refs_7_) | copy-start | bytes 1179652
  30.0 12.0 %collective-permute-start.8 = (bf16[192,1024]{1,0:T(8,128)(2,1)S(1)}, bf16[192,1024]{1,0:T(8,128)(2,1)S(1)}, u32[]{:S(2)}, u32[]{:S(2)}) collective-permute-start(bf16[192,1024]{1,0:T(8,128)(2,1)S(1)} %collective-permute-done.6.refs_7_), channel_id=1, source_target_pairs={{0,4},{1,5},{4,8},{5,9},{8,12},{9,13},{12,14},{13,15},{14,10},{15,... | collective-permute-start | bytes 1179656 | tf_op jit(solution)/shard_map/ppermute | solution.py:381
  32.0 3.8 %copy-start.8 = (bf16[192,1024]{1,0:T(8,128)(2,1)}, bf16[192,1024]{1,0:T(8,128)(2,1)S(1)}, u32[]{:S(2)}) copy-start(bf16[192,1024]{1,0:T(8,128)(2,1)S(1)} %collective-permute-done.7.refs_8_) | copy-start | bytes 1179652
  32.0 12.0 %collective-permute-start.9 = (bf16[192,1024]{1,0:T(8,128)(2,1)S(1)}, bf16[192,1024]{1,0:T(8,128)(2,1)S(1)}, u32[]{:S(2)}, u32[]{:S(2)}) collective-permute-start(bf16[192,1024]{1,0:T(8,128)(2,1)S(1)} %collective-permute-done.7.refs_8_), channel_id=1, source_target_pairs={{0,2},{1,3},{4,0},{5,1},{8,4},{9,5},{12,8},{13,9},{14,12},{15,13},... | collective-permute-start | bytes 1179656 | tf_op jit(solution)/shard_map/ppermute | solution.py:381
  35.9 0.8 copy-start.18
  36.7 27.5 %collective-permute-start.1 = (bf16[256,1024]{1,0:T(8,128)(2,1)S(1)}, bf16[256,1024]{1,0:T(8,128)(2,1)S(1)}, u32[]{:S(2)}, u32[]{:S(2)}) collective-permute-start(bf16[256,1024]{1,0:T(8,128)(2,1)S(1)} %get-tuple-element.28.refs_0_), channel_id=1, source_target_pairs={{14,0},{15,1},{0,2},{1,3},{2,4},{3,5},{4,6},{5,7},{6,8},{7,9},{8,1... | collective-permute-start | bytes 1572872 | tf_op jit(solution)/shard_map/ppermute | solution.py:369
  38.4 26.1 %collective-permute-start.3 = (bf16[256,1024]{1,0:T(8,128)(2,1)S(1)}, bf16[256,1024]{1,0:T(8,128)(2,1)S(1)}, u32[]{:S(2)}, u32[]{:S(2)}) collective-permute-start(bf16[256,1024]{1,0:T(8,128)(2,1)S(1)} %get-tuple-element.28.refs_0_), channel_id=1, source_target_pairs={{2,0},{3,1},{4,2},{5,3},{6,4},{7,5},{8,6},{9,7},{10,8},{11,9},{12,... | collective-permute-start | bytes 1572872 | tf_op jit(solution)/shard_map/ppermute | solution.py:369
  42.0 30.2 %collective-permute-start.10 = (bf16[192,1024]{1,0:T(8,128)(2,1)S(1)}, bf16[192,1024]{1,0:T(8,128)(2,1)S(1)}, u32[]{:S(2)}, u32[]{:S(2)}) collective-permute-start(bf16[192,1024]{1,0:T(8,128)(2,1)S(1)} %collective-permute-done.8.refs_9_), channel_id=1, source_target_pairs={{0,4},{1,5},{4,8},{5,9},{8,12},{9,13},{12,14},{13,15},{14,10},{15,... | collective-permute-start | bytes 1179656 | tf_op jit(solution)/shard_map/ppermute | solution.py:381
  43.0 0.7 copy-start.10
  44.0 28.1 %collective-permute-start.11 = (bf16[192,1024]{1,0:T(8,128)(2,1)S(1)}, bf16[192,1024]{1,0:T(8,128)(2,1)S(1)}, u32[]{:S(2)}, u32[]{:S(2)}) collective-permute-start(bf16[192,1024]{1,0:T(8,128)(2,1)S(1)} %collective-permute-done.9.refs_10_), channel_id=1, source_target_pairs={{0,2},{1,3},{4,0},{5,1},{8,4},{9,5},{12,8},{13,9},{14,12},{15,13},... | collective-permute-start | bytes 1179656 | tf_op jit(solution)/shard_map/ppermute | solution.py:381
  45.6 0.8 copy-start.12
  46.3 26.7 %collective-permute-start = (bf16[256,1024]{1,0:T(8,128)(2,1)S(1)}, bf16[256,1024]{1,0:T(8,128)(2,1)S(1)}, u32[]{:S(2)}, u32[]{:S(2)}) collective-permute-start(bf16[256,1024]{1,0:T(8,128)(2,1)S(1)} %get-tuple-element.28.refs_0_), channel_id=1, source_target_pairs={{0,1},{1,0},{2,3},{3,2},{4,5},{5,4},{6,7},{7,6},{8,9},{9,8},{10,11... | collective-permute-start | bytes 1572872 | tf_op jit(solution)/shard_map/ppermute | solution.py:364
  64.2 8.8 %collective-permute-start.2 = (bf16[256,1024]{1,0:T(8,128)(2,1)S(1)}, bf16[256,1024]{1,0:T(8,128)(2,1)}, u32[]{:S(2)}, u32[]{:S(2)}) collective-permute-start(bf16[256,1024]{1,0:T(8,128)(2,1)S(1)} %collective-permute-done.1.refs_2_), channel_id=1, source_target_pairs={{0,1},{1,0},{2,3},{3,2},{4,5},{5,4},{6,7},{7,6},{8,9},{9,8},{10,11... | collective-permute-start | bytes 1572872 | tf_op jit(solution)/shard_map/ppermute | solution.py:364
  64.5 8.5 %collective-permute-start.4 = (bf16[256,1024]{1,0:T(8,128)(2,1)S(1)}, bf16[256,1024]{1,0:T(8,128)(2,1)}, u32[]{:S(2)}, u32[]{:S(2)}) collective-permute-start(bf16[256,1024]{1,0:T(8,128)(2,1)S(1)} %collective-permute-done.3.refs_4_), channel_id=1, source_target_pairs={{0,1},{1,0},{2,3},{3,2},{4,5},{5,4},{6,7},{7,6},{8,9},{9,8},{10,11... | collective-permute-start | bytes 1572872 | tf_op jit(solution)/shard_map/ppermute | solution.py:364
  72.9 8.1 %collective-permute-start.12 = (bf16[192,1024]{1,0:T(8,128)(2,1)}, bf16[192,1024]{1,0:T(8,128)(2,1)}, u32[]{:S(2)}, u32[]{:S(2)}) collective-permute-start(bf16[192,1024]{1,0:T(8,128)(2,1)} %broadcast_select_fusion), channel_id=1, source_target_pairs={{0,4},{1,3},{4,8},{5,1},{8,12},{9,5},{12,14},{13,9},{14,10},{15,13... | collective-permute-start | bytes 1179656 | tf_op jit(solution)/shard_map/ppermute | solution.py:381
  73.0 30.3 %copy-start.3 = (bf16[1024,1024]{1,0:T(8,128)(2,1)S(1)}, bf16[1024,1024]{1,0:T(8,128)(2,1)}, u32[]{:S(2)}) copy-start(bf16[1024,1024]{1,0:T(8,128)(2,1)} %param.21) | copy-start | bytes 6291460
  81.0 1.0 copy-start.7
  82.0 1.0 copy-start.9
  83.0 1.0 copy-start.11
  84.0 1.0 copy-start.13
  85.0 18.3 %copy-start.19 = (bf16[256,1024]{1,0:T(8,128)(2,1)S(1)}, bf16[256,1024]{1,0:T(8,128)(2,1)}, u32[]{:S(2)}) copy-start(bf16[256,1024]{1,0:T(8,128)(2,1)} %copy-done.18) | copy-start | bytes 1572868
  101.7 1.6 %collective-permute-start.13 = (bf16[4,256,128]{2,1,0:T(8,128)(2,1)S(1)}, bf16[4,256,128]{2,1,0:T(8,128)(2,1)S(1)}, u32[]{:S(2)}, u32[]{:S(2)}) collective-permute-start(bf16[4,256,128]{2,1,0:T(8,128)(2,1)S(1)} %get-tuple-element.30), channel_id=1, source_target_pairs={{0,1},{1,0},{2,3},{3,2},{4,5},{5,4},{6,7},{7,6},{8,9},{9,8},{10,11... | collective-permute-start | bytes 786440 | tf_op jit(solution)/shard_map/ppermute | solution.py:364

commit v2 on v1

v2 whole, which is shorter than its diff:
```python
import functools
import math

import jax
import jax.numpy as jnp
from jax import lax
from jax.experimental import pallas as pl
from jax.experimental.pallas import tpu as pltpu
from jax.sharding import PartitionSpec as P

BF16 = jnp.bfloat16
F32 = jnp.float32
LANES = 128
WHOLE_VMEM = 60 * 1024 * 1024
PART_VMEM = 24 * 1024 * 1024
RING = (0, 2, 4, 6, 7, 5, 3, 1)


def dot(left, right):
    return jnp.dot(left, right, preferred_element_type=F32)


def dot_t(left, right):
    return lax.dot_general(left, right, (((1,), (1,)), ((), ())), preferred_element_type=F32)


def chip_at(index, step):
    if step is None:
        return 0
    chip = index // 2
    here = jnp.where(chip % 2 == 0, chip // 2, 7 - chip // 2)
    at = (here + step + 8) % 8
    return jnp.where(at < 4, 2 * at, 2 * (7 - at) + 1)


def iota(shape, dim):
    return lax.broadcasted_iota(jnp.int32, shape, dim)


def fetch(pairs, sems):
    copies = [pltpu.make_async_copy(src, dst, sems.at[i]) for i, (src, dst) in enumerate(pairs)]
    for copy in copies:
        copy.start()
    return [copy.wait for copy in copies]


def table_kernel(
    order_ref,
    embed_hbm,
    var_embed_hbm,
    keys_hbm,
    value_hbm,
    high_ref,
    low_ref,
    row_ref,
    values_ref,
    offset_ref,
    embed_ref,
    var_embed_ref,
    keys_ref,
    value_ref,
    table_ref,
    sems,
):
    var_count, pixels, width = embed_ref.shape
    heads = keys_ref.shape[0]
    spread = var_count * heads
    waits = fetch(
        (
            (var_embed_hbm, var_embed_ref),
            (keys_hbm, keys_ref),
            (embed_hbm, embed_ref),
            (value_hbm, value_ref),
        ),
        sems,
    )
    line = iota((var_count, var_count), 0)
    order = jnp.zeros((var_count, var_count), jnp.int32)
    for j in range(var_count):
        order = jnp.where(line == j, order_ref[j], order)
    select = (order == iota((var_count, var_count), 1)).astype(F32).astype(BF16)
    waits[0]()
    offsets = dot(select, var_embed_ref[...]).astype(BF16)
    waits[1]()
    repeat = (iota((LANES, heads), 0) % heads == iota((LANES, heads), 1)).astype(F32).astype(BF16)
    keys = dot(repeat, keys_ref[...]).astype(BF16)
    waits[2]()
    for j in range(var_count):
        table_ref[j] = embed_ref[order_ref[j]]
    table = table_ref[...].reshape(var_count * pixels, width)
    table_keys = dot_t(table, keys)
    offset_keys = dot_t(offsets, keys)
    high = table_keys.astype(BF16)
    high_ref[...] = high
    low_ref[...] = (table_keys - high.astype(F32)).astype(BF16)
    for block in range(spread // LANES):
        cols = slice(block * LANES, (block + 1) * LANES)
        channel = (iota((var_count, LANES), 1) + block * LANES) // heads
        row_ref[:, cols] = jnp.sum(
            jnp.where(channel == iota((var_count, LANES), 0), offset_keys, 0.0),
            axis=0,
            keepdims=True,
        )
    waits[3]()
    values = dot(table, value_ref[...]).astype(BF16)
    offset_values = dot(offsets, value_ref[...]).astype(BF16)
    half = width // 2
    for side in range(2):
        values_ref[side] = values[:, side * half : (side + 1) * half]
        offset_ref[side] = offset_values[:, side * half : (side + 1) * half]


def spread_offsets(offset_half, heads, head_size, first):
    var_count, half = offset_half.shape
    spread = var_count * heads
    picks = (iota((spread, var_count), 0) // heads == iota((spread, var_count), 1)).astype(F32)
    rows = dot(picks.astype(BF16), offset_half).astype(BF16)
    mine = iota((spread, half), 0) % heads == iota((spread, half), 1) // head_size + first
    return jnp.where(mine, rows, jnp.zeros_like(rows))


def mix_heads(probs, patches, table_values, base, first, pairs, heads, head_size, pixels):
    tokens, spread = probs.shape
    group = math.gcd(spread, 256)
    row_g, col_g = iota((group, group), 0), iota((group, group), 1)
    same = row_g // heads == col_g // pixels
    left_half = iota((tokens, 2 * head_size), 1) < head_size
    values = []
    for pair in range(pairs):
        halves = []
        cols = slice(pair * 2 * head_size, (pair + 1) * 2 * head_size)
        for head in (first + 2 * pair, first + 2 * pair + 1):
            pick = jnp.where(same & (row_g % heads == head), 1.0, 0.0).astype(BF16)
            weights = jnp.concatenate(
                [
                    dot(probs[:, g * group : (g + 1) * group], pick).astype(BF16)
                    for g in range(spread // group)
                ],
                axis=1,
            )
            halves.append(dot(weights * patches, table_values[:, cols]))
        values.append((jnp.where(left_half, halves[0], halves[1]) + base[:, cols]).astype(BF16))
    return jnp.concatenate(values, axis=1)


def early_kernel(
    patches_hbm,
    high_hbm,
    low_hbm,
    row_hbm,
    values_hbm,
    offset_hbm,
    probs_ref,
    half_ref,
    patches_ref,
    high_ref,
    low_ref,
    row_ref,
    values_ref,
    offset_ref,
    sems,
    *,
    heads,
):
    waits = fetch(
        (
            (high_hbm, high_ref),
            (low_hbm, low_ref),
            (row_hbm, row_ref),
            (patches_hbm, patches_ref),
            (offset_hbm.at[0], offset_ref),
            (values_hbm.at[0], values_ref),
        ),
        sems,
    )
    spread = row_ref.shape[1]
    head_size = offset_ref.shape[1] * 2 // heads
    rows = high_ref.shape[0]
    pixels = rows * heads // spread
    scale = 1.0 / math.sqrt(head_size)
    for wait in waits[:4]:
        wait()
    patches = patches_ref[...]
    high, low = high_ref[...], low_ref[...]
    rows_of = iota((rows, LANES), 0) // pixels
    cols_of = iota((rows, LANES), 1) // heads
    scores = []
    for block in range(spread // LANES):
        here = rows_of == cols_of + block * (LANES // heads)
        part = dot(patches, jnp.where(here, high, jnp.zeros_like(high)))
        part = part + dot(patches, jnp.where(here, low, jnp.zeros_like(low)))
        scores.append((part + row_ref[:, block * LANES : (block + 1) * LANES]) * scale)
    top = functools.reduce(jnp.maximum, scores)
    step = heads
    while step < LANES:
        top = jnp.maximum(top, pltpu.roll(top, step, 1))
        step *= 2
    exps = [jnp.exp(s - top) for s in scores]
    total = functools.reduce(jnp.add, exps)
    step = heads
    while step < LANES:
        total = total + pltpu.roll(total, step, 1)
        step *= 2
    probs = jnp.concatenate([(e / total).astype(BF16) for e in exps], axis=1)
    probs_ref[...] = probs
    waits[4]()
    base = dot(probs, spread_offsets(offset_ref[...], heads, head_size, 0))
    waits[5]()
    half_ref[...] = mix_heads(
        probs, patches, values_ref, base, 0, heads // 4, heads, head_size, pixels
    )


def late_kernel(
    patches_hbm,
    probs_hbm,
    half_hbm,
    values_hbm,
    offset_hbm,
    out_w_hbm,
    pos_hbm,
    gain_hbm,
    tokens_ref,
    normed_ref,
    patches_ref,
    probs_ref,
    half_ref,
    values_ref,
    offset_ref,
    out_w_ref,
    pos_ref,
    gain_ref,
    sems,
    *,
    heads,
):
    waits = fetch(
        (
            (probs_hbm, probs_ref),
            (offset_hbm.at[1], offset_ref),
            (patches_hbm, patches_ref),
            (values_hbm.at[1], values_ref),
            (half_hbm, half_ref),
            (out_w_hbm, out_w_ref),
            (pos_hbm, pos_ref),
            (gain_hbm, gain_ref),
        ),
        sems,
    )
    spread = probs_ref.shape[1]
    head_size = out_w_ref.shape[0] // heads
    pixels = patches_ref.shape[1] * heads // spread
    waits[0]()
    waits[1]()
    probs = probs_ref[...]
    base = dot(probs, spread_offsets(offset_ref[...], heads, head_size, heads // 2))
    waits[2]()
    waits[3]()
    late = mix_heads(
        probs,
        patches_ref[...],
        values_ref,
        base,
        heads // 2,
        heads // 4,
        heads,
        head_size,
        pixels,
    )
    for wait in waits[4:]:
        wait()
    values = jnp.concatenate([half_ref[...], late], axis=1)
    tokens_zero = (dot(values, out_w_ref[...]) + pos_ref[...].astype(F32)).astype(BF16)
    tokens_ref[...] = tokens_zero
    full = tokens_zero.astype(F32)
    centred = full - jnp.mean(full, axis=-1, keepdims=True)
    variance = jnp.mean(centred * centred, axis=-1, keepdims=True)
    normed_ref[...] = (centred * lax.rsqrt(variance + 1e-05) * gain_ref[...]).astype(BF16)


def cost(gflops, mib, exps=0):
    return pl.CostEstimate(
        flops=int(gflops * 1e9), bytes_accessed=int(mib * (1 << 20)), transcendentals=exps
    )


VMEM = pl.BlockSpec(memory_space=pltpu.VMEM)
SMEM = pl.BlockSpec(memory_space=pltpu.SMEM)
HBM = pl.BlockSpec(memory_space=pltpu.HBM)


def like(*arrays):
    return [pltpu.VMEM(a.shape, a.dtype) for a in arrays]


def tables(var_order, embed_weight, var_embed, keys, value):
    var_count, pixels, width = embed_weight.shape
    heads = keys.shape[0]
    rows, spread, half = var_count * pixels, var_count * heads, width // 2
    return pl.pallas_call(
        table_kernel,
        out_shape=[
            jax.ShapeDtypeStruct((rows, LANES), BF16),
            jax.ShapeDtypeStruct((rows, LANES), BF16),
            jax.ShapeDtypeStruct((1, spread), F32),
            jax.ShapeDtypeStruct((2, rows, half), BF16),
            jax.ShapeDtypeStruct((2, var_count, half), BF16),
        ],
        in_specs=[SMEM] + [HBM] * 4,
        out_specs=[VMEM] * 5,
        scratch_shapes=like(embed_weight, var_embed, keys, value, embed_weight)
        + [pltpu.SemaphoreType.DMA((4,))],
        compiler_params=pltpu.CompilerParams(vmem_limit_bytes=WHOLE_VMEM),
        cost_estimate=cost(5, 7),
        name="tables",
    )(var_order, embed_weight, var_embed, keys, value)


def early_heads(patches, made, heads):
    high, low, row, values, offset = made
    tokens = patches.shape[0]
    half = values.shape[2]
    return pl.pallas_call(
        functools.partial(early_kernel, heads=heads),
        out_shape=[
            jax.ShapeDtypeStruct((tokens, row.shape[1]), BF16),
            jax.ShapeDtypeStruct((tokens, half), BF16),
        ],
        in_specs=[HBM] * 6,
        out_specs=[VMEM] * 2,
        scratch_shapes=like(patches, high, low, row)
        + [
            pltpu.VMEM(values.shape[1:], BF16),
            pltpu.VMEM(offset.shape[1:], BF16),
            pltpu.SemaphoreType.DMA((6,)),
        ],
        compiler_params=pltpu.CompilerParams(vmem_limit_bytes=WHOLE_VMEM),
        cost_estimate=cost(6, 6, 1 << 18),
        name="early_heads",
    )(patches, high, low, row, values, offset)


def late_heads(patches, probs, early, made, out_w, pos, gain, heads):
    values, offset = made[3:]
    tokens, width = pos.shape
    gain = gain.reshape(1, width)
    return pl.pallas_call(
        functools.partial(late_kernel, heads=heads),
        out_shape=[jax.ShapeDtypeStruct((tokens, width), BF16)] * 2,
        in_specs=[HBM] * 8,
        out_specs=[VMEM] * 2,
        scratch_shapes=like(patches, probs, early)
        + [pltpu.VMEM(values.shape[1:], BF16), pltpu.VMEM(offset.shape[1:], BF16)]
        + like(out_w, pos, gain)
        + [pltpu.SemaphoreType.DMA((8,))],
        compiler_params=pltpu.CompilerParams(vmem_limit_bytes=WHOLE_VMEM),
        cost_estimate=cost(6, 6),
        name="late_heads",
    )(patches, probs, early, values, offset, out_w, pos, gain)


def attend_kernel(*refs, spots):
    count = len(spots)
    weight_refs = refs[6 : 6 + count]
    mine_ref, other_ref, rows_s, query_s, key_s, value_s, weight_s, sems = refs[6 + count :]
    index, plane = lax.axis_index("space"), lax.axis_index("groups")
    side = index % 2
    moves = [(ref, rows_s.at[i]) for i, ref in enumerate(refs[:6])]
    for ref, (step, share) in zip(weight_refs, spots):
        rows = ref.shape[0]
        start = 0 if share is None else pl.multiple_of((plane + share) % 2 * rows, 32)
        moves.append((ref, weight_s.at[chip_at(index, step), pl.ds(start, rows), :]))
    for wait in fetch(moves, sems):
        wait()
    own_ref, sib_ref, left_own_ref, left_sib_ref, right_own_ref, right_sib_ref = (
        rows_s.at[i] for i in range(6)
    )
    tokens, width = own_ref.shape
    pairs = mine_ref.shape[0]
    cols = pairs * LANES
    weight = weight_s[...].reshape(3, cols, width)
    head_size = LANES // 2
    scale = 1.0 / math.sqrt(head_size)
    pieces = [
        (left_own_ref, side),
        (left_sib_ref, 1 - side),
        (own_ref, 2 + side),
        (sib_ref, 3 - side),
        (right_own_ref, 4 + side),
        (right_sib_ref, 5 - side),
    ]
    ones = jnp.ones((tokens, LANES), BF16)
    for number, (ref, place) in enumerate(pieces):
        rows = ref[...]
        key_s[place] = dot_t(weight[1], rows).astype(BF16)
        value = dot_t(rows, weight[2]).astype(BF16)
        for pair in range(pairs):
            value_s[place, pair] = jnp.concatenate(
                [value[:, pair * LANES : (pair + 1) * LANES], ones], axis=1
            )
        if number in (2, 3):
            query = (dot_t(rows, weight[0]).astype(BF16).astype(F32) * scale).astype(BF16)
            for pair in range(pairs):
                query_s[number - 2, pair] = query[:, pair * LANES : (pair + 1) * LANES]

    left_half = iota((tokens, LANES), 1) < head_size

    def attend(pair, carry):
        row = pl.multiple_of(pair * LANES, LANES)
        for number, (out_ref, sector) in enumerate(((mine_ref, side), (other_ref, 1 - side))):
            query = query_s[number, pair]
            halves = []
            for half in range(2):
                keep = left_half if half == 0 else jnp.logical_not(left_half)
                masked = jnp.where(keep, query, jnp.zeros_like(query))
                scores = [
                    dot(masked, key_s[sector + k, pl.ds(row, LANES), :]) for k in range(5)
                ]
                top = jnp.max(functools.reduce(jnp.maximum, scores), axis=-1, keepdims=True)
                acc = None
                for k in range(5):
                    part = dot(jnp.exp(scores[k] - top).astype(BF16), value_s[sector + k, pair])
                    acc = part if acc is None else acc + part
                halves.append(acc[:, :LANES] / acc[:, LANES:])
            out_ref[pair] = jnp.where(left_half, halves[0], halves[1]).astype(BF16)
        return carry

    lax.fori_loop(0, pairs, attend, 0)


def attend(pieces, weights):
    tokens, width = pieces[0].shape
    spots = tuple(spot for _, spot in weights)
    weights = [piece for piece, _ in weights]
    rows = weights[0].shape[0]
    blocks = 1 if len(weights) == 1 else len(RING)
    cols = rows * blocks // 3
    pairs = cols // LANES
    return pl.pallas_call(
        functools.partial(attend_kernel, spots=spots),
        out_shape=[jax.ShapeDtypeStruct((pairs, tokens, LANES), BF16)] * 2,
        in_specs=[HBM] * (6 + len(weights)),
        out_specs=[VMEM, VMEM],
        scratch_shapes=[
            pltpu.VMEM((6, tokens, width), BF16),
            pltpu.VMEM((2, pairs, tokens, LANES), BF16),
            pltpu.VMEM((6, cols, tokens), BF16),
            pltpu.VMEM((6, pairs, tokens, 2 * LANES), BF16),
            pltpu.VMEM((blocks, rows, width), BF16),
            pltpu.SemaphoreType.DMA((6 + len(weights),)),
        ],
        compiler_params=pltpu.CompilerParams(vmem_limit_bytes=PART_VMEM),
        cost_estimate=cost(10, 8, 5 << 20),
        name="attend",
    )(*pieces, *weights)


def finish_kernel(tokens_ref, mine_ref, other_ref, weight_ref, out_ref):
    side = lax.axis_index("space") % 2
    pairs, tokens, lanes = mine_ref.shape
    width = tokens_ref.shape[1]

    def part(ref, parity):
        rows = jnp.concatenate([ref[pair] for pair in range(pairs)], axis=1)
        return dot(rows, weight_ref[:, parity].reshape(pairs * lanes, width))

    update = part(mine_ref, side) + part(other_ref, 1 - side)
    out_ref[...] = (tokens_ref[...].astype(F32) + update).astype(BF16)


def finish(tokens_zero, mine, other, attn_out):
    tokens, width = tokens_zero.shape
    return pl.pallas_call(
        finish_kernel,
        out_shape=jax.ShapeDtypeStruct((tokens, width), BF16),
        in_specs=[VMEM] * 4,
        out_specs=VMEM,
        compiler_params=pltpu.CompilerParams(vmem_limit_bytes=PART_VMEM),
        cost_estimate=cost(1, 4),
        name="finish",
    )(tokens_zero, mine, other, attn_out.reshape(-1, 2, LANES // 2, width))


def sibling(value):
    length = lax.axis_size("space")
    return lax.ppermute(value, "space", [(i, i ^ 1) for i in range(length)])


def from_chip(value, by):
    length = lax.axis_size("space")
    return lax.ppermute(value, "space", [((i + 2 * by) % length, i) for i in range(length)])


def around(value, by):
    pairs = []
    for place, chip in enumerate(RING):
        for core in range(2):
            step = by if isinstance(by, int) else by[core]
            pairs.append((2 * chip + core, 2 * RING[(place + step) % len(RING)] + core))
    return lax.ppermute(value, "space", pairs)


def across(value):
    return lax.ppermute(value, "groups", [(0, 1), (1, 0)])


def together(*values):
    return lax.optimization_barrier(values)


def parity_block(qkv_weight, side, head_size):
    rows = qkv_weight.T
    low, middle, high = (rows[i * head_size : (i + 1) * head_size] for i in range(3))
    given = sibling(middle)
    return jnp.where(
        side == 0,
        jnp.concatenate([low, high, given], axis=0),
        jnp.concatenate([given, low, high], axis=0),
    )


def parity_weight(qkv_weight, side, head_size):
    rows = lax.all_gather(qkv_weight.T, "space", axis=0, tiled=True)
    blocks = rows.reshape(-1, 2, head_size, rows.shape[1])
    picked = lax.dynamic_index_in_dim(blocks, side, 1, keepdims=False)
    return [(picked.reshape(-1, rows.shape[1]), (None, None))]


def per_device(
    patches,
    var_order,
    embed_weight,
    var_embed,
    agg_keys,
    agg_value,
    agg_out,
    pos_embed,
    norm_gain,
    qkv_weight,
    attn_out,
):
    heads = agg_keys.shape[0]
    head_size = embed_weight.shape[2] // heads
    side = lax.axis_index("space") % 2
    ringed = (
        lax.axis_size("space") == 2 * len(RING)
        and lax.axis_size("groups") == 2
        and qkv_weight.shape[1] == 3 * head_size
    )
    if ringed:
        block = parity_block(qkv_weight, side, head_size)
        block, embed_weight = together(block, embed_weight)
        rows = block.shape[0] // 2
        share = lax.dynamic_slice_in_dim(block, lax.axis_index("groups") * rows, rows, 0)
        weights = [(block, (0, None))]
        up1, down1 = around(share, 1), around(share, -1)
    else:
        weights = parity_weight(qkv_weight, side, head_size)
    made = tables(var_order, embed_weight, var_embed, agg_keys, agg_value)
    if ringed:
        patches, up1, down1 = together(patches, up1, down1)
        up2, down2 = around(up1, 1), around(down1, -1)
        weights += [(up1, (-1, 0)), (down1, (1, 0))]
        near = across(up1), across(down1)
    probs, early = early_heads(patches, made, heads)
    if ringed:
        early, up2, down2 = together(early, up2, down2)
        up3, down3 = around(up2, 1), around(down2, -1)
        weights += [(up2, (-2, 0)), (down2, (2, 0))]
    tokens_zero, normed = late_heads(
        patches, probs, early, made, agg_out, pos_embed, norm_gain, heads
    )
    if ringed:
        normed, up3, down3, *near = together(normed, up3, down3, *near)
        weights += [(near[0], (-1, 1)), (near[1], (1, 1))]
        far = around(jnp.where(side == 0, up3, down3), (1, -1))
        next_near = across(up2), across(down2)
    left = from_chip(normed, -1)
    right = from_chip(normed, 1)
    if ringed:
        up3, down3, far, *next_near = together(up3, down3, far, *next_near)
        weights += [(next_near[0], (-2, 1)), (next_near[1], (2, 1))]
        weights += [(up3, (-3, 0)), (down3, (3, 0)), (far, (4, 0))]
        last = across(up3), across(down3), across(far)
        left, right, *last = together(left, right, *last)
        weights += [(last[0], (-3, 1)), (last[1], (3, 1)), (last[2], (4, 1))]
    pieces = (normed, sibling(normed), left, sibling(left), right, sibling(right))
    mine, other = attend(pieces, weights)
    return finish(tokens_zero, mine, sibling(other), attn_out)


def solution(mesh):
    in_specs = (
        P(("groups", "space"), None),
        P(),
        P(),
        P(),
        P(),
        P(),
        P(),
        P("space", None),
        P(),
        P(None, "space"),
        P(),
    )
    out_specs = P(("groups", "space"), None)
    return jax.shard_map(
        per_device, mesh=mesh, in_specs=in_specs, out_specs=out_specs, check_vma=False
    )
```

time: 106 us -> 101 us (0.953)
  local copies, waits for them, and re-layouts: 22.2 us -> 2.13 us
  starting transfers between devices: 13.1 us -> 21.2 us
  Pallas kernels: 33.1 us -> 41 us
    unnamed x60 -> x6, local copies, waits for them, and re-layouts: 21.1 us -> 1.05 us
    ppermute x2, waiting for transfers between devices: 18.2 us -> 0.01 us  [from_chip(): lax.ppermute(value, 'space', [((i + 2 * by) % length, i) for i in range(l...]
    ppermute x0 -> x7, waiting for transfers between devices: none -> 12.2 us  [across(): return lax.ppermute(value, 'groups', [(0, 1), (1, 0)])]
    pallas_call x4, Pallas kernels: 31.1 us -> 39.5 us  [the longest x1 17.7 us: attend(): pl.pallas_call(functools.partial(attend_kernel, spots=spots), out_shape=[...]
    ppermute x0 -> x7, starting transfers between devices: none -> 8.25 us  [across(): return lax.ppermute(value, 'groups', [(0, 1), (1, 0)])]
    ppermute x7, waiting for transfers between devices: 16.2 us -> 19.6 us  [around(): return lax.ppermute(value, 'space', pairs)]
    ppermute x5, waiting for transfers between devices: 1.53 us -> 4.53 us  [sibling(): return lax.ppermute(value, 'space', [(i, i ^ 1) for i in range(length)])]
  transfers between devices with their start and end apart: 14 -> 21, of which waited for: 7 -> 9; matrix products, arithmetic and copies ran while one was open for 1% -> 0% of each run, Pallas kernels for 14% -> 22%
where the time goes in v2:
time: 101 us
  Pallas kernels  41 us (41%)
  waiting for transfers between devices  36.3 us (36%)
  starting transfers between devices  21.2 us (21%)
  local copies, waits for them, and re-layouts  2.13 us (2%)
    ppermute x7, waiting for transfers between devices, around(): return lax.ppermute(value, 'space', pairs)  19.6 us
    pallas_call x1, Pallas kernels, attend(): pl.pallas_call(functools.partial(attend_kernel, spots=spots), out_shape=[...  17.7 us
    ppermute x7, waiting for transfers between devices, across(): return lax.ppermute(value, 'groups', [(0, 1), (1, 0)])  12.2 us
    pallas_call x1, Pallas kernels, early_heads(): pl.pallas_call(functools.partial(early_kernel, heads=heads), out_shape=[j...  8.62 us
    ppermute x7, starting transfers between devices, across(): return lax.ppermute(value, 'groups', [(0, 1), (1, 0)])  8.25 us
    pallas_call x1, Pallas kernels, tables(): pl.pallas_call(table_kernel, out_shape=[jax.ShapeDtypeStruct((rows, LANES...  7.16 us
    ppermute x7, starting transfers between devices, around(): return lax.ppermute(value, 'space', pairs)  6.77 us
    pallas_call x1, Pallas kernels, late_heads(): pl.pallas_call(functools.partial(late_kernel, heads=heads), out_shape=[ja...  6.05 us
  transfers between devices with their start and end apart: 21, of which 9 were waited for; matrix products, arithmetic and copies ran while one was open for 0% of the time, Pallas kernels for 22%

profile of v2, /device:TPU:0, one launch (start us, length us, event | category | flops | bytes accessed | tf_op | source)
XLA Modules:
  0.0 100.9 jit_solution(6685433016488392647)
XLA Ops:
  0.0 1.1 %fusion = (bf16[64,1024]{1,0:T(8,128)(2,1)S(1)}, bf16[64,1024]{1,0:T(8,128)(2,1)S(1)}, bf16[64,1024]{1,0:T(8,128)(2,1)S(1)}) fusion(bf16[192,1024]{1,0:T(8,128)(2,1)} %bitcast.4), kind=kLoop, calls=%fused_computation.3 | loop fusion | bytes 786432 | tf_op jit(solution)/shard_map/slice | solution.py:513
  1.1 0.5 collective-permute-start
  1.6 1.0 collective-permute-done
  2.6 0.1 maximum_select_fusion.refs_6_
  2.7 2.9 %collective-permute-start.2 = (bf16[96,1024]{1,0:T(8,128)(2,1)S(1)}, bf16[96,1024]{1,0:T(8,128)(2,1)S(1)}, u32[]{:S(2)}, u32[]{:S(2)}) collective-permute-start(bf16[96,1024]{1,0:T(8,128)(2,1)S(1)} %constant_dynamic-slice_fusion), channel_id=1, source_target_pairs={{0,2},{1,3},{4,0},{5,1},{8,4},{9,5},{12,8},{13,9},{14,12},{15,13},... | collective-permute-start | bytes 589832 | tf_op jit(solution)/shard_map/ppermute | solution.py:500
  5.6 0.1 collective-permute-start.1
  5.7 7.2 %tables.1 = (bf16[1024,128]{1,0:T(8,128)(2,1)}, bf16[1024,128]{1,0:T(8,128)(2,1)}, f32[1,1024]{1,0:T(1,128)}, bf16[2,1024,512]{2,1,0:T(8,128)(2,1)}, bf16[2,64,512]{2,1,0:T(8,128)(2,1)}) custom-call(s32[64]{0:T(128)} %order_ref.1, bf16[64,16,1024]{2,1,0:T(8,128)(2,1)} %embed_hbm, bf16[64,1024]{1,0:T(8,128)(2,1)} %var_embed_hbm.1, bf16[16,1024]{1,0:T(8,128)(2,1)} %keys_hbm.1, ...), custom_call_target="tpu_custom_call" | custom-call | flops 5000000000 | bytes 7340032 | tf_op jit(solution)/shard_map/tables/pallas_call | solution.py:300
  12.9 0.0 collective-permute-done.2.refs_8_
  12.9 0.0 collective-permute-done.1.refs_7_
  12.9 1.9 %collective-permute-start.7 = (bf16[96,1024]{1,0:T(8,128)(2,1)S(1)}, bf16[96,1024]{1,0:T(8,128)(2,1)S(1)}, u32[]{:S(2)}, u32[]{:S(2)}) collective-permute-start(bf16[96,1024]{1,0:T(8,128)(2,1)S(1)} %collective-permute-done.1.refs_7_), channel_id=1, source_target_pairs={{0,16},{16,0},{1,17},{17,1},{2,18},{18,2},{3,19},{19,3},{4,20},{20... | collective-permute-start | bytes 589832 | tf_op jit(solution)/shard_map/ppermute | solution.py:504
  14.9 1.6 %collective-permute-start.3 = (bf16[96,1024]{1,0:T(8,128)(2,1)S(1)}, bf16[96,1024]{1,0:T(8,128)(2,1)S(1)}, u32[]{:S(2)}, u32[]{:S(2)}) collective-permute-start(bf16[96,1024]{1,0:T(8,128)(2,1)S(1)} %collective-permute-done.1.refs_7_), channel_id=1, source_target_pairs={{0,4},{1,5},{4,8},{5,9},{8,12},{9,13},{12,14},{13,15},{14,10},{15,... | collective-permute-start | bytes 589832 | tf_op jit(solution)/shard_map/ppermute | solution.py:500
  16.4 0.5 collective-permute-start.8
  17.0 0.1 collective-permute-start.4
  17.0 8.6 %early_heads.1 = (bf16[256,1024]{1,0:T(8,128)(2,1)}, bf16[256,512]{1,0:T(8,128)(2,1)}) custom-call(bf16[256,1024]{1,0:T(8,128)(2,1)} %patches_hbm.1, bf16[1024,128]{1,0:T(8,128)(2,1)} %get-tuple-element.42.high_hbm, bf16[1024,128]{1,0:T(8,128)(2,1)} %get-tuple-element.43.low_hbm, f32[1,1024]{1,0:T(1,128)} %get-tuple-element.44.row_hbm, ...), custom_call_target="tpu_custom_call" | custom-call | flops 6000000000 | bytes 6291456 | tf_op jit(solution)/shard_map/early_heads/pallas_call | solution.py:323
  25.7 0.0 collective-permute-done.3.refs_9_
  25.7 0.0 collective-permute-done.4.refs_10_
  25.7 1.9 %collective-permute-start.13 = (bf16[96,1024]{1,0:T(8,128)(2,1)S(1)}, bf16[96,1024]{1,0:T(8,128)(2,1)S(1)}, u32[]{:S(2)}, u32[]{:S(2)}) collective-permute-start(bf16[96,1024]{1,0:T(8,128)(2,1)S(1)} %collective-permute-done.3.refs_9_), channel_id=1, source_target_pairs={{0,16},{16,0},{1,17},{17,1},{2,18},{18,2},{3,19},{19,3},{4,20},{20... | collective-permute-start | bytes 589832 | tf_op jit(solution)/shard_map/ppermute | solution.py:504
  27.6 1.6 %collective-permute-start.5 = (bf16[96,1024]{1,0:T(8,128)(2,1)S(1)}, bf16[96,1024]{1,0:T(8,128)(2,1)S(1)}, u32[]{:S(2)}, u32[]{:S(2)}) collective-permute-start(bf16[96,1024]{1,0:T(8,128)(2,1)S(1)} %collective-permute-done.3.refs_9_), channel_id=1, source_target_pairs={{0,4},{1,5},{4,8},{5,9},{8,12},{9,13},{12,14},{13,15},{14,10},{15,... | collective-permute-start | bytes 589832 | tf_op jit(solution)/shard_map/ppermute | solution.py:500
  29.2 0.4 collective-permute-start.6
  29.7 6.1 %late_heads.1 = (bf16[256,1024]{1,0:T(8,128)(2,1)}, bf16[256,1024]{1,0:T(8,128)(2,1)}) custom-call(bf16[256,1024]{1,0:T(8,128)(2,1)} %patches_hbm.1, bf16[256,1024]{1,0:T(8,128)(2,1)} %get-tuple-element.47.probs_hbm, bf16[256,512]{1,0:T(8,128)(2,1)} %get-tuple-element.51.half_hbm, bf16[2,1024,512]{2,1,0:T(8,128)(2,1)} %get-tuple-element.45.values_hbm, ...), custom_call_target="tpu_custom_call" | custom-call | flops 6000000000 | bytes 6291456 | tf_op jit(solution)/shard_map/late_heads/pallas_call | solution.py:347
  35.7 0.0 collective-permute-done.7.refs_11_
  35.7 0.2 collective-permute-start.14
  36.0 0.0 collective-permute-done.8.refs_12_
  36.0 0.0 collective-permute-done.5.refs_15_
  36.0 0.0 collective-permute-done.6.refs_16_
  36.0 5.0 %collective-permute-start.11 = (bf16[256,1024]{1,0:T(8,128)(2,1)}, bf16[256,1024]{1,0:T(8,128)(2,1)S(1)}, u32[]{:S(2)}, u32[]{:S(2)}) collective-permute-start(bf16[256,1024]{1,0:T(8,128)(2,1)} %get-tuple-element.56.refs_0_), channel_id=1, source_target_pairs={{2,0},{3,1},{4,2},{5,3},{6,4},{7,5},{8,6},{9,7},{10,8},{11,9},{12,... | collective-permute-start | bytes 1572872 | tf_op jit(solution)/shard_map/ppermute | solution.py:491
  41.0 0.0 collective-permute-start.10
  41.0 0.0 copy-start.2
  41.0 0.0 copy-start
  41.0 0.1 collective-permute-start.12
  41.1 0.0 collective-permute-done.13.refs_13_
  41.1 0.4 collective-permute-done.14.refs_14_
  41.5 19.5 %collective-permute-done.12.refs_17_ = bf16[96,1024]{1,0:T(8,128)(2,1)S(1)} collective-permute-done((bf16[96,1024]{1,0:T(8,128)(2,1)S(1)}, bf16[96,1024]{1,0:T(8,128)(2,1)S(1)}, u32[]{:S(2)}, u32[]{:S(2)}) %collective-permute-start.12) | collective-permute-done | bytes 196640 | tf_op jit(solution)/shard_map/ppermute | solution.py:500
  61.0 1.6 %collective-permute-start.15 = (bf16[96,1024]{1,0:T(8,128)(2,1)S(1)}, bf16[96,1024]{1,0:T(8,128)(2,1)S(1)}, u32[]{:S(2)}, u32[]{:S(2)}) collective-permute-start(bf16[96,1024]{1,0:T(8,128)(2,1)S(1)} %collective-permute-done.5.refs_15_), channel_id=1, source_target_pairs={{0,16},{16,0},{1,17},{17,1},{2,18},{18,2},{3,19},{19,3},{4,20},{20... | collective-permute-start | bytes 589832 | tf_op jit(solution)/shard_map/ppermute | solution.py:504
  62.6 0.4 collective-permute-start.16
  63.0 1.6 %collective-permute-start.17 = (bf16[96,1024]{1,0:T(8,128)(2,1)S(1)}, bf16[96,1024]{1,0:T(8,128)(2,1)S(1)}, u32[]{:S(2)}, u32[]{:S(2)}) collective-permute-start(bf16[96,1024]{1,0:T(8,128)(2,1)S(1)} %collective-permute-done.12.refs_17_), channel_id=1, source_target_pairs={{0,16},{16,0},{1,17},{17,1},{2,18},{18,2},{3,19},{19,3},{4,20},{20... | collective-permute-start | bytes 589832 | tf_op jit(solution)/shard_map/ppermute | solution.py:504
  64.6 4.1 %collective-permute-done.15.refs_18_ = bf16[96,1024]{1,0:T(8,128)(2,1)S(1)} collective-permute-done((bf16[96,1024]{1,0:T(8,128)(2,1)S(1)}, bf16[96,1024]{1,0:T(8,128)(2,1)S(1)}, u32[]{:S(2)}, u32[]{:S(2)}) %collective-permute-start.15) | collective-permute-done | bytes 196640 | tf_op jit(solution)/shard_map/ppermute | solution.py:504
  68.8 0.0 collective-permute-start.9
  68.8 4.2 %collective-permute-done.16.refs_19_ = bf16[96,1024]{1,0:T(8,128)(2,1)S(1)} collective-permute-done((bf16[96,1024]{1,0:T(8,128)(2,1)S(1)}, bf16[96,1024]{1,0:T(8,128)(2,1)S(1)}, u32[]{:S(2)}, u32[]{:S(2)}) %collective-permute-start.16) | collective-permute-done | bytes 196640 | tf_op jit(solution)/shard_map/ppermute | solution.py:504
  73.0 3.4 %collective-permute-done.17.refs_20_ = bf16[96,1024]{1,0:T(8,128)(2,1)S(1)} collective-permute-done((bf16[96,1024]{1,0:T(8,128)(2,1)S(1)}, bf16[96,1024]{1,0:T(8,128)(2,1)S(1)}, u32[]{:S(2)}, u32[]{:S(2)}) %collective-permute-start.17) | collective-permute-done | bytes 196640 | tf_op jit(solution)/shard_map/ppermute | solution.py:504
  76.4 0.0 collective-permute-done.11.refs_4_
  76.4 0.0 collective-permute-done.10.refs_2_
  76.4 0.0 collective-permute-start.18
  76.4 0.5 collective-permute-start.19
  76.9 0.0 collective-permute-done.9.refs_1_
  76.9 1.4 %collective-permute-done.18.refs_3_ = bf16[256,1024]{1,0:T(8,128)(2,1)S(1)} collective-permute-done((bf16[256,1024]{1,0:T(8,128)(2,1)S(1)}, bf16[256,1024]{1,0:T(8,128)(2,1)S(1)}, u32[]{:S(2)}, u32[]{:S(2)}) %collective-permute-start.18) | collective-permute-done | bytes 524320 | tf_op jit(solution)/shard_map/ppermute | solution.py:486
  78.3 0.7 collective-permute-done.19.refs_5_
  79.1 0.0 copy-start.1
  79.1 1.0 %copy-done.1 = bf16[256,1024]{1,0:T(8,128)(2,1)S(1)} copy-done((bf16[256,1024]{1,0:T(8,128)(2,1)S(1)}, bf16[256,1024]{1,0:T(8,128)(2,1)}, u32[]{:S(2)}) %copy-start.1) | copy-done | bytes 524312
  80.1 17.7 %attend.1 = (bf16[4,256,128]{2,1,0:T(8,128)(2,1)S(1)}, bf16[4,256,128]{2,1,0:T(8,128)(2,1)S(1)}) custom-call(bf16[256,1024]{1,0:T(8,128)(2,1)S(1)} %copy-done.1, bf16[256,1024]{1,0:T(8,128)(2,1)S(1)} %collective-permute-done.9.refs_1_, bf16[256,1024]{1,0:T(8,128)(2,1)S(1)} %collective-permute-done.10.refs_2_, ...), custom_call_target="tpu_custom_call" | custom-call | flops 10000000000 | bytes 8388608 | tf_op jit(solution)/shard_map/attend/pallas_call | solution.py:439
  97.8 0.2 collective-permute-start.20
  98.0 1.4 %collective-permute-done.20.other_ref = bf16[4,256,128]{2,1,0:T(8,128)(2,1)S(1)} collective-permute-done((bf16[4,256,128]{2,1,0:T(8,128)(2,1)S(1)}, bf16[4,256,128]{2,1,0:T(8,128)(2,1)S(1)}, u32[]{:S(2)}, u32[]{:S(2)}) %collective-permute-start.20) | collective-permute-done | bytes 262176 | tf_op jit(solution)/shard_map/ppermute | solution.py:486
  99.4 0.0 copy-done.2
  99.4 0.0 copy-done
  99.4 1.5 %finish.1 = bf16[256,1024]{1,0:T(8,128)(2,1)} custom-call(bf16[256,1024]{1,0:T(8,128)(2,1)S(1)} %copy-done.2, bf16[4,256,128]{2,1,0:T(8,128)(2,1)S(1)} %get-tuple-element.71.mine_ref, bf16[4,256,128]{2,1,0:T(8,128)(2,1)S(1)} %collective-permute-done.20.other_ref, bf16[8,2,64,1024]{3,2,1,0:T(8,128)(2,1)S(1)} %bitcast.3), custom_call_target="tpu_custom_call" | custom-call | flops 1000000000 | bytes 4194304 | tf_op jit(solution)/shard_map/finish/pallas_call | solution.py:473
  (2 shorter events, 0.0 us)
Async XLA Ops:
  1.1 1.5 %collective-permute-start = (bf16[64,1024]{1,0:T(8,128)(2,1)S(1)}, bf16[64,1024]{1,0:T(8,128)(2,1)S(1)}, u32[]{:S(2)}, u32[]{:S(2)}) collective-permute-start(bf16[64,1024]{1,0:T(8,128)(2,1)S(1)} %get-tuple-element.74), channel_id=1, source_target_pairs={{0,1},{1,0},{2,3},{3,2},{4,5},{5,4},{6,7},{7,6},{8,9},{9,8},{10,11... | collective-permute-start | bytes 393224 | tf_op jit(solution)/shard_map/ppermute | solution.py:486
  2.7 10.2 %collective-permute-start.2 = (bf16[96,1024]{1,0:T(8,128)(2,1)S(1)}, bf16[96,1024]{1,0:T(8,128)(2,1)S(1)}, u32[]{:S(2)}, u32[]{:S(2)}) collective-permute-start(bf16[96,1024]{1,0:T(8,128)(2,1)S(1)} %constant_dynamic-slice_fusion), channel_id=1, source_target_pairs={{0,2},{1,3},{4,0},{5,1},{8,4},{9,5},{12,8},{13,9},{14,12},{15,13},... | collective-permute-start | bytes 589832 | tf_op jit(solution)/shard_map/ppermute | solution.py:500
  5.6 7.3 %collective-permute-start.1 = (bf16[96,1024]{1,0:T(8,128)(2,1)S(1)}, bf16[96,1024]{1,0:T(8,128)(2,1)S(1)}, u32[]{:S(2)}, u32[]{:S(2)}) collective-permute-start(bf16[96,1024]{1,0:T(8,128)(2,1)S(1)} %constant_dynamic-slice_fusion), channel_id=1, source_target_pairs={{0,4},{1,5},{4,8},{5,9},{8,12},{9,13},{12,14},{13,15},{14,10},{15,... | collective-permute-start | bytes 589832 | tf_op jit(solution)/shard_map/ppermute | solution.py:500
  12.9 22.8 %collective-permute-start.7 = (bf16[96,1024]{1,0:T(8,128)(2,1)S(1)}, bf16[96,1024]{1,0:T(8,128)(2,1)S(1)}, u32[]{:S(2)}, u32[]{:S(2)}) collective-permute-start(bf16[96,1024]{1,0:T(8,128)(2,1)S(1)} %collective-permute-done.1.refs_7_), channel_id=1, source_target_pairs={{0,16},{16,0},{1,17},{17,1},{2,18},{18,2},{3,19},{19,3},{4,20},{20... | collective-permute-start | bytes 589832 | tf_op jit(solution)/shard_map/ppermute | solution.py:504
  14.9 10.8 %collective-permute-start.3 = (bf16[96,1024]{1,0:T(8,128)(2,1)S(1)}, bf16[96,1024]{1,0:T(8,128)(2,1)S(1)}, u32[]{:S(2)}, u32[]{:S(2)}) collective-permute-start(bf16[96,1024]{1,0:T(8,128)(2,1)S(1)} %collective-permute-done.1.refs_7_), channel_id=1, source_target_pairs={{0,4},{1,5},{4,8},{5,9},{8,12},{9,13},{12,14},{13,15},{14,10},{15,... | collective-permute-start | bytes 589832 | tf_op jit(solution)/shard_map/ppermute | solution.py:500
  16.4 19.5 %collective-permute-start.8 = (bf16[96,1024]{1,0:T(8,128)(2,1)S(1)}, bf16[96,1024]{1,0:T(8,128)(2,1)S(1)}, u32[]{:S(2)}, u32[]{:S(2)}) collective-permute-start(bf16[96,1024]{1,0:T(8,128)(2,1)S(1)} %collective-permute-done.2.refs_8_), channel_id=1, source_target_pairs={{0,16},{16,0},{1,17},{17,1},{2,18},{18,2},{3,19},{19,3},{4,20},{20... | collective-permute-start | bytes 589832 | tf_op jit(solution)/shard_map/ppermute | solution.py:504
  17.0 8.7 %collective-permute-start.4 = (bf16[96,1024]{1,0:T(8,128)(2,1)S(1)}, bf16[96,1024]{1,0:T(8,128)(2,1)S(1)}, u32[]{:S(2)}, u32[]{:S(2)}) collective-permute-start(bf16[96,1024]{1,0:T(8,128)(2,1)S(1)} %collective-permute-done.2.refs_8_), channel_id=1, source_target_pairs={{0,2},{1,3},{4,0},{5,1},{8,4},{9,5},{12,8},{13,9},{14,12},{15,13},... | collective-permute-start | bytes 589832 | tf_op jit(solution)/shard_map/ppermute | solution.py:500
  25.7 15.4 %collective-permute-start.13 = (bf16[96,1024]{1,0:T(8,128)(2,1)S(1)}, bf16[96,1024]{1,0:T(8,128)(2,1)S(1)}, u32[]{:S(2)}, u32[]{:S(2)}) collective-permute-start(bf16[96,1024]{1,0:T(8,128)(2,1)S(1)} %collective-permute-done.3.refs_9_), channel_id=1, source_target_pairs={{0,16},{16,0},{1,17},{17,1},{2,18},{18,2},{3,19},{19,3},{4,20},{20... | collective-permute-start | bytes 589832 | tf_op jit(solution)/shard_map/ppermute | solution.py:504
  27.6 8.3 %collective-permute-start.5 = (bf16[96,1024]{1,0:T(8,128)(2,1)S(1)}, bf16[96,1024]{1,0:T(8,128)(2,1)S(1)}, u32[]{:S(2)}, u32[]{:S(2)}) collective-permute-start(bf16[96,1024]{1,0:T(8,128)(2,1)S(1)} %collective-permute-done.3.refs_9_), channel_id=1, source_target_pairs={{0,4},{1,5},{4,8},{5,9},{8,12},{9,13},{12,14},{13,15},{14,10},{15,... | collective-permute-start | bytes 589832 | tf_op jit(solution)/shard_map/ppermute | solution.py:500
  29.2 6.7 %collective-permute-start.6 = (bf16[96,1024]{1,0:T(8,128)(2,1)S(1)}, bf16[96,1024]{1,0:T(8,128)(2,1)S(1)}, u32[]{:S(2)}, u32[]{:S(2)}) collective-permute-start(bf16[96,1024]{1,0:T(8,128)(2,1)S(1)} %collective-permute-done.4.refs_10_), channel_id=1, source_target_pairs={{0,2},{1,3},{4,0},{5,1},{8,4},{9,5},{12,8},{13,9},{14,12},{15,13},... | collective-permute-start | bytes 589832 | tf_op jit(solution)/shard_map/ppermute | solution.py:500
  35.7 5.7 %collective-permute-start.14 = (bf16[96,1024]{1,0:T(8,128)(2,1)S(1)}, bf16[96,1024]{1,0:T(8,128)(2,1)S(1)}, u32[]{:S(2)}, u32[]{:S(2)}) collective-permute-start(bf16[96,1024]{1,0:T(8,128)(2,1)S(1)} %collective-permute-done.4.refs_10_), channel_id=1, source_target_pairs={{0,16},{16,0},{1,17},{17,1},{2,18},{18,2},{3,19},{19,3},{4,20},{20... | collective-permute-start | bytes 589832 | tf_op jit(solution)/shard_map/ppermute | solution.py:504
  36.0 40.4 %collective-permute-start.11 = (bf16[256,1024]{1,0:T(8,128)(2,1)}, bf16[256,1024]{1,0:T(8,128)(2,1)S(1)}, u32[]{:S(2)}, u32[]{:S(2)}) collective-permute-start(bf16[256,1024]{1,0:T(8,128)(2,1)} %get-tuple-element.56.refs_0_), channel_id=1, source_target_pairs={{2,0},{3,1},{4,2},{5,3},{6,4},{7,5},{8,6},{9,7},{10,8},{11,9},{12,... | collective-permute-start | bytes 1572872 | tf_op jit(solution)/shard_map/ppermute | solution.py:491
  41.0 35.5 %collective-permute-start.10 = (bf16[256,1024]{1,0:T(8,128)(2,1)}, bf16[256,1024]{1,0:T(8,128)(2,1)S(1)}, u32[]{:S(2)}, u32[]{:S(2)}) collective-permute-start(bf16[256,1024]{1,0:T(8,128)(2,1)} %get-tuple-element.56.refs_0_), channel_id=1, source_target_pairs={{14,0},{15,1},{0,2},{1,3},{2,4},{3,5},{4,6},{5,7},{6,8},{7,9},{8,1... | collective-permute-start | bytes 1572872 | tf_op jit(solution)/shard_map/ppermute | solution.py:491
  41.0 58.4 %copy-start.2 = (bf16[256,1024]{1,0:T(8,128)(2,1)S(1)}, bf16[256,1024]{1,0:T(8,128)(2,1)}, u32[]{:S(2)}) copy-start(bf16[256,1024]{1,0:T(8,128)(2,1)} %get-tuple-element.52.tokens_ref) | copy-start | bytes 1572868
  41.0 58.4 %copy-start = (bf16[1024,1024]{1,0:T(8,128)(2,1)S(1)}, bf16[1024,1024]{1,0:T(8,128)(2,1)}, u32[]{:S(2)}) copy-start(bf16[1024,1024]{1,0:T(8,128)(2,1)} %param.21) | copy-start | bytes 6291460
  41.0 20.0 %collective-permute-start.12 = (bf16[96,1024]{1,0:T(8,128)(2,1)S(1)}, bf16[96,1024]{1,0:T(8,128)(2,1)S(1)}, u32[]{:S(2)}, u32[]{:S(2)}) collective-permute-start(bf16[96,1024]{1,0:T(8,128)(2,1)S(1)} %broadcast_select_fusion), channel_id=1, source_target_pairs={{0,4},{1,3},{4,8},{5,1},{8,12},{9,5},{12,14},{13,9},{14,10},{15,13... | collective-permute-start | bytes 589832 | tf_op jit(solution)/shard_map/ppermute | solution.py:500
  61.0 7.7 %collective-permute-start.15 = (bf16[96,1024]{1,0:T(8,128)(2,1)S(1)}, bf16[96,1024]{1,0:T(8,128)(2,1)S(1)}, u32[]{:S(2)}, u32[]{:S(2)}) collective-permute-start(bf16[96,1024]{1,0:T(8,128)(2,1)S(1)} %collective-permute-done.5.refs_15_), channel_id=1, source_target_pairs={{0,16},{16,0},{1,17},{17,1},{2,18},{18,2},{3,19},{19,3},{4,20},{20... | collective-permute-start | bytes 589832 | tf_op jit(solution)/shard_map/ppermute | solution.py:504
  62.6 10.4 %collective-permute-start.16 = (bf16[96,1024]{1,0:T(8,128)(2,1)S(1)}, bf16[96,1024]{1,0:T(8,128)(2,1)S(1)}, u32[]{:S(2)}, u32[]{:S(2)}) collective-permute-start(bf16[96,1024]{1,0:T(8,128)(2,1)S(1)} %collective-permute-done.6.refs_16_), channel_id=1, source_target_pairs={{0,16},{16,0},{1,17},{17,1},{2,18},{18,2},{3,19},{19,3},{4,20},{20... | collective-permute-start | bytes 589832 | tf_op jit(solution)/shard_map/ppermute | solution.py:504
  63.0 13.4 %collective-permute-start.17 = (bf16[96,1024]{1,0:T(8,128)(2,1)S(1)}, bf16[96,1024]{1,0:T(8,128)(2,1)S(1)}, u32[]{:S(2)}, u32[]{:S(2)}) collective-permute-start(bf16[96,1024]{1,0:T(8,128)(2,1)S(1)} %collective-permute-done.12.refs_17_), channel_id=1, source_target_pairs={{0,16},{16,0},{1,17},{17,1},{2,18},{18,2},{3,19},{19,3},{4,20},{20... | collective-permute-start | bytes 589832 | tf_op jit(solution)/shard_map/ppermute | solution.py:504
  68.8 8.2 %collective-permute-start.9 = (bf16[256,1024]{1,0:T(8,128)(2,1)}, bf16[256,1024]{1,0:T(8,128)(2,1)S(1)}, u32[]{:S(2)}, u32[]{:S(2)}) collective-permute-start(bf16[256,1024]{1,0:T(8,128)(2,1)} %get-tuple-element.56.refs_0_), channel_id=1, source_target_pairs={{0,1},{1,0},{2,3},{3,2},{4,5},{5,4},{6,7},{7,6},{8,9},{9,8},{10,11... | collective-permute-start | bytes 1572872 | tf_op jit(solution)/shard_map/ppermute | solution.py:486
  76.4 1.9 %collective-permute-start.18 = (bf16[256,1024]{1,0:T(8,128)(2,1)S(1)}, bf16[256,1024]{1,0:T(8,128)(2,1)S(1)}, u32[]{:S(2)}, u32[]{:S(2)}) collective-permute-start(bf16[256,1024]{1,0:T(8,128)(2,1)S(1)} %collective-permute-done.10.refs_2_), channel_id=1, source_target_pairs={{0,1},{1,0},{2,3},{3,2},{4,5},{5,4},{6,7},{7,6},{8,9},{9,8},{10,11... | collective-permute-start | bytes 1572872 | tf_op jit(solution)/shard_map/ppermute | solution.py:486
  76.4 2.7 %collective-permute-start.19 = (bf16[256,1024]{1,0:T(8,128)(2,1)S(1)}, bf16[256,1024]{1,0:T(8,128)(2,1)S(1)}, u32[]{:S(2)}, u32[]{:S(2)}) collective-permute-start(bf16[256,1024]{1,0:T(8,128)(2,1)S(1)} %collective-permute-done.11.refs_4_), channel_id=1, source_target_pairs={{0,1},{1,0},{2,3},{3,2},{4,5},{5,4},{6,7},{7,6},{8,9},{9,8},{10,11... | collective-permute-start | bytes 1572872 | tf_op jit(solution)/shard_map/ppermute | solution.py:486
  79.1 1.0 %copy-start.1 = (bf16[256,1024]{1,0:T(8,128)(2,1)S(1)}, bf16[256,1024]{1,0:T(8,128)(2,1)}, u32[]{:S(2)}) copy-start(bf16[256,1024]{1,0:T(8,128)(2,1)} %get-tuple-element.56.refs_0_) | copy-start | bytes 1572868
  97.8 1.6 %collective-permute-start.20 = (bf16[4,256,128]{2,1,0:T(8,128)(2,1)S(1)}, bf16[4,256,128]{2,1,0:T(8,128)(2,1)S(1)}, u32[]{:S(2)}, u32[]{:S(2)}) collective-permute-start(bf16[4,256,128]{2,1,0:T(8,128)(2,1)S(1)} %get-tuple-element.72), channel_id=1, source_target_pairs={{0,1},{1,0},{2,3},{3,2},{4,5},{5,4},{6,7},{7,6},{8,9},{9,8},{10,11... | collective-permute-start | bytes 786440 | tf_op jit(solution)/shard_map/ppermute | solution.py:486

commit v3 on v2

--- a/solution.py
+++ b/solution.py
@@ -42,72 +42,6 @@
     for copy in copies:
         copy.start()
     return [copy.wait for copy in copies]
-
-
-def table_kernel(
-    order_ref,
-    embed_hbm,
-    var_embed_hbm,
-    keys_hbm,
-    value_hbm,
-    high_ref,
-    low_ref,
-    row_ref,
-    values_ref,
-    offset_ref,
-    embed_ref,
-    var_embed_ref,
-    keys_ref,
-    value_ref,
-    table_ref,
-    sems,
-):
-    var_count, pixels, width = embed_ref.shape
-    heads = keys_ref.shape[0]
-    spread = var_count * heads
-    waits = fetch(
-        (
-            (var_embed_hbm, var_embed_ref),
-            (keys_hbm, keys_ref),
-            (embed_hbm, embed_ref),
-            (value_hbm, value_ref),
-        ),
-        sems,
-    )
-    line = iota((var_count, var_count), 0)
-    order = jnp.zeros((var_count, var_count), jnp.int32)
-    for j in range(var_count):
-        order = jnp.where(line == j, order_ref[j], order)
-    select = (order == iota((var_count, var_count), 1)).astype(F32).astype(BF16)
-    waits[0]()
-    offsets = dot(select, var_embed_ref[...]).astype(BF16)
-    waits[1]()
-    repeat = (iota((LANES, heads), 0) % heads == iota((LANES, heads), 1)).astype(F32).astype(BF16)
-    keys = dot(repeat, keys_ref[...]).astype(BF16)
-    waits[2]()
-    for j in range(var_count):
-        table_ref[j] = embed_ref[order_ref[j]]
-    table = table_ref[...].reshape(var_count * pixels, width)
-    table_keys = dot_t(table, keys)
-    offset_keys = dot_t(offsets, keys)
-    high = table_keys.astype(BF16)
-    high_ref[...] = high
-    low_ref[...] = (table_keys - high.astype(F32)).astype(BF16)
-    for block in range(spread // LANES):
-        cols = slice(block * LANES, (block + 1) * LANES)
-        channel = (iota((var_count, LANES), 1) + block * LANES) // heads
-        row_ref[:, cols] = jnp.sum(
-            jnp.where(channel == iota((var_count, LANES), 0), offset_keys, 0.0),
-            axis=0,
-            keepdims=True,
-        )
-    waits[3]()
-    values = dot(table, value_ref[...]).astype(BF16)
-    offset_values = dot(offsets, value_ref[...]).astype(BF16)
-    half = width // 2
-    for side in range(2):
-        values_ref[side] = values[:, side * half : (side + 1) * half]
-        offset_ref[side] = offset_values[:, side * half : (side + 1) * half]
 
 
 def spread_offsets(offset_half, heads, head_size, first):
@@ -143,53 +77,86 @@
     return jnp.concatenate(values, axis=1)
 
 
-def early_kernel(
+def aggregate_kernel(
+    order_ref,
+    var_embed_hbm,
+    keys_hbm,
+    embed_hbm,
     patches_hbm,
-    high_hbm,
-    low_hbm,
-    row_hbm,
-    values_hbm,
-    offset_hbm,
-    probs_ref,
-    half_ref,
+    value_hbm,
+    out_w_hbm,
+    pos_hbm,
+    gain_hbm,
+    tokens_ref,
+    normed_ref,
+    var_embed_ref,
+    keys_ref,
+    embed_ref,
     patches_ref,
-    high_ref,
-    low_ref,
-    row_ref,
+    value_ref,
+    out_w_ref,
+    pos_ref,
+    gain_ref,
+    table_ref,
     values_ref,
-    offset_ref,
     sems,
-    *,
-    heads,
 ):
+    var_count, pixels, width = embed_ref.shape
+    heads = keys_ref.shape[0]
+    head_size = width // heads
+    rows, spread = var_count * pixels, var_count * heads
+    scale = 1.0 / math.sqrt(head_size)
     waits = fetch(
         (
-            (high_hbm, high_ref),
-            (low_hbm, low_ref),
-            (row_hbm, row_ref),
+            (var_embed_hbm, var_embed_ref),
+            (keys_hbm, keys_ref),
+            (embed_hbm, embed_ref),
             (patches_hbm, patches_ref),
-            (offset_hbm.at[0], offset_ref),
-            (values_hbm.at[0], values_ref),
+            (value_hbm, value_ref),
+            (out_w_hbm, out_w_ref),
+            (pos_hbm, pos_ref),
+            (gain_hbm, gain_ref),
         ),
         sems,
     )
-    spread = row_ref.shape[1]
-    head_size = offset_ref.shape[1] * 2 // heads
-    rows = high_ref.shape[0]
-    pixels = rows * heads // spread
-    scale = 1.0 / math.sqrt(head_size)
-    for wait in waits[:4]:
-        wait()
+    line = iota((var_count, var_count), 0)
+    order = jnp.zeros((var_count, var_count), jnp.int32)
+    for j in range(var_count):
+        order = jnp.where(line == j, order_ref[j], order)
+    select = (order == iota((var_count, var_count), 1)).astype(F32).astype(BF16)
+    waits[0]()
+    offsets = dot(select, var_embed_ref[...]).astype(BF16)
+    waits[1]()
+    repeat = (iota((LANES, heads), 0) % heads == iota((LANES, heads), 1)).astype(F32).astype(BF16)
+    keys = dot(repeat, keys_ref[...]).astype(BF16)
+    offset_keys = dot_t(offsets, keys)
+    waits[2]()
+    for j in range(var_count):
+        table_ref[j] = embed_ref[order_ref[j]]
+    table = table_ref[...].reshape(rows, width)
+    table_keys = dot_t(table, keys)
+    high = table_keys.astype(BF16)
+    low = (table_keys - high.astype(F32)).astype(BF16)
+    waits[3]()
     patches = patches_ref[...]
-    high, low = high_ref[...], low_ref[...]
     rows_of = iota((rows, LANES), 0) // pixels
     cols_of = iota((rows, LANES), 1) // heads
+    channel = iota((var_count, LANES), 1) // heads
     scores = []
     for block in range(spread // LANES):
-        here = rows_of == cols_of + block * (LANES // heads)
+        first = block * (LANES // heads)
+        here = rows_of == cols_of + first
+        row = jnp.sum(
+            jnp.where(channel + first == iota((var_count, LANES), 0), offset_keys, 0.0),
+            axis=0,
+            keepdims=True,
+        )
         part = dot(patches, jnp.where(here, high, jnp.zeros_like(high)))
         part = part + dot(patches, jnp.where(here, low, jnp.zeros_like(low)))
-        scores.append((part + row_ref[:, block * LANES : (block + 1) * LANES]) * scale)
+        scores.append((part + row) * scale)
+    waits[4]()
+    values_ref[...] = dot(table, value_ref[...]).astype(BF16)
+    offset_values = dot(offsets, value_ref[...]).astype(BF16)
     top = functools.reduce(jnp.maximum, scores)
     step = heads
     while step < LANES:
@@ -202,74 +169,12 @@
         total = total + pltpu.roll(total, step, 1)
         step *= 2
     probs = jnp.concatenate([(e / total).astype(BF16) for e in exps], axis=1)
-    probs_ref[...] = probs
-    waits[4]()
-    base = dot(probs, spread_offsets(offset_ref[...], heads, head_size, 0))
-    waits[5]()
-    half_ref[...] = mix_heads(
-        probs, patches, values_ref, base, 0, heads // 4, heads, head_size, pixels
-    )
-
-
-def late_kernel(
-    patches_hbm,
-    probs_hbm,
-    half_hbm,
-    values_hbm,
-    offset_hbm,
-    out_w_hbm,
-    pos_hbm,
-    gain_hbm,
-    tokens_ref,
-    normed_ref,
-    patches_ref,
-    probs_ref,
-    half_ref,
-    values_ref,
-    offset_ref,
-    out_w_ref,
-    pos_ref,
-    gain_ref,
-    sems,
-    *,
-    heads,
-):
-    waits = fetch(
-        (
-            (probs_hbm, probs_ref),
-            (offset_hbm.at[1], offset_ref),
-            (patches_hbm, patches_ref),
-            (values_hbm.at[1], values_ref),
-            (half_hbm, half_ref),
-            (out_w_hbm, out_w_ref),
-            (pos_hbm, pos_ref),
-            (gain_hbm, gain_ref),
-        ),
-        sems,
-    )
-    spread = probs_ref.shape[1]
-    head_size = out_w_ref.shape[0] // heads
-    pixels = patches_ref.shape[1] * heads // spread
-    waits[0]()
-    waits[1]()
-    probs = probs_ref[...]
-    base = dot(probs, spread_offsets(offset_ref[...], heads, head_size, heads // 2))
-    waits[2]()
-    waits[3]()
-    late = mix_heads(
-        probs,
-        patches_ref[...],
-        values_ref,
-        base,
-        heads // 2,
-        heads // 4,
-        heads,
-        head_size,
-        pixels,
-    )
-    for wait in waits[4:]:
+    base = dot(probs, spread_offsets(offset_values, heads, head_size, 0))
+    values = mix_heads(
+        probs, patches, values_ref, base, 0, heads // 2, heads, head_size, pixels
+    )
+    for wait in waits[5:]:
         wait()
-    values = jnp.concatenate([half_ref[...], late], axis=1)
     tokens_zero = (dot(values, out_w_ref[...]) + pos_ref[...].astype(F32)).astype(BF16)
     tokens_ref[...] = tokens_zero
     full = tokens_zero.astype(F32)
@@ -293,70 +198,23 @@
     return [pltpu.VMEM(a.shape, a.dtype) for a in arrays]
 
 
-def tables(var_order, embed_weight, var_embed, keys, value):
-    var_count, pixels, width = embed_weight.shape
-    heads = keys.shape[0]
-    rows, spread, half = var_count * pixels, var_count * heads, width // 2
+def aggregate(var_order, var_embed, keys, embed_weight, patches, value, out_w, pos, gain):
+    tokens, width = pos.shape
+    var_count, pixels, _ = embed_weight.shape
+    arrays = (var_embed, keys, embed_weight, patches, value, out_w, pos, gain.reshape(1, width))
     return pl.pallas_call(
-        table_kernel,
-        out_shape=[
-            jax.ShapeDtypeStruct((rows, LANES), BF16),
-            jax.ShapeDtypeStruct((rows, LANES), BF16),
-            jax.ShapeDtypeStruct((1, spread), F32),
-            jax.ShapeDtypeStruct((2, rows, half), BF16),
-            jax.ShapeDtypeStruct((2, var_count, half), BF16),
-        ],
-        in_specs=[SMEM] + [HBM] * 4,
-        out_specs=[VMEM] * 5,
-        scratch_shapes=like(embed_weight, var_embed, keys, value, embed_weight)
-        + [pltpu.SemaphoreType.DMA((4,))],
+        aggregate_kernel,
+        out_shape=[jax.ShapeDtypeStruct((tokens, width), BF16)] * 2,
+        in_specs=[SMEM] + [HBM] * len(arrays),
+        out_specs=[VMEM] * 2,
+        scratch_shapes=like(*arrays)
+        + like(embed_weight)
+        + [pltpu.VMEM((var_count * pixels, width), BF16)]
+        + [pltpu.SemaphoreType.DMA((len(arrays),))],
         compiler_params=pltpu.CompilerParams(vmem_limit_bytes=WHOLE_VMEM),
-        cost_estimate=cost(5, 7),
-        name="tables",
-    )(var_order, embed_weight, var_embed, keys, value)
-
-
-def early_heads(patches, made, heads):
-    high, low, row, values, offset = made
-    tokens = patches.shape[0]
-    half = values.shape[2]
-    return pl.pallas_call(
-        functools.partial(early_kernel, heads=heads),
-        out_shape=[
-            jax.ShapeDtypeStruct((tokens, row.shape[1]), BF16),
-            jax.ShapeDtypeStruct((tokens, half), BF16),
-        ],
-        in_specs=[HBM] * 6,
-        out_specs=[VMEM] * 2,
-        scratch_shapes=like(patches, high, low, row)
-        + [
-            pltpu.VMEM(values.shape[1:], BF16),
-            pltpu.VMEM(offset.shape[1:], BF16),
-            pltpu.SemaphoreType.DMA((6,)),
-        ],
-        compiler_params=pltpu.CompilerParams(vmem_limit_bytes=WHOLE_VMEM),
-        cost_estimate=cost(6, 6, 1 << 18),
-        name="early_heads",
-    )(patches, high, low, row, values, offset)
-
-
-def late_heads(patches, probs, early, made, out_w, pos, gain, heads):
-    values, offset = made[3:]
-    tokens, width = pos.shape
-    gain = gain.reshape(1, width)
-    return pl.pallas_call(
-        functools.partial(late_kernel, heads=heads),
-        out_shape=[jax.ShapeDtypeStruct((tokens, width), BF16)] * 2,
-        in_specs=[HBM] * 8,
-        out_specs=[VMEM] * 2,
-        scratch_shapes=like(patches, probs, early)
-        + [pltpu.VMEM(values.shape[1:], BF16), pltpu.VMEM(offset.shape[1:], BF16)]
-        + like(out_w, pos, gain)
-        + [pltpu.SemaphoreType.DMA((8,))],
-        compiler_params=pltpu.CompilerParams(vmem_limit_bytes=WHOLE_VMEM),
-        cost_estimate=cost(6, 6),
-        name="late_heads",
-    )(patches, probs, early, values, offset, out_w, pos, gain)
+        cost_estimate=cost(16, 8, 1 << 18),
+        name="aggregate",
+    )(var_order, *arrays)
 
 
 def attend_kernel(*refs, spots):
@@ -368,8 +226,17 @@
     moves = [(ref, rows_s.at[i]) for i, ref in enumerate(refs[:6])]
     for ref, (step, share) in zip(weight_refs, spots):
         rows = ref.shape[0]
-        start = 0 if share is None else pl.multiple_of((plane + share) % 2 * rows, 32)
-        moves.append((ref, weight_s.at[chip_at(index, step), pl.ds(start, rows), :]))
+        if share == "ring":
+            start = pl.multiple_of(plane * (rows // 2), 32)
+            moves.append((ref, weight_s.at[chip_at(index, step), pl.ds(start, rows), :]))
+        elif share == "swap":
+            rows = rows // len(step)
+            start = pl.multiple_of((1 - plane) * (2 * rows), 32)
+            for i, one in enumerate(step):
+                place = weight_s.at[chip_at(index, one), pl.ds(start, rows), :]
+                moves.append((ref.at[pl.ds(i * rows, rows), :], place))
+        else:
+            moves.append((ref, weight_s.at[chip_at(index, step)]))
     for wait in fetch(moves, sems):
         wait()
     own_ref, sib_ref, left_own_ref, left_sib_ref, right_own_ref, right_sib_ref = (
@@ -447,7 +314,7 @@
             pltpu.VMEM((6, cols, tokens), BF16),
             pltpu.VMEM((6, pairs, tokens, 2 * LANES), BF16),
             pltpu.VMEM((blocks, rows, width), BF16),
-            pltpu.SemaphoreType.DMA((6 + len(weights),)),
+            pltpu.SemaphoreType.DMA((32,)),
         ],
         compiler_params=pltpu.CompilerParams(vmem_limit_bytes=PART_VMEM),
         cost_estimate=cost(10, 8, 5 << 20),
@@ -550,40 +417,38 @@
     if ringed:
         block = parity_block(qkv_weight, side, head_size)
         block, embed_weight = together(block, embed_weight)
-        rows = block.shape[0] // 2
-        share = lax.dynamic_slice_in_dim(block, lax.axis_index("groups") * rows, rows, 0)
+        third = block.shape[0] // 3
+        plane = lax.axis_index("groups")
+        share = lax.dynamic_slice_in_dim(block, plane * third, 2 * third, 0)
+        early = [around(share, step) for step in (1, -1, 2, -2)]
         weights = [(block, (0, None))]
-        up1, down1 = around(share, 1), around(share, -1)
     else:
         weights = parity_weight(qkv_weight, side, head_size)
-    made = tables(var_order, embed_weight, var_embed, agg_keys, agg_value)
+    tokens_zero, normed = aggregate(
+        var_order, var_embed, agg_keys, embed_weight, patches, agg_value, agg_out, pos_embed, norm_gain
+    )
     if ringed:
-        patches, up1, down1 = together(patches, up1, down1)
-        up2, down2 = around(up1, 1), around(down1, -1)
-        weights += [(up1, (-1, 0)), (down1, (1, 0))]
-        near = across(up1), across(down1)
-    probs, early = early_heads(patches, made, heads)
-    if ringed:
-        early, up2, down2 = together(early, up2, down2)
-        up3, down3 = around(up2, 1), around(down2, -1)
-        weights += [(up2, (-2, 0)), (down2, (2, 0))]
-    tokens_zero, normed = late_heads(
-        patches, probs, early, made, agg_out, pos_embed, norm_gain, heads
-    )
-    if ringed:
-        normed, up3, down3, *near = together(normed, up3, down3, *near)
-        weights += [(near[0], (-1, 1)), (near[1], (1, 1))]
-        far = around(jnp.where(side == 0, up3, down3), (1, -1))
-        next_near = across(up2), across(down2)
-    left = from_chip(normed, -1)
-    right = from_chip(normed, 1)
-    if ringed:
-        up3, down3, far, *next_near = together(up3, down3, far, *next_near)
-        weights += [(next_near[0], (-2, 1)), (next_near[1], (2, 1))]
-        weights += [(up3, (-3, 0)), (down3, (3, 0)), (far, (4, 0))]
-        last = across(up3), across(down3), across(far)
-        left, right, *last = together(left, right, *last)
-        weights += [(last[0], (-3, 1)), (last[1], (3, 1)), (last[2], (4, 1))]
+
+        def swapped(blocks):
+            parts = [lax.dynamic_slice_in_dim(b, plane * third, third, 0) for b in blocks]
+            return across(jnp.concatenate(parts, axis=0))
+
+        normed, *early = together(normed, *early)
+        weights += [(b, (-step, "ring")) for b, step in zip(early, (1, -1, 2, -2))]
+        swap = swapped(early)
+        late = [around(early[2], 1), around(early[3], -1)]
+        late.append(around(jnp.where(side == 0, early[2], early[3]), (2, -2)))
+        left = from_chip(normed, -1)
+        right = from_chip(normed, 1)
+        swap, *late = together(swap, *late)
+        weights += [(b, (-step, "ring")) for b, step in zip(late, (3, -3, 4))]
+        weights.append((swap, ((-1, 1, -2, 2), "swap")))
+        last = swapped(late)
+        left, right, last = together(left, right, last)
+        weights.append((last, ((-3, 3, -4), "swap")))
+    else:
+        left = from_chip(normed, -1)
+        right = from_chip(normed, 1)
     pieces = (normed, sibling(normed), left, sibling(left), right, sibling(right))
     mine, other = attend(pieces, weights)
     return finish(tokens_zero, mine, sibling(other), attn_out)

time: 101 us -> 83.7 us (0.83)
  waiting for transfers between devices: 36.3 us -> 29.1 us
  Pallas kernels: 41 us -> 34 us
  starting transfers between devices: 21.2 us -> 19 us
    ppermute x2, waiting for transfers between devices: 0.01 us -> 18.8 us  [from_chip(): lax.ppermute(value, 'space', [((i + 2 * by) % length, i) for i in range(l...]
    ppermute x7, waiting for transfers between devices: 19.6 us -> 5.78 us  [around(): return lax.ppermute(value, 'space', pairs)]
    ppermute x7 -> x2, waiting for transfers between devices: 12.2 us -> 0.01 us  [across(): return lax.ppermute(value, 'groups', [(0, 1), (1, 0)])]
    ppermute x7 -> x2, starting transfers between devices: 8.25 us -> 2.43 us  [across(): return lax.ppermute(value, 'groups', [(0, 1), (1, 0)])]
    pallas_call x3 -> x1, Pallas kernels: 21.8 us -> 17.1 us  [aggregate(): pl.pallas_call(aggregate_kernel, out_shape=[jax.ShapeDtypeStruct((tokens,...]
    ppermute x7, starting transfers between devices: 6.77 us -> 10.8 us  [around(): return lax.ppermute(value, 'space', pairs)]
    pallas_call x1, Pallas kernels: 17.7 us -> 15.3 us  [attend(): pl.pallas_call(functools.partial(attend_kernel, spots=spots), out_shape=[...]
    unnamed x6, local copies, waits for them, and re-layouts: 1.05 us -> 0.02 us
  transfers between devices with their start and end apart: 21 -> 16, of which waited for: 9 -> 7; matrix products, arithmetic and copies ran while one was open for 0% -> 0% of each run, Pallas kernels for 22% -> 20%
where the time goes in v3:
time: 83.7 us; the launch traced here: 83.6 us
  Pallas kernels  34 us (41%)
  waiting for transfers between devices  29.1 us (35%)
  starting transfers between devices  19 us (23%)
  local copies, waits for them, and re-layouts  1.2 us (1%)
    ppermute x2, waiting for transfers between devices, from_chip(): lax.ppermute(value, 'space', [((i + 2 * by) % length, i) for i in range(l...  18.8 us
    pallas_call x1, Pallas kernels, aggregate(): pl.pallas_call(aggregate_kernel, out_shape=[jax.ShapeDtypeStruct((tokens,...  17.1 us
    pallas_call x1, Pallas kernels, attend(): pl.pallas_call(functools.partial(attend_kernel, spots=spots), out_shape=[...  15.3 us
    ppermute x7, starting transfers between devices, around(): return lax.ppermute(value, 'space', pairs)  10.8 us
    ppermute x7, waiting for transfers between devices, around(): return lax.ppermute(value, 'space', pairs)  5.78 us
    ppermute x2, starting transfers between devices, from_chip(): lax.ppermute(value, 'space', [((i + 2 * by) % length, i) for i in range(l...  4.58 us
    ppermute x5, waiting for transfers between devices, sibling(): return lax.ppermute(value, 'space', [(i, i ^ 1) for i in range(length)])  4.54 us
    ppermute x2, starting transfers between devices, across(): return lax.ppermute(value, 'groups', [(0, 1), (1, 0)])  2.43 us
  transfers between devices with their start and end apart: 16, of which 7 were waited for; matrix products, arithmetic and copies ran while one was open for 0% of the time, Pallas kernels for 20%

profile of v3, /device:TPU:0, one launch (start us, length us, event | category | flops | bytes accessed | tf_op | source)
XLA Modules:
  0.0 83.6 jit_solution(9505004870640319600)
XLA Ops:
  0.0 1.1 %fusion = (bf16[64,1024]{1,0:T(8,128)(2,1)S(1)}, bf16[64,1024]{1,0:T(8,128)(2,1)S(1)}, bf16[64,1024]{1,0:T(8,128)(2,1)S(1)}) fusion(bf16[192,1024]{1,0:T(8,128)(2,1)} %bitcast.4), kind=kLoop, calls=%fused_computation.12 | loop fusion | bytes 786432 | tf_op jit(solution)/shard_map/slice | solution.py:380
  1.1 0.5 collective-permute-start
  1.6 1.0 %collective-permute-done = bf16[64,1024]{1,0:T(8,128)(2,1)S(1)} collective-permute-done((bf16[64,1024]{1,0:T(8,128)(2,1)S(1)}, bf16[64,1024]{1,0:T(8,128)(2,1)S(1)}, u32[]{:S(2)}, u32[]{:S(2)}) %collective-permute-start) | collective-permute-done | bytes 131104 | tf_op jit(solution)/shard_map/ppermute | solution.py:353
  2.6 0.1 maximum_select_fusion.refs_6_
  2.7 3.9 %collective-permute-start.4 = (bf16[128,1024]{1,0:T(8,128)(2,1)S(1)}, bf16[128,1024]{1,0:T(8,128)(2,1)S(1)}, u32[]{:S(2)}, u32[]{:S(2)}) collective-permute-start(bf16[128,1024]{1,0:T(8,128)(2,1)S(1)} %constant_dynamic-slice_fusion.7), channel_id=1, source_target_pairs={{0,6},{1,7},{4,2},{5,3},{8,0},{9,1},{12,4},{13,5},{14,8},{15,9},{1... | collective-permute-start | bytes 786440 | tf_op jit(solution)/shard_map/ppermute | solution.py:367
  6.6 0.1 collective-permute-start.3
  6.8 1.8 %collective-permute-start.2 = (bf16[128,1024]{1,0:T(8,128)(2,1)S(1)}, bf16[128,1024]{1,0:T(8,128)(2,1)S(1)}, u32[]{:S(2)}, u32[]{:S(2)}) collective-permute-start(bf16[128,1024]{1,0:T(8,128)(2,1)S(1)} %constant_dynamic-slice_fusion.7), channel_id=1, source_target_pairs={{0,2},{1,3},{4,0},{5,1},{8,4},{9,5},{12,8},{13,9},{14,12},{15,13},... | collective-permute-start | bytes 786440 | tf_op jit(solution)/shard_map/ppermute | solution.py:367
  8.5 0.2 collective-permute-start.1
  8.8 17.1 %aggregate.1 = (bf16[256,1024]{1,0:T(8,128)(2,1)}, bf16[256,1024]{1,0:T(8,128)(2,1)}) custom-call(s32[64]{0:T(128)} %order_ref.1, bf16[64,1024]{1,0:T(8,128)(2,1)} %var_embed_hbm.1, bf16[16,1024]{1,0:T(8,128)(2,1)} %keys_hbm.1, bf16[64,16,1024]{2,1,0:T(8,128)(2,1)} %embed_hbm, bf16[256,1024]{1,0:T(8,128)(2,1)} %patches_hbm.1, bf16[1024,1024]{1,0:T(8,128)(2,1)} %value_hbm.1, ...), custom_call_target="tpu_custom_call" | custom-call | flops 16000000000 | bytes 8388608 | tf_op jit(solution)/shard_map/aggregate/pallas_call | solution.py:205
  25.9 0.0 copy-start.1
  25.9 0.0 collective-permute-done.4.refs_10_
  25.9 0.0 collective-permute-done.3.refs_9_
  25.9 0.0 collective-permute-done.2.refs_8_
  25.9 0.0 collective-permute-done.1.refs_7_
  26.1 1.8 %collective-permute-start.8 = (bf16[256,1024]{1,0:T(8,128)(2,1)S(1)}, bf16[256,1024]{1,0:T(8,128)(2,1)S(1)}, u32[]{:S(2)}, u32[]{:S(2)}) collective-permute-start(bf16[256,1024]{1,0:T(8,128)(2,1)S(1)} %pad_maximum_fusion), channel_id=1, source_target_pairs={{0,16},{16,0},{1,17},{17,1},{2,18},{18,2},{3,19},{19,3},{4,20},{20... | collective-permute-start | bytes 1572872 | tf_op jit(solution)/shard_map/ppermute | solution.py:371
  27.9 2.6 %collective-permute-start.11 = (bf16[128,1024]{1,0:T(8,128)(2,1)S(1)}, bf16[128,1024]{1,0:T(8,128)(2,1)S(1)}, u32[]{:S(2)}, u32[]{:S(2)}) collective-permute-start(bf16[128,1024]{1,0:T(8,128)(2,1)S(1)} %broadcast_select_fusion), channel_id=1, source_target_pairs={{0,8},{1,7},{4,12},{5,3},{8,14},{9,1},{12,10},{13,5},{14,6},{15,9}... | collective-permute-start | bytes 786440 | tf_op jit(solution)/shard_map/ppermute | solution.py:367
  30.6 1.6 %collective-permute-start.9 = (bf16[128,1024]{1,0:T(8,128)(2,1)S(1)}, bf16[128,1024]{1,0:T(8,128)(2,1)S(1)}, u32[]{:S(2)}, u32[]{:S(2)}) collective-permute-start(bf16[128,1024]{1,0:T(8,128)(2,1)S(1)} %collective-permute-done.3.refs_9_), channel_id=1, source_target_pairs={{0,4},{1,5},{4,8},{5,9},{8,12},{9,13},{12,14},{13,15},{14,10},{15,... | collective-permute-start | bytes 786440 | tf_op jit(solution)/shard_map/ppermute | solution.py:367
  32.1 0.4 collective-permute-start.10
  32.6 0.0 copy-done.1
  32.6 2.3 %collective-permute-start.7 = (bf16[256,1024]{1,0:T(8,128)(2,1)S(1)}, bf16[256,1024]{1,0:T(8,128)(2,1)S(1)}, u32[]{:S(2)}, u32[]{:S(2)}) collective-permute-start(bf16[256,1024]{1,0:T(8,128)(2,1)S(1)} %copy-done.1), channel_id=1, source_target_pairs={{2,0},{3,1},{4,2},{5,3},{6,4},{7,5},{8,6},{9,7},{10,8},{11,9},{12,... | collective-permute-start | bytes 1572872 | tf_op jit(solution)/shard_map/ppermute | solution.py:358
  34.9 5.0 %collective-permute-done.11.refs_13_ = bf16[128,1024]{1,0:T(8,128)(2,1)S(1)} collective-permute-done((bf16[128,1024]{1,0:T(8,128)(2,1)S(1)}, bf16[128,1024]{1,0:T(8,128)(2,1)S(1)}, u32[]{:S(2)}, u32[]{:S(2)}) %collective-permute-start.11) | collective-permute-done | bytes 262176 | tf_op jit(solution)/shard_map/ppermute | solution.py:367
  39.9 2.3 %collective-permute-start.6 = (bf16[256,1024]{1,0:T(8,128)(2,1)S(1)}, bf16[256,1024]{1,0:T(8,128)(2,1)S(1)}, u32[]{:S(2)}, u32[]{:S(2)}) collective-permute-start(bf16[256,1024]{1,0:T(8,128)(2,1)S(1)} %copy-done.1), channel_id=1, source_target_pairs={{14,0},{15,1},{0,2},{1,3},{2,4},{3,5},{4,6},{5,7},{6,8},{7,9},{8,1... | collective-permute-start | bytes 1572872 | tf_op jit(solution)/shard_map/ppermute | solution.py:358
  42.2 0.8 collective-permute-done.9.refs_11_
  42.9 0.0 collective-permute-done.10.refs_12_
  43.0 0.0 collective-permute-done.8.refs_14_
  43.1 0.0 copy-start
  43.1 0.0 copy-start.2
  43.1 0.6 collective-permute-start.12
  43.7 0.0 collective-permute-start.5
  43.7 18.8 %collective-permute-done.7.refs_4_ = bf16[256,1024]{1,0:T(8,128)(2,1)S(1)} collective-permute-done((bf16[256,1024]{1,0:T(8,128)(2,1)S(1)}, bf16[256,1024]{1,0:T(8,128)(2,1)S(1)}, u32[]{:S(2)}, u32[]{:S(2)}) %collective-permute-start.7) | collective-permute-done | bytes 524320 | tf_op jit(solution)/shard_map/ppermute | solution.py:358
  62.5 0.0 collective-permute-done.6.refs_2_
  62.5 0.0 collective-permute-done.12.refs_15_
  62.5 0.0 collective-permute-start.13
  62.5 0.5 collective-permute-start.14
  63.0 0.0 collective-permute-done.5.refs_1_
  63.0 1.4 %collective-permute-done.13.refs_3_ = bf16[256,1024]{1,0:T(8,128)(2,1)S(1)} collective-permute-done((bf16[256,1024]{1,0:T(8,128)(2,1)S(1)}, bf16[256,1024]{1,0:T(8,128)(2,1)S(1)}, u32[]{:S(2)}, u32[]{:S(2)}) %collective-permute-start.13) | collective-permute-done | bytes 524320 | tf_op jit(solution)/shard_map/ppermute | solution.py:353
  64.4 0.7 collective-permute-done.14.refs_5_
  65.1 15.3 %attend.1 = (bf16[4,256,128]{2,1,0:T(8,128)(2,1)S(1)}, bf16[4,256,128]{2,1,0:T(8,128)(2,1)S(1)}) custom-call(bf16[256,1024]{1,0:T(8,128)(2,1)S(1)} %copy-done.1, bf16[256,1024]{1,0:T(8,128)(2,1)S(1)} %collective-permute-done.5.refs_1_, bf16[256,1024]{1,0:T(8,128)(2,1)S(1)} %collective-permute-done.6.refs_2_, ...), custom_call_target="tpu_custom_call" | custom-call | flops 10000000000 | bytes 8388608 | tf_op jit(solution)/shard_map/attend/pallas_call | solution.py:306
  80.5 0.2 collective-permute-start.15
  80.7 1.4 %collective-permute-done.15.other_ref = bf16[4,256,128]{2,1,0:T(8,128)(2,1)S(1)} collective-permute-done((bf16[4,256,128]{2,1,0:T(8,128)(2,1)S(1)}, bf16[4,256,128]{2,1,0:T(8,128)(2,1)S(1)}, u32[]{:S(2)}, u32[]{:S(2)}) %collective-permute-start.15) | collective-permute-done | bytes 262176 | tf_op jit(solution)/shard_map/ppermute | solution.py:353
  82.1 0.0 copy-done
  82.1 0.0 copy-done.2
  82.1 1.5 %finish.1 = bf16[256,1024]{1,0:T(8,128)(2,1)} custom-call(bf16[256,1024]{1,0:T(8,128)(2,1)S(1)} %copy-done.2, bf16[4,256,128]{2,1,0:T(8,128)(2,1)S(1)} %get-tuple-element.39.mine_ref, bf16[4,256,128]{2,1,0:T(8,128)(2,1)S(1)} %collective-permute-done.15.other_ref, bf16[8,2,64,1024]{3,2,1,0:T(8,128)(2,1)S(1)} %bitcast.3), custom_call_target="tpu_custom_call" | custom-call | flops 1000000000 | bytes 4194304 | tf_op jit(solution)/shard_map/finish/pallas_call | solution.py:340
  (9 shorter events, 0.2 us)
Async XLA Ops:
  1.1 1.5 %collective-permute-start = (bf16[64,1024]{1,0:T(8,128)(2,1)S(1)}, bf16[64,1024]{1,0:T(8,128)(2,1)S(1)}, u32[]{:S(2)}, u32[]{:S(2)}) collective-permute-start(bf16[64,1024]{1,0:T(8,128)(2,1)S(1)} %get-tuple-element.42), channel_id=1, source_target_pairs={{0,1},{1,0},{2,3},{3,2},{4,5},{5,4},{6,7},{7,6},{8,9},{9,8},{10,11... | collective-permute-start | bytes 393224 | tf_op jit(solution)/shard_map/ppermute | solution.py:353
  2.7 23.2 %collective-permute-start.4 = (bf16[128,1024]{1,0:T(8,128)(2,1)S(1)}, bf16[128,1024]{1,0:T(8,128)(2,1)S(1)}, u32[]{:S(2)}, u32[]{:S(2)}) collective-permute-start(bf16[128,1024]{1,0:T(8,128)(2,1)S(1)} %constant_dynamic-slice_fusion.7), channel_id=1, source_target_pairs={{0,6},{1,7},{4,2},{5,3},{8,0},{9,1},{12,4},{13,5},{14,8},{15,9},{1... | collective-permute-start | bytes 786440 | tf_op jit(solution)/shard_map/ppermute | solution.py:367
  6.6 19.3 %collective-permute-start.3 = (bf16[128,1024]{1,0:T(8,128)(2,1)S(1)}, bf16[128,1024]{1,0:T(8,128)(2,1)S(1)}, u32[]{:S(2)}, u32[]{:S(2)}) collective-permute-start(bf16[128,1024]{1,0:T(8,128)(2,1)S(1)} %constant_dynamic-slice_fusion.7), channel_id=1, source_target_pairs={{0,8},{1,9},{4,12},{5,13},{8,14},{9,15},{12,10},{13,11},{14,6},{15... | collective-permute-start | bytes 786440 | tf_op jit(solution)/shard_map/ppermute | solution.py:367
  6.8 19.2 %collective-permute-start.2 = (bf16[128,1024]{1,0:T(8,128)(2,1)S(1)}, bf16[128,1024]{1,0:T(8,128)(2,1)S(1)}, u32[]{:S(2)}, u32[]{:S(2)}) collective-permute-start(bf16[128,1024]{1,0:T(8,128)(2,1)S(1)} %constant_dynamic-slice_fusion.7), channel_id=1, source_target_pairs={{0,2},{1,3},{4,0},{5,1},{8,4},{9,5},{12,8},{13,9},{14,12},{15,13},... | collective-permute-start | bytes 786440 | tf_op jit(solution)/shard_map/ppermute | solution.py:367
  8.5 17.4 %collective-permute-start.1 = (bf16[128,1024]{1,0:T(8,128)(2,1)S(1)}, bf16[128,1024]{1,0:T(8,128)(2,1)S(1)}, u32[]{:S(2)}, u32[]{:S(2)}) collective-permute-start(bf16[128,1024]{1,0:T(8,128)(2,1)S(1)} %constant_dynamic-slice_fusion.7), channel_id=1, source_target_pairs={{0,4},{1,5},{4,8},{5,9},{8,12},{9,13},{12,14},{13,15},{14,10},{15,... | collective-permute-start | bytes 786440 | tf_op jit(solution)/shard_map/ppermute | solution.py:367
  25.9 6.7 %copy-start.1 = (bf16[256,1024]{1,0:T(8,128)(2,1)S(1)}, bf16[256,1024]{1,0:T(8,128)(2,1)}, u32[]{:S(2)}) copy-start(bf16[256,1024]{1,0:T(8,128)(2,1)} %get-tuple-element.27.refs_0_) | copy-start | bytes 1572868
  26.1 16.9 %collective-permute-start.8 = (bf16[256,1024]{1,0:T(8,128)(2,1)S(1)}, bf16[256,1024]{1,0:T(8,128)(2,1)S(1)}, u32[]{:S(2)}, u32[]{:S(2)}) collective-permute-start(bf16[256,1024]{1,0:T(8,128)(2,1)S(1)} %pad_maximum_fusion), channel_id=1, source_target_pairs={{0,16},{16,0},{1,17},{17,1},{2,18},{18,2},{3,19},{19,3},{4,20},{20... | collective-permute-start | bytes 1572872 | tf_op jit(solution)/shard_map/ppermute | solution.py:371
  27.9 12.0 %collective-permute-start.11 = (bf16[128,1024]{1,0:T(8,128)(2,1)S(1)}, bf16[128,1024]{1,0:T(8,128)(2,1)S(1)}, u32[]{:S(2)}, u32[]{:S(2)}) collective-permute-start(bf16[128,1024]{1,0:T(8,128)(2,1)S(1)} %broadcast_select_fusion), channel_id=1, source_target_pairs={{0,8},{1,7},{4,12},{5,3},{8,14},{9,1},{12,10},{13,5},{14,6},{15,9}... | collective-permute-start | bytes 786440 | tf_op jit(solution)/shard_map/ppermute | solution.py:367
  30.6 12.4 %collective-permute-start.9 = (bf16[128,1024]{1,0:T(8,128)(2,1)S(1)}, bf16[128,1024]{1,0:T(8,128)(2,1)S(1)}, u32[]{:S(2)}, u32[]{:S(2)}) collective-permute-start(bf16[128,1024]{1,0:T(8,128)(2,1)S(1)} %collective-permute-done.3.refs_9_), channel_id=1, source_target_pairs={{0,4},{1,5},{4,8},{5,9},{8,12},{9,13},{12,14},{13,15},{14,10},{15,... | collective-permute-start | bytes 786440 | tf_op jit(solution)/shard_map/ppermute | solution.py:367
  32.1 10.8 %collective-permute-start.10 = (bf16[128,1024]{1,0:T(8,128)(2,1)S(1)}, bf16[128,1024]{1,0:T(8,128)(2,1)S(1)}, u32[]{:S(2)}, u32[]{:S(2)}) collective-permute-start(bf16[128,1024]{1,0:T(8,128)(2,1)S(1)} %collective-permute-done.4.refs_10_), channel_id=1, source_target_pairs={{0,2},{1,3},{4,0},{5,1},{8,4},{9,5},{12,8},{13,9},{14,12},{15,13},... | collective-permute-start | bytes 786440 | tf_op jit(solution)/shard_map/ppermute | solution.py:367
  32.6 29.9 %collective-permute-start.7 = (bf16[256,1024]{1,0:T(8,128)(2,1)S(1)}, bf16[256,1024]{1,0:T(8,128)(2,1)S(1)}, u32[]{:S(2)}, u32[]{:S(2)}) collective-permute-start(bf16[256,1024]{1,0:T(8,128)(2,1)S(1)} %copy-done.1), channel_id=1, source_target_pairs={{2,0},{3,1},{4,2},{5,3},{6,4},{7,5},{8,6},{9,7},{10,8},{11,9},{12,... | collective-permute-start | bytes 1572872 | tf_op jit(solution)/shard_map/ppermute | solution.py:358
  39.9 22.6 %collective-permute-start.6 = (bf16[256,1024]{1,0:T(8,128)(2,1)S(1)}, bf16[256,1024]{1,0:T(8,128)(2,1)S(1)}, u32[]{:S(2)}, u32[]{:S(2)}) collective-permute-start(bf16[256,1024]{1,0:T(8,128)(2,1)S(1)} %copy-done.1), channel_id=1, source_target_pairs={{14,0},{15,1},{0,2},{1,3},{2,4},{3,5},{4,6},{5,7},{6,8},{7,9},{8,1... | collective-permute-start | bytes 1572872 | tf_op jit(solution)/shard_map/ppermute | solution.py:358
  43.1 39.0 %copy-start = (bf16[1024,1024]{1,0:T(8,128)(2,1)S(1)}, bf16[1024,1024]{1,0:T(8,128)(2,1)}, u32[]{:S(2)}) copy-start(bf16[1024,1024]{1,0:T(8,128)(2,1)} %param.21) | copy-start | bytes 6291460
  43.1 39.0 %copy-start.2 = (bf16[256,1024]{1,0:T(8,128)(2,1)S(1)}, bf16[256,1024]{1,0:T(8,128)(2,1)}, u32[]{:S(2)}) copy-start(bf16[256,1024]{1,0:T(8,128)(2,1)} %get-tuple-element.24.tokens_ref) | copy-start | bytes 1572868
  43.1 19.4 %collective-permute-start.12 = (bf16[192,1024]{1,0:T(8,128)(2,1)S(1)}, bf16[192,1024]{1,0:T(8,128)(2,1)S(1)}, u32[]{:S(2)}, u32[]{:S(2)}) collective-permute-start(bf16[192,1024]{1,0:T(8,128)(2,1)S(1)} %pad_maximum_fusion.1), channel_id=1, source_target_pairs={{0,16},{16,0},{1,17},{17,1},{2,18},{18,2},{3,19},{19,3},{4,20},{20... | collective-permute-start | bytes 1179656 | tf_op jit(solution)/shard_map/ppermute | solution.py:371
  43.7 19.3 %collective-permute-start.5 = (bf16[256,1024]{1,0:T(8,128)(2,1)S(1)}, bf16[256,1024]{1,0:T(8,128)(2,1)S(1)}, u32[]{:S(2)}, u32[]{:S(2)}) collective-permute-start(bf16[256,1024]{1,0:T(8,128)(2,1)S(1)} %copy-done.1), channel_id=1, source_target_pairs={{0,1},{1,0},{2,3},{3,2},{4,5},{5,4},{6,7},{7,6},{8,9},{9,8},{10,11... | collective-permute-start | bytes 1572872 | tf_op jit(solution)/shard_map/ppermute | solution.py:353
  62.5 1.9 %collective-permute-start.13 = (bf16[256,1024]{1,0:T(8,128)(2,1)S(1)}, bf16[256,1024]{1,0:T(8,128)(2,1)S(1)}, u32[]{:S(2)}, u32[]{:S(2)}) collective-permute-start(bf16[256,1024]{1,0:T(8,128)(2,1)S(1)} %collective-permute-done.6.refs_2_), channel_id=1, source_target_pairs={{0,1},{1,0},{2,3},{3,2},{4,5},{5,4},{6,7},{7,6},{8,9},{9,8},{10,11... | collective-permute-start | bytes 1572872 | tf_op jit(solution)/shard_map/ppermute | solution.py:353
  62.5 2.7 %collective-permute-start.14 = (bf16[256,1024]{1,0:T(8,128)(2,1)S(1)}, bf16[256,1024]{1,0:T(8,128)(2,1)S(1)}, u32[]{:S(2)}, u32[]{:S(2)}) collective-permute-start(bf16[256,1024]{1,0:T(8,128)(2,1)S(1)} %collective-permute-done.7.refs_4_), channel_id=1, source_target_pairs={{0,1},{1,0},{2,3},{3,2},{4,5},{5,4},{6,7},{7,6},{8,9},{9,8},{10,11... | collective-permute-start | bytes 1572872 | tf_op jit(solution)/shard_map/ppermute | solution.py:353
  80.5 1.6 %collective-permute-start.15 = (bf16[4,256,128]{2,1,0:T(8,128)(2,1)S(1)}, bf16[4,256,128]{2,1,0:T(8,128)(2,1)S(1)}, u32[]{:S(2)}, u32[]{:S(2)}) collective-permute-start(bf16[4,256,128]{2,1,0:T(8,128)(2,1)S(1)} %get-tuple-element.40), channel_id=1, source_target_pairs={{0,1},{1,0},{2,3},{3,2},{4,5},{5,4},{6,7},{7,6},{8,9},{9,8},{10,11... | collective-permute-start | bytes 786440 | tf_op jit(solution)/shard_map/ppermute | solution.py:353

commit v4 on v3

--- a/solution.py
+++ b/solution.py
@@ -239,36 +239,28 @@
             moves.append((ref, weight_s.at[chip_at(index, step)]))
     for wait in fetch(moves, sems):
         wait()
-    own_ref, sib_ref, left_own_ref, left_sib_ref, right_own_ref, right_sib_ref = (
-        rows_s.at[i] for i in range(6)
-    )
-    tokens, width = own_ref.shape
+    flip = index // 2 % 2 if spots[0][0] is not None else 0
+    near, far = 4 - 4 * flip, 4 * flip
+    _, tokens, width = rows_s.shape
     pairs = mine_ref.shape[0]
     cols = pairs * LANES
     weight = weight_s[...].reshape(3, cols, width)
     head_size = LANES // 2
     scale = 1.0 / math.sqrt(head_size)
-    pieces = [
-        (left_own_ref, side),
-        (left_sib_ref, 1 - side),
-        (own_ref, 2 + side),
-        (sib_ref, 3 - side),
-        (right_own_ref, 4 + side),
-        (right_sib_ref, 5 - side),
-    ]
+    pieces = (2 + side, 3 - side, near + side, near + 1 - side, far + side, far + 1 - side)
     ones = jnp.ones((tokens, LANES), BF16)
-    for number, (ref, place) in enumerate(pieces):
-        rows = ref[...]
+    for number, place in enumerate(pieces):
+        rows = rows_s[number]
         key_s[place] = dot_t(weight[1], rows).astype(BF16)
         value = dot_t(rows, weight[2]).astype(BF16)
         for pair in range(pairs):
             value_s[place, pair] = jnp.concatenate(
                 [value[:, pair * LANES : (pair + 1) * LANES], ones], axis=1
             )
-        if number in (2, 3):
+        if number < 2:
             query = (dot_t(rows, weight[0]).astype(BF16).astype(F32) * scale).astype(BF16)
             for pair in range(pairs):
-                query_s[number - 2, pair] = query[:, pair * LANES : (pair + 1) * LANES]
+                query_s[number, pair] = query[:, pair * LANES : (pair + 1) * LANES]
 
     left_half = iota((tokens, LANES), 1) < head_size
 
@@ -367,6 +359,16 @@
     return lax.ppermute(value, "space", pairs)
 
 
+def beside(value):
+    return lax.ppermute(value, "space", [(i, i ^ 2) for i in range(2 * len(RING))])
+
+
+def onward(value):
+    length = 2 * len(RING)
+    pairs = [(i, (i + (4 if i & 2 == 0 else -4)) % length) for i in range(length)]
+    return lax.ppermute(value, "space", pairs)
+
+
 def across(value):
     return lax.ppermute(value, "groups", [(0, 1), (1, 0)])
 
@@ -438,18 +440,18 @@
         swap = swapped(early)
         late = [around(early[2], 1), around(early[3], -1)]
         late.append(around(jnp.where(side == 0, early[2], early[3]), (2, -2)))
-        left = from_chip(normed, -1)
-        right = from_chip(normed, 1)
-        swap, *late = together(swap, *late)
+        near = beside(normed)
+        far, near_sib = onward(near), sibling(near)
+        swap, near_sib, *late = together(swap, near_sib, *late)
         weights += [(b, (-step, "ring")) for b, step in zip(late, (3, -3, 4))]
         weights.append((swap, ((-1, 1, -2, 2), "swap")))
         last = swapped(late)
-        left, right, last = together(left, right, last)
+        far, last = together(far, last)
         weights.append((last, ((-3, 3, -4), "swap")))
     else:
-        left = from_chip(normed, -1)
-        right = from_chip(normed, 1)
-    pieces = (normed, sibling(normed), left, sibling(left), right, sibling(right))
+        near, far = from_chip(normed, 1), from_chip(normed, -1)
+        near_sib = sibling(near)
+    pieces = (normed, sibling(normed), near, near_sib, far, sibling(far))
     mine, other = attend(pieces, weights)
     return finish(tokens_zero, mine, sibling(other), attn_out)
 

time: 83.7 us -> 87.5 us (1.045)
  waiting for transfers between devices: 29.1 us -> 34.2 us
  starting transfers between devices: 19 us -> 17.7 us
    ppermute x7, waiting for transfers between devices: 5.78 us -> 9.31 us  [around(): return lax.ppermute(value, 'space', pairs)]
    ppermute x2, starting transfers between devices: 4.58 us -> 2.77 us  [the longest x1 1.86 us: beside(): lax.ppermute(value, 'space', [(i, i ^ 2) for i in range(2 * len(RING))])]
    ppermute x2, waiting for transfers between devices: 18.8 us -> 20.5 us  [the longest x1 10.7 us: onward(): return lax.ppermute(value, 'space', pairs)]
where the time goes in v4:
time: 87.5 us; the launch traced here: 87.4 us
  waiting for transfers between devices  34.2 us (39%)
  Pallas kernels  34 us (39%)
  starting transfers between devices  17.7 us (20%)
  local copies, waits for them, and re-layouts  1.2 us (1%)
    pallas_call x1, Pallas kernels, aggregate(): pl.pallas_call(aggregate_kernel, out_shape=[jax.ShapeDtypeStruct((tokens,...  17.1 us
    pallas_call x1, Pallas kernels, attend(): pl.pallas_call(functools.partial(attend_kernel, spots=spots), out_shape=[...  15.4 us
    ppermute x7, starting transfers between devices, around(): return lax.ppermute(value, 'space', pairs)  10.8 us
    ppermute x1, waiting for transfers between devices, onward(): return lax.ppermute(value, 'space', pairs)  10.7 us
    ppermute x1, waiting for transfers between devices, beside(): lax.ppermute(value, 'space', [(i, i ^ 2) for i in range(2 * len(RING))])  9.89 us
    ppermute x7, waiting for transfers between devices, around(): return lax.ppermute(value, 'space', pairs)  9.31 us
    ppermute x5, waiting for transfers between devices, sibling(): return lax.ppermute(value, 'space', [(i, i ^ 1) for i in range(length)])  4.29 us
    ppermute x2, starting transfers between devices, across(): return lax.ppermute(value, 'groups', [(0, 1), (1, 0)])  3.11 us
  transfers between devices with their start and end apart: 16, of which 7 were waited for; matrix products, arithmetic and copies ran while one was open for 0% of the time, Pallas kernels for 20%

profile of v4, /device:TPU:0, one launch (start us, length us, event | category | flops | bytes accessed | tf_op | source)
XLA Modules:
  0.0 87.4 jit_solution(4941631240231727984)
XLA Ops:
  0.0 1.1 %fusion = (bf16[64,1024]{1,0:T(8,128)(2,1)S(1)}, bf16[64,1024]{1,0:T(8,128)(2,1)S(1)}, bf16[64,1024]{1,0:T(8,128)(2,1)S(1)}) fusion(bf16[192,1024]{1,0:T(8,128)(2,1)} %bitcast.4), kind=kLoop, calls=%fused_computation.12 | loop fusion | bytes 786432 | tf_op jit(solution)/shard_map/slice | solution.py:382
  1.1 0.5 collective-permute-start
  1.6 1.0 %collective-permute-done = bf16[64,1024]{1,0:T(8,128)(2,1)S(1)} collective-permute-done((bf16[64,1024]{1,0:T(8,128)(2,1)S(1)}, bf16[64,1024]{1,0:T(8,128)(2,1)S(1)}, u32[]{:S(2)}, u32[]{:S(2)}) %collective-permute-start) | collective-permute-done | bytes 131104 | tf_op jit(solution)/shard_map/ppermute | solution.py:345
  2.6 0.1 maximum_select_fusion.refs_6_
  2.7 3.9 %collective-permute-start.4 = (bf16[128,1024]{1,0:T(8,128)(2,1)S(1)}, bf16[128,1024]{1,0:T(8,128)(2,1)S(1)}, u32[]{:S(2)}, u32[]{:S(2)}) collective-permute-start(bf16[128,1024]{1,0:T(8,128)(2,1)S(1)} %constant_dynamic-slice_fusion.7), channel_id=1, source_target_pairs={{0,6},{1,7},{4,2},{5,3},{8,0},{9,1},{12,4},{13,5},{14,8},{15,9},{1... | collective-permute-start | bytes 786440 | tf_op jit(solution)/shard_map/ppermute | solution.py:359
  6.6 0.1 collective-permute-start.3
  6.8 1.8 %collective-permute-start.2 = (bf16[128,1024]{1,0:T(8,128)(2,1)S(1)}, bf16[128,1024]{1,0:T(8,128)(2,1)S(1)}, u32[]{:S(2)}, u32[]{:S(2)}) collective-permute-start(bf16[128,1024]{1,0:T(8,128)(2,1)S(1)} %constant_dynamic-slice_fusion.7), channel_id=1, source_target_pairs={{0,2},{1,3},{4,0},{5,1},{8,4},{9,5},{12,8},{13,9},{14,12},{15,13},... | collective-permute-start | bytes 786440 | tf_op jit(solution)/shard_map/ppermute | solution.py:359
  8.5 0.2 collective-permute-start.1
  8.8 17.1 %aggregate.1 = (bf16[256,1024]{1,0:T(8,128)(2,1)}, bf16[256,1024]{1,0:T(8,128)(2,1)}) custom-call(s32[64]{0:T(128)} %order_ref.1, bf16[64,1024]{1,0:T(8,128)(2,1)} %var_embed_hbm.1, bf16[16,1024]{1,0:T(8,128)(2,1)} %keys_hbm.1, bf16[64,16,1024]{2,1,0:T(8,128)(2,1)} %embed_hbm, bf16[256,1024]{1,0:T(8,128)(2,1)} %patches_hbm.1, bf16[1024,1024]{1,0:T(8,128)(2,1)} %value_hbm.1, ...), custom_call_target="tpu_custom_call" | custom-call | flops 16000000000 | bytes 8388608 | tf_op jit(solution)/shard_map/aggregate/pallas_call | solution.py:205
  25.9 0.0 collective-permute-done.4.refs_10_
  25.9 0.0 collective-permute-done.3.refs_9_
  25.9 0.0 collective-permute-done.2.refs_8_
  25.9 0.0 collective-permute-done.1.refs_7_
  25.9 1.9 %collective-permute-start.6 = (bf16[256,1024]{1,0:T(8,128)(2,1)}, bf16[256,1024]{1,0:T(8,128)(2,1)S(1)}, u32[]{:S(2)}, u32[]{:S(2)}) collective-permute-start(bf16[256,1024]{1,0:T(8,128)(2,1)} %get-tuple-element.27.refs_0_), channel_id=1, source_target_pairs={{0,2},{1,3},{2,0},{3,1},{4,6},{5,7},{6,4},{7,5},{8,10},{9,11},{10,... | collective-permute-start | bytes 1572872 | tf_op jit(solution)/shard_map/ppermute | solution.py:363
  27.8 0.0 copy-start.1
  27.9 1.6 %collective-permute-start.7 = (bf16[256,1024]{1,0:T(8,128)(2,1)S(1)}, bf16[256,1024]{1,0:T(8,128)(2,1)S(1)}, u32[]{:S(2)}, u32[]{:S(2)}) collective-permute-start(bf16[256,1024]{1,0:T(8,128)(2,1)S(1)} %pad_maximum_fusion), channel_id=1, source_target_pairs={{0,16},{16,0},{1,17},{17,1},{2,18},{18,2},{3,19},{19,3},{4,20},{20... | collective-permute-start | bytes 1572872 | tf_op jit(solution)/shard_map/ppermute | solution.py:373
  29.5 9.9 %collective-permute-done.6.refs_2_ = bf16[256,1024]{1,0:T(8,128)(2,1)S(1)} collective-permute-done((bf16[256,1024]{1,0:T(8,128)(2,1)}, bf16[256,1024]{1,0:T(8,128)(2,1)S(1)}, u32[]{:S(2)}, u32[]{:S(2)}) %collective-permute-start.6) | collective-permute-done | bytes 524320 | tf_op jit(solution)/shard_map/ppermute | solution.py:363
  39.4 0.0 collective-permute-start.8
  39.4 2.6 %collective-permute-start.11 = (bf16[128,1024]{1,0:T(8,128)(2,1)S(1)}, bf16[128,1024]{1,0:T(8,128)(2,1)S(1)}, u32[]{:S(2)}, u32[]{:S(2)}) collective-permute-start(bf16[128,1024]{1,0:T(8,128)(2,1)S(1)} %broadcast_select_fusion), channel_id=1, source_target_pairs={{0,8},{1,7},{4,12},{5,3},{8,14},{9,1},{12,10},{13,5},{14,6},{15,9}... | collective-permute-start | bytes 786440 | tf_op jit(solution)/shard_map/ppermute | solution.py:359
  42.0 1.6 %collective-permute-start.9 = (bf16[128,1024]{1,0:T(8,128)(2,1)S(1)}, bf16[128,1024]{1,0:T(8,128)(2,1)S(1)}, u32[]{:S(2)}, u32[]{:S(2)}) collective-permute-start(bf16[128,1024]{1,0:T(8,128)(2,1)S(1)} %collective-permute-done.3.refs_9_), channel_id=1, source_target_pairs={{0,4},{1,5},{4,8},{5,9},{8,12},{9,13},{12,14},{13,15},{14,10},{15,... | collective-permute-start | bytes 786440 | tf_op jit(solution)/shard_map/ppermute | solution.py:359
  43.6 0.4 collective-permute-start.10
  44.0 6.8 %collective-permute-done.11.refs_13_ = bf16[128,1024]{1,0:T(8,128)(2,1)S(1)} collective-permute-done((bf16[128,1024]{1,0:T(8,128)(2,1)S(1)}, bf16[128,1024]{1,0:T(8,128)(2,1)S(1)}, u32[]{:S(2)}, u32[]{:S(2)}) %collective-permute-start.11) | collective-permute-done | bytes 262176 | tf_op jit(solution)/shard_map/ppermute | solution.py:359
  50.8 0.9 %collective-permute-start.12 = (bf16[256,1024]{1,0:T(8,128)(2,1)S(1)}, bf16[256,1024]{1,0:T(8,128)(2,1)S(1)}, u32[]{:S(2)}, u32[]{:S(2)}) collective-permute-start(bf16[256,1024]{1,0:T(8,128)(2,1)S(1)} %collective-permute-done.6.refs_2_), channel_id=1, source_target_pairs={{0,4},{1,5},{2,14},{3,15},{4,8},{5,9},{6,2},{7,3},{8,12},{9,13},{1... | collective-permute-start | bytes 1572872 | tf_op jit(solution)/shard_map/ppermute | solution.py:369
  51.7 2.5 %collective-permute-done.9.refs_11_ = bf16[128,1024]{1,0:T(8,128)(2,1)S(1)} collective-permute-done((bf16[128,1024]{1,0:T(8,128)(2,1)S(1)}, bf16[128,1024]{1,0:T(8,128)(2,1)S(1)}, u32[]{:S(2)}, u32[]{:S(2)}) %collective-permute-start.9) | collective-permute-done | bytes 262176 | tf_op jit(solution)/shard_map/ppermute | solution.py:359
  54.3 0.0 collective-permute-done.10.refs_12_
  54.3 0.0 collective-permute-done.7.refs_14_
  54.3 0.0 collective-permute-done.8.refs_3_
  54.4 0.0 copy-start
  54.4 0.0 copy-start.2
  54.4 1.6 %collective-permute-start.13 = (bf16[192,1024]{1,0:T(8,128)(2,1)S(1)}, bf16[192,1024]{1,0:T(8,128)(2,1)S(1)}, u32[]{:S(2)}, u32[]{:S(2)}) collective-permute-start(bf16[192,1024]{1,0:T(8,128)(2,1)S(1)} %pad_maximum_fusion.1), channel_id=1, source_target_pairs={{0,16},{16,0},{1,17},{17,1},{2,18},{18,2},{3,19},{19,3},{4,20},{20... | collective-permute-start | bytes 1179656 | tf_op jit(solution)/shard_map/ppermute | solution.py:373
  56.0 0.0 copy-done.1
  56.0 0.3 collective-permute-start.5
  56.3 10.7 %collective-permute-done.12.refs_4_ = bf16[256,1024]{1,0:T(8,128)(2,1)S(1)} collective-permute-done((bf16[256,1024]{1,0:T(8,128)(2,1)S(1)}, bf16[256,1024]{1,0:T(8,128)(2,1)S(1)}, u32[]{:S(2)}, u32[]{:S(2)}) %collective-permute-start.12) | collective-permute-done | bytes 524320 | tf_op jit(solution)/shard_map/ppermute | solution.py:369
  67.0 0.0 collective-permute-done.13.refs_15_
  67.0 0.0 collective-permute-start.14
  67.0 0.0 collective-permute-done.5.refs_1_
  67.0 1.9 %collective-permute-done.14.refs_5_ = bf16[256,1024]{1,0:T(8,128)(2,1)S(1)} collective-permute-done((bf16[256,1024]{1,0:T(8,128)(2,1)S(1)}, bf16[256,1024]{1,0:T(8,128)(2,1)S(1)}, u32[]{:S(2)}, u32[]{:S(2)}) %collective-permute-start.14) | collective-permute-done | bytes 524320 | tf_op jit(solution)/shard_map/ppermute | solution.py:345
  68.9 15.4 %attend.1 = (bf16[4,256,128]{2,1,0:T(8,128)(2,1)S(1)}, bf16[4,256,128]{2,1,0:T(8,128)(2,1)S(1)}) custom-call(bf16[256,1024]{1,0:T(8,128)(2,1)S(1)} %copy-done.1, bf16[256,1024]{1,0:T(8,128)(2,1)S(1)} %collective-permute-done.5.refs_1_, bf16[256,1024]{1,0:T(8,128)(2,1)S(1)} %collective-permute-done.6.refs_2_, ...), custom_call_target="tpu_custom_call" | custom-call | flops 10000000000 | bytes 8388608 | tf_op jit(solution)/shard_map/attend/pallas_call | solution.py:298
  84.3 0.2 collective-permute-start.15
  84.5 1.4 %collective-permute-done.15.other_ref = bf16[4,256,128]{2,1,0:T(8,128)(2,1)S(1)} collective-permute-done((bf16[4,256,128]{2,1,0:T(8,128)(2,1)S(1)}, bf16[4,256,128]{2,1,0:T(8,128)(2,1)S(1)}, u32[]{:S(2)}, u32[]{:S(2)}) %collective-permute-start.15) | collective-permute-done | bytes 262176 | tf_op jit(solution)/shard_map/ppermute | solution.py:345
  85.9 0.0 copy-done
  85.9 0.0 copy-done.2
  85.9 1.5 %finish.1 = bf16[256,1024]{1,0:T(8,128)(2,1)} custom-call(bf16[256,1024]{1,0:T(8,128)(2,1)S(1)} %copy-done.2, bf16[4,256,128]{2,1,0:T(8,128)(2,1)S(1)} %get-tuple-element.39.mine_ref, bf16[4,256,128]{2,1,0:T(8,128)(2,1)S(1)} %collective-permute-done.15.other_ref, bf16[8,2,64,1024]{3,2,1,0:T(8,128)(2,1)S(1)} %bitcast.3), custom_call_target="tpu_custom_call" | custom-call | flops 1000000000 | bytes 4194304 | tf_op jit(solution)/shard_map/finish/pallas_call | solution.py:332
  (9 shorter events, 0.2 us)
Async XLA Ops:
  1.1 1.5 %collective-permute-start = (bf16[64,1024]{1,0:T(8,128)(2,1)S(1)}, bf16[64,1024]{1,0:T(8,128)(2,1)S(1)}, u32[]{:S(2)}, u32[]{:S(2)}) collective-permute-start(bf16[64,1024]{1,0:T(8,128)(2,1)S(1)} %get-tuple-element.42), channel_id=1, source_target_pairs={{0,1},{1,0},{2,3},{3,2},{4,5},{5,4},{6,7},{7,6},{8,9},{9,8},{10,11... | collective-permute-start | bytes 393224 | tf_op jit(solution)/shard_map/ppermute | solution.py:345
  2.7 23.2 %collective-permute-start.4 = (bf16[128,1024]{1,0:T(8,128)(2,1)S(1)}, bf16[128,1024]{1,0:T(8,128)(2,1)S(1)}, u32[]{:S(2)}, u32[]{:S(2)}) collective-permute-start(bf16[128,1024]{1,0:T(8,128)(2,1)S(1)} %constant_dynamic-slice_fusion.7), channel_id=1, source_target_pairs={{0,6},{1,7},{4,2},{5,3},{8,0},{9,1},{12,4},{13,5},{14,8},{15,9},{1... | collective-permute-start | bytes 786440 | tf_op jit(solution)/shard_map/ppermute | solution.py:359
  6.6 19.3 %collective-permute-start.3 = (bf16[128,1024]{1,0:T(8,128)(2,1)S(1)}, bf16[128,1024]{1,0:T(8,128)(2,1)S(1)}, u32[]{:S(2)}, u32[]{:S(2)}) collective-permute-start(bf16[128,1024]{1,0:T(8,128)(2,1)S(1)} %constant_dynamic-slice_fusion.7), channel_id=1, source_target_pairs={{0,8},{1,9},{4,12},{5,13},{8,14},{9,15},{12,10},{13,11},{14,6},{15... | collective-permute-start | bytes 786440 | tf_op jit(solution)/shard_map/ppermute | solution.py:359
  6.8 19.2 %collective-permute-start.2 = (bf16[128,1024]{1,0:T(8,128)(2,1)S(1)}, bf16[128,1024]{1,0:T(8,128)(2,1)S(1)}, u32[]{:S(2)}, u32[]{:S(2)}) collective-permute-start(bf16[128,1024]{1,0:T(8,128)(2,1)S(1)} %constant_dynamic-slice_fusion.7), channel_id=1, source_target_pairs={{0,2},{1,3},{4,0},{5,1},{8,4},{9,5},{12,8},{13,9},{14,12},{15,13},... | collective-permute-start | bytes 786440 | tf_op jit(solution)/shard_map/ppermute | solution.py:359
  8.5 17.4 %collective-permute-start.1 = (bf16[128,1024]{1,0:T(8,128)(2,1)S(1)}, bf16[128,1024]{1,0:T(8,128)(2,1)S(1)}, u32[]{:S(2)}, u32[]{:S(2)}) collective-permute-start(bf16[128,1024]{1,0:T(8,128)(2,1)S(1)} %constant_dynamic-slice_fusion.7), channel_id=1, source_target_pairs={{0,4},{1,5},{4,8},{5,9},{8,12},{9,13},{12,14},{13,15},{14,10},{15,... | collective-permute-start | bytes 786440 | tf_op jit(solution)/shard_map/ppermute | solution.py:359
  25.9 13.4 %collective-permute-start.6 = (bf16[256,1024]{1,0:T(8,128)(2,1)}, bf16[256,1024]{1,0:T(8,128)(2,1)S(1)}, u32[]{:S(2)}, u32[]{:S(2)}) collective-permute-start(bf16[256,1024]{1,0:T(8,128)(2,1)} %get-tuple-element.27.refs_0_), channel_id=1, source_target_pairs={{0,2},{1,3},{2,0},{3,1},{4,6},{5,7},{6,4},{7,5},{8,10},{9,11},{10,... | collective-permute-start | bytes 1572872 | tf_op jit(solution)/shard_map/ppermute | solution.py:363
  27.8 28.2 %copy-start.1 = (bf16[256,1024]{1,0:T(8,128)(2,1)S(1)}, bf16[256,1024]{1,0:T(8,128)(2,1)}, u32[]{:S(2)}) copy-start(bf16[256,1024]{1,0:T(8,128)(2,1)} %get-tuple-element.27.refs_0_) | copy-start | bytes 1572868
  27.9 26.4 %collective-permute-start.7 = (bf16[256,1024]{1,0:T(8,128)(2,1)S(1)}, bf16[256,1024]{1,0:T(8,128)(2,1)S(1)}, u32[]{:S(2)}, u32[]{:S(2)}) collective-permute-start(bf16[256,1024]{1,0:T(8,128)(2,1)S(1)} %pad_maximum_fusion), channel_id=1, source_target_pairs={{0,16},{16,0},{1,17},{17,1},{2,18},{18,2},{3,19},{19,3},{4,20},{20... | collective-permute-start | bytes 1572872 | tf_op jit(solution)/shard_map/ppermute | solution.py:373
  39.4 14.9 %collective-permute-start.8 = (bf16[256,1024]{1,0:T(8,128)(2,1)S(1)}, bf16[256,1024]{1,0:T(8,128)(2,1)S(1)}, u32[]{:S(2)}, u32[]{:S(2)}) collective-permute-start(bf16[256,1024]{1,0:T(8,128)(2,1)S(1)} %collective-permute-done.6.refs_2_), channel_id=1, source_target_pairs={{0,1},{1,0},{2,3},{3,2},{4,5},{5,4},{6,7},{7,6},{8,9},{9,8},{10,11... | collective-permute-start | bytes 1572872 | tf_op jit(solution)/shard_map/ppermute | solution.py:345
  39.4 11.4 %collective-permute-start.11 = (bf16[128,1024]{1,0:T(8,128)(2,1)S(1)}, bf16[128,1024]{1,0:T(8,128)(2,1)S(1)}, u32[]{:S(2)}, u32[]{:S(2)}) collective-permute-start(bf16[128,1024]{1,0:T(8,128)(2,1)S(1)} %broadcast_select_fusion), channel_id=1, source_target_pairs={{0,8},{1,7},{4,12},{5,3},{8,14},{9,1},{12,10},{13,5},{14,6},{15,9}... | collective-permute-start | bytes 786440 | tf_op jit(solution)/shard_map/ppermute | solution.py:359
  42.0 12.2 %collective-permute-start.9 = (bf16[128,1024]{1,0:T(8,128)(2,1)S(1)}, bf16[128,1024]{1,0:T(8,128)(2,1)S(1)}, u32[]{:S(2)}, u32[]{:S(2)}) collective-permute-start(bf16[128,1024]{1,0:T(8,128)(2,1)S(1)} %collective-permute-done.3.refs_9_), channel_id=1, source_target_pairs={{0,4},{1,5},{4,8},{5,9},{8,12},{9,13},{12,14},{13,15},{14,10},{15,... | collective-permute-start | bytes 786440 | tf_op jit(solution)/shard_map/ppermute | solution.py:359
  43.6 10.7 %collective-permute-start.10 = (bf16[128,1024]{1,0:T(8,128)(2,1)S(1)}, bf16[128,1024]{1,0:T(8,128)(2,1)S(1)}, u32[]{:S(2)}, u32[]{:S(2)}) collective-permute-start(bf16[128,1024]{1,0:T(8,128)(2,1)S(1)} %collective-permute-done.4.refs_10_), channel_id=1, source_target_pairs={{0,2},{1,3},{4,0},{5,1},{8,4},{9,5},{12,8},{13,9},{14,12},{15,13},... | collective-permute-start | bytes 786440 | tf_op jit(solution)/shard_map/ppermute | solution.py:359
  50.8 16.1 %collective-permute-start.12 = (bf16[256,1024]{1,0:T(8,128)(2,1)S(1)}, bf16[256,1024]{1,0:T(8,128)(2,1)S(1)}, u32[]{:S(2)}, u32[]{:S(2)}) collective-permute-start(bf16[256,1024]{1,0:T(8,128)(2,1)S(1)} %collective-permute-done.6.refs_2_), channel_id=1, source_target_pairs={{0,4},{1,5},{2,14},{3,15},{4,8},{5,9},{6,2},{7,3},{8,12},{9,13},{1... | collective-permute-start | bytes 1572872 | tf_op jit(solution)/shard_map/ppermute | solution.py:369
  54.4 31.5 %copy-start = (bf16[1024,1024]{1,0:T(8,128)(2,1)S(1)}, bf16[1024,1024]{1,0:T(8,128)(2,1)}, u32[]{:S(2)}) copy-start(bf16[1024,1024]{1,0:T(8,128)(2,1)} %param.21) | copy-start | bytes 6291460
  54.4 31.5 %copy-start.2 = (bf16[256,1024]{1,0:T(8,128)(2,1)S(1)}, bf16[256,1024]{1,0:T(8,128)(2,1)}, u32[]{:S(2)}) copy-start(bf16[256,1024]{1,0:T(8,128)(2,1)} %get-tuple-element.24.tokens_ref) | copy-start | bytes 1572868
  54.4 12.6 %collective-permute-start.13 = (bf16[192,1024]{1,0:T(8,128)(2,1)S(1)}, bf16[192,1024]{1,0:T(8,128)(2,1)S(1)}, u32[]{:S(2)}, u32[]{:S(2)}) collective-permute-start(bf16[192,1024]{1,0:T(8,128)(2,1)S(1)} %pad_maximum_fusion.1), channel_id=1, source_target_pairs={{0,16},{16,0},{1,17},{17,1},{2,18},{18,2},{3,19},{19,3},{4,20},{20... | collective-permute-start | bytes 1179656 | tf_op jit(solution)/shard_map/ppermute | solution.py:373
  56.0 11.0 %collective-permute-start.5 = (bf16[256,1024]{1,0:T(8,128)(2,1)S(1)}, bf16[256,1024]{1,0:T(8,128)(2,1)S(1)}, u32[]{:S(2)}, u32[]{:S(2)}) collective-permute-start(bf16[256,1024]{1,0:T(8,128)(2,1)S(1)} %copy-done.1), channel_id=1, source_target_pairs={{0,1},{1,0},{2,3},{3,2},{4,5},{5,4},{6,7},{7,6},{8,9},{9,8},{10,11... | collective-permute-start | bytes 1572872 | tf_op jit(solution)/shard_map/ppermute | solution.py:345
  67.0 1.9 %collective-permute-start.14 = (bf16[256,1024]{1,0:T(8,128)(2,1)S(1)}, bf16[256,1024]{1,0:T(8,128)(2,1)S(1)}, u32[]{:S(2)}, u32[]{:S(2)}) collective-permute-start(bf16[256,1024]{1,0:T(8,128)(2,1)S(1)} %collective-permute-done.12.refs_4_), channel_id=1, source_target_pairs={{0,1},{1,0},{2,3},{3,2},{4,5},{5,4},{6,7},{7,6},{8,9},{9,8},{10,11... | collective-permute-start | bytes 1572872 | tf_op jit(solution)/shard_map/ppermute | solution.py:345
  84.3 1.6 %collective-permute-start.15 = (bf16[4,256,128]{2,1,0:T(8,128)(2,1)S(1)}, bf16[4,256,128]{2,1,0:T(8,128)(2,1)S(1)}, u32[]{:S(2)}, u32[]{:S(2)}) collective-permute-start(bf16[4,256,128]{2,1,0:T(8,128)(2,1)S(1)} %get-tuple-element.40), channel_id=1, source_target_pairs={{0,1},{1,0},{2,3},{3,2},{4,5},{5,4},{6,7},{7,6},{8,9},{9,8},{10,11... | collective-permute-start | bytes 786440 | tf_op jit(solution)/shard_map/ppermute | solution.py:345

commit v5 on v4

--- a/solution.py
+++ b/solution.py
@@ -24,11 +24,19 @@
     return lax.dot_general(left, right, (((1,), (1,)), ((), ())), preferred_element_type=F32)
 
 
+def ring_place(index):
+    chip = index // 2
+    return jnp.where(chip % 2 == 0, chip // 2, 7 - chip // 2)
+
+
 def chip_at(index, step):
     if step is None:
         return 0
-    chip = index // 2
-    here = jnp.where(chip % 2 == 0, chip // 2, 7 - chip // 2)
+    here = ring_place(index)
+    if step == "beside":
+        step = jnp.where(here % 2 == 0, -3, 3)
+    elif step == "pair":
+        step = jnp.where(here % 2 == 0, 3, -3)
     at = (here + step + 8) % 8
     return jnp.where(at < 4, 2 * at, 2 * (7 - at) + 1)
 
@@ -359,8 +367,8 @@
     return lax.ppermute(value, "space", pairs)
 
 
-def beside(value):
-    return lax.ppermute(value, "space", [(i, i ^ 2) for i in range(2 * len(RING))])
+def crossed(value, bits):
+    return lax.ppermute(value, "space", [(i, i ^ bits) for i in range(2 * len(RING))])
 
 
 def onward(value):
@@ -438,16 +446,19 @@
         normed, *early = together(normed, *early)
         weights += [(b, (-step, "ring")) for b, step in zip(early, (1, -1, 2, -2))]
         swap = swapped(early)
-        late = [around(early[2], 1), around(early[3], -1)]
-        late.append(around(jnp.where(side == 0, early[2], early[3]), (2, -2)))
-        near = beside(normed)
+        place = ring_place(lax.axis_index("space"))
+        near = crossed(normed, 2)
+        pair = crossed(jnp.where(place % 2 == 0, early[2], early[3]), 4)
+        near, pair = together(near, pair)
         far, near_sib = onward(near), sibling(near)
+        other = jnp.where(place % 4 < 2, early[3], early[2])
+        late = [pair, crossed(other, 2), crossed(other, 6)]
         swap, near_sib, *late = together(swap, near_sib, *late)
-        weights += [(b, (-step, "ring")) for b, step in zip(late, (3, -3, 4))]
+        weights += [(b, (step, "ring")) for b, step in zip(late, ("pair", "beside", 4))]
         weights.append((swap, ((-1, 1, -2, 2), "swap")))
         last = swapped(late)
         far, last = together(far, last)
-        weights.append((last, ((-3, 3, -4), "swap")))
+        weights.append((last, (("pair", "beside", 4), "swap")))
     else:
         near, far = from_chip(normed, 1), from_chip(normed, -1)
         near_sib = sibling(near)

time: 87.5 us -> 87.7 us (level); the launches traced: 87.4 us -> 86.3 us
    ppermute x1 -> x4, waiting for transfers between devices: 9.89 us -> 19.9 us  [crossed(): lax.ppermute(value, 'space', [(i, i ^ bits) for i in range(2 * len(RING))])]
    ppermute x7 -> x4, waiting for transfers between devices: 9.31 us -> 0.01 us  [around(): return lax.ppermute(value, 'space', pairs)]
    ppermute x1 -> x4, starting transfers between devices: 1.86 us -> 6.54 us  [crossed(): lax.ppermute(value, 'space', [(i, i ^ bits) for i in range(2 * len(RING))])]
    ppermute x7 -> x4, starting transfers between devices: 10.8 us -> 6.09 us  [around(): return lax.ppermute(value, 'space', pairs)]
    ppermute x1, waiting for transfers between devices: 10.7 us -> 6.03 us  [onward(): return lax.ppermute(value, 'space', pairs)]
    ppermute x2, waiting for transfers between devices: 0.01 us -> 3.53 us  [across(): return lax.ppermute(value, 'groups', [(0, 1), (1, 0)])]
  transfers between devices with their start and end apart: 16 -> 16, of which waited for: 7 -> 9; matrix products, arithmetic and copies ran while one was open for 0% -> 0% of each run, Pallas kernels for 20% -> 20%
where the time goes in v5:
time: 87.7 us; the launch traced here: 86.3 us
  Pallas kernels  34 us (39%)
  waiting for transfers between devices  33.8 us (39%)
  starting transfers between devices  16.9 us (19%)
  local copies, waits for them, and re-layouts  1.19 us (1%)
    ppermute x4, waiting for transfers between devices, crossed(): lax.ppermute(value, 'space', [(i, i ^ bits) for i in range(2 * len(RING))])  19.9 us
    pallas_call x1, Pallas kernels, aggregate(): pl.pallas_call(aggregate_kernel, out_shape=[jax.ShapeDtypeStruct((tokens,...  17.1 us
    pallas_call x1, Pallas kernels, attend(): pl.pallas_call(functools.partial(attend_kernel, spots=spots), out_shape=[...  15.4 us
    ppermute x4, starting transfers between devices, crossed(): lax.ppermute(value, 'space', [(i, i ^ bits) for i in range(2 * len(RING))])  6.54 us
    ppermute x4, starting transfers between devices, around(): return lax.ppermute(value, 'space', pairs)  6.09 us
    ppermute x1, waiting for transfers between devices, onward(): return lax.ppermute(value, 'space', pairs)  6.03 us
    ppermute x5, waiting for transfers between devices, sibling(): return lax.ppermute(value, 'space', [(i, i ^ 1) for i in range(length)])  4.29 us
    ppermute x2, waiting for transfers between devices, across(): return lax.ppermute(value, 'groups', [(0, 1), (1, 0)])  3.53 us
  transfers between devices with their start and end apart: 16, of which 9 were waited for; matrix products, arithmetic and copies ran while one was open for 0% of the time, Pallas kernels for 20%

profile of v5, /device:TPU:0, one launch (start us, length us, event | category | flops | bytes accessed | tf_op | source)
XLA Modules:
  0.0 86.3 jit_solution(11303814184520053024)
XLA Ops:
  0.0 1.1 %fusion = (bf16[64,1024]{1,0:T(8,128)(2,1)S(1)}, bf16[64,1024]{1,0:T(8,128)(2,1)S(1)}, bf16[64,1024]{1,0:T(8,128)(2,1)S(1)}) fusion(bf16[192,1024]{1,0:T(8,128)(2,1)} %bitcast.4), kind=kLoop, calls=%fused_computation.13 | loop fusion | bytes 786432 | tf_op jit(solution)/shard_map/slice | solution.py:390
  1.1 0.5 collective-permute-start
  1.6 1.0 %collective-permute-done = bf16[64,1024]{1,0:T(8,128)(2,1)S(1)} collective-permute-done((bf16[64,1024]{1,0:T(8,128)(2,1)S(1)}, bf16[64,1024]{1,0:T(8,128)(2,1)S(1)}, u32[]{:S(2)}, u32[]{:S(2)}) %collective-permute-start) | collective-permute-done | bytes 131104 | tf_op jit(solution)/shard_map/ppermute | solution.py:353
  2.6 0.1 maximum_select_fusion.refs_6_
  2.7 3.9 %collective-permute-start.4 = (bf16[128,1024]{1,0:T(8,128)(2,1)S(1)}, bf16[128,1024]{1,0:T(8,128)(2,1)S(1)}, u32[]{:S(2)}, u32[]{:S(2)}) collective-permute-start(bf16[128,1024]{1,0:T(8,128)(2,1)S(1)} %constant_dynamic-slice_fusion.7), channel_id=1, source_target_pairs={{0,6},{1,7},{4,2},{5,3},{8,0},{9,1},{12,4},{13,5},{14,8},{15,9},{1... | collective-permute-start | bytes 786440 | tf_op jit(solution)/shard_map/ppermute | solution.py:367
  6.6 0.1 collective-permute-start.3
  6.8 1.8 %collective-permute-start.2 = (bf16[128,1024]{1,0:T(8,128)(2,1)S(1)}, bf16[128,1024]{1,0:T(8,128)(2,1)S(1)}, u32[]{:S(2)}, u32[]{:S(2)}) collective-permute-start(bf16[128,1024]{1,0:T(8,128)(2,1)S(1)} %constant_dynamic-slice_fusion.7), channel_id=1, source_target_pairs={{0,2},{1,3},{4,0},{5,1},{8,4},{9,5},{12,8},{13,9},{14,12},{15,13},... | collective-permute-start | bytes 786440 | tf_op jit(solution)/shard_map/ppermute | solution.py:367
  8.5 0.2 collective-permute-start.1
  8.8 17.1 %aggregate.1 = (bf16[256,1024]{1,0:T(8,128)(2,1)}, bf16[256,1024]{1,0:T(8,128)(2,1)}) custom-call(s32[64]{0:T(128)} %order_ref.1, bf16[64,1024]{1,0:T(8,128)(2,1)} %var_embed_hbm.1, bf16[16,1024]{1,0:T(8,128)(2,1)} %keys_hbm.1, bf16[64,16,1024]{2,1,0:T(8,128)(2,1)} %embed_hbm, bf16[256,1024]{1,0:T(8,128)(2,1)} %patches_hbm.1, bf16[1024,1024]{1,0:T(8,128)(2,1)} %value_hbm.1, ...), custom_call_target="tpu_custom_call" | custom-call | flops 16000000000 | bytes 8388608 | tf_op jit(solution)/shard_map/aggregate/pallas_call | solution.py:213
  25.9 0.0 collective-permute-done.4.refs_10_
  25.9 0.0 collective-permute-done.3.refs_9_
  25.9 0.0 collective-permute-done.2.refs_8_
  25.9 0.0 collective-permute-done.1.refs_7_
  25.9 1.9 %collective-permute-start.6 = (bf16[256,1024]{1,0:T(8,128)(2,1)}, bf16[256,1024]{1,0:T(8,128)(2,1)S(1)}, u32[]{:S(2)}, u32[]{:S(2)}) collective-permute-start(bf16[256,1024]{1,0:T(8,128)(2,1)} %get-tuple-element.29.refs_0_), channel_id=1, source_target_pairs={{0,2},{1,3},{2,0},{3,1},{4,6},{5,7},{6,4},{7,5},{8,10},{9,11},{10,... | collective-permute-start | bytes 1572872 | tf_op jit(solution)/shard_map/ppermute | solution.py:371
  27.8 0.0 copy-start.1
  27.9 1.6 %collective-permute-start.7 = (bf16[128,1024]{1,0:T(8,128)(2,1)S(1)}, bf16[128,1024]{1,0:T(8,128)(2,1)S(1)}, u32[]{:S(2)}, u32[]{:S(2)}) collective-permute-start(bf16[128,1024]{1,0:T(8,128)(2,1)S(1)} %get-tuple-element.46), channel_id=1, source_target_pairs={{0,4},{1,5},{2,6},{3,7},{4,0},{5,1},{6,2},{7,3},{8,12},{9,13},{10,... | collective-permute-start | bytes 786440 | tf_op jit(solution)/shard_map/ppermute | solution.py:371
  29.6 1.6 %collective-permute-start.8 = (bf16[256,1024]{1,0:T(8,128)(2,1)S(1)}, bf16[256,1024]{1,0:T(8,128)(2,1)S(1)}, u32[]{:S(2)}, u32[]{:S(2)}) collective-permute-start(bf16[256,1024]{1,0:T(8,128)(2,1)S(1)} %pad_maximum_fusion), channel_id=1, source_target_pairs={{0,16},{16,0},{1,17},{17,1},{2,18},{18,2},{3,19},{19,3},{4,20},{20... | collective-permute-start | bytes 1572872 | tf_op jit(solution)/shard_map/ppermute | solution.py:381
  31.2 3.7 %collective-permute-done.7.refs_11_ = bf16[128,1024]{1,0:T(8,128)(2,1)S(1)} collective-permute-done((bf16[128,1024]{1,0:T(8,128)(2,1)S(1)}, bf16[128,1024]{1,0:T(8,128)(2,1)S(1)}, u32[]{:S(2)}, u32[]{:S(2)}) %collective-permute-start.7) | collective-permute-done | bytes 262176 | tf_op jit(solution)/shard_map/ppermute | solution.py:371
  34.9 4.5 %collective-permute-done.6.refs_2_ = bf16[256,1024]{1,0:T(8,128)(2,1)S(1)} collective-permute-done((bf16[256,1024]{1,0:T(8,128)(2,1)}, bf16[256,1024]{1,0:T(8,128)(2,1)S(1)}, u32[]{:S(2)}, u32[]{:S(2)}) %collective-permute-start.6) | collective-permute-done | bytes 524320 | tf_op jit(solution)/shard_map/ppermute | solution.py:371
  39.4 0.0 collective-permute-start.9
  39.4 2.5 %collective-permute-start.11 = (bf16[128,1024]{1,0:T(8,128)(2,1)S(1)}, bf16[128,1024]{1,0:T(8,128)(2,1)S(1)}, u32[]{:S(2)}, u32[]{:S(2)}) collective-permute-start(bf16[128,1024]{1,0:T(8,128)(2,1)S(1)} %get-tuple-element.45), channel_id=1, source_target_pairs={{0,6},{1,7},{2,4},{3,5},{4,2},{5,3},{6,0},{7,1},{8,14},{9,15},{10,... | collective-permute-start | bytes 786440 | tf_op jit(solution)/shard_map/ppermute | solution.py:371
  41.9 0.5 collective-permute-start.10
  42.4 0.4 collective-permute-start.12
  42.9 6.6 %collective-permute-done.11.refs_13_ = bf16[128,1024]{1,0:T(8,128)(2,1)S(1)} collective-permute-done((bf16[128,1024]{1,0:T(8,128)(2,1)S(1)}, bf16[128,1024]{1,0:T(8,128)(2,1)S(1)}, u32[]{:S(2)}, u32[]{:S(2)}) %collective-permute-start.11) | collective-permute-done | bytes 262176 | tf_op jit(solution)/shard_map/ppermute | solution.py:371
  49.4 5.2 %collective-permute-done.10.refs_12_ = bf16[128,1024]{1,0:T(8,128)(2,1)S(1)} collective-permute-done((bf16[128,1024]{1,0:T(8,128)(2,1)S(1)}, bf16[128,1024]{1,0:T(8,128)(2,1)S(1)}, u32[]{:S(2)}, u32[]{:S(2)}) %collective-permute-start.10) | collective-permute-done | bytes 262176 | tf_op jit(solution)/shard_map/ppermute | solution.py:371
  54.6 0.0 collective-permute-done.8.refs_14_
  54.6 0.0 collective-permute-done.9.refs_3_
  54.7 0.0 copy-start
  54.7 0.0 copy-start.2
  54.7 1.6 %collective-permute-start.13 = (bf16[192,1024]{1,0:T(8,128)(2,1)S(1)}, bf16[192,1024]{1,0:T(8,128)(2,1)S(1)}, u32[]{:S(2)}, u32[]{:S(2)}) collective-permute-start(bf16[192,1024]{1,0:T(8,128)(2,1)S(1)} %pad_maximum_fusion.1), channel_id=1, source_target_pairs={{0,16},{16,0},{1,17},{17,1},{2,18},{18,2},{3,19},{19,3},{4,20},{20... | collective-permute-start | bytes 1179656 | tf_op jit(solution)/shard_map/ppermute | solution.py:381
  56.3 0.0 copy-done.1
  56.3 0.0 collective-permute-start.5
  56.3 6.0 %collective-permute-done.12.refs_4_ = bf16[256,1024]{1,0:T(8,128)(2,1)S(1)} collective-permute-done((bf16[256,1024]{1,0:T(8,128)(2,1)S(1)}, bf16[256,1024]{1,0:T(8,128)(2,1)S(1)}, u32[]{:S(2)}, u32[]{:S(2)}) %collective-permute-start.12) | collective-permute-done | bytes 524320 | tf_op jit(solution)/shard_map/ppermute | solution.py:377
  62.3 3.5 %collective-permute-done.13.refs_15_ = bf16[192,1024]{1,0:T(8,128)(2,1)S(1)} collective-permute-done((bf16[192,1024]{1,0:T(8,128)(2,1)S(1)}, bf16[192,1024]{1,0:T(8,128)(2,1)S(1)}, u32[]{:S(2)}, u32[]{:S(2)}) %collective-permute-start.13) | collective-permute-done | bytes 393248 | tf_op jit(solution)/shard_map/ppermute | solution.py:381
  65.9 0.0 collective-permute-start.14
  65.9 0.0 collective-permute-done.5.refs_1_
  65.9 1.9 %collective-permute-done.14.refs_5_ = bf16[256,1024]{1,0:T(8,128)(2,1)S(1)} collective-permute-done((bf16[256,1024]{1,0:T(8,128)(2,1)S(1)}, bf16[256,1024]{1,0:T(8,128)(2,1)S(1)}, u32[]{:S(2)}, u32[]{:S(2)}) %collective-permute-start.14) | collective-permute-done | bytes 524320 | tf_op jit(solution)/shard_map/ppermute | solution.py:353
  67.8 15.4 %attend.1 = (bf16[4,256,128]{2,1,0:T(8,128)(2,1)S(1)}, bf16[4,256,128]{2,1,0:T(8,128)(2,1)S(1)}) custom-call(bf16[256,1024]{1,0:T(8,128)(2,1)S(1)} %copy-done.1, bf16[256,1024]{1,0:T(8,128)(2,1)S(1)} %collective-permute-done.5.refs_1_, bf16[256,1024]{1,0:T(8,128)(2,1)S(1)} %collective-permute-done.6.refs_2_, ...), custom_call_target="tpu_custom_call" | custom-call | flops 10000000000 | bytes 8388608 | tf_op jit(solution)/shard_map/attend/pallas_call | solution.py:306
  83.1 0.2 collective-permute-start.15
  83.4 1.4 %collective-permute-done.15.other_ref = bf16[4,256,128]{2,1,0:T(8,128)(2,1)S(1)} collective-permute-done((bf16[4,256,128]{2,1,0:T(8,128)(2,1)S(1)}, bf16[4,256,128]{2,1,0:T(8,128)(2,1)S(1)}, u32[]{:S(2)}, u32[]{:S(2)}) %collective-permute-start.15) | collective-permute-done | bytes 262176 | tf_op jit(solution)/shard_map/ppermute | solution.py:353
  84.7 0.0 copy-done
  84.8 0.0 copy-done.2
  84.8 1.5 %finish.1 = bf16[256,1024]{1,0:T(8,128)(2,1)} custom-call(bf16[256,1024]{1,0:T(8,128)(2,1)S(1)} %copy-done.2, bf16[4,256,128]{2,1,0:T(8,128)(2,1)S(1)} %get-tuple-element.43.mine_ref, bf16[4,256,128]{2,1,0:T(8,128)(2,1)S(1)} %collective-permute-done.15.other_ref, bf16[8,2,64,1024]{3,2,1,0:T(8,128)(2,1)S(1)} %bitcast.3), custom_call_target="tpu_custom_call" | custom-call | flops 1000000000 | bytes 4194304 | tf_op jit(solution)/shard_map/finish/pallas_call | solution.py:340
  (9 shorter events, 0.2 us)
Async XLA Ops:
  1.1 1.5 %collective-permute-start = (bf16[64,1024]{1,0:T(8,128)(2,1)S(1)}, bf16[64,1024]{1,0:T(8,128)(2,1)S(1)}, u32[]{:S(2)}, u32[]{:S(2)}) collective-permute-start(bf16[64,1024]{1,0:T(8,128)(2,1)S(1)} %get-tuple-element.48), channel_id=1, source_target_pairs={{0,1},{1,0},{2,3},{3,2},{4,5},{5,4},{6,7},{7,6},{8,9},{9,8},{10,11... | collective-permute-start | bytes 393224 | tf_op jit(solution)/shard_map/ppermute | solution.py:353
  2.7 23.2 %collective-permute-start.4 = (bf16[128,1024]{1,0:T(8,128)(2,1)S(1)}, bf16[128,1024]{1,0:T(8,128)(2,1)S(1)}, u32[]{:S(2)}, u32[]{:S(2)}) collective-permute-start(bf16[128,1024]{1,0:T(8,128)(2,1)S(1)} %constant_dynamic-slice_fusion.7), channel_id=1, source_target_pairs={{0,6},{1,7},{4,2},{5,3},{8,0},{9,1},{12,4},{13,5},{14,8},{15,9},{1... | collective-permute-start | bytes 786440 | tf_op jit(solution)/shard_map/ppermute | solution.py:367
  6.6 19.3 %collective-permute-start.3 = (bf16[128,1024]{1,0:T(8,128)(2,1)S(1)}, bf16[128,1024]{1,0:T(8,128)(2,1)S(1)}, u32[]{:S(2)}, u32[]{:S(2)}) collective-permute-start(bf16[128,1024]{1,0:T(8,128)(2,1)S(1)} %constant_dynamic-slice_fusion.7), channel_id=1, source_target_pairs={{0,8},{1,9},{4,12},{5,13},{8,14},{9,15},{12,10},{13,11},{14,6},{15... | collective-permute-start | bytes 786440 | tf_op jit(solution)/shard_map/ppermute | solution.py:367
  6.8 19.2 %collective-permute-start.2 = (bf16[128,1024]{1,0:T(8,128)(2,1)S(1)}, bf16[128,1024]{1,0:T(8,128)(2,1)S(1)}, u32[]{:S(2)}, u32[]{:S(2)}) collective-permute-start(bf16[128,1024]{1,0:T(8,128)(2,1)S(1)} %constant_dynamic-slice_fusion.7), channel_id=1, source_target_pairs={{0,2},{1,3},{4,0},{5,1},{8,4},{9,5},{12,8},{13,9},{14,12},{15,13},... | collective-permute-start | bytes 786440 | tf_op jit(solution)/shard_map/ppermute | solution.py:367
  8.5 17.4 %collective-permute-start.1 = (bf16[128,1024]{1,0:T(8,128)(2,1)S(1)}, bf16[128,1024]{1,0:T(8,128)(2,1)S(1)}, u32[]{:S(2)}, u32[]{:S(2)}) collective-permute-start(bf16[128,1024]{1,0:T(8,128)(2,1)S(1)} %constant_dynamic-slice_fusion.7), channel_id=1, source_target_pairs={{0,4},{1,5},{4,8},{5,9},{8,12},{9,13},{12,14},{13,15},{14,10},{15,... | collective-permute-start | bytes 786440 | tf_op jit(solution)/shard_map/ppermute | solution.py:367
  25.9 13.4 %collective-permute-start.6 = (bf16[256,1024]{1,0:T(8,128)(2,1)}, bf16[256,1024]{1,0:T(8,128)(2,1)S(1)}, u32[]{:S(2)}, u32[]{:S(2)}) collective-permute-start(bf16[256,1024]{1,0:T(8,128)(2,1)} %get-tuple-element.29.refs_0_), channel_id=1, source_target_pairs={{0,2},{1,3},{2,0},{3,1},{4,6},{5,7},{6,4},{7,5},{8,10},{9,11},{10,... | collective-permute-start | bytes 1572872 | tf_op jit(solution)/shard_map/ppermute | solution.py:371
  27.8 28.4 %copy-start.1 = (bf16[256,1024]{1,0:T(8,128)(2,1)S(1)}, bf16[256,1024]{1,0:T(8,128)(2,1)}, u32[]{:S(2)}) copy-start(bf16[256,1024]{1,0:T(8,128)(2,1)} %get-tuple-element.29.refs_0_) | copy-start | bytes 1572868
  27.9 7.0 %collective-permute-start.7 = (bf16[128,1024]{1,0:T(8,128)(2,1)S(1)}, bf16[128,1024]{1,0:T(8,128)(2,1)S(1)}, u32[]{:S(2)}, u32[]{:S(2)}) collective-permute-start(bf16[128,1024]{1,0:T(8,128)(2,1)S(1)} %get-tuple-element.46), channel_id=1, source_target_pairs={{0,4},{1,5},{2,6},{3,7},{4,0},{5,1},{6,2},{7,3},{8,12},{9,13},{10,... | collective-permute-start | bytes 786440 | tf_op jit(solution)/shard_map/ppermute | solution.py:371
  29.6 25.0 %collective-permute-start.8 = (bf16[256,1024]{1,0:T(8,128)(2,1)S(1)}, bf16[256,1024]{1,0:T(8,128)(2,1)S(1)}, u32[]{:S(2)}, u32[]{:S(2)}) collective-permute-start(bf16[256,1024]{1,0:T(8,128)(2,1)S(1)} %pad_maximum_fusion), channel_id=1, source_target_pairs={{0,16},{16,0},{1,17},{17,1},{2,18},{18,2},{3,19},{19,3},{4,20},{20... | collective-permute-start | bytes 1572872 | tf_op jit(solution)/shard_map/ppermute | solution.py:381
  39.4 15.2 %collective-permute-start.9 = (bf16[256,1024]{1,0:T(8,128)(2,1)S(1)}, bf16[256,1024]{1,0:T(8,128)(2,1)S(1)}, u32[]{:S(2)}, u32[]{:S(2)}) collective-permute-start(bf16[256,1024]{1,0:T(8,128)(2,1)S(1)} %collective-permute-done.6.refs_2_), channel_id=1, source_target_pairs={{0,1},{1,0},{2,3},{3,2},{4,5},{5,4},{6,7},{7,6},{8,9},{9,8},{10,11... | collective-permute-start | bytes 1572872 | tf_op jit(solution)/shard_map/ppermute | solution.py:353
  39.4 10.0 %collective-permute-start.11 = (bf16[128,1024]{1,0:T(8,128)(2,1)S(1)}, bf16[128,1024]{1,0:T(8,128)(2,1)S(1)}, u32[]{:S(2)}, u32[]{:S(2)}) collective-permute-start(bf16[128,1024]{1,0:T(8,128)(2,1)S(1)} %get-tuple-element.45), channel_id=1, source_target_pairs={{0,6},{1,7},{2,4},{3,5},{4,2},{5,3},{6,0},{7,1},{8,14},{9,15},{10,... | collective-permute-start | bytes 786440 | tf_op jit(solution)/shard_map/ppermute | solution.py:371
  41.9 12.7 %collective-permute-start.10 = (bf16[128,1024]{1,0:T(8,128)(2,1)S(1)}, bf16[128,1024]{1,0:T(8,128)(2,1)S(1)}, u32[]{:S(2)}, u32[]{:S(2)}) collective-permute-start(bf16[128,1024]{1,0:T(8,128)(2,1)S(1)} %get-tuple-element.45), channel_id=1, source_target_pairs={{0,2},{1,3},{2,0},{3,1},{4,6},{5,7},{6,4},{7,5},{8,10},{9,11},{10,... | collective-permute-start | bytes 786440 | tf_op jit(solution)/shard_map/ppermute | solution.py:371
  42.4 19.9 %collective-permute-start.12 = (bf16[256,1024]{1,0:T(8,128)(2,1)S(1)}, bf16[256,1024]{1,0:T(8,128)(2,1)S(1)}, u32[]{:S(2)}, u32[]{:S(2)}) collective-permute-start(bf16[256,1024]{1,0:T(8,128)(2,1)S(1)} %collective-permute-done.6.refs_2_), channel_id=1, source_target_pairs={{0,4},{1,5},{2,14},{3,15},{4,8},{5,9},{6,2},{7,3},{8,12},{9,13},{1... | collective-permute-start | bytes 1572872 | tf_op jit(solution)/shard_map/ppermute | solution.py:377
  54.7 30.0 %copy-start = (bf16[1024,1024]{1,0:T(8,128)(2,1)S(1)}, bf16[1024,1024]{1,0:T(8,128)(2,1)}, u32[]{:S(2)}) copy-start(bf16[1024,1024]{1,0:T(8,128)(2,1)} %param.21) | copy-start | bytes 6291460
  54.7 30.0 %copy-start.2 = (bf16[256,1024]{1,0:T(8,128)(2,1)S(1)}, bf16[256,1024]{1,0:T(8,128)(2,1)}, u32[]{:S(2)}) copy-start(bf16[256,1024]{1,0:T(8,128)(2,1)} %get-tuple-element.26.tokens_ref) | copy-start | bytes 1572868
  54.7 11.1 %collective-permute-start.13 = (bf16[192,1024]{1,0:T(8,128)(2,1)S(1)}, bf16[192,1024]{1,0:T(8,128)(2,1)S(1)}, u32[]{:S(2)}, u32[]{:S(2)}) collective-permute-start(bf16[192,1024]{1,0:T(8,128)(2,1)S(1)} %pad_maximum_fusion.1), channel_id=1, source_target_pairs={{0,16},{16,0},{1,17},{17,1},{2,18},{18,2},{3,19},{19,3},{4,20},{20... | collective-permute-start | bytes 1179656 | tf_op jit(solution)/shard_map/ppermute | solution.py:381
  56.3 9.6 %collective-permute-start.5 = (bf16[256,1024]{1,0:T(8,128)(2,1)S(1)}, bf16[256,1024]{1,0:T(8,128)(2,1)S(1)}, u32[]{:S(2)}, u32[]{:S(2)}) collective-permute-start(bf16[256,1024]{1,0:T(8,128)(2,1)S(1)} %copy-done.1), channel_id=1, source_target_pairs={{0,1},{1,0},{2,3},{3,2},{4,5},{5,4},{6,7},{7,6},{8,9},{9,8},{10,11... | collective-permute-start | bytes 1572872 | tf_op jit(solution)/shard_map/ppermute | solution.py:353
  65.9 1.9 %collective-permute-start.14 = (bf16[256,1024]{1,0:T(8,128)(2,1)S(1)}, bf16[256,1024]{1,0:T(8,128)(2,1)S(1)}, u32[]{:S(2)}, u32[]{:S(2)}) collective-permute-start(bf16[256,1024]{1,0:T(8,128)(2,1)S(1)} %collective-permute-done.12.refs_4_), channel_id=1, source_target_pairs={{0,1},{1,0},{2,3},{3,2},{4,5},{5,4},{6,7},{7,6},{8,9},{9,8},{10,11... | collective-permute-start | bytes 1572872 | tf_op jit(solution)/shard_map/ppermute | solution.py:353
  83.1 1.6 %collective-permute-start.15 = (bf16[4,256,128]{2,1,0:T(8,128)(2,1)S(1)}, bf16[4,256,128]{2,1,0:T(8,128)(2,1)S(1)}, u32[]{:S(2)}, u32[]{:S(2)}) collective-permute-start(bf16[4,256,128]{2,1,0:T(8,128)(2,1)S(1)} %get-tuple-element.44), channel_id=1, source_target_pairs={{0,1},{1,0},{2,3},{3,2},{4,5},{5,4},{6,7},{7,6},{8,9},{9,8},{10,11... | collective-permute-start | bytes 786440 | tf_op jit(solution)/shard_map/ppermute | solution.py:353

commit v6 on v5

--- a/solution.py
+++ b/solution.py
@@ -449,16 +449,18 @@
         place = ring_place(lax.axis_index("space"))
         near = crossed(normed, 2)
         pair = crossed(jnp.where(place % 2 == 0, early[2], early[3]), 4)
-        near, pair = together(near, pair)
+        low = place % 4 < 2
+        opposite = crossed(jnp.where(low, early[2], early[3]), 8)
+        near, pair, opposite = together(near, pair, opposite)
         far, near_sib = onward(near), sibling(near)
-        other = jnp.where(place % 4 < 2, early[3], early[2])
-        late = [pair, crossed(other, 2), crossed(other, 6)]
-        swap, near_sib, *late = together(swap, near_sib, *late)
-        weights += [(b, (step, "ring")) for b, step in zip(late, ("pair", "beside", 4))]
-        weights.append((swap, ((-1, 1, -2, 2), "swap")))
-        last = swapped(late)
-        far, last = together(far, last)
-        weights.append((last, (("pair", "beside", 4), "swap")))
+        beside = crossed(jnp.where(low, early[3], early[2]), 2)
+        first = swapped([pair, opposite])
+        swap, near_sib, beside = together(swap, near_sib, beside)
+        second = swapped([beside])
+        first, second, far = together(first, second, far)
+        weights += [(pair, ("pair", "ring")), (opposite, (4, "ring")), (beside, ("beside", "ring"))]
+        weights += [(swap, ((-1, 1, -2, 2), "swap"))]
+        weights += [(first, (("pair", 4), "swap")), (second, (("beside",), "swap"))]
     else:
         near, far = from_chip(normed, 1), from_chip(normed, -1)
         near_sib = sibling(near)

time: 87.7 us -> 78.4 us (0.89); the launches traced: 86.3 us -> 78.2 us
  waiting for transfers between devices: 33.8 us -> 21.4 us
  starting transfers between devices: 16.9 us -> 21.3 us
    ppermute x4, waiting for transfers between devices: 19.9 us -> 13 us  [crossed(): lax.ppermute(value, 'space', [(i, i ^ bits) for i in range(2 * len(RING))])]
    ppermute x2 -> x3, waiting for transfers between devices: 3.53 us -> 0.01 us  [across(): return lax.ppermute(value, 'groups', [(0, 1), (1, 0)])]
    ppermute x1, waiting for transfers between devices: 6.03 us -> 4.12 us  [onward(): return lax.ppermute(value, 'space', pairs)]
    ppermute x4, starting transfers between devices: 6.54 us -> 8.41 us  [crossed(): lax.ppermute(value, 'space', [(i, i ^ bits) for i in range(2 * len(RING))])]
    ppermute x2 -> x3, starting transfers between devices: 3.12 us -> 4.66 us  [across(): return lax.ppermute(value, 'groups', [(0, 1), (1, 0)])]
    ppermute x1, starting transfers between devices: 0.44 us -> 1.44 us  [onward(): return lax.ppermute(value, 'space', pairs)]
  transfers between devices with their start and end apart: 16 -> 17, of which waited for: 9 -> 7; matrix products, arithmetic and copies ran while one was open for 0% -> 0% of each run, Pallas kernels for 20% -> 22%
where the time goes in v6:
time: 78.4 us; the launch traced here: 78.2 us
  Pallas kernels  34 us (43%)
  waiting for transfers between devices  21.4 us (27%)
  starting transfers between devices  21.3 us (27%)
  local copies, waits for them, and re-layouts  1.17 us (1%)
    pallas_call x1, Pallas kernels, aggregate(): pl.pallas_call(aggregate_kernel, out_shape=[jax.ShapeDtypeStruct((tokens,...  17.1 us
    pallas_call x1, Pallas kernels, attend(): pl.pallas_call(functools.partial(attend_kernel, spots=spots), out_shape=[...  15.4 us
    ppermute x4, waiting for transfers between devices, crossed(): lax.ppermute(value, 'space', [(i, i ^ bits) for i in range(2 * len(RING))])  13 us
    ppermute x4, starting transfers between devices, crossed(): lax.ppermute(value, 'space', [(i, i ^ bits) for i in range(2 * len(RING))])  8.41 us
    ppermute x4, starting transfers between devices, around(): return lax.ppermute(value, 'space', pairs)  6.09 us
    ppermute x3, starting transfers between devices, across(): return lax.ppermute(value, 'groups', [(0, 1), (1, 0)])  4.66 us
    ppermute x5, waiting for transfers between devices, sibling(): return lax.ppermute(value, 'space', [(i, i ^ 1) for i in range(length)])  4.28 us
    ppermute x1, waiting for transfers between devices, onward(): return lax.ppermute(value, 'space', pairs)  4.12 us
  transfers between devices with their start and end apart: 17, of which 7 were waited for; matrix products, arithmetic and copies ran while one was open for 0% of the time, Pallas kernels for 22%

profile of v6, /device:TPU:0, one launch (start us, length us, event | category | flops | bytes accessed | tf_op | source)
XLA Modules:
  0.0 78.2 jit_solution(14705875271332156113)
XLA Ops:
  0.0 1.1 %fusion = (bf16[64,1024]{1,0:T(8,128)(2,1)S(1)}, bf16[64,1024]{1,0:T(8,128)(2,1)S(1)}, bf16[64,1024]{1,0:T(8,128)(2,1)S(1)}) fusion(bf16[192,1024]{1,0:T(8,128)(2,1)} %bitcast.4), kind=kLoop, calls=%fused_computation.14 | loop fusion | bytes 786432 | tf_op jit(solution)/shard_map/slice | solution.py:390
  1.1 0.5 collective-permute-start
  1.6 1.0 %collective-permute-done = bf16[64,1024]{1,0:T(8,128)(2,1)S(1)} collective-permute-done((bf16[64,1024]{1,0:T(8,128)(2,1)S(1)}, bf16[64,1024]{1,0:T(8,128)(2,1)S(1)}, u32[]{:S(2)}, u32[]{:S(2)}) %collective-permute-start) | collective-permute-done | bytes 131104 | tf_op jit(solution)/shard_map/ppermute | solution.py:353
  2.6 0.1 maximum_select_fusion.refs_6_
  2.7 3.9 %collective-permute-start.4 = (bf16[128,1024]{1,0:T(8,128)(2,1)S(1)}, bf16[128,1024]{1,0:T(8,128)(2,1)S(1)}, u32[]{:S(2)}, u32[]{:S(2)}) collective-permute-start(bf16[128,1024]{1,0:T(8,128)(2,1)S(1)} %constant_dynamic-slice_fusion.7), channel_id=1, source_target_pairs={{0,6},{1,7},{4,2},{5,3},{8,0},{9,1},{12,4},{13,5},{14,8},{15,9},{1... | collective-permute-start | bytes 786440 | tf_op jit(solution)/shard_map/ppermute | solution.py:367
  6.6 0.1 collective-permute-start.3
  6.8 1.8 %collective-permute-start.2 = (bf16[128,1024]{1,0:T(8,128)(2,1)S(1)}, bf16[128,1024]{1,0:T(8,128)(2,1)S(1)}, u32[]{:S(2)}, u32[]{:S(2)}) collective-permute-start(bf16[128,1024]{1,0:T(8,128)(2,1)S(1)} %constant_dynamic-slice_fusion.7), channel_id=1, source_target_pairs={{0,2},{1,3},{4,0},{5,1},{8,4},{9,5},{12,8},{13,9},{14,12},{15,13},... | collective-permute-start | bytes 786440 | tf_op jit(solution)/shard_map/ppermute | solution.py:367
  8.5 0.2 collective-permute-start.1
  8.8 17.1 %aggregate.1 = (bf16[256,1024]{1,0:T(8,128)(2,1)}, bf16[256,1024]{1,0:T(8,128)(2,1)}) custom-call(s32[64]{0:T(128)} %order_ref.1, bf16[64,1024]{1,0:T(8,128)(2,1)} %var_embed_hbm.1, bf16[16,1024]{1,0:T(8,128)(2,1)} %keys_hbm.1, bf16[64,16,1024]{2,1,0:T(8,128)(2,1)} %embed_hbm, bf16[256,1024]{1,0:T(8,128)(2,1)} %patches_hbm.1, bf16[1024,1024]{1,0:T(8,128)(2,1)} %value_hbm.1, ...), custom_call_target="tpu_custom_call" | custom-call | flops 16000000000 | bytes 8388608 | tf_op jit(solution)/shard_map/aggregate/pallas_call | solution.py:213
  25.9 0.0 collective-permute-done.4.refs_10_
  25.9 0.0 collective-permute-done.3.refs_9_
  25.9 0.0 collective-permute-done.2.refs_8_
  25.9 0.0 collective-permute-done.1.refs_7_
  25.9 0.0 copy-start.1
  25.9 1.9 %collective-permute-start.6 = (bf16[256,1024]{1,0:T(8,128)(2,1)}, bf16[256,1024]{1,0:T(8,128)(2,1)S(1)}, u32[]{:S(2)}, u32[]{:S(2)}) collective-permute-start(bf16[256,1024]{1,0:T(8,128)(2,1)} %get-tuple-element.29.refs_0_), channel_id=1, source_target_pairs={{0,2},{1,3},{2,0},{3,1},{4,6},{5,7},{6,4},{7,5},{8,10},{9,11},{10,... | collective-permute-start | bytes 1572872 | tf_op jit(solution)/shard_map/ppermute | solution.py:371
  27.8 0.1 broadcast_select_fusion
  27.9 2.7 %collective-permute-start.8 = (bf16[128,1024]{1,0:T(8,128)(2,1)S(1)}, bf16[128,1024]{1,0:T(8,128)(2,1)S(1)}, u32[]{:S(2)}, u32[]{:S(2)}) collective-permute-start(bf16[128,1024]{1,0:T(8,128)(2,1)S(1)} %get-tuple-element.46), channel_id=1, source_target_pairs={{0,8},{1,9},{2,10},{3,11},{4,12},{5,13},{6,14},{7,15},{8,0},{9,1},... | collective-permute-start | bytes 786440 | tf_op jit(solution)/shard_map/ppermute | solution.py:371
  30.5 1.6 %collective-permute-start.7 = (bf16[128,1024]{1,0:T(8,128)(2,1)S(1)}, bf16[128,1024]{1,0:T(8,128)(2,1)S(1)}, u32[]{:S(2)}, u32[]{:S(2)}) collective-permute-start(bf16[128,1024]{1,0:T(8,128)(2,1)S(1)} %get-tuple-element.47), channel_id=1, source_target_pairs={{0,4},{1,5},{2,6},{3,7},{4,0},{5,1},{6,2},{7,3},{8,12},{9,13},{10,... | collective-permute-start | bytes 786440 | tf_op jit(solution)/shard_map/ppermute | solution.py:371
  32.2 1.6 %collective-permute-start.9 = (bf16[256,1024]{1,0:T(8,128)(2,1)S(1)}, bf16[256,1024]{1,0:T(8,128)(2,1)S(1)}, u32[]{:S(2)}, u32[]{:S(2)}) collective-permute-start(bf16[256,1024]{1,0:T(8,128)(2,1)S(1)} %pad_maximum_fusion), channel_id=1, source_target_pairs={{0,16},{16,0},{1,17},{17,1},{2,18},{18,2},{3,19},{19,3},{4,20},{20... | collective-permute-start | bytes 1572872 | tf_op jit(solution)/shard_map/ppermute | solution.py:381
  33.7 7.8 %collective-permute-done.8.refs_12_ = bf16[128,1024]{1,0:T(8,128)(2,1)S(1)} collective-permute-done((bf16[128,1024]{1,0:T(8,128)(2,1)S(1)}, bf16[128,1024]{1,0:T(8,128)(2,1)S(1)}, u32[]{:S(2)}, u32[]{:S(2)}) %collective-permute-start.8) | collective-permute-done | bytes 262176 | tf_op jit(solution)/shard_map/ppermute | solution.py:371
  41.5 0.2 collective-permute-done.7.refs_11_
  41.7 0.0 collective-permute-done.6.refs_2_
  41.7 0.0 collective-permute-start.10
  41.7 1.4 %collective-permute-start.14 = (bf16[256,1024]{1,0:T(8,128)(2,1)S(1)}, bf16[256,1024]{1,0:T(8,128)(2,1)S(1)}, u32[]{:S(2)}, u32[]{:S(2)}) collective-permute-start(bf16[256,1024]{1,0:T(8,128)(2,1)S(1)} %collective-permute-done.6.refs_2_), channel_id=1, source_target_pairs={{0,4},{1,5},{2,14},{3,15},{4,8},{5,9},{6,2},{7,3},{8,12},{9,13},{1... | collective-permute-start | bytes 1572872 | tf_op jit(solution)/shard_map/ppermute | solution.py:377
  43.1 2.3 %collective-permute-start.11 = (bf16[128,1024]{1,0:T(8,128)(2,1)S(1)}, bf16[128,1024]{1,0:T(8,128)(2,1)S(1)}, u32[]{:S(2)}, u32[]{:S(2)}) collective-permute-start(bf16[128,1024]{1,0:T(8,128)(2,1)S(1)} %get-tuple-element.45), channel_id=1, source_target_pairs={{0,2},{1,3},{2,0},{3,1},{4,6},{5,7},{6,4},{7,5},{8,10},{9,11},{10,... | collective-permute-start | bytes 786440 | tf_op jit(solution)/shard_map/ppermute | solution.py:371
  45.5 1.6 %collective-permute-start.12 = (bf16[128,1024]{1,0:T(8,128)(2,1)S(1)}, bf16[128,1024]{1,0:T(8,128)(2,1)S(1)}, u32[]{:S(2)}, u32[]{:S(2)}) collective-permute-start(bf16[128,1024]{1,0:T(8,128)(2,1)S(1)} %pad_maximum_fusion.1), channel_id=1, source_target_pairs={{0,16},{16,0},{1,17},{17,1},{2,18},{18,2},{3,19},{19,3},{4,20},{20... | collective-permute-start | bytes 786440 | tf_op jit(solution)/shard_map/ppermute | solution.py:381
  47.1 5.0 %collective-permute-done.11.refs_13_ = bf16[128,1024]{1,0:T(8,128)(2,1)S(1)} collective-permute-done((bf16[128,1024]{1,0:T(8,128)(2,1)S(1)}, bf16[128,1024]{1,0:T(8,128)(2,1)S(1)}, u32[]{:S(2)}, u32[]{:S(2)}) %collective-permute-start.11) | collective-permute-done | bytes 262176 | tf_op jit(solution)/shard_map/ppermute | solution.py:371
  52.1 0.0 collective-permute-done.9.refs_14_
  52.1 0.0 collective-permute-done.10.refs_3_
  52.1 0.0 copy-start
  52.1 0.0 copy-start.2
  52.2 1.6 %collective-permute-start.13 = (bf16[64,1024]{1,0:T(8,128)(2,1)S(1)}, bf16[64,1024]{1,0:T(8,128)(2,1)S(1)}, u32[]{:S(2)}, u32[]{:S(2)}) collective-permute-start(bf16[64,1024]{1,0:T(8,128)(2,1)S(1)} %constant_dynamic-slice_fusion), channel_id=1, source_target_pairs={{0,16},{16,0},{1,17},{17,1},{2,18},{18,2},{3,19},{19,3},{4,20},{20... | collective-permute-start | bytes 393224 | tf_op jit(solution)/shard_map/ppermute | solution.py:381
  53.7 0.0 copy-done.1
  53.7 0.0 collective-permute-start.5
  53.7 0.0 collective-permute-done.12.refs_15_
  53.7 4.1 %collective-permute-done.14.refs_4_ = bf16[256,1024]{1,0:T(8,128)(2,1)S(1)} collective-permute-done((bf16[256,1024]{1,0:T(8,128)(2,1)S(1)}, bf16[256,1024]{1,0:T(8,128)(2,1)S(1)}, u32[]{:S(2)}, u32[]{:S(2)}) %collective-permute-start.14) | collective-permute-done | bytes 524320 | tf_op jit(solution)/shard_map/ppermute | solution.py:377
  57.8 0.0 collective-permute-done.13.refs_16_
  57.8 0.0 collective-permute-start.15
  57.8 0.0 collective-permute-done.5.refs_1_
  57.9 1.9 %collective-permute-done.15.refs_5_ = bf16[256,1024]{1,0:T(8,128)(2,1)S(1)} collective-permute-done((bf16[256,1024]{1,0:T(8,128)(2,1)S(1)}, bf16[256,1024]{1,0:T(8,128)(2,1)S(1)}, u32[]{:S(2)}, u32[]{:S(2)}) %collective-permute-start.15) | collective-permute-done | bytes 524320 | tf_op jit(solution)/shard_map/ppermute | solution.py:353
  59.8 15.4 %attend.1 = (bf16[4,256,128]{2,1,0:T(8,128)(2,1)S(1)}, bf16[4,256,128]{2,1,0:T(8,128)(2,1)S(1)}) custom-call(bf16[256,1024]{1,0:T(8,128)(2,1)S(1)} %copy-done.1, bf16[256,1024]{1,0:T(8,128)(2,1)S(1)} %collective-permute-done.5.refs_1_, bf16[256,1024]{1,0:T(8,128)(2,1)S(1)} %collective-permute-done.6.refs_2_, ...), custom_call_target="tpu_custom_call" | custom-call | flops 10000000000 | bytes 8388608 | tf_op jit(solution)/shard_map/attend/pallas_call | solution.py:306
  75.1 0.2 collective-permute-start.16
  75.3 1.4 %collective-permute-done.16.other_ref = bf16[4,256,128]{2,1,0:T(8,128)(2,1)S(1)} collective-permute-done((bf16[4,256,128]{2,1,0:T(8,128)(2,1)S(1)}, bf16[4,256,128]{2,1,0:T(8,128)(2,1)S(1)}, u32[]{:S(2)}, u32[]{:S(2)}) %collective-permute-start.16) | collective-permute-done | bytes 262176 | tf_op jit(solution)/shard_map/ppermute | solution.py:353
  76.7 0.0 copy-done
  76.7 0.0 copy-done.2
  76.7 1.5 %finish.1 = bf16[256,1024]{1,0:T(8,128)(2,1)} custom-call(bf16[256,1024]{1,0:T(8,128)(2,1)S(1)} %copy-done.2, bf16[4,256,128]{2,1,0:T(8,128)(2,1)S(1)} %get-tuple-element.43.mine_ref, bf16[4,256,128]{2,1,0:T(8,128)(2,1)S(1)} %collective-permute-done.16.other_ref, bf16[8,2,64,1024]{3,2,1,0:T(8,128)(2,1)S(1)} %bitcast.3), custom_call_target="tpu_custom_call" | custom-call | flops 1000000000 | bytes 4194304 | tf_op jit(solution)/shard_map/finish/pallas_call | solution.py:340
  (7 shorter events, 0.2 us)
Async XLA Ops:
  1.1 1.5 %collective-permute-start = (bf16[64,1024]{1,0:T(8,128)(2,1)S(1)}, bf16[64,1024]{1,0:T(8,128)(2,1)S(1)}, u32[]{:S(2)}, u32[]{:S(2)}) collective-permute-start(bf16[64,1024]{1,0:T(8,128)(2,1)S(1)} %get-tuple-element.49), channel_id=1, source_target_pairs={{0,1},{1,0},{2,3},{3,2},{4,5},{5,4},{6,7},{7,6},{8,9},{9,8},{10,11... | collective-permute-start | bytes 393224 | tf_op jit(solution)/shard_map/ppermute | solution.py:353
  2.7 23.2 %collective-permute-start.4 = (bf16[128,1024]{1,0:T(8,128)(2,1)S(1)}, bf16[128,1024]{1,0:T(8,128)(2,1)S(1)}, u32[]{:S(2)}, u32[]{:S(2)}) collective-permute-start(bf16[128,1024]{1,0:T(8,128)(2,1)S(1)} %constant_dynamic-slice_fusion.7), channel_id=1, source_target_pairs={{0,6},{1,7},{4,2},{5,3},{8,0},{9,1},{12,4},{13,5},{14,8},{15,9},{1... | collective-permute-start | bytes 786440 | tf_op jit(solution)/shard_map/ppermute | solution.py:367
  6.6 19.3 %collective-permute-start.3 = (bf16[128,1024]{1,0:T(8,128)(2,1)S(1)}, bf16[128,1024]{1,0:T(8,128)(2,1)S(1)}, u32[]{:S(2)}, u32[]{:S(2)}) collective-permute-start(bf16[128,1024]{1,0:T(8,128)(2,1)S(1)} %constant_dynamic-slice_fusion.7), channel_id=1, source_target_pairs={{0,8},{1,9},{4,12},{5,13},{8,14},{9,15},{12,10},{13,11},{14,6},{15... | collective-permute-start | bytes 786440 | tf_op jit(solution)/shard_map/ppermute | solution.py:367
  6.8 19.2 %collective-permute-start.2 = (bf16[128,1024]{1,0:T(8,128)(2,1)S(1)}, bf16[128,1024]{1,0:T(8,128)(2,1)S(1)}, u32[]{:S(2)}, u32[]{:S(2)}) collective-permute-start(bf16[128,1024]{1,0:T(8,128)(2,1)S(1)} %constant_dynamic-slice_fusion.7), channel_id=1, source_target_pairs={{0,2},{1,3},{4,0},{5,1},{8,4},{9,5},{12,8},{13,9},{14,12},{15,13},... | collective-permute-start | bytes 786440 | tf_op jit(solution)/shard_map/ppermute | solution.py:367
  8.5 17.4 %collective-permute-start.1 = (bf16[128,1024]{1,0:T(8,128)(2,1)S(1)}, bf16[128,1024]{1,0:T(8,128)(2,1)S(1)}, u32[]{:S(2)}, u32[]{:S(2)}) collective-permute-start(bf16[128,1024]{1,0:T(8,128)(2,1)S(1)} %constant_dynamic-slice_fusion.7), channel_id=1, source_target_pairs={{0,4},{1,5},{4,8},{5,9},{8,12},{9,13},{12,14},{13,15},{14,10},{15,... | collective-permute-start | bytes 786440 | tf_op jit(solution)/shard_map/ppermute | solution.py:367
  25.9 27.8 %copy-start.1 = (bf16[256,1024]{1,0:T(8,128)(2,1)S(1)}, bf16[256,1024]{1,0:T(8,128)(2,1)}, u32[]{:S(2)}) copy-start(bf16[256,1024]{1,0:T(8,128)(2,1)} %get-tuple-element.29.refs_0_) | copy-start | bytes 1572868
  25.9 15.8 %collective-permute-start.6 = (bf16[256,1024]{1,0:T(8,128)(2,1)}, bf16[256,1024]{1,0:T(8,128)(2,1)S(1)}, u32[]{:S(2)}, u32[]{:S(2)}) collective-permute-start(bf16[256,1024]{1,0:T(8,128)(2,1)} %get-tuple-element.29.refs_0_), channel_id=1, source_target_pairs={{0,2},{1,3},{2,0},{3,1},{4,6},{5,7},{6,4},{7,5},{8,10},{9,11},{10,... | collective-permute-start | bytes 1572872 | tf_op jit(solution)/shard_map/ppermute | solution.py:371
  27.9 13.6 %collective-permute-start.8 = (bf16[128,1024]{1,0:T(8,128)(2,1)S(1)}, bf16[128,1024]{1,0:T(8,128)(2,1)S(1)}, u32[]{:S(2)}, u32[]{:S(2)}) collective-permute-start(bf16[128,1024]{1,0:T(8,128)(2,1)S(1)} %get-tuple-element.46), channel_id=1, source_target_pairs={{0,8},{1,9},{2,10},{3,11},{4,12},{5,13},{6,14},{7,15},{8,0},{9,1},... | collective-permute-start | bytes 786440 | tf_op jit(solution)/shard_map/ppermute | solution.py:371
  30.5 11.2 %collective-permute-start.7 = (bf16[128,1024]{1,0:T(8,128)(2,1)S(1)}, bf16[128,1024]{1,0:T(8,128)(2,1)S(1)}, u32[]{:S(2)}, u32[]{:S(2)}) collective-permute-start(bf16[128,1024]{1,0:T(8,128)(2,1)S(1)} %get-tuple-element.47), channel_id=1, source_target_pairs={{0,4},{1,5},{2,6},{3,7},{4,0},{5,1},{6,2},{7,3},{8,12},{9,13},{10,... | collective-permute-start | bytes 786440 | tf_op jit(solution)/shard_map/ppermute | solution.py:371
  32.2 19.9 %collective-permute-start.9 = (bf16[256,1024]{1,0:T(8,128)(2,1)S(1)}, bf16[256,1024]{1,0:T(8,128)(2,1)S(1)}, u32[]{:S(2)}, u32[]{:S(2)}) collective-permute-start(bf16[256,1024]{1,0:T(8,128)(2,1)S(1)} %pad_maximum_fusion), channel_id=1, source_target_pairs={{0,16},{16,0},{1,17},{17,1},{2,18},{18,2},{3,19},{19,3},{4,20},{20... | collective-permute-start | bytes 1572872 | tf_op jit(solution)/shard_map/ppermute | solution.py:381
  41.7 10.4 %collective-permute-start.10 = (bf16[256,1024]{1,0:T(8,128)(2,1)S(1)}, bf16[256,1024]{1,0:T(8,128)(2,1)S(1)}, u32[]{:S(2)}, u32[]{:S(2)}) collective-permute-start(bf16[256,1024]{1,0:T(8,128)(2,1)S(1)} %collective-permute-done.6.refs_2_), channel_id=1, source_target_pairs={{0,1},{1,0},{2,3},{3,2},{4,5},{5,4},{6,7},{7,6},{8,9},{9,8},{10,11... | collective-permute-start | bytes 1572872 | tf_op jit(solution)/shard_map/ppermute | solution.py:353
  41.7 16.1 %collective-permute-start.14 = (bf16[256,1024]{1,0:T(8,128)(2,1)S(1)}, bf16[256,1024]{1,0:T(8,128)(2,1)S(1)}, u32[]{:S(2)}, u32[]{:S(2)}) collective-permute-start(bf16[256,1024]{1,0:T(8,128)(2,1)S(1)} %collective-permute-done.6.refs_2_), channel_id=1, source_target_pairs={{0,4},{1,5},{2,14},{3,15},{4,8},{5,9},{6,2},{7,3},{8,12},{9,13},{1... | collective-permute-start | bytes 1572872 | tf_op jit(solution)/shard_map/ppermute | solution.py:377
  43.1 9.0 %collective-permute-start.11 = (bf16[128,1024]{1,0:T(8,128)(2,1)S(1)}, bf16[128,1024]{1,0:T(8,128)(2,1)S(1)}, u32[]{:S(2)}, u32[]{:S(2)}) collective-permute-start(bf16[128,1024]{1,0:T(8,128)(2,1)S(1)} %get-tuple-element.45), channel_id=1, source_target_pairs={{0,2},{1,3},{2,0},{3,1},{4,6},{5,7},{6,4},{7,5},{8,10},{9,11},{10,... | collective-permute-start | bytes 786440 | tf_op jit(solution)/shard_map/ppermute | solution.py:371
  45.5 8.2 %collective-permute-start.12 = (bf16[128,1024]{1,0:T(8,128)(2,1)S(1)}, bf16[128,1024]{1,0:T(8,128)(2,1)S(1)}, u32[]{:S(2)}, u32[]{:S(2)}) collective-permute-start(bf16[128,1024]{1,0:T(8,128)(2,1)S(1)} %pad_maximum_fusion.1), channel_id=1, source_target_pairs={{0,16},{16,0},{1,17},{17,1},{2,18},{18,2},{3,19},{19,3},{4,20},{20... | collective-permute-start | bytes 786440 | tf_op jit(solution)/shard_map/ppermute | solution.py:381
  52.1 24.6 %copy-start = (bf16[1024,1024]{1,0:T(8,128)(2,1)S(1)}, bf16[1024,1024]{1,0:T(8,128)(2,1)}, u32[]{:S(2)}) copy-start(bf16[1024,1024]{1,0:T(8,128)(2,1)} %param.21) | copy-start | bytes 6291460
  52.1 24.6 %copy-start.2 = (bf16[256,1024]{1,0:T(8,128)(2,1)S(1)}, bf16[256,1024]{1,0:T(8,128)(2,1)}, u32[]{:S(2)}) copy-start(bf16[256,1024]{1,0:T(8,128)(2,1)} %get-tuple-element.26.tokens_ref) | copy-start | bytes 1572868
  52.2 5.7 %collective-permute-start.13 = (bf16[64,1024]{1,0:T(8,128)(2,1)S(1)}, bf16[64,1024]{1,0:T(8,128)(2,1)S(1)}, u32[]{:S(2)}, u32[]{:S(2)}) collective-permute-start(bf16[64,1024]{1,0:T(8,128)(2,1)S(1)} %constant_dynamic-slice_fusion), channel_id=1, source_target_pairs={{0,16},{16,0},{1,17},{17,1},{2,18},{18,2},{3,19},{19,3},{4,20},{20... | collective-permute-start | bytes 393224 | tf_op jit(solution)/shard_map/ppermute | solution.py:381
  53.7 4.1 %collective-permute-start.5 = (bf16[256,1024]{1,0:T(8,128)(2,1)S(1)}, bf16[256,1024]{1,0:T(8,128)(2,1)S(1)}, u32[]{:S(2)}, u32[]{:S(2)}) collective-permute-start(bf16[256,1024]{1,0:T(8,128)(2,1)S(1)} %copy-done.1), channel_id=1, source_target_pairs={{0,1},{1,0},{2,3},{3,2},{4,5},{5,4},{6,7},{7,6},{8,9},{9,8},{10,11... | collective-permute-start | bytes 1572872 | tf_op jit(solution)/shard_map/ppermute | solution.py:353
  57.8 1.9 %collective-permute-start.15 = (bf16[256,1024]{1,0:T(8,128)(2,1)S(1)}, bf16[256,1024]{1,0:T(8,128)(2,1)S(1)}, u32[]{:S(2)}, u32[]{:S(2)}) collective-permute-start(bf16[256,1024]{1,0:T(8,128)(2,1)S(1)} %collective-permute-done.14.refs_4_), channel_id=1, source_target_pairs={{0,1},{1,0},{2,3},{3,2},{4,5},{5,4},{6,7},{7,6},{8,9},{9,8},{10,11... | collective-permute-start | bytes 1572872 | tf_op jit(solution)/shard_map/ppermute | solution.py:353
  75.1 1.6 %collective-permute-start.16 = (bf16[4,256,128]{2,1,0:T(8,128)(2,1)S(1)}, bf16[4,256,128]{2,1,0:T(8,128)(2,1)S(1)}, u32[]{:S(2)}, u32[]{:S(2)}) collective-permute-start(bf16[4,256,128]{2,1,0:T(8,128)(2,1)S(1)} %get-tuple-element.44), channel_id=1, source_target_pairs={{0,1},{1,0},{2,3},{3,2},{4,5},{5,4},{6,7},{7,6},{8,9},{9,8},{10,11... | collective-permute-start | bytes 786440 | tf_op jit(solution)/shard_map/ppermute | solution.py:353

commit v7 on v6

--- a/solution.py
+++ b/solution.py
@@ -45,6 +45,14 @@
     return lax.broadcasted_iota(jnp.int32, shape, dim)
 
 
+def over(x, n):
+    return x >> (n.bit_length() - 1) if n & (n - 1) == 0 else x // n
+
+
+def within(x, n):
+    return x & (n - 1) if n & (n - 1) == 0 else x % n
+
+
 def fetch(pairs, sems):
     copies = [pltpu.make_async_copy(src, dst, sems.at[i]) for i, (src, dst) in enumerate(pairs)]
     for copy in copies:
@@ -55,9 +63,9 @@
 def spread_offsets(offset_half, heads, head_size, first):
     var_count, half = offset_half.shape
     spread = var_count * heads
-    picks = (iota((spread, var_count), 0) // heads == iota((spread, var_count), 1)).astype(F32)
+    picks = (over(iota((spread, var_count), 0), heads) == iota((spread, var_count), 1)).astype(F32)
     rows = dot(picks.astype(BF16), offset_half).astype(BF16)
-    mine = iota((spread, half), 0) % heads == iota((spread, half), 1) // head_size + first
+    mine = within(iota((spread, half), 0), heads) == over(iota((spread, half), 1), head_size) + first
     return jnp.where(mine, rows, jnp.zeros_like(rows))
 
 
@@ -65,14 +73,15 @@
     tokens, spread = probs.shape
     group = math.gcd(spread, 256)
     row_g, col_g = iota((group, group), 0), iota((group, group), 1)
-    same = row_g // heads == col_g // pixels
+    same = over(row_g, heads) == over(col_g, pixels)
+    head_g = jnp.where(same, within(row_g, heads), -1)
     left_half = iota((tokens, 2 * head_size), 1) < head_size
     values = []
     for pair in range(pairs):
         halves = []
         cols = slice(pair * 2 * head_size, (pair + 1) * 2 * head_size)
         for head in (first + 2 * pair, first + 2 * pair + 1):
-            pick = jnp.where(same & (row_g % heads == head), 1.0, 0.0).astype(BF16)
+            pick = jnp.where(head_g == head, 1.0, 0.0).astype(BF16)
             weights = jnp.concatenate(
                 [
                     dot(probs[:, g * group : (g + 1) * group], pick).astype(BF16)
@@ -96,7 +105,8 @@
     pos_hbm,
     gain_hbm,
     tokens_ref,
-    normed_ref,
+    upper_ref,
+    lower_ref,
     var_embed_ref,
     keys_ref,
     embed_ref,
@@ -135,7 +145,7 @@
     waits[0]()
     offsets = dot(select, var_embed_ref[...]).astype(BF16)
     waits[1]()
-    repeat = (iota((LANES, heads), 0) % heads == iota((LANES, heads), 1)).astype(F32).astype(BF16)
+    repeat = (within(iota((LANES, heads), 0), heads) == iota((LANES, heads), 1)).astype(F32).astype(BF16)
     keys = dot(repeat, keys_ref[...]).astype(BF16)
     offset_keys = dot_t(offsets, keys)
     waits[2]()
@@ -147,21 +157,26 @@
     low = (table_keys - high.astype(F32)).astype(BF16)
     waits[3]()
     patches = patches_ref[...]
-    rows_of = iota((rows, LANES), 0) // pixels
-    cols_of = iota((rows, LANES), 1) // heads
-    channel = iota((var_count, LANES), 1) // heads
+    group = math.gcd(spread, 256)
+    lines = group // heads * pixels
+    same = over(iota((lines, LANES), 0), pixels)
+    cols_of = over(iota((lines, LANES), 1), heads)
+    channel = over(iota((var_count, LANES), 1), heads)
     scores = []
-    for block in range(spread // LANES):
-        first = block * (LANES // heads)
-        here = rows_of == cols_of + first
-        row = jnp.sum(
-            jnp.where(channel + first == iota((var_count, LANES), 0), offset_keys, 0.0),
-            axis=0,
-            keepdims=True,
-        )
-        part = dot(patches, jnp.where(here, high, jnp.zeros_like(high)))
-        part = part + dot(patches, jnp.where(here, low, jnp.zeros_like(low)))
-        scores.append((part + row) * scale)
+    for part in range(spread // group):
+        here = slice(part * lines, (part + 1) * lines)
+        highs, lows, shifts = [], [], []
+        for block in range(group // LANES):
+            first = block * (LANES // heads)
+            match = same == cols_of + first
+            highs.append(jnp.where(match, high[here], jnp.zeros_like(high[here])))
+            lows.append(jnp.where(match, low[here], jnp.zeros_like(low[here])))
+            match = channel + (first + part * (group // heads)) == iota((var_count, LANES), 0)
+            shifts.append(jnp.sum(jnp.where(match, offset_keys, 0.0), axis=0, keepdims=True))
+        total = dot(patches[:, here], jnp.concatenate(highs, axis=1))
+        total = total + dot(patches[:, here], jnp.concatenate(lows, axis=1))
+        for block, shift in enumerate(shifts):
+            scores.append((total[:, block * LANES : (block + 1) * LANES] + shift) * scale)
     waits[4]()
     values_ref[...] = dot(table, value_ref[...]).astype(BF16)
     offset_values = dot(offsets, value_ref[...]).astype(BF16)
@@ -188,7 +203,10 @@
     full = tokens_zero.astype(F32)
     centred = full - jnp.mean(full, axis=-1, keepdims=True)
     variance = jnp.mean(centred * centred, axis=-1, keepdims=True)
-    normed_ref[...] = (centred * lax.rsqrt(variance + 1e-05) * gain_ref[...]).astype(BF16)
+    normed = (centred * lax.rsqrt(variance + 1e-05) * gain_ref[...]).astype(BF16)
+    half = upper_ref.shape[0]
+    upper_ref[...] = normed[:half]
+    lower_ref[...] = normed[half:]
 
 
 def cost(gflops, mib, exps=0):
@@ -212,9 +230,13 @@
     arrays = (var_embed, keys, embed_weight, patches, value, out_w, pos, gain.reshape(1, width))
     return pl.pallas_call(
         aggregate_kernel,
-        out_shape=[jax.ShapeDtypeStruct((tokens, width), BF16)] * 2,
+        out_shape=[
+            jax.ShapeDtypeStruct((tokens, width), BF16),
+            jax.ShapeDtypeStruct((tokens // 2, width), BF16),
+            jax.ShapeDtypeStruct((tokens // 2, width), BF16),
+        ],
         in_specs=[SMEM] + [HBM] * len(arrays),
-        out_specs=[VMEM] * 2,
+        out_specs=[VMEM] * 3,
         scratch_shapes=like(*arrays)
         + like(embed_weight)
         + [pltpu.VMEM((var_count * pixels, width), BF16)]
@@ -227,11 +249,14 @@
 
 def attend_kernel(*refs, spots):
     count = len(spots)
-    weight_refs = refs[6 : 6 + count]
-    mine_ref, other_ref, rows_s, query_s, key_s, value_s, weight_s, sems = refs[6 + count :]
+    weight_refs = refs[12 : 12 + count]
+    mine_ref, other_ref, rows_s, query_s, key_s, value_s, weight_s, sems = refs[12 + count :]
     index, plane = lax.axis_index("space"), lax.axis_index("groups")
     side = index % 2
-    moves = [(ref, rows_s.at[i]) for i, ref in enumerate(refs[:6])]
+    half = rows_s.shape[1] // 2
+    moves = [
+        (ref, rows_s.at[i // 2, pl.ds(i % 2 * half, half), :]) for i, ref in enumerate(refs[:12])
+    ]
     for ref, (step, share) in zip(weight_refs, spots):
         rows = ref.shape[0]
         if share == "ring":
@@ -292,11 +317,12 @@
             out_ref[pair] = jnp.where(left_half, halves[0], halves[1]).astype(BF16)
         return carry
 
-    lax.fori_loop(0, pairs, attend, 0)
+    lax.fori_loop(0, pairs, attend, 0, unroll=True)
 
 
 def attend(pieces, weights):
-    tokens, width = pieces[0].shape
+    pieces = [half for piece in pieces for half in piece]
+    tokens, width = 2 * pieces[0].shape[0], pieces[0].shape[1]
     spots = tuple(spot for _, spot in weights)
     weights = [piece for piece, _ in weights]
     rows = weights[0].shape[0]
@@ -306,7 +332,7 @@
     return pl.pallas_call(
         functools.partial(attend_kernel, spots=spots),
         out_shape=[jax.ShapeDtypeStruct((pairs, tokens, LANES), BF16)] * 2,
-        in_specs=[HBM] * (6 + len(weights)),
+        in_specs=[HBM] * (12 + len(weights)),
         out_specs=[VMEM, VMEM],
         scratch_shapes=[
             pltpu.VMEM((6, tokens, width), BF16),
@@ -434,7 +460,7 @@
         weights = [(block, (0, None))]
     else:
         weights = parity_weight(qkv_weight, side, head_size)
-    tokens_zero, normed = aggregate(
+    tokens_zero, *normed = aggregate(
         var_order, var_embed, agg_keys, embed_weight, patches, agg_value, agg_out, pos_embed, norm_gain
     )
     if ringed:
@@ -443,28 +469,34 @@
             parts = [lax.dynamic_slice_in_dim(b, plane * third, third, 0) for b in blocks]
             return across(jnp.concatenate(parts, axis=0))
 
-        normed, *early = together(normed, *early)
+        upper, lower, *early = together(*normed, *early)
         weights += [(b, (-step, "ring")) for b, step in zip(early, (1, -1, 2, -2))]
+        place = ring_place(lax.axis_index("space"))
+        low = place % 4 < 2
+        near0, near1 = crossed(upper, 2), crossed(lower, 2)
+        pair = crossed(jnp.where(place % 2 == 0, early[2], early[3]), 4)
+        opposite = crossed(jnp.where(low, early[2], early[3]), 8)
         swap = swapped(early)
-        place = ring_place(lax.axis_index("space"))
-        near = crossed(normed, 2)
-        pair = crossed(jnp.where(place % 2 == 0, early[2], early[3]), 4)
-        low = place % 4 < 2
-        opposite = crossed(jnp.where(low, early[2], early[3]), 8)
-        near, pair, opposite = together(near, pair, opposite)
-        far, near_sib = onward(near), sibling(near)
+        far0, near_sib0 = onward(near0), sibling(near0)
         beside = crossed(jnp.where(low, early[3], early[2]), 2)
+        near1, far0, pair, opposite, swap = together(near1, far0, pair, opposite, swap)
+        far1, near_sib1 = onward(near1), sibling(near1)
         first = swapped([pair, opposite])
-        swap, near_sib, beside = together(swap, near_sib, beside)
+        near_sib1, beside = together(near_sib1, beside)
         second = swapped([beside])
-        first, second, far = together(first, second, far)
+        first, second, far1 = together(first, second, far1)
         weights += [(pair, ("pair", "ring")), (opposite, (4, "ring")), (beside, ("beside", "ring"))]
         weights += [(swap, ((-1, 1, -2, 2), "swap"))]
         weights += [(first, (("pair", 4), "swap")), (second, (("beside",), "swap"))]
+        near, near_sib, far = (near0, near1), (near_sib0, near_sib1), (far0, far1)
+        normed = (upper, lower)
     else:
-        near, far = from_chip(normed, 1), from_chip(normed, -1)
-        near_sib = sibling(near)
-    pieces = (normed, sibling(normed), near, near_sib, far, sibling(far))
+        near = [from_chip(half, 1) for half in normed]
+        far = [from_chip(half, -1) for half in normed]
+        near_sib = [sibling(half) for half in near]
+    sib = [sibling(half) for half in normed]
+    far_sib = [sibling(half) for half in far]
+    pieces = (normed, sib, near, near_sib, far, far_sib)
     mine, other = attend(pieces, weights)
     return finish(tokens_zero, mine, sibling(other), attn_out)
 

time: 78.4 us -> 78.5 us (level)
  waiting for transfers between devices: 21.4 us -> 27.2 us
  Pallas kernels: 34 us -> 28.9 us
    ppermute x3, waiting for transfers between devices: 0.01 us -> 6.82 us  [across(): return lax.ppermute(value, 'groups', [(0, 1), (1, 0)])]
    ppermute x4 -> x5, waiting for transfers between devices: 13 us -> 7.85 us  [crossed(): lax.ppermute(value, 'space', [(i, i ^ bits) for i in range(2 * len(RING))])]
    ppermute x1 -> x2, waiting for transfers between devices: 4.12 us -> 6.95 us  [onward(): return lax.ppermute(value, 'space', pairs)]
    pallas_call x1, Pallas kernels: 17.1 us -> 14.5 us  [aggregate(): pl.pallas_call(aggregate_kernel, out_shape=[jax.ShapeDtypeStruct((tokens,...]
    pallas_call x1, Pallas kernels: 15.4 us -> 12.9 us  [attend(): pl.pallas_call(functools.partial(attend_kernel, spots=spots), out_shape=[...]
    ppermute x3, starting transfers between devices: 4.66 us -> 3.24 us  [across(): return lax.ppermute(value, 'groups', [(0, 1), (1, 0)])]
    ppermute x4, waiting for transfers between devices: 0.01 us -> 1.24 us  [around(): return lax.ppermute(value, 'space', pairs)]
    ppermute x1 -> x2, starting transfers between devices: 1.44 us -> 2 us  [onward(): return lax.ppermute(value, 'space', pairs)]
  transfers between devices with their start and end apart: 17 -> 22, of which waited for: 7 -> 13; matrix products, arithmetic and copies ran while one was open for 0% -> 0% of each run, Pallas kernels for 22% -> 19%
where the time goes in v7:
time: 78.5 us; the launch traced here: 78.3 us
  Pallas kernels  28.9 us (37%)
  waiting for transfers between devices  27.2 us (35%)
  starting transfers between devices  20.6 us (26%)
  local copies, waits for them, and re-layouts  1.19 us (2%)
    pallas_call x1, Pallas kernels, aggregate(): pl.pallas_call(aggregate_kernel, out_shape=[jax.ShapeDtypeStruct((tokens,...  14.5 us
    pallas_call x1, Pallas kernels, attend(): pl.pallas_call(functools.partial(attend_kernel, spots=spots), out_shape=[...  12.9 us
    ppermute x5, starting transfers between devices, crossed(): lax.ppermute(value, 'space', [(i, i ^ bits) for i in range(2 * len(RING))])  8.07 us
    ppermute x5, waiting for transfers between devices, crossed(): lax.ppermute(value, 'space', [(i, i ^ bits) for i in range(2 * len(RING))])  7.85 us
    ppermute x2, waiting for transfers between devices, onward(): return lax.ppermute(value, 'space', pairs)  6.95 us
    ppermute x3, waiting for transfers between devices, across(): return lax.ppermute(value, 'groups', [(0, 1), (1, 0)])  6.82 us
    ppermute x4, starting transfers between devices, around(): return lax.ppermute(value, 'space', pairs)  6.09 us
    ppermute x8, waiting for transfers between devices, sibling(): return lax.ppermute(value, 'space', [(i, i ^ 1) for i in range(length)])  4.39 us
  transfers between devices with their start and end apart: 22, of which 13 were waited for; matrix products, arithmetic and copies ran while one was open for 0% of the time, Pallas kernels for 19%

profile of v7, /device:TPU:0, one launch (start us, length us, event | category | flops | bytes accessed | tf_op | source)
XLA Modules:
  0.0 78.3 jit_solution(6683859988129000187)
XLA Ops:
  0.0 1.1 %fusion = (bf16[64,1024]{1,0:T(8,128)(2,1)S(1)}, bf16[64,1024]{1,0:T(8,128)(2,1)S(1)}, bf16[64,1024]{1,0:T(8,128)(2,1)S(1)}) fusion(bf16[192,1024]{1,0:T(8,128)(2,1)} %bitcast.4), kind=kLoop, calls=%fused_computation.14 | loop fusion | bytes 786432 | tf_op jit(solution)/shard_map/slice | solution.py:416
  1.1 0.5 collective-permute-start
  1.6 1.0 %collective-permute-done = bf16[64,1024]{1,0:T(8,128)(2,1)S(1)} collective-permute-done((bf16[64,1024]{1,0:T(8,128)(2,1)S(1)}, bf16[64,1024]{1,0:T(8,128)(2,1)S(1)}, u32[]{:S(2)}, u32[]{:S(2)}) %collective-permute-start) | collective-permute-done | bytes 131104 | tf_op jit(solution)/shard_map/ppermute | solution.py:379
  2.6 0.1 maximum_select_fusion.refs_12_
  2.7 3.9 %collective-permute-start.4 = (bf16[128,1024]{1,0:T(8,128)(2,1)S(1)}, bf16[128,1024]{1,0:T(8,128)(2,1)S(1)}, u32[]{:S(2)}, u32[]{:S(2)}) collective-permute-start(bf16[128,1024]{1,0:T(8,128)(2,1)S(1)} %constant_dynamic-slice_fusion.7), channel_id=1, source_target_pairs={{0,6},{1,7},{4,2},{5,3},{8,0},{9,1},{12,4},{13,5},{14,8},{15,9},{1... | collective-permute-start | bytes 786440 | tf_op jit(solution)/shard_map/ppermute | solution.py:393
  6.6 0.1 collective-permute-start.3
  6.8 1.8 %collective-permute-start.2 = (bf16[128,1024]{1,0:T(8,128)(2,1)S(1)}, bf16[128,1024]{1,0:T(8,128)(2,1)S(1)}, u32[]{:S(2)}, u32[]{:S(2)}) collective-permute-start(bf16[128,1024]{1,0:T(8,128)(2,1)S(1)} %constant_dynamic-slice_fusion.7), channel_id=1, source_target_pairs={{0,2},{1,3},{4,0},{5,1},{8,4},{9,5},{12,8},{13,9},{14,12},{15,13},... | collective-permute-start | bytes 786440 | tf_op jit(solution)/shard_map/ppermute | solution.py:393
  8.5 0.2 collective-permute-start.1
  8.8 14.5 %aggregate.1 = (bf16[256,1024]{1,0:T(8,128)(2,1)}, bf16[128,1024]{1,0:T(8,128)(2,1)}, bf16[128,1024]{1,0:T(8,128)(2,1)}) custom-call(s32[64]{0:T(128)} %order_ref.1, bf16[64,1024]{1,0:T(8,128)(2,1)} %var_embed_hbm.1, bf16[16,1024]{1,0:T(8,128)(2,1)} %keys_hbm.1, bf16[64,16,1024]{2,1,0:T(8,128)(2,1)} %embed_hbm, bf16[256,1024]{1,0:T(8,128)(2,1)} %patches_hbm.1, ...), custom_call_target="tpu_custom_call" | custom-call | flops 16000000000 | bytes 8388608 | tf_op jit(solution)/shard_map/aggregate/pallas_call | solution.py:231
  23.3 0.0 copy-start.2
  23.3 0.0 collective-permute-done.4.refs_16_
  23.3 0.0 collective-permute-done.3.refs_15_
  23.4 1.2 %collective-permute-done.2.refs_14_ = bf16[128,1024]{1,0:T(8,128)(2,1)S(1)} collective-permute-done((bf16[128,1024]{1,0:T(8,128)(2,1)S(1)}, bf16[128,1024]{1,0:T(8,128)(2,1)S(1)}, u32[]{:S(2)}, u32[]{:S(2)}) %collective-permute-start.2) | collective-permute-done | bytes 262176 | tf_op jit(solution)/shard_map/ppermute | solution.py:393
  24.6 0.0 collective-permute-done.1.refs_13_
  24.6 2.8 %collective-permute-start.7 = (bf16[128,1024]{1,0:T(8,128)(2,1)}, bf16[128,1024]{1,0:T(8,128)(2,1)S(1)}, u32[]{:S(2)}, u32[]{:S(2)}) collective-permute-start(bf16[128,1024]{1,0:T(8,128)(2,1)} %get-tuple-element.33.refs_0_), channel_id=1, source_target_pairs={{0,2},{1,3},{2,0},{3,1},{4,6},{5,7},{6,4},{7,5},{8,10},{9,11},{10,... | collective-permute-start | bytes 786440 | tf_op jit(solution)/shard_map/ppermute | solution.py:397
  27.4 0.0 copy-start.1
  27.5 1.6 %collective-permute-start.12 = (bf16[256,1024]{1,0:T(8,128)(2,1)S(1)}, bf16[256,1024]{1,0:T(8,128)(2,1)S(1)}, u32[]{:S(2)}, u32[]{:S(2)}) collective-permute-start(bf16[256,1024]{1,0:T(8,128)(2,1)S(1)} %pad_maximum_fusion), channel_id=1, source_target_pairs={{0,16},{16,0},{1,17},{17,1},{2,18},{18,2},{3,19},{19,3},{4,20},{20... | collective-permute-start | bytes 1572872 | tf_op jit(solution)/shard_map/ppermute | solution.py:407
  29.1 0.0 copy-done.2
  29.1 0.0 collective-permute-start.8
  29.1 0.1 broadcast_select_fusion
  29.1 2.1 %collective-permute-start.11 = (bf16[128,1024]{1,0:T(8,128)(2,1)S(1)}, bf16[128,1024]{1,0:T(8,128)(2,1)S(1)}, u32[]{:S(2)}, u32[]{:S(2)}) collective-permute-start(bf16[128,1024]{1,0:T(8,128)(2,1)S(1)} %get-tuple-element.52), channel_id=1, source_target_pairs={{0,8},{1,9},{2,10},{3,11},{4,12},{5,13},{6,14},{7,15},{8,0},{9,1},... | collective-permute-start | bytes 786440 | tf_op jit(solution)/shard_map/ppermute | solution.py:397
  31.2 1.4 %collective-permute-start.10 = (bf16[128,1024]{1,0:T(8,128)(2,1)S(1)}, bf16[128,1024]{1,0:T(8,128)(2,1)S(1)}, u32[]{:S(2)}, u32[]{:S(2)}) collective-permute-start(bf16[128,1024]{1,0:T(8,128)(2,1)S(1)} %get-tuple-element.53), channel_id=1, source_target_pairs={{0,4},{1,5},{2,6},{3,7},{4,0},{5,1},{6,2},{7,3},{8,12},{9,13},{10,... | collective-permute-start | bytes 786440 | tf_op jit(solution)/shard_map/ppermute | solution.py:397
  32.6 2.2 %collective-permute-done.7.refs_4_ = bf16[128,1024]{1,0:T(8,128)(2,1)S(1)} collective-permute-done((bf16[128,1024]{1,0:T(8,128)(2,1)}, bf16[128,1024]{1,0:T(8,128)(2,1)S(1)}, u32[]{:S(2)}, u32[]{:S(2)}) %collective-permute-start.7) | collective-permute-done | bytes 262176 | tf_op jit(solution)/shard_map/ppermute | solution.py:397
  34.8 1.6 %collective-permute-start.9 = (bf16[128,1024]{1,0:T(8,128)(2,1)S(1)}, bf16[128,1024]{1,0:T(8,128)(2,1)S(1)}, u32[]{:S(2)}, u32[]{:S(2)}) collective-permute-start(bf16[128,1024]{1,0:T(8,128)(2,1)S(1)} %collective-permute-done.7.refs_4_), channel_id=1, source_target_pairs={{0,4},{1,5},{2,14},{3,15},{4,8},{5,9},{6,2},{7,3},{8,12},{9,13},{1... | collective-permute-start | bytes 786440 | tf_op jit(solution)/shard_map/ppermute | solution.py:403
  36.5 2.3 %collective-permute-done.8.refs_5_ = bf16[128,1024]{1,0:T(8,128)(2,1)S(1)} collective-permute-done((bf16[128,1024]{1,0:T(8,128)(2,1)S(1)}, bf16[128,1024]{1,0:T(8,128)(2,1)S(1)}, u32[]{:S(2)}, u32[]{:S(2)}) %collective-permute-start.8) | collective-permute-done | bytes 262176 | tf_op jit(solution)/shard_map/ppermute | solution.py:397
  38.7 1.7 %collective-permute-start.15 = (bf16[128,1024]{1,0:T(8,128)(2,1)S(1)}, bf16[128,1024]{1,0:T(8,128)(2,1)S(1)}, u32[]{:S(2)}, u32[]{:S(2)}) collective-permute-start(bf16[128,1024]{1,0:T(8,128)(2,1)S(1)} %get-tuple-element.51), channel_id=1, source_target_pairs={{0,2},{1,3},{2,0},{3,1},{4,6},{5,7},{6,4},{7,5},{8,10},{9,11},{10,... | collective-permute-start | bytes 786440 | tf_op jit(solution)/shard_map/ppermute | solution.py:397
  40.5 3.4 %collective-permute-done.11.refs_18_ = bf16[128,1024]{1,0:T(8,128)(2,1)S(1)} collective-permute-done((bf16[128,1024]{1,0:T(8,128)(2,1)S(1)}, bf16[128,1024]{1,0:T(8,128)(2,1)S(1)}, u32[]{:S(2)}, u32[]{:S(2)}) %collective-permute-start.11) | collective-permute-done | bytes 262176 | tf_op jit(solution)/shard_map/ppermute | solution.py:397
  43.9 0.0 collective-permute-done.10.refs_17_
  43.9 5.3 %collective-permute-done.9.refs_8_ = bf16[128,1024]{1,0:T(8,128)(2,1)S(1)} collective-permute-done((bf16[128,1024]{1,0:T(8,128)(2,1)S(1)}, bf16[128,1024]{1,0:T(8,128)(2,1)S(1)}, u32[]{:S(2)}, u32[]{:S(2)}) %collective-permute-start.9) | collective-permute-done | bytes 262176 | tf_op jit(solution)/shard_map/ppermute | solution.py:403
  49.1 0.0 collective-permute-done.12.refs_20_
  49.1 0.0 collective-permute-start.14
  49.2 0.6 collective-permute-start.16
  49.8 0.4 collective-permute-start.18
  50.2 0.0 collective-permute-done.15.refs_19_
  50.2 0.5 collective-permute-done.14.refs_7_
  50.7 0.0 copy-start
  50.7 0.0 copy-start.3
  50.7 1.1 %collective-permute-start.17 = (bf16[64,1024]{1,0:T(8,128)(2,1)S(1)}, bf16[64,1024]{1,0:T(8,128)(2,1)S(1)}, u32[]{:S(2)}, u32[]{:S(2)}) collective-permute-start(bf16[64,1024]{1,0:T(8,128)(2,1)S(1)} %constant_dynamic-slice_fusion), channel_id=1, source_target_pairs={{0,16},{16,0},{1,17},{17,1},{2,18},{18,2},{3,19},{19,3},{4,20},{20... | collective-permute-start | bytes 393224 | tf_op jit(solution)/shard_map/ppermute | solution.py:407
  51.8 0.0 copy-done.1
  51.8 0.0 collective-permute-start.5
  51.8 0.5 collective-permute-start.6
  52.3 6.1 %collective-permute-done.16.refs_21_ = bf16[128,1024]{1,0:T(8,128)(2,1)S(1)} collective-permute-done((bf16[128,1024]{1,0:T(8,128)(2,1)S(1)}, bf16[128,1024]{1,0:T(8,128)(2,1)S(1)}, u32[]{:S(2)}, u32[]{:S(2)}) %collective-permute-start.16) | collective-permute-done | bytes 262176 | tf_op jit(solution)/shard_map/ppermute | solution.py:407
  58.4 0.0 collective-permute-start.13
  58.4 1.7 %collective-permute-done.18.refs_9_ = bf16[128,1024]{1,0:T(8,128)(2,1)S(1)} collective-permute-done((bf16[128,1024]{1,0:T(8,128)(2,1)S(1)}, bf16[128,1024]{1,0:T(8,128)(2,1)S(1)}, u32[]{:S(2)}, u32[]{:S(2)}) %collective-permute-start.18) | collective-permute-done | bytes 262176 | tf_op jit(solution)/shard_map/ppermute | solution.py:403
  60.1 0.0 collective-permute-start.19
  60.1 0.8 collective-permute-done.17.refs_22_
  60.8 0.0 collective-permute-start.20
  60.8 0.0 collective-permute-done.5.refs_2_
  60.8 0.0 collective-permute-done.6.refs_3_
  60.8 0.0 collective-permute-done.13.refs_6_
  60.8 0.8 collective-permute-done.19.refs_10_
  61.6 0.8 collective-permute-done.20.refs_11_
  62.3 12.9 %attend.1 = (bf16[4,256,128]{2,1,0:T(8,128)(2,1)S(1)}, bf16[4,256,128]{2,1,0:T(8,128)(2,1)S(1)}) custom-call(bf16[128,1024]{1,0:T(8,128)(2,1)S(1)} %copy-done.1, bf16[128,1024]{1,0:T(8,128)(2,1)S(1)} %copy-done.2, bf16[128,1024]{1,0:T(8,128)(2,1)S(1)} %collective-permute-done.5.refs_2_, bf16[128,1024]{1,0:T(8,128)(2,1)S(1)} %collective-permute-done.6.refs_3_, ...), custom_call_target="tpu_custom_call" | custom-call | flops 10000000000 | bytes 8388608 | tf_op jit(solution)/shard_map/attend/pallas_call | solution.py:332
  75.2 0.2 collective-permute-start.21
  75.4 1.4 %collective-permute-done.21.other_ref = bf16[4,256,128]{2,1,0:T(8,128)(2,1)S(1)} collective-permute-done((bf16[4,256,128]{2,1,0:T(8,128)(2,1)S(1)}, bf16[4,256,128]{2,1,0:T(8,128)(2,1)S(1)}, u32[]{:S(2)}, u32[]{:S(2)}) %collective-permute-start.21) | collective-permute-done | bytes 262176 | tf_op jit(solution)/shard_map/ppermute | solution.py:379
  76.8 0.0 copy-done
  76.8 0.0 copy-done.3
  76.8 1.5 %finish.1 = bf16[256,1024]{1,0:T(8,128)(2,1)} custom-call(bf16[256,1024]{1,0:T(8,128)(2,1)S(1)} %copy-done.3, bf16[4,256,128]{2,1,0:T(8,128)(2,1)S(1)} %get-tuple-element.49.mine_ref, bf16[4,256,128]{2,1,0:T(8,128)(2,1)S(1)} %collective-permute-done.21.other_ref, bf16[8,2,64,1024]{3,2,1,0:T(8,128)(2,1)S(1)} %bitcast.3), custom_call_target="tpu_custom_call" | custom-call | flops 1000000000 | bytes 4194304 | tf_op jit(solution)/shard_map/finish/pallas_call | solution.py:366
  (8 shorter events, 0.2 us)
Async XLA Ops:
  1.1 1.5 %collective-permute-start = (bf16[64,1024]{1,0:T(8,128)(2,1)S(1)}, bf16[64,1024]{1,0:T(8,128)(2,1)S(1)}, u32[]{:S(2)}, u32[]{:S(2)}) collective-permute-start(bf16[64,1024]{1,0:T(8,128)(2,1)S(1)} %get-tuple-element.55), channel_id=1, source_target_pairs={{0,1},{1,0},{2,3},{3,2},{4,5},{5,4},{6,7},{7,6},{8,9},{9,8},{10,11... | collective-permute-start | bytes 393224 | tf_op jit(solution)/shard_map/ppermute | solution.py:379
  2.7 20.6 %collective-permute-start.4 = (bf16[128,1024]{1,0:T(8,128)(2,1)S(1)}, bf16[128,1024]{1,0:T(8,128)(2,1)S(1)}, u32[]{:S(2)}, u32[]{:S(2)}) collective-permute-start(bf16[128,1024]{1,0:T(8,128)(2,1)S(1)} %constant_dynamic-slice_fusion.7), channel_id=1, source_target_pairs={{0,6},{1,7},{4,2},{5,3},{8,0},{9,1},{12,4},{13,5},{14,8},{15,9},{1... | collective-permute-start | bytes 786440 | tf_op jit(solution)/shard_map/ppermute | solution.py:393
  6.6 16.7 %collective-permute-start.3 = (bf16[128,1024]{1,0:T(8,128)(2,1)S(1)}, bf16[128,1024]{1,0:T(8,128)(2,1)S(1)}, u32[]{:S(2)}, u32[]{:S(2)}) collective-permute-start(bf16[128,1024]{1,0:T(8,128)(2,1)S(1)} %constant_dynamic-slice_fusion.7), channel_id=1, source_target_pairs={{0,8},{1,9},{4,12},{5,13},{8,14},{9,15},{12,10},{13,11},{14,6},{15... | collective-permute-start | bytes 786440 | tf_op jit(solution)/shard_map/ppermute | solution.py:393
  6.8 17.8 %collective-permute-start.2 = (bf16[128,1024]{1,0:T(8,128)(2,1)S(1)}, bf16[128,1024]{1,0:T(8,128)(2,1)S(1)}, u32[]{:S(2)}, u32[]{:S(2)}) collective-permute-start(bf16[128,1024]{1,0:T(8,128)(2,1)S(1)} %constant_dynamic-slice_fusion.7), channel_id=1, source_target_pairs={{0,2},{1,3},{4,0},{5,1},{8,4},{9,5},{12,8},{13,9},{14,12},{15,13},... | collective-permute-start | bytes 786440 | tf_op jit(solution)/shard_map/ppermute | solution.py:393
  8.5 16.0 %collective-permute-start.1 = (bf16[128,1024]{1,0:T(8,128)(2,1)S(1)}, bf16[128,1024]{1,0:T(8,128)(2,1)S(1)}, u32[]{:S(2)}, u32[]{:S(2)}) collective-permute-start(bf16[128,1024]{1,0:T(8,128)(2,1)S(1)} %constant_dynamic-slice_fusion.7), channel_id=1, source_target_pairs={{0,4},{1,5},{4,8},{5,9},{8,12},{9,13},{12,14},{13,15},{14,10},{15,... | collective-permute-start | bytes 786440 | tf_op jit(solution)/shard_map/ppermute | solution.py:393
  23.3 5.8 %copy-start.2 = (bf16[128,1024]{1,0:T(8,128)(2,1)S(1)}, bf16[128,1024]{1,0:T(8,128)(2,1)}, u32[]{:S(2)}) copy-start(bf16[128,1024]{1,0:T(8,128)(2,1)} %get-tuple-element.34.refs_1_) | copy-start | bytes 786436
  24.6 10.3 %collective-permute-start.7 = (bf16[128,1024]{1,0:T(8,128)(2,1)}, bf16[128,1024]{1,0:T(8,128)(2,1)S(1)}, u32[]{:S(2)}, u32[]{:S(2)}) collective-permute-start(bf16[128,1024]{1,0:T(8,128)(2,1)} %get-tuple-element.33.refs_0_), channel_id=1, source_target_pairs={{0,2},{1,3},{2,0},{3,1},{4,6},{5,7},{6,4},{7,5},{8,10},{9,11},{10,... | collective-permute-start | bytes 786440 | tf_op jit(solution)/shard_map/ppermute | solution.py:397
  27.4 24.4 %copy-start.1 = (bf16[128,1024]{1,0:T(8,128)(2,1)S(1)}, bf16[128,1024]{1,0:T(8,128)(2,1)}, u32[]{:S(2)}) copy-start(bf16[128,1024]{1,0:T(8,128)(2,1)} %get-tuple-element.33.refs_0_) | copy-start | bytes 786436
  27.5 21.6 %collective-permute-start.12 = (bf16[256,1024]{1,0:T(8,128)(2,1)S(1)}, bf16[256,1024]{1,0:T(8,128)(2,1)S(1)}, u32[]{:S(2)}, u32[]{:S(2)}) collective-permute-start(bf16[256,1024]{1,0:T(8,128)(2,1)S(1)} %pad_maximum_fusion), channel_id=1, source_target_pairs={{0,16},{16,0},{1,17},{17,1},{2,18},{18,2},{3,19},{19,3},{4,20},{20... | collective-permute-start | bytes 1572872 | tf_op jit(solution)/shard_map/ppermute | solution.py:407
  29.1 9.6 %collective-permute-start.8 = (bf16[128,1024]{1,0:T(8,128)(2,1)S(1)}, bf16[128,1024]{1,0:T(8,128)(2,1)S(1)}, u32[]{:S(2)}, u32[]{:S(2)}) collective-permute-start(bf16[128,1024]{1,0:T(8,128)(2,1)S(1)} %copy-done.2), channel_id=1, source_target_pairs={{0,2},{1,3},{2,0},{3,1},{4,6},{5,7},{6,4},{7,5},{8,10},{9,11},{10,... | collective-permute-start | bytes 786440 | tf_op jit(solution)/shard_map/ppermute | solution.py:397
  29.1 14.7 %collective-permute-start.11 = (bf16[128,1024]{1,0:T(8,128)(2,1)S(1)}, bf16[128,1024]{1,0:T(8,128)(2,1)S(1)}, u32[]{:S(2)}, u32[]{:S(2)}) collective-permute-start(bf16[128,1024]{1,0:T(8,128)(2,1)S(1)} %get-tuple-element.52), channel_id=1, source_target_pairs={{0,8},{1,9},{2,10},{3,11},{4,12},{5,13},{6,14},{7,15},{8,0},{9,1},... | collective-permute-start | bytes 786440 | tf_op jit(solution)/shard_map/ppermute | solution.py:397
  31.2 12.6 %collective-permute-start.10 = (bf16[128,1024]{1,0:T(8,128)(2,1)S(1)}, bf16[128,1024]{1,0:T(8,128)(2,1)S(1)}, u32[]{:S(2)}, u32[]{:S(2)}) collective-permute-start(bf16[128,1024]{1,0:T(8,128)(2,1)S(1)} %get-tuple-element.53), channel_id=1, source_target_pairs={{0,4},{1,5},{2,6},{3,7},{4,0},{5,1},{6,2},{7,3},{8,12},{9,13},{10,... | collective-permute-start | bytes 786440 | tf_op jit(solution)/shard_map/ppermute | solution.py:397
  34.8 14.3 %collective-permute-start.9 = (bf16[128,1024]{1,0:T(8,128)(2,1)S(1)}, bf16[128,1024]{1,0:T(8,128)(2,1)S(1)}, u32[]{:S(2)}, u32[]{:S(2)}) collective-permute-start(bf16[128,1024]{1,0:T(8,128)(2,1)S(1)} %collective-permute-done.7.refs_4_), channel_id=1, source_target_pairs={{0,4},{1,5},{2,14},{3,15},{4,8},{5,9},{6,2},{7,3},{8,12},{9,13},{1... | collective-permute-start | bytes 786440 | tf_op jit(solution)/shard_map/ppermute | solution.py:403
  38.7 11.5 %collective-permute-start.15 = (bf16[128,1024]{1,0:T(8,128)(2,1)S(1)}, bf16[128,1024]{1,0:T(8,128)(2,1)S(1)}, u32[]{:S(2)}, u32[]{:S(2)}) collective-permute-start(bf16[128,1024]{1,0:T(8,128)(2,1)S(1)} %get-tuple-element.51), channel_id=1, source_target_pairs={{0,2},{1,3},{2,0},{3,1},{4,6},{5,7},{6,4},{7,5},{8,10},{9,11},{10,... | collective-permute-start | bytes 786440 | tf_op jit(solution)/shard_map/ppermute | solution.py:397
  49.1 1.5 %collective-permute-start.14 = (bf16[128,1024]{1,0:T(8,128)(2,1)S(1)}, bf16[128,1024]{1,0:T(8,128)(2,1)S(1)}, u32[]{:S(2)}, u32[]{:S(2)}) collective-permute-start(bf16[128,1024]{1,0:T(8,128)(2,1)S(1)} %collective-permute-done.8.refs_5_), channel_id=1, source_target_pairs={{0,1},{1,0},{2,3},{3,2},{4,5},{5,4},{6,7},{7,6},{8,9},{9,8},{10,11... | collective-permute-start | bytes 786440 | tf_op jit(solution)/shard_map/ppermute | solution.py:379
  49.2 9.2 %collective-permute-start.16 = (bf16[128,1024]{1,0:T(8,128)(2,1)S(1)}, bf16[128,1024]{1,0:T(8,128)(2,1)S(1)}, u32[]{:S(2)}, u32[]{:S(2)}) collective-permute-start(bf16[128,1024]{1,0:T(8,128)(2,1)S(1)} %pad_maximum_fusion.1), channel_id=1, source_target_pairs={{0,16},{16,0},{1,17},{17,1},{2,18},{18,2},{3,19},{19,3},{4,20},{20... | collective-permute-start | bytes 786440 | tf_op jit(solution)/shard_map/ppermute | solution.py:407
  49.8 10.2 %collective-permute-start.18 = (bf16[128,1024]{1,0:T(8,128)(2,1)S(1)}, bf16[128,1024]{1,0:T(8,128)(2,1)S(1)}, u32[]{:S(2)}, u32[]{:S(2)}) collective-permute-start(bf16[128,1024]{1,0:T(8,128)(2,1)S(1)} %collective-permute-done.8.refs_5_), channel_id=1, source_target_pairs={{0,4},{1,5},{2,14},{3,15},{4,8},{5,9},{6,2},{7,3},{8,12},{9,13},{1... | collective-permute-start | bytes 786440 | tf_op jit(solution)/shard_map/ppermute | solution.py:403
  50.7 26.1 %copy-start = (bf16[1024,1024]{1,0:T(8,128)(2,1)S(1)}, bf16[1024,1024]{1,0:T(8,128)(2,1)}, u32[]{:S(2)}) copy-start(bf16[1024,1024]{1,0:T(8,128)(2,1)} %param.21) | copy-start | bytes 6291460
  50.7 26.1 %copy-start.3 = (bf16[256,1024]{1,0:T(8,128)(2,1)S(1)}, bf16[256,1024]{1,0:T(8,128)(2,1)}, u32[]{:S(2)}) copy-start(bf16[256,1024]{1,0:T(8,128)(2,1)} %get-tuple-element.29.tokens_ref) | copy-start | bytes 1572868
  50.7 10.1 %collective-permute-start.17 = (bf16[64,1024]{1,0:T(8,128)(2,1)S(1)}, bf16[64,1024]{1,0:T(8,128)(2,1)S(1)}, u32[]{:S(2)}, u32[]{:S(2)}) collective-permute-start(bf16[64,1024]{1,0:T(8,128)(2,1)S(1)} %constant_dynamic-slice_fusion), channel_id=1, source_target_pairs={{0,16},{16,0},{1,17},{17,1},{2,18},{18,2},{3,19},{19,3},{4,20},{20... | collective-permute-start | bytes 393224 | tf_op jit(solution)/shard_map/ppermute | solution.py:407
  51.8 9.0 %collective-permute-start.5 = (bf16[128,1024]{1,0:T(8,128)(2,1)S(1)}, bf16[128,1024]{1,0:T(8,128)(2,1)S(1)}, u32[]{:S(2)}, u32[]{:S(2)}) collective-permute-start(bf16[128,1024]{1,0:T(8,128)(2,1)S(1)} %copy-done.1), channel_id=1, source_target_pairs={{0,1},{1,0},{2,3},{3,2},{4,5},{5,4},{6,7},{7,6},{8,9},{9,8},{10,11... | collective-permute-start | bytes 786440 | tf_op jit(solution)/shard_map/ppermute | solution.py:379
  51.8 9.0 %collective-permute-start.6 = (bf16[128,1024]{1,0:T(8,128)(2,1)S(1)}, bf16[128,1024]{1,0:T(8,128)(2,1)S(1)}, u32[]{:S(2)}, u32[]{:S(2)}) collective-permute-start(bf16[128,1024]{1,0:T(8,128)(2,1)S(1)} %copy-done.2), channel_id=1, source_target_pairs={{0,1},{1,0},{2,3},{3,2},{4,5},{5,4},{6,7},{7,6},{8,9},{9,8},{10,11... | collective-permute-start | bytes 786440 | tf_op jit(solution)/shard_map/ppermute | solution.py:379
  58.4 2.4 %collective-permute-start.13 = (bf16[128,1024]{1,0:T(8,128)(2,1)S(1)}, bf16[128,1024]{1,0:T(8,128)(2,1)S(1)}, u32[]{:S(2)}, u32[]{:S(2)}) collective-permute-start(bf16[128,1024]{1,0:T(8,128)(2,1)S(1)} %collective-permute-done.7.refs_4_), channel_id=1, source_target_pairs={{0,1},{1,0},{2,3},{3,2},{4,5},{5,4},{6,7},{7,6},{8,9},{9,8},{10,11... | collective-permute-start | bytes 786440 | tf_op jit(solution)/shard_map/ppermute | solution.py:379
  60.1 1.5 %collective-permute-start.19 = (bf16[128,1024]{1,0:T(8,128)(2,1)S(1)}, bf16[128,1024]{1,0:T(8,128)(2,1)S(1)}, u32[]{:S(2)}, u32[]{:S(2)}) collective-permute-start(bf16[128,1024]{1,0:T(8,128)(2,1)S(1)} %collective-permute-done.9.refs_8_), channel_id=1, source_target_pairs={{0,1},{1,0},{2,3},{3,2},{4,5},{5,4},{6,7},{7,6},{8,9},{9,8},{10,11... | collective-permute-start | bytes 786440 | tf_op jit(solution)/shard_map/ppermute | solution.py:379
  60.8 1.5 %collective-permute-start.20 = (bf16[128,1024]{1,0:T(8,128)(2,1)S(1)}, bf16[128,1024]{1,0:T(8,128)(2,1)S(1)}, u32[]{:S(2)}, u32[]{:S(2)}) collective-permute-start(bf16[128,1024]{1,0:T(8,128)(2,1)S(1)} %collective-permute-done.18.refs_9_), channel_id=1, source_target_pairs={{0,1},{1,0},{2,3},{3,2},{4,5},{5,4},{6,7},{7,6},{8,9},{9,8},{10,11... | collective-permute-start | bytes 786440 | tf_op jit(solution)/shard_map/ppermute | solution.py:379
  75.2 1.6 %collective-permute-start.21 = (bf16[4,256,128]{2,1,0:T(8,128)(2,1)S(1)}, bf16[4,256,128]{2,1,0:T(8,128)(2,1)S(1)}, u32[]{:S(2)}, u32[]{:S(2)}) collective-permute-start(bf16[4,256,128]{2,1,0:T(8,128)(2,1)S(1)} %get-tuple-element.50), channel_id=1, source_target_pairs={{0,1},{1,0},{2,3},{3,2},{4,5},{5,4},{6,7},{7,6},{8,9},{9,8},{10,11... | collective-permute-start | bytes 786440 | tf_op jit(solution)/shard_map/ppermute | solution.py:379

commit v8 on v7

--- a/solution.py
+++ b/solution.py
@@ -105,8 +105,7 @@
     pos_hbm,
     gain_hbm,
     tokens_ref,
-    upper_ref,
-    lower_ref,
+    normed_ref,
     var_embed_ref,
     keys_ref,
     embed_ref,
@@ -203,10 +202,7 @@
     full = tokens_zero.astype(F32)
     centred = full - jnp.mean(full, axis=-1, keepdims=True)
     variance = jnp.mean(centred * centred, axis=-1, keepdims=True)
-    normed = (centred * lax.rsqrt(variance + 1e-05) * gain_ref[...]).astype(BF16)
-    half = upper_ref.shape[0]
-    upper_ref[...] = normed[:half]
-    lower_ref[...] = normed[half:]
+    normed_ref[...] = (centred * lax.rsqrt(variance + 1e-05) * gain_ref[...]).astype(BF16)
 
 
 def cost(gflops, mib, exps=0):
@@ -230,13 +226,9 @@
     arrays = (var_embed, keys, embed_weight, patches, value, out_w, pos, gain.reshape(1, width))
     return pl.pallas_call(
         aggregate_kernel,
-        out_shape=[
-            jax.ShapeDtypeStruct((tokens, width), BF16),
-            jax.ShapeDtypeStruct((tokens // 2, width), BF16),
-            jax.ShapeDtypeStruct((tokens // 2, width), BF16),
-        ],
+        out_shape=[jax.ShapeDtypeStruct((tokens, width), BF16)] * 2,
         in_specs=[SMEM] + [HBM] * len(arrays),
-        out_specs=[VMEM] * 3,
+        out_specs=[VMEM] * 2,
         scratch_shapes=like(*arrays)
         + like(embed_weight)
         + [pltpu.VMEM((var_count * pixels, width), BF16)]
@@ -249,14 +241,11 @@
 
 def attend_kernel(*refs, spots):
     count = len(spots)
-    weight_refs = refs[12 : 12 + count]
-    mine_ref, other_ref, rows_s, query_s, key_s, value_s, weight_s, sems = refs[12 + count :]
+    weight_refs = refs[6 : 6 + count]
+    mine_ref, other_ref, query_s, key_s, value_s, weight_s, sems = refs[6 + count :]
     index, plane = lax.axis_index("space"), lax.axis_index("groups")
     side = index % 2
-    half = rows_s.shape[1] // 2
-    moves = [
-        (ref, rows_s.at[i // 2, pl.ds(i % 2 * half, half), :]) for i, ref in enumerate(refs[:12])
-    ]
+    moves = []
     for ref, (step, share) in zip(weight_refs, spots):
         rows = ref.shape[0]
         if share == "ring":
@@ -274,45 +263,44 @@
         wait()
     flip = index // 2 % 2 if spots[0][0] is not None else 0
     near, far = 4 - 4 * flip, 4 * flip
-    _, tokens, width = rows_s.shape
+    tokens, width = refs[0].shape
     pairs = mine_ref.shape[0]
     cols = pairs * LANES
-    weight = weight_s[...].reshape(3, cols, width)
+    weight = weight_s[...].reshape(3 * cols, width)
     head_size = LANES // 2
     scale = 1.0 / math.sqrt(head_size)
     pieces = (2 + side, 3 - side, near + side, near + 1 - side, far + side, far + 1 - side)
     ones = jnp.ones((tokens, LANES), BF16)
     for number, place in enumerate(pieces):
-        rows = rows_s[number]
-        key_s[place] = dot_t(weight[1], rows).astype(BF16)
-        value = dot_t(rows, weight[2]).astype(BF16)
+        rows = refs[number][...]
+        both = dot_t(rows, weight[cols:]).astype(BF16)
+        spot = pl.ds(pl.multiple_of(place * tokens, tokens), tokens)
         for pair in range(pairs):
-            value_s[place, pair] = jnp.concatenate(
-                [value[:, pair * LANES : (pair + 1) * LANES], ones], axis=1
-            )
+            lanes = slice(pair * LANES, (pair + 1) * LANES)
+            key_s[pair, spot, :] = both[:, :cols][:, lanes]
+            value_s[pair, spot, :] = jnp.concatenate([both[:, cols:][:, lanes], ones], axis=1)
         if number < 2:
-            query = (dot_t(rows, weight[0]).astype(BF16).astype(F32) * scale).astype(BF16)
+            query = (dot_t(rows, weight[:cols]).astype(BF16).astype(F32) * scale).astype(BF16)
             for pair in range(pairs):
                 query_s[number, pair] = query[:, pair * LANES : (pair + 1) * LANES]
 
     left_half = iota((tokens, LANES), 1) < head_size
 
     def attend(pair, carry):
-        row = pl.multiple_of(pair * LANES, LANES)
         for number, (out_ref, sector) in enumerate(((mine_ref, side), (other_ref, 1 - side))):
             query = query_s[number, pair]
             halves = []
             for half in range(2):
                 keep = left_half if half == 0 else jnp.logical_not(left_half)
                 masked = jnp.where(keep, query, jnp.zeros_like(query))
+                start = pl.multiple_of(sector * tokens, tokens)
                 scores = [
-                    dot(masked, key_s[sector + k, pl.ds(row, LANES), :]) for k in range(5)
+                    dot_t(masked, key_s[pair, pl.ds(start + k * tokens, tokens), :])
+                    for k in range(5)
                 ]
                 top = jnp.max(functools.reduce(jnp.maximum, scores), axis=-1, keepdims=True)
-                acc = None
-                for k in range(5):
-                    part = dot(jnp.exp(scores[k] - top).astype(BF16), value_s[sector + k, pair])
-                    acc = part if acc is None else acc + part
+                probs = jnp.concatenate([jnp.exp(s - top).astype(BF16) for s in scores], axis=1)
+                acc = dot(probs, value_s[pair, pl.ds(start, 5 * tokens), :])
                 halves.append(acc[:, :LANES] / acc[:, LANES:])
             out_ref[pair] = jnp.where(left_half, halves[0], halves[1]).astype(BF16)
         return carry
@@ -321,8 +309,7 @@
 
 
 def attend(pieces, weights):
-    pieces = [half for piece in pieces for half in piece]
-    tokens, width = 2 * pieces[0].shape[0], pieces[0].shape[1]
+    tokens, width = pieces[0].shape
     spots = tuple(spot for _, spot in weights)
     weights = [piece for piece, _ in weights]
     rows = weights[0].shape[0]
@@ -332,13 +319,12 @@
     return pl.pallas_call(
         functools.partial(attend_kernel, spots=spots),
         out_shape=[jax.ShapeDtypeStruct((pairs, tokens, LANES), BF16)] * 2,
-        in_specs=[HBM] * (12 + len(weights)),
+        in_specs=[VMEM] * 6 + [HBM] * len(weights),
         out_specs=[VMEM, VMEM],
         scratch_shapes=[
-            pltpu.VMEM((6, tokens, width), BF16),
             pltpu.VMEM((2, pairs, tokens, LANES), BF16),
-            pltpu.VMEM((6, cols, tokens), BF16),
-            pltpu.VMEM((6, pairs, tokens, 2 * LANES), BF16),
+            pltpu.VMEM((pairs, 6 * tokens, LANES), BF16),
+            pltpu.VMEM((pairs, 6 * tokens, 2 * LANES), BF16),
             pltpu.VMEM((blocks, rows, width), BF16),
             pltpu.SemaphoreType.DMA((32,)),
         ],
@@ -460,7 +446,7 @@
         weights = [(block, (0, None))]
     else:
         weights = parity_weight(qkv_weight, side, head_size)
-    tokens_zero, *normed = aggregate(
+    tokens_zero, normed = aggregate(
         var_order, var_embed, agg_keys, embed_weight, patches, agg_value, agg_out, pos_embed, norm_gain
     )
     if ringed:
@@ -469,34 +455,28 @@
             parts = [lax.dynamic_slice_in_dim(b, plane * third, third, 0) for b in blocks]
             return across(jnp.concatenate(parts, axis=0))
 
-        upper, lower, *early = together(*normed, *early)
+        normed, *early = together(normed, *early)
         weights += [(b, (-step, "ring")) for b, step in zip(early, (1, -1, 2, -2))]
+        swap = swapped(early)
         place = ring_place(lax.axis_index("space"))
+        near = crossed(normed, 2)
+        pair = crossed(jnp.where(place % 2 == 0, early[2], early[3]), 4)
         low = place % 4 < 2
-        near0, near1 = crossed(upper, 2), crossed(lower, 2)
-        pair = crossed(jnp.where(place % 2 == 0, early[2], early[3]), 4)
         opposite = crossed(jnp.where(low, early[2], early[3]), 8)
-        swap = swapped(early)
-        far0, near_sib0 = onward(near0), sibling(near0)
+        near, pair, opposite, swap = together(near, pair, opposite, swap)
+        far, near_sib = onward(near), sibling(near)
         beside = crossed(jnp.where(low, early[3], early[2]), 2)
-        near1, far0, pair, opposite, swap = together(near1, far0, pair, opposite, swap)
-        far1, near_sib1 = onward(near1), sibling(near1)
         first = swapped([pair, opposite])
-        near_sib1, beside = together(near_sib1, beside)
+        near_sib, beside = together(near_sib, beside)
         second = swapped([beside])
-        first, second, far1 = together(first, second, far1)
+        first, second, far = together(first, second, far)
         weights += [(pair, ("pair", "ring")), (opposite, (4, "ring")), (beside, ("beside", "ring"))]
         weights += [(swap, ((-1, 1, -2, 2), "swap"))]
         weights += [(first, (("pair", 4), "swap")), (second, (("beside",), "swap"))]
-        near, near_sib, far = (near0, near1), (near_sib0, near_sib1), (far0, far1)
-        normed = (upper, lower)
     else:
-        near = [from_chip(half, 1) for half in normed]
-        far = [from_chip(half, -1) for half in normed]
-        near_sib = [sibling(half) for half in near]
-    sib = [sibling(half) for half in normed]
-    far_sib = [sibling(half) for half in far]
-    pieces = (normed, sib, near, near_sib, far, far_sib)
+        near, far = from_chip(normed, 1), from_chip(normed, -1)
+        near_sib = sibling(near)
+    pieces = (normed, sibling(normed), near, near_sib, far, sibling(far))
     mine, other = attend(pieces, weights)
     return finish(tokens_zero, mine, sibling(other), attn_out)
 

time: 78.5 us -> 76.3 us (0.972)
  starting transfers between devices: 20.6 us -> 16.3 us
  waiting for transfers between devices: 27.2 us -> 29.8 us
    ppermute x5 -> x4, waiting for transfers between devices: 7.85 us -> 17.5 us  [crossed(): lax.ppermute(value, 'space', [(i, i ^ bits) for i in range(2 * len(RING))])]
    ppermute x3, waiting for transfers between devices: 6.82 us -> 0.64 us  [across(): return lax.ppermute(value, 'groups', [(0, 1), (1, 0)])]
    ppermute x5 -> x4, starting transfers between devices: 8.07 us -> 5.22 us  [crossed(): lax.ppermute(value, 'space', [(i, i ^ bits) for i in range(2 * len(RING))])]
    ppermute x2 -> x1, waiting for transfers between devices: 6.95 us -> 6.18 us  [onward(): return lax.ppermute(value, 'space', pairs)]
    ppermute x2 -> x1, starting transfers between devices: 2 us -> 1.39 us  [onward(): return lax.ppermute(value, 'space', pairs)]
    ppermute x8 -> x5, waiting for transfers between devices: 4.39 us -> 4.28 us  [sibling(): return lax.ppermute(value, 'space', [(i, i ^ 1) for i in range(length)])]
  transfers between devices with their start and end apart: 22 -> 17, of which waited for: 13 -> 8; matrix products, arithmetic and copies ran while one was open for 0% -> 0% of each run, Pallas kernels for 19% -> 19%
where the time goes in v8:
time: 76.3 us; the launch traced here: 76.1 us
  waiting for transfers between devices  29.8 us (39%)
  Pallas kernels  28.6 us (37%)
  starting transfers between devices  16.3 us (21%)
  local copies, waits for them, and re-layouts  1.18 us (2%)
    ppermute x4, waiting for transfers between devices, crossed(): lax.ppermute(value, 'space', [(i, i ^ bits) for i in range(2 * len(RING))])  17.5 us
    pallas_call x1, Pallas kernels, aggregate(): pl.pallas_call(aggregate_kernel, out_shape=[jax.ShapeDtypeStruct((tokens,...  14.6 us
    pallas_call x1, Pallas kernels, attend(): pl.pallas_call(functools.partial(attend_kernel, spots=spots), out_shape=[...  12.5 us
    ppermute x1, waiting for transfers between devices, onward(): return lax.ppermute(value, 'space', pairs)  6.18 us
    ppermute x4, starting transfers between devices, around(): return lax.ppermute(value, 'space', pairs)  6.09 us
    ppermute x4, starting transfers between devices, crossed(): lax.ppermute(value, 'space', [(i, i ^ bits) for i in range(2 * len(RING))])  5.22 us
    ppermute x5, waiting for transfers between devices, sibling(): return lax.ppermute(value, 'space', [(i, i ^ 1) for i in range(length)])  4.28 us
    ppermute x3, starting transfers between devices, across(): return lax.ppermute(value, 'groups', [(0, 1), (1, 0)])  2.81 us
  transfers between devices with their start and end apart: 17, of which 8 were waited for; matrix products, arithmetic and copies ran while one was open for 0% of the time, Pallas kernels for 19%

profile of v8, /device:TPU:0, one launch (start us, length us, event | category | flops | bytes accessed | tf_op | source)
XLA Modules:
  0.0 76.1 jit_solution(3983636823788182671)
XLA Ops:
  0.0 1.1 %fusion = (bf16[64,1024]{1,0:T(8,128)(2,1)S(1)}, bf16[64,1024]{1,0:T(8,128)(2,1)S(1)}, bf16[64,1024]{1,0:T(8,128)(2,1)S(1)}) fusion(bf16[192,1024]{1,0:T(8,128)(2,1)} %bitcast.4), kind=kLoop, calls=%fused_computation.14 | loop fusion | bytes 786432 | tf_op jit(solution)/shard_map/slice | solution.py:402
  1.1 0.5 collective-permute-start
  1.6 1.0 %collective-permute-done = bf16[64,1024]{1,0:T(8,128)(2,1)S(1)} collective-permute-done((bf16[64,1024]{1,0:T(8,128)(2,1)S(1)}, bf16[64,1024]{1,0:T(8,128)(2,1)S(1)}, u32[]{:S(2)}, u32[]{:S(2)}) %collective-permute-start) | collective-permute-done | bytes 131104 | tf_op jit(solution)/shard_map/ppermute | solution.py:365
  2.6 0.1 maximum_select_fusion.refs_6_
  2.7 3.9 %collective-permute-start.4 = (bf16[128,1024]{1,0:T(8,128)(2,1)S(1)}, bf16[128,1024]{1,0:T(8,128)(2,1)S(1)}, u32[]{:S(2)}, u32[]{:S(2)}) collective-permute-start(bf16[128,1024]{1,0:T(8,128)(2,1)S(1)} %constant_dynamic-slice_fusion.7), channel_id=1, source_target_pairs={{0,6},{1,7},{4,2},{5,3},{8,0},{9,1},{12,4},{13,5},{14,8},{15,9},{1... | collective-permute-start | bytes 786440 | tf_op jit(solution)/shard_map/ppermute | solution.py:379
  6.6 0.1 collective-permute-start.3
  6.8 1.8 %collective-permute-start.2 = (bf16[128,1024]{1,0:T(8,128)(2,1)S(1)}, bf16[128,1024]{1,0:T(8,128)(2,1)S(1)}, u32[]{:S(2)}, u32[]{:S(2)}) collective-permute-start(bf16[128,1024]{1,0:T(8,128)(2,1)S(1)} %constant_dynamic-slice_fusion.7), channel_id=1, source_target_pairs={{0,2},{1,3},{4,0},{5,1},{8,4},{9,5},{12,8},{13,9},{14,12},{15,13},... | collective-permute-start | bytes 786440 | tf_op jit(solution)/shard_map/ppermute | solution.py:379
  8.5 0.2 collective-permute-start.1
  8.8 14.6 %aggregate.1 = (bf16[256,1024]{1,0:T(8,128)(2,1)}, bf16[256,1024]{1,0:T(8,128)(2,1)}) custom-call(s32[64]{0:T(128)} %order_ref.1, bf16[64,1024]{1,0:T(8,128)(2,1)} %var_embed_hbm.1, bf16[16,1024]{1,0:T(8,128)(2,1)} %keys_hbm.1, bf16[64,16,1024]{2,1,0:T(8,128)(2,1)} %embed_hbm, bf16[256,1024]{1,0:T(8,128)(2,1)} %patches_hbm.1, bf16[1024,1024]{1,0:T(8,128)(2,1)} %value_hbm.1, ...), custom_call_target="tpu_custom_call" | custom-call | flops 16000000000 | bytes 8388608 | tf_op jit(solution)/shard_map/aggregate/pallas_call | solution.py:227
  23.4 0.0 copy-start.1
  23.4 0.0 collective-permute-done.4.refs_10_
  23.4 0.0 collective-permute-done.3.refs_9_
  23.4 1.2 %collective-permute-done.2.refs_8_ = bf16[128,1024]{1,0:T(8,128)(2,1)S(1)} collective-permute-done((bf16[128,1024]{1,0:T(8,128)(2,1)S(1)}, bf16[128,1024]{1,0:T(8,128)(2,1)S(1)}, u32[]{:S(2)}, u32[]{:S(2)}) %collective-permute-start.2) | collective-permute-done | bytes 262176 | tf_op jit(solution)/shard_map/ppermute | solution.py:379
  24.6 0.0 collective-permute-done.1.refs_7_
  24.7 1.6 %collective-permute-start.9 = (bf16[256,1024]{1,0:T(8,128)(2,1)S(1)}, bf16[256,1024]{1,0:T(8,128)(2,1)S(1)}, u32[]{:S(2)}, u32[]{:S(2)}) collective-permute-start(bf16[256,1024]{1,0:T(8,128)(2,1)S(1)} %pad_maximum_fusion), channel_id=1, source_target_pairs={{0,16},{16,0},{1,17},{17,1},{2,18},{18,2},{3,19},{19,3},{4,20},{20... | collective-permute-start | bytes 1572872 | tf_op jit(solution)/shard_map/ppermute | solution.py:393
  26.3 0.0 copy-done.1
  26.3 2.8 %collective-permute-start.6 = (bf16[256,1024]{1,0:T(8,128)(2,1)S(1)}, bf16[256,1024]{1,0:T(8,128)(2,1)S(1)}, u32[]{:S(2)}, u32[]{:S(2)}) collective-permute-start(bf16[256,1024]{1,0:T(8,128)(2,1)S(1)} %copy-done.1), channel_id=1, source_target_pairs={{0,2},{1,3},{2,0},{3,1},{4,6},{5,7},{6,4},{7,5},{8,10},{9,11},{10,... | collective-permute-start | bytes 1572872 | tf_op jit(solution)/shard_map/ppermute | solution.py:383
  29.1 0.1 broadcast_select_fusion
  29.1 1.4 %collective-permute-start.8 = (bf16[128,1024]{1,0:T(8,128)(2,1)S(1)}, bf16[128,1024]{1,0:T(8,128)(2,1)S(1)}, u32[]{:S(2)}, u32[]{:S(2)}) collective-permute-start(bf16[128,1024]{1,0:T(8,128)(2,1)S(1)} %get-tuple-element.46), channel_id=1, source_target_pairs={{0,8},{1,9},{2,10},{3,11},{4,12},{5,13},{6,14},{7,15},{8,0},{9,1},... | collective-permute-start | bytes 786440 | tf_op jit(solution)/shard_map/ppermute | solution.py:383
  30.5 0.7 collective-permute-start.7
  31.2 11.2 %collective-permute-done.8.refs_12_ = bf16[128,1024]{1,0:T(8,128)(2,1)S(1)} collective-permute-done((bf16[128,1024]{1,0:T(8,128)(2,1)S(1)}, bf16[128,1024]{1,0:T(8,128)(2,1)S(1)}, u32[]{:S(2)}, u32[]{:S(2)}) %collective-permute-start.8) | collective-permute-done | bytes 262176 | tf_op jit(solution)/shard_map/ppermute | solution.py:383
  42.4 0.0 collective-permute-done.7.refs_11_
  42.4 0.0 collective-permute-done.9.refs_14_
  42.4 0.0 collective-permute-done.6.refs_2_
  42.4 0.1 collective-permute-start.10
  42.5 0.4 collective-permute-start.11
  42.9 1.4 %collective-permute-start.14 = (bf16[256,1024]{1,0:T(8,128)(2,1)S(1)}, bf16[256,1024]{1,0:T(8,128)(2,1)S(1)}, u32[]{:S(2)}, u32[]{:S(2)}) collective-permute-start(bf16[256,1024]{1,0:T(8,128)(2,1)S(1)} %collective-permute-done.6.refs_2_), channel_id=1, source_target_pairs={{0,4},{1,5},{2,14},{3,15},{4,8},{5,9},{6,2},{7,3},{8,12},{9,13},{1... | collective-permute-start | bytes 1572872 | tf_op jit(solution)/shard_map/ppermute | solution.py:389
  44.3 0.6 collective-permute-start.12
  44.9 6.3 %collective-permute-done.11.refs_13_ = bf16[128,1024]{1,0:T(8,128)(2,1)S(1)} collective-permute-done((bf16[128,1024]{1,0:T(8,128)(2,1)S(1)}, bf16[128,1024]{1,0:T(8,128)(2,1)S(1)}, u32[]{:S(2)}, u32[]{:S(2)}) %collective-permute-start.11) | collective-permute-done | bytes 262176 | tf_op jit(solution)/shard_map/ppermute | solution.py:383
  51.2 0.0 collective-permute-done.10.refs_3_
  51.2 0.0 copy-start
  51.2 0.0 copy-start.2
  51.2 0.6 collective-permute-start.13
  51.8 0.0 collective-permute-start.5
  51.8 0.6 collective-permute-done.12.refs_15_
  52.5 6.2 %collective-permute-done.14.refs_4_ = bf16[256,1024]{1,0:T(8,128)(2,1)S(1)} collective-permute-done((bf16[256,1024]{1,0:T(8,128)(2,1)S(1)}, bf16[256,1024]{1,0:T(8,128)(2,1)S(1)}, u32[]{:S(2)}, u32[]{:S(2)}) %collective-permute-start.14) | collective-permute-done | bytes 524320 | tf_op jit(solution)/shard_map/ppermute | solution.py:389
  58.7 0.0 collective-permute-done.13.refs_16_
  58.7 0.0 collective-permute-start.15
  58.7 0.0 collective-permute-done.5.refs_1_
  58.7 1.9 %collective-permute-done.15.refs_5_ = bf16[256,1024]{1,0:T(8,128)(2,1)S(1)} collective-permute-done((bf16[256,1024]{1,0:T(8,128)(2,1)S(1)}, bf16[256,1024]{1,0:T(8,128)(2,1)S(1)}, u32[]{:S(2)}, u32[]{:S(2)}) %collective-permute-start.15) | collective-permute-done | bytes 524320 | tf_op jit(solution)/shard_map/ppermute | solution.py:365
  60.6 12.5 %attend.1 = (bf16[4,256,128]{2,1,0:T(8,128)(2,1)S(1)}, bf16[4,256,128]{2,1,0:T(8,128)(2,1)S(1)}) custom-call(bf16[256,1024]{1,0:T(8,128)(2,1)S(1)} %copy-done.1, bf16[256,1024]{1,0:T(8,128)(2,1)S(1)} %collective-permute-done.5.refs_1_, bf16[256,1024]{1,0:T(8,128)(2,1)S(1)} %collective-permute-done.6.refs_2_, ...), custom_call_target="tpu_custom_call" | custom-call | flops 10000000000 | bytes 8388608 | tf_op jit(solution)/shard_map/attend/pallas_call | solution.py:319
  73.0 0.2 collective-permute-start.16
  73.2 1.4 %collective-permute-done.16.other_ref = bf16[4,256,128]{2,1,0:T(8,128)(2,1)S(1)} collective-permute-done((bf16[4,256,128]{2,1,0:T(8,128)(2,1)S(1)}, bf16[4,256,128]{2,1,0:T(8,128)(2,1)S(1)}, u32[]{:S(2)}, u32[]{:S(2)}) %collective-permute-start.16) | collective-permute-done | bytes 262176 | tf_op jit(solution)/shard_map/ppermute | solution.py:365
  74.6 0.0 copy-done
  74.6 0.0 copy-done.2
  74.6 1.5 %finish.1 = bf16[256,1024]{1,0:T(8,128)(2,1)} custom-call(bf16[256,1024]{1,0:T(8,128)(2,1)S(1)} %copy-done.2, bf16[4,256,128]{2,1,0:T(8,128)(2,1)S(1)} %get-tuple-element.43.mine_ref, bf16[4,256,128]{2,1,0:T(8,128)(2,1)S(1)} %collective-permute-done.16.other_ref, bf16[8,2,64,1024]{3,2,1,0:T(8,128)(2,1)S(1)} %bitcast.3), custom_call_target="tpu_custom_call" | custom-call | flops 1000000000 | bytes 4194304 | tf_op jit(solution)/shard_map/finish/pallas_call | solution.py:352
  (8 shorter events, 0.2 us)
Async XLA Ops:
  1.1 1.5 %collective-permute-start = (bf16[64,1024]{1,0:T(8,128)(2,1)S(1)}, bf16[64,1024]{1,0:T(8,128)(2,1)S(1)}, u32[]{:S(2)}, u32[]{:S(2)}) collective-permute-start(bf16[64,1024]{1,0:T(8,128)(2,1)S(1)} %get-tuple-element.49), channel_id=1, source_target_pairs={{0,1},{1,0},{2,3},{3,2},{4,5},{5,4},{6,7},{7,6},{8,9},{9,8},{10,11... | collective-permute-start | bytes 393224 | tf_op jit(solution)/shard_map/ppermute | solution.py:365
  2.7 20.7 %collective-permute-start.4 = (bf16[128,1024]{1,0:T(8,128)(2,1)S(1)}, bf16[128,1024]{1,0:T(8,128)(2,1)S(1)}, u32[]{:S(2)}, u32[]{:S(2)}) collective-permute-start(bf16[128,1024]{1,0:T(8,128)(2,1)S(1)} %constant_dynamic-slice_fusion.7), channel_id=1, source_target_pairs={{0,6},{1,7},{4,2},{5,3},{8,0},{9,1},{12,4},{13,5},{14,8},{15,9},{1... | collective-permute-start | bytes 786440 | tf_op jit(solution)/shard_map/ppermute | solution.py:379
  6.6 16.8 %collective-permute-start.3 = (bf16[128,1024]{1,0:T(8,128)(2,1)S(1)}, bf16[128,1024]{1,0:T(8,128)(2,1)S(1)}, u32[]{:S(2)}, u32[]{:S(2)}) collective-permute-start(bf16[128,1024]{1,0:T(8,128)(2,1)S(1)} %constant_dynamic-slice_fusion.7), channel_id=1, source_target_pairs={{0,8},{1,9},{4,12},{5,13},{8,14},{9,15},{12,10},{13,11},{14,6},{15... | collective-permute-start | bytes 786440 | tf_op jit(solution)/shard_map/ppermute | solution.py:379
  6.8 17.8 %collective-permute-start.2 = (bf16[128,1024]{1,0:T(8,128)(2,1)S(1)}, bf16[128,1024]{1,0:T(8,128)(2,1)S(1)}, u32[]{:S(2)}, u32[]{:S(2)}) collective-permute-start(bf16[128,1024]{1,0:T(8,128)(2,1)S(1)} %constant_dynamic-slice_fusion.7), channel_id=1, source_target_pairs={{0,2},{1,3},{4,0},{5,1},{8,4},{9,5},{12,8},{13,9},{14,12},{15,13},... | collective-permute-start | bytes 786440 | tf_op jit(solution)/shard_map/ppermute | solution.py:379
  8.5 16.0 %collective-permute-start.1 = (bf16[128,1024]{1,0:T(8,128)(2,1)S(1)}, bf16[128,1024]{1,0:T(8,128)(2,1)S(1)}, u32[]{:S(2)}, u32[]{:S(2)}) collective-permute-start(bf16[128,1024]{1,0:T(8,128)(2,1)S(1)} %constant_dynamic-slice_fusion.7), channel_id=1, source_target_pairs={{0,4},{1,5},{4,8},{5,9},{8,12},{9,13},{12,14},{13,15},{14,10},{15,... | collective-permute-start | bytes 786440 | tf_op jit(solution)/shard_map/ppermute | solution.py:379
  23.4 2.9 %copy-start.1 = (bf16[256,1024]{1,0:T(8,128)(2,1)S(1)}, bf16[256,1024]{1,0:T(8,128)(2,1)}, u32[]{:S(2)}) copy-start(bf16[256,1024]{1,0:T(8,128)(2,1)} %get-tuple-element.29.refs_0_) | copy-start | bytes 1572868
  24.7 17.7 %collective-permute-start.9 = (bf16[256,1024]{1,0:T(8,128)(2,1)S(1)}, bf16[256,1024]{1,0:T(8,128)(2,1)S(1)}, u32[]{:S(2)}, u32[]{:S(2)}) collective-permute-start(bf16[256,1024]{1,0:T(8,128)(2,1)S(1)} %pad_maximum_fusion), channel_id=1, source_target_pairs={{0,16},{16,0},{1,17},{17,1},{2,18},{18,2},{3,19},{19,3},{4,20},{20... | collective-permute-start | bytes 1572872 | tf_op jit(solution)/shard_map/ppermute | solution.py:393
  26.3 16.1 %collective-permute-start.6 = (bf16[256,1024]{1,0:T(8,128)(2,1)S(1)}, bf16[256,1024]{1,0:T(8,128)(2,1)S(1)}, u32[]{:S(2)}, u32[]{:S(2)}) collective-permute-start(bf16[256,1024]{1,0:T(8,128)(2,1)S(1)} %copy-done.1), channel_id=1, source_target_pairs={{0,2},{1,3},{2,0},{3,1},{4,6},{5,7},{6,4},{7,5},{8,10},{9,11},{10,... | collective-permute-start | bytes 1572872 | tf_op jit(solution)/shard_map/ppermute | solution.py:383
  29.1 13.3 %collective-permute-start.8 = (bf16[128,1024]{1,0:T(8,128)(2,1)S(1)}, bf16[128,1024]{1,0:T(8,128)(2,1)S(1)}, u32[]{:S(2)}, u32[]{:S(2)}) collective-permute-start(bf16[128,1024]{1,0:T(8,128)(2,1)S(1)} %get-tuple-element.46), channel_id=1, source_target_pairs={{0,8},{1,9},{2,10},{3,11},{4,12},{5,13},{6,14},{7,15},{8,0},{9,1},... | collective-permute-start | bytes 786440 | tf_op jit(solution)/shard_map/ppermute | solution.py:383
  30.5 11.9 %collective-permute-start.7 = (bf16[128,1024]{1,0:T(8,128)(2,1)S(1)}, bf16[128,1024]{1,0:T(8,128)(2,1)S(1)}, u32[]{:S(2)}, u32[]{:S(2)}) collective-permute-start(bf16[128,1024]{1,0:T(8,128)(2,1)S(1)} %get-tuple-element.47), channel_id=1, source_target_pairs={{0,4},{1,5},{2,6},{3,7},{4,0},{5,1},{6,2},{7,3},{8,12},{9,13},{10,... | collective-permute-start | bytes 786440 | tf_op jit(solution)/shard_map/ppermute | solution.py:383
  42.4 8.8 %collective-permute-start.10 = (bf16[256,1024]{1,0:T(8,128)(2,1)S(1)}, bf16[256,1024]{1,0:T(8,128)(2,1)S(1)}, u32[]{:S(2)}, u32[]{:S(2)}) collective-permute-start(bf16[256,1024]{1,0:T(8,128)(2,1)S(1)} %collective-permute-done.6.refs_2_), channel_id=1, source_target_pairs={{0,1},{1,0},{2,3},{3,2},{4,5},{5,4},{6,7},{7,6},{8,9},{9,8},{10,11... | collective-permute-start | bytes 1572872 | tf_op jit(solution)/shard_map/ppermute | solution.py:365
  42.5 8.7 %collective-permute-start.11 = (bf16[128,1024]{1,0:T(8,128)(2,1)S(1)}, bf16[128,1024]{1,0:T(8,128)(2,1)S(1)}, u32[]{:S(2)}, u32[]{:S(2)}) collective-permute-start(bf16[128,1024]{1,0:T(8,128)(2,1)S(1)} %get-tuple-element.45), channel_id=1, source_target_pairs={{0,2},{1,3},{2,0},{3,1},{4,6},{5,7},{6,4},{7,5},{8,10},{9,11},{10,... | collective-permute-start | bytes 786440 | tf_op jit(solution)/shard_map/ppermute | solution.py:383
  42.9 15.8 %collective-permute-start.14 = (bf16[256,1024]{1,0:T(8,128)(2,1)S(1)}, bf16[256,1024]{1,0:T(8,128)(2,1)S(1)}, u32[]{:S(2)}, u32[]{:S(2)}) collective-permute-start(bf16[256,1024]{1,0:T(8,128)(2,1)S(1)} %collective-permute-done.6.refs_2_), channel_id=1, source_target_pairs={{0,4},{1,5},{2,14},{3,15},{4,8},{5,9},{6,2},{7,3},{8,12},{9,13},{1... | collective-permute-start | bytes 1572872 | tf_op jit(solution)/shard_map/ppermute | solution.py:389
  44.3 8.2 %collective-permute-start.12 = (bf16[128,1024]{1,0:T(8,128)(2,1)S(1)}, bf16[128,1024]{1,0:T(8,128)(2,1)S(1)}, u32[]{:S(2)}, u32[]{:S(2)}) collective-permute-start(bf16[128,1024]{1,0:T(8,128)(2,1)S(1)} %pad_maximum_fusion.1), channel_id=1, source_target_pairs={{0,16},{16,0},{1,17},{17,1},{2,18},{18,2},{3,19},{19,3},{4,20},{20... | collective-permute-start | bytes 786440 | tf_op jit(solution)/shard_map/ppermute | solution.py:393
  51.2 23.4 %copy-start = (bf16[1024,1024]{1,0:T(8,128)(2,1)S(1)}, bf16[1024,1024]{1,0:T(8,128)(2,1)}, u32[]{:S(2)}) copy-start(bf16[1024,1024]{1,0:T(8,128)(2,1)} %param.21) | copy-start | bytes 6291460
  51.2 23.4 %copy-start.2 = (bf16[256,1024]{1,0:T(8,128)(2,1)S(1)}, bf16[256,1024]{1,0:T(8,128)(2,1)}, u32[]{:S(2)}) copy-start(bf16[256,1024]{1,0:T(8,128)(2,1)} %get-tuple-element.26.tokens_ref) | copy-start | bytes 1572868
  51.2 7.4 %collective-permute-start.13 = (bf16[64,1024]{1,0:T(8,128)(2,1)S(1)}, bf16[64,1024]{1,0:T(8,128)(2,1)S(1)}, u32[]{:S(2)}, u32[]{:S(2)}) collective-permute-start(bf16[64,1024]{1,0:T(8,128)(2,1)S(1)} %constant_dynamic-slice_fusion), channel_id=1, source_target_pairs={{0,16},{16,0},{1,17},{17,1},{2,18},{18,2},{3,19},{19,3},{4,20},{20... | collective-permute-start | bytes 393224 | tf_op jit(solution)/shard_map/ppermute | solution.py:393
  51.8 6.8 %collective-permute-start.5 = (bf16[256,1024]{1,0:T(8,128)(2,1)S(1)}, bf16[256,1024]{1,0:T(8,128)(2,1)S(1)}, u32[]{:S(2)}, u32[]{:S(2)}) collective-permute-start(bf16[256,1024]{1,0:T(8,128)(2,1)S(1)} %copy-done.1), channel_id=1, source_target_pairs={{0,1},{1,0},{2,3},{3,2},{4,5},{5,4},{6,7},{7,6},{8,9},{9,8},{10,11... | collective-permute-start | bytes 1572872 | tf_op jit(solution)/shard_map/ppermute | solution.py:365
  58.7 1.9 %collective-permute-start.15 = (bf16[256,1024]{1,0:T(8,128)(2,1)S(1)}, bf16[256,1024]{1,0:T(8,128)(2,1)S(1)}, u32[]{:S(2)}, u32[]{:S(2)}) collective-permute-start(bf16[256,1024]{1,0:T(8,128)(2,1)S(1)} %collective-permute-done.14.refs_4_), channel_id=1, source_target_pairs={{0,1},{1,0},{2,3},{3,2},{4,5},{5,4},{6,7},{7,6},{8,9},{9,8},{10,11... | collective-permute-start | bytes 1572872 | tf_op jit(solution)/shard_map/ppermute | solution.py:365
  73.0 1.6 %collective-permute-start.16 = (bf16[4,256,128]{2,1,0:T(8,128)(2,1)S(1)}, bf16[4,256,128]{2,1,0:T(8,128)(2,1)S(1)}, u32[]{:S(2)}, u32[]{:S(2)}) collective-permute-start(bf16[4,256,128]{2,1,0:T(8,128)(2,1)S(1)} %get-tuple-element.44), channel_id=1, source_target_pairs={{0,1},{1,0},{2,3},{3,2},{4,5},{5,4},{6,7},{7,6},{8,9},{9,8},{10,11... | collective-permute-start | bytes 786440 | tf_op jit(solution)/shard_map/ppermute | solution.py:365

commit v9 on v8

--- a/solution.py
+++ b/solution.py
@@ -455,7 +455,7 @@
             parts = [lax.dynamic_slice_in_dim(b, plane * third, third, 0) for b in blocks]
             return across(jnp.concatenate(parts, axis=0))
 
-        normed, *early = together(normed, *early)
+        tokens_zero, *early = together(tokens_zero, *early)
         weights += [(b, (-step, "ring")) for b, step in zip(early, (1, -1, 2, -2))]
         swap = swapped(early)
         place = ring_place(lax.axis_index("space"))
@@ -463,11 +463,11 @@
         pair = crossed(jnp.where(place % 2 == 0, early[2], early[3]), 4)
         low = place % 4 < 2
         opposite = crossed(jnp.where(low, early[2], early[3]), 8)
-        near, pair, opposite, swap = together(near, pair, opposite, swap)
+        near, pair, opposite = together(near, pair, opposite)
         far, near_sib = onward(near), sibling(near)
         beside = crossed(jnp.where(low, early[3], early[2]), 2)
         first = swapped([pair, opposite])
-        near_sib, beside = together(near_sib, beside)
+        swap, near_sib, beside = together(swap, near_sib, beside)
         second = swapped([beside])
         first, second, far = together(first, second, far)
         weights += [(pair, ("pair", "ring")), (opposite, (4, "ring")), (beside, ("beside", "ring"))]

time: 76.3 us -> 73.4 us (0.962)
  waiting for transfers between devices: 29.8 us -> 22.3 us
  starting transfers between devices: 16.3 us -> 20.9 us
    ppermute x4, waiting for transfers between devices: 17.5 us -> 13.5 us  [crossed(): lax.ppermute(value, 'space', [(i, i ^ bits) for i in range(2 * len(RING))])]
    ppermute x4, starting transfers between devices: 5.22 us -> 8.47 us  [crossed(): lax.ppermute(value, 'space', [(i, i ^ bits) for i in range(2 * len(RING))])]
    ppermute x3, starting transfers between devices: 2.81 us -> 4.66 us  [across(): return lax.ppermute(value, 'groups', [(0, 1), (1, 0)])]
    ppermute x1, waiting for transfers between devices: 6.18 us -> 4.5 us  [onward(): return lax.ppermute(value, 'space', pairs)]
    ppermute x4, waiting for transfers between devices: 1.18 us -> 0.01 us  [around(): return lax.ppermute(value, 'space', pairs)]
  transfers between devices with their start and end apart: 17 -> 17, of which waited for: 8 -> 8; matrix products, arithmetic and copies ran while one was open for 0% -> 0% of each run, Pallas kernels for 19% -> 20%
where the time goes in v9:
time: 73.4 us; the launch traced here: 73.3 us
  Pallas kernels  28.6 us (39%)
  waiting for transfers between devices  22.3 us (30%)
  starting transfers between devices  20.9 us (28%)
  local copies, waits for them, and re-layouts  1.17 us (2%)
    pallas_call x1, Pallas kernels, aggregate(): pl.pallas_call(aggregate_kernel, out_shape=[jax.ShapeDtypeStruct((tokens,...  14.6 us
    ppermute x4, waiting for transfers between devices, crossed(): lax.ppermute(value, 'space', [(i, i ^ bits) for i in range(2 * len(RING))])  13.5 us
    pallas_call x1, Pallas kernels, attend(): pl.pallas_call(functools.partial(attend_kernel, spots=spots), out_shape=[...  12.5 us
    ppermute x4, starting transfers between devices, crossed(): lax.ppermute(value, 'space', [(i, i ^ bits) for i in range(2 * len(RING))])  8.47 us
    ppermute x4, starting transfers between devices, around(): return lax.ppermute(value, 'space', pairs)  6.09 us
    ppermute x3, starting transfers between devices, across(): return lax.ppermute(value, 'groups', [(0, 1), (1, 0)])  4.66 us
    ppermute x1, waiting for transfers between devices, onward(): return lax.ppermute(value, 'space', pairs)  4.5 us
    ppermute x5, waiting for transfers between devices, sibling(): return lax.ppermute(value, 'space', [(i, i ^ 1) for i in range(length)])  4.3 us
  transfers between devices with their start and end apart: 17, of which 8 were waited for; matrix products, arithmetic and copies ran while one was open for 0% of the time, Pallas kernels for 20%

profile of v9, /device:TPU:0, one launch (start us, length us, event | category | flops | bytes accessed | tf_op | source)
XLA Modules:
  0.0 73.3 jit_solution(15050382960528732524)
XLA Ops:
  0.0 1.1 %fusion = (bf16[64,1024]{1,0:T(8,128)(2,1)S(1)}, bf16[64,1024]{1,0:T(8,128)(2,1)S(1)}, bf16[64,1024]{1,0:T(8,128)(2,1)S(1)}) fusion(bf16[192,1024]{1,0:T(8,128)(2,1)} %bitcast.4), kind=kLoop, calls=%fused_computation.14 | loop fusion | bytes 786432 | tf_op jit(solution)/shard_map/slice | solution.py:402
  1.1 0.5 collective-permute-start
  1.6 1.0 %collective-permute-done = bf16[64,1024]{1,0:T(8,128)(2,1)S(1)} collective-permute-done((bf16[64,1024]{1,0:T(8,128)(2,1)S(1)}, bf16[64,1024]{1,0:T(8,128)(2,1)S(1)}, u32[]{:S(2)}, u32[]{:S(2)}) %collective-permute-start) | collective-permute-done | bytes 131104 | tf_op jit(solution)/shard_map/ppermute | solution.py:365
  2.6 0.1 maximum_select_fusion.refs_6_
  2.7 3.9 %collective-permute-start.4 = (bf16[128,1024]{1,0:T(8,128)(2,1)S(1)}, bf16[128,1024]{1,0:T(8,128)(2,1)S(1)}, u32[]{:S(2)}, u32[]{:S(2)}) collective-permute-start(bf16[128,1024]{1,0:T(8,128)(2,1)S(1)} %constant_dynamic-slice_fusion.7), channel_id=1, source_target_pairs={{0,6},{1,7},{4,2},{5,3},{8,0},{9,1},{12,4},{13,5},{14,8},{15,9},{1... | collective-permute-start | bytes 786440 | tf_op jit(solution)/shard_map/ppermute | solution.py:379
  6.6 0.1 collective-permute-start.3
  6.8 1.8 %collective-permute-start.2 = (bf16[128,1024]{1,0:T(8,128)(2,1)S(1)}, bf16[128,1024]{1,0:T(8,128)(2,1)S(1)}, u32[]{:S(2)}, u32[]{:S(2)}) collective-permute-start(bf16[128,1024]{1,0:T(8,128)(2,1)S(1)} %constant_dynamic-slice_fusion.7), channel_id=1, source_target_pairs={{0,2},{1,3},{4,0},{5,1},{8,4},{9,5},{12,8},{13,9},{14,12},{15,13},... | collective-permute-start | bytes 786440 | tf_op jit(solution)/shard_map/ppermute | solution.py:379
  8.5 0.2 collective-permute-start.1
  8.8 14.6 %aggregate.1 = (bf16[256,1024]{1,0:T(8,128)(2,1)}, bf16[256,1024]{1,0:T(8,128)(2,1)}) custom-call(s32[64]{0:T(128)} %order_ref.1, bf16[64,1024]{1,0:T(8,128)(2,1)} %var_embed_hbm.1, bf16[16,1024]{1,0:T(8,128)(2,1)} %keys_hbm.1, bf16[64,16,1024]{2,1,0:T(8,128)(2,1)} %embed_hbm, bf16[256,1024]{1,0:T(8,128)(2,1)} %patches_hbm.1, bf16[1024,1024]{1,0:T(8,128)(2,1)} %value_hbm.1, ...), custom_call_target="tpu_custom_call" | custom-call | flops 16000000000 | bytes 8388608 | tf_op jit(solution)/shard_map/aggregate/pallas_call | solution.py:227
  23.4 1.9 %collective-permute-start.6 = (bf16[256,1024]{1,0:T(8,128)(2,1)}, bf16[256,1024]{1,0:T(8,128)(2,1)S(1)}, u32[]{:S(2)}, u32[]{:S(2)}) collective-permute-start(bf16[256,1024]{1,0:T(8,128)(2,1)} %get-tuple-element.29.refs_0_), channel_id=1, source_target_pairs={{0,2},{1,3},{2,0},{3,1},{4,6},{5,7},{6,4},{7,5},{8,10},{9,11},{10,... | collective-permute-start | bytes 1572872 | tf_op jit(solution)/shard_map/ppermute | solution.py:383
  25.2 0.0 collective-permute-done.4.refs_10_
  25.2 0.0 collective-permute-done.3.refs_9_
  25.2 0.0 collective-permute-done.2.refs_8_
  25.2 0.0 collective-permute-done.1.refs_7_
  25.3 0.0 copy-start.1
  25.3 0.1 broadcast_select_fusion
  25.3 2.7 %collective-permute-start.8 = (bf16[128,1024]{1,0:T(8,128)(2,1)S(1)}, bf16[128,1024]{1,0:T(8,128)(2,1)S(1)}, u32[]{:S(2)}, u32[]{:S(2)}) collective-permute-start(bf16[128,1024]{1,0:T(8,128)(2,1)S(1)} %get-tuple-element.46), channel_id=1, source_target_pairs={{0,8},{1,9},{2,10},{3,11},{4,12},{5,13},{6,14},{7,15},{8,0},{9,1},... | collective-permute-start | bytes 786440 | tf_op jit(solution)/shard_map/ppermute | solution.py:383
  28.0 1.6 %collective-permute-start.7 = (bf16[128,1024]{1,0:T(8,128)(2,1)S(1)}, bf16[128,1024]{1,0:T(8,128)(2,1)S(1)}, u32[]{:S(2)}, u32[]{:S(2)}) collective-permute-start(bf16[128,1024]{1,0:T(8,128)(2,1)S(1)} %get-tuple-element.47), channel_id=1, source_target_pairs={{0,4},{1,5},{2,6},{3,7},{4,0},{5,1},{6,2},{7,3},{8,12},{9,13},{10,... | collective-permute-start | bytes 786440 | tf_op jit(solution)/shard_map/ppermute | solution.py:383
  29.7 1.6 %collective-permute-start.9 = (bf16[256,1024]{1,0:T(8,128)(2,1)S(1)}, bf16[256,1024]{1,0:T(8,128)(2,1)S(1)}, u32[]{:S(2)}, u32[]{:S(2)}) collective-permute-start(bf16[256,1024]{1,0:T(8,128)(2,1)S(1)} %pad_maximum_fusion), channel_id=1, source_target_pairs={{0,16},{16,0},{1,17},{17,1},{2,18},{18,2},{3,19},{19,3},{4,20},{20... | collective-permute-start | bytes 1572872 | tf_op jit(solution)/shard_map/ppermute | solution.py:393
  31.2 5.6 %collective-permute-done.6.refs_2_ = bf16[256,1024]{1,0:T(8,128)(2,1)S(1)} collective-permute-done((bf16[256,1024]{1,0:T(8,128)(2,1)}, bf16[256,1024]{1,0:T(8,128)(2,1)S(1)}, u32[]{:S(2)}, u32[]{:S(2)}) %collective-permute-start.6) | collective-permute-done | bytes 524320 | tf_op jit(solution)/shard_map/ppermute | solution.py:383
  36.8 2.8 %collective-permute-done.8.refs_12_ = bf16[128,1024]{1,0:T(8,128)(2,1)S(1)} collective-permute-done((bf16[128,1024]{1,0:T(8,128)(2,1)S(1)}, bf16[128,1024]{1,0:T(8,128)(2,1)S(1)}, u32[]{:S(2)}, u32[]{:S(2)}) %collective-permute-start.8) | collective-permute-done | bytes 262176 | tf_op jit(solution)/shard_map/ppermute | solution.py:383
  39.6 0.1 collective-permute-done.7.refs_11_
  39.7 0.0 collective-permute-start.10
  39.7 0.9 %collective-permute-start.14 = (bf16[256,1024]{1,0:T(8,128)(2,1)S(1)}, bf16[256,1024]{1,0:T(8,128)(2,1)S(1)}, u32[]{:S(2)}, u32[]{:S(2)}) collective-permute-start(bf16[256,1024]{1,0:T(8,128)(2,1)S(1)} %collective-permute-done.6.refs_2_), channel_id=1, source_target_pairs={{0,4},{1,5},{2,14},{3,15},{4,8},{5,9},{6,2},{7,3},{8,12},{9,13},{1... | collective-permute-start | bytes 1572872 | tf_op jit(solution)/shard_map/ppermute | solution.py:389
  40.6 2.4 %collective-permute-start.11 = (bf16[128,1024]{1,0:T(8,128)(2,1)S(1)}, bf16[128,1024]{1,0:T(8,128)(2,1)S(1)}, u32[]{:S(2)}, u32[]{:S(2)}) collective-permute-start(bf16[128,1024]{1,0:T(8,128)(2,1)S(1)} %get-tuple-element.45), channel_id=1, source_target_pairs={{0,2},{1,3},{2,0},{3,1},{4,6},{5,7},{6,4},{7,5},{8,10},{9,11},{10,... | collective-permute-start | bytes 786440 | tf_op jit(solution)/shard_map/ppermute | solution.py:383
  43.0 1.6 %collective-permute-start.12 = (bf16[128,1024]{1,0:T(8,128)(2,1)S(1)}, bf16[128,1024]{1,0:T(8,128)(2,1)S(1)}, u32[]{:S(2)}, u32[]{:S(2)}) collective-permute-start(bf16[128,1024]{1,0:T(8,128)(2,1)S(1)} %pad_maximum_fusion.1), channel_id=1, source_target_pairs={{0,16},{16,0},{1,17},{17,1},{2,18},{18,2},{3,19},{19,3},{4,20},{20... | collective-permute-start | bytes 786440 | tf_op jit(solution)/shard_map/ppermute | solution.py:393
  44.6 5.1 %collective-permute-done.11.refs_13_ = bf16[128,1024]{1,0:T(8,128)(2,1)S(1)} collective-permute-done((bf16[128,1024]{1,0:T(8,128)(2,1)S(1)}, bf16[128,1024]{1,0:T(8,128)(2,1)S(1)}, u32[]{:S(2)}, u32[]{:S(2)}) %collective-permute-start.11) | collective-permute-done | bytes 262176 | tf_op jit(solution)/shard_map/ppermute | solution.py:383
  49.7 0.0 collective-permute-done.9.refs_14_
  49.7 0.0 collective-permute-done.10.refs_3_
  49.7 0.0 copy-start
  49.7 0.0 copy-start.2
  49.7 1.6 %collective-permute-start.13 = (bf16[64,1024]{1,0:T(8,128)(2,1)S(1)}, bf16[64,1024]{1,0:T(8,128)(2,1)S(1)}, u32[]{:S(2)}, u32[]{:S(2)}) collective-permute-start(bf16[64,1024]{1,0:T(8,128)(2,1)S(1)} %constant_dynamic-slice_fusion), channel_id=1, source_target_pairs={{0,16},{16,0},{1,17},{17,1},{2,18},{18,2},{3,19},{19,3},{4,20},{20... | collective-permute-start | bytes 393224 | tf_op jit(solution)/shard_map/ppermute | solution.py:393
  51.3 0.0 copy-done.1
  51.3 0.0 collective-permute-start.5
  51.3 0.0 collective-permute-done.12.refs_15_
  51.3 4.5 %collective-permute-done.14.refs_4_ = bf16[256,1024]{1,0:T(8,128)(2,1)S(1)} collective-permute-done((bf16[256,1024]{1,0:T(8,128)(2,1)S(1)}, bf16[256,1024]{1,0:T(8,128)(2,1)S(1)}, u32[]{:S(2)}, u32[]{:S(2)}) %collective-permute-start.14) | collective-permute-done | bytes 524320 | tf_op jit(solution)/shard_map/ppermute | solution.py:389
  55.8 0.0 collective-permute-done.13.refs_16_
  55.8 0.0 collective-permute-start.15
  55.8 0.0 collective-permute-done.5.refs_1_
  55.8 1.9 %collective-permute-done.15.refs_5_ = bf16[256,1024]{1,0:T(8,128)(2,1)S(1)} collective-permute-done((bf16[256,1024]{1,0:T(8,128)(2,1)S(1)}, bf16[256,1024]{1,0:T(8,128)(2,1)S(1)}, u32[]{:S(2)}, u32[]{:S(2)}) %collective-permute-start.15) | collective-permute-done | bytes 524320 | tf_op jit(solution)/shard_map/ppermute | solution.py:365
  57.7 12.5 %attend.1 = (bf16[4,256,128]{2,1,0:T(8,128)(2,1)S(1)}, bf16[4,256,128]{2,1,0:T(8,128)(2,1)S(1)}) custom-call(bf16[256,1024]{1,0:T(8,128)(2,1)S(1)} %copy-done.1, bf16[256,1024]{1,0:T(8,128)(2,1)S(1)} %collective-permute-done.5.refs_1_, bf16[256,1024]{1,0:T(8,128)(2,1)S(1)} %collective-permute-done.6.refs_2_, ...), custom_call_target="tpu_custom_call" | custom-call | flops 10000000000 | bytes 8388608 | tf_op jit(solution)/shard_map/attend/pallas_call | solution.py:319
  70.2 0.2 collective-permute-start.16
  70.4 1.4 %collective-permute-done.16.other_ref = bf16[4,256,128]{2,1,0:T(8,128)(2,1)S(1)} collective-permute-done((bf16[4,256,128]{2,1,0:T(8,128)(2,1)S(1)}, bf16[4,256,128]{2,1,0:T(8,128)(2,1)S(1)}, u32[]{:S(2)}, u32[]{:S(2)}) %collective-permute-start.16) | collective-permute-done | bytes 262176 | tf_op jit(solution)/shard_map/ppermute | solution.py:365
  71.8 0.0 copy-done
  71.8 0.0 copy-done.2
  71.8 1.5 %finish.1 = bf16[256,1024]{1,0:T(8,128)(2,1)} custom-call(bf16[256,1024]{1,0:T(8,128)(2,1)S(1)} %copy-done.2, bf16[4,256,128]{2,1,0:T(8,128)(2,1)S(1)} %get-tuple-element.43.mine_ref, bf16[4,256,128]{2,1,0:T(8,128)(2,1)S(1)} %collective-permute-done.16.other_ref, bf16[8,2,64,1024]{3,2,1,0:T(8,128)(2,1)S(1)} %bitcast.3), custom_call_target="tpu_custom_call" | custom-call | flops 1000000000 | bytes 4194304 | tf_op jit(solution)/shard_map/finish/pallas_call | solution.py:352
  (7 shorter events, 0.2 us)
Async XLA Ops:
  1.1 1.5 %collective-permute-start = (bf16[64,1024]{1,0:T(8,128)(2,1)S(1)}, bf16[64,1024]{1,0:T(8,128)(2,1)S(1)}, u32[]{:S(2)}, u32[]{:S(2)}) collective-permute-start(bf16[64,1024]{1,0:T(8,128)(2,1)S(1)} %get-tuple-element.49), channel_id=1, source_target_pairs={{0,1},{1,0},{2,3},{3,2},{4,5},{5,4},{6,7},{7,6},{8,9},{9,8},{10,11... | collective-permute-start | bytes 393224 | tf_op jit(solution)/shard_map/ppermute | solution.py:365
  2.7 22.5 %collective-permute-start.4 = (bf16[128,1024]{1,0:T(8,128)(2,1)S(1)}, bf16[128,1024]{1,0:T(8,128)(2,1)S(1)}, u32[]{:S(2)}, u32[]{:S(2)}) collective-permute-start(bf16[128,1024]{1,0:T(8,128)(2,1)S(1)} %constant_dynamic-slice_fusion.7), channel_id=1, source_target_pairs={{0,6},{1,7},{4,2},{5,3},{8,0},{9,1},{12,4},{13,5},{14,8},{15,9},{1... | collective-permute-start | bytes 786440 | tf_op jit(solution)/shard_map/ppermute | solution.py:379
  6.6 18.6 %collective-permute-start.3 = (bf16[128,1024]{1,0:T(8,128)(2,1)S(1)}, bf16[128,1024]{1,0:T(8,128)(2,1)S(1)}, u32[]{:S(2)}, u32[]{:S(2)}) collective-permute-start(bf16[128,1024]{1,0:T(8,128)(2,1)S(1)} %constant_dynamic-slice_fusion.7), channel_id=1, source_target_pairs={{0,8},{1,9},{4,12},{5,13},{8,14},{9,15},{12,10},{13,11},{14,6},{15... | collective-permute-start | bytes 786440 | tf_op jit(solution)/shard_map/ppermute | solution.py:379
  6.8 18.5 %collective-permute-start.2 = (bf16[128,1024]{1,0:T(8,128)(2,1)S(1)}, bf16[128,1024]{1,0:T(8,128)(2,1)S(1)}, u32[]{:S(2)}, u32[]{:S(2)}) collective-permute-start(bf16[128,1024]{1,0:T(8,128)(2,1)S(1)} %constant_dynamic-slice_fusion.7), channel_id=1, source_target_pairs={{0,2},{1,3},{4,0},{5,1},{8,4},{9,5},{12,8},{13,9},{14,12},{15,13},... | collective-permute-start | bytes 786440 | tf_op jit(solution)/shard_map/ppermute | solution.py:379
  8.5 16.7 %collective-permute-start.1 = (bf16[128,1024]{1,0:T(8,128)(2,1)S(1)}, bf16[128,1024]{1,0:T(8,128)(2,1)S(1)}, u32[]{:S(2)}, u32[]{:S(2)}) collective-permute-start(bf16[128,1024]{1,0:T(8,128)(2,1)S(1)} %constant_dynamic-slice_fusion.7), channel_id=1, source_target_pairs={{0,4},{1,5},{4,8},{5,9},{8,12},{9,13},{12,14},{13,15},{14,10},{15,... | collective-permute-start | bytes 786440 | tf_op jit(solution)/shard_map/ppermute | solution.py:379
  23.4 13.4 %collective-permute-start.6 = (bf16[256,1024]{1,0:T(8,128)(2,1)}, bf16[256,1024]{1,0:T(8,128)(2,1)S(1)}, u32[]{:S(2)}, u32[]{:S(2)}) collective-permute-start(bf16[256,1024]{1,0:T(8,128)(2,1)} %get-tuple-element.29.refs_0_), channel_id=1, source_target_pairs={{0,2},{1,3},{2,0},{3,1},{4,6},{5,7},{6,4},{7,5},{8,10},{9,11},{10,... | collective-permute-start | bytes 1572872 | tf_op jit(solution)/shard_map/ppermute | solution.py:383
  25.3 26.0 %copy-start.1 = (bf16[256,1024]{1,0:T(8,128)(2,1)S(1)}, bf16[256,1024]{1,0:T(8,128)(2,1)}, u32[]{:S(2)}) copy-start(bf16[256,1024]{1,0:T(8,128)(2,1)} %get-tuple-element.29.refs_0_) | copy-start | bytes 1572868
  25.3 14.3 %collective-permute-start.8 = (bf16[128,1024]{1,0:T(8,128)(2,1)S(1)}, bf16[128,1024]{1,0:T(8,128)(2,1)S(1)}, u32[]{:S(2)}, u32[]{:S(2)}) collective-permute-start(bf16[128,1024]{1,0:T(8,128)(2,1)S(1)} %get-tuple-element.46), channel_id=1, source_target_pairs={{0,8},{1,9},{2,10},{3,11},{4,12},{5,13},{6,14},{7,15},{8,0},{9,1},... | collective-permute-start | bytes 786440 | tf_op jit(solution)/shard_map/ppermute | solution.py:383
  28.0 11.7 %collective-permute-start.7 = (bf16[128,1024]{1,0:T(8,128)(2,1)S(1)}, bf16[128,1024]{1,0:T(8,128)(2,1)S(1)}, u32[]{:S(2)}, u32[]{:S(2)}) collective-permute-start(bf16[128,1024]{1,0:T(8,128)(2,1)S(1)} %get-tuple-element.47), channel_id=1, source_target_pairs={{0,4},{1,5},{2,6},{3,7},{4,0},{5,1},{6,2},{7,3},{8,12},{9,13},{10,... | collective-permute-start | bytes 786440 | tf_op jit(solution)/shard_map/ppermute | solution.py:383
  29.7 20.0 %collective-permute-start.9 = (bf16[256,1024]{1,0:T(8,128)(2,1)S(1)}, bf16[256,1024]{1,0:T(8,128)(2,1)S(1)}, u32[]{:S(2)}, u32[]{:S(2)}) collective-permute-start(bf16[256,1024]{1,0:T(8,128)(2,1)S(1)} %pad_maximum_fusion), channel_id=1, source_target_pairs={{0,16},{16,0},{1,17},{17,1},{2,18},{18,2},{3,19},{19,3},{4,20},{20... | collective-permute-start | bytes 1572872 | tf_op jit(solution)/shard_map/ppermute | solution.py:393
  39.7 10.0 %collective-permute-start.10 = (bf16[256,1024]{1,0:T(8,128)(2,1)S(1)}, bf16[256,1024]{1,0:T(8,128)(2,1)S(1)}, u32[]{:S(2)}, u32[]{:S(2)}) collective-permute-start(bf16[256,1024]{1,0:T(8,128)(2,1)S(1)} %collective-permute-done.6.refs_2_), channel_id=1, source_target_pairs={{0,1},{1,0},{2,3},{3,2},{4,5},{5,4},{6,7},{7,6},{8,9},{9,8},{10,11... | collective-permute-start | bytes 1572872 | tf_op jit(solution)/shard_map/ppermute | solution.py:365
  39.7 16.1 %collective-permute-start.14 = (bf16[256,1024]{1,0:T(8,128)(2,1)S(1)}, bf16[256,1024]{1,0:T(8,128)(2,1)S(1)}, u32[]{:S(2)}, u32[]{:S(2)}) collective-permute-start(bf16[256,1024]{1,0:T(8,128)(2,1)S(1)} %collective-permute-done.6.refs_2_), channel_id=1, source_target_pairs={{0,4},{1,5},{2,14},{3,15},{4,8},{5,9},{6,2},{7,3},{8,12},{9,13},{1... | collective-permute-start | bytes 1572872 | tf_op jit(solution)/shard_map/ppermute | solution.py:389
  40.6 9.1 %collective-permute-start.11 = (bf16[128,1024]{1,0:T(8,128)(2,1)S(1)}, bf16[128,1024]{1,0:T(8,128)(2,1)S(1)}, u32[]{:S(2)}, u32[]{:S(2)}) collective-permute-start(bf16[128,1024]{1,0:T(8,128)(2,1)S(1)} %get-tuple-element.45), channel_id=1, source_target_pairs={{0,2},{1,3},{2,0},{3,1},{4,6},{5,7},{6,4},{7,5},{8,10},{9,11},{10,... | collective-permute-start | bytes 786440 | tf_op jit(solution)/shard_map/ppermute | solution.py:383
  43.0 8.3 %collective-permute-start.12 = (bf16[128,1024]{1,0:T(8,128)(2,1)S(1)}, bf16[128,1024]{1,0:T(8,128)(2,1)S(1)}, u32[]{:S(2)}, u32[]{:S(2)}) collective-permute-start(bf16[128,1024]{1,0:T(8,128)(2,1)S(1)} %pad_maximum_fusion.1), channel_id=1, source_target_pairs={{0,16},{16,0},{1,17},{17,1},{2,18},{18,2},{3,19},{19,3},{4,20},{20... | collective-permute-start | bytes 786440 | tf_op jit(solution)/shard_map/ppermute | solution.py:393
  49.7 22.1 %copy-start = (bf16[1024,1024]{1,0:T(8,128)(2,1)S(1)}, bf16[1024,1024]{1,0:T(8,128)(2,1)}, u32[]{:S(2)}) copy-start(bf16[1024,1024]{1,0:T(8,128)(2,1)} %param.21) | copy-start | bytes 6291460
  49.7 22.1 %copy-start.2 = (bf16[256,1024]{1,0:T(8,128)(2,1)S(1)}, bf16[256,1024]{1,0:T(8,128)(2,1)}, u32[]{:S(2)}) copy-start(bf16[256,1024]{1,0:T(8,128)(2,1)} %get-tuple-element.28.tokens_ref) | copy-start | bytes 1572868
  49.7 6.1 %collective-permute-start.13 = (bf16[64,1024]{1,0:T(8,128)(2,1)S(1)}, bf16[64,1024]{1,0:T(8,128)(2,1)S(1)}, u32[]{:S(2)}, u32[]{:S(2)}) collective-permute-start(bf16[64,1024]{1,0:T(8,128)(2,1)S(1)} %constant_dynamic-slice_fusion), channel_id=1, source_target_pairs={{0,16},{16,0},{1,17},{17,1},{2,18},{18,2},{3,19},{19,3},{4,20},{20... | collective-permute-start | bytes 393224 | tf_op jit(solution)/shard_map/ppermute | solution.py:393
  51.3 4.5 %collective-permute-start.5 = (bf16[256,1024]{1,0:T(8,128)(2,1)S(1)}, bf16[256,1024]{1,0:T(8,128)(2,1)S(1)}, u32[]{:S(2)}, u32[]{:S(2)}) collective-permute-start(bf16[256,1024]{1,0:T(8,128)(2,1)S(1)} %copy-done.1), channel_id=1, source_target_pairs={{0,1},{1,0},{2,3},{3,2},{4,5},{5,4},{6,7},{7,6},{8,9},{9,8},{10,11... | collective-permute-start | bytes 1572872 | tf_op jit(solution)/shard_map/ppermute | solution.py:365
  55.8 1.9 %collective-permute-start.15 = (bf16[256,1024]{1,0:T(8,128)(2,1)S(1)}, bf16[256,1024]{1,0:T(8,128)(2,1)S(1)}, u32[]{:S(2)}, u32[]{:S(2)}) collective-permute-start(bf16[256,1024]{1,0:T(8,128)(2,1)S(1)} %collective-permute-done.14.refs_4_), channel_id=1, source_target_pairs={{0,1},{1,0},{2,3},{3,2},{4,5},{5,4},{6,7},{7,6},{8,9},{9,8},{10,11... | collective-permute-start | bytes 1572872 | tf_op jit(solution)/shard_map/ppermute | solution.py:365
  70.2 1.6 %collective-permute-start.16 = (bf16[4,256,128]{2,1,0:T(8,128)(2,1)S(1)}, bf16[4,256,128]{2,1,0:T(8,128)(2,1)S(1)}, u32[]{:S(2)}, u32[]{:S(2)}) collective-permute-start(bf16[4,256,128]{2,1,0:T(8,128)(2,1)S(1)} %get-tuple-element.44), channel_id=1, source_target_pairs={{0,1},{1,0},{2,3},{3,2},{4,5},{5,4},{6,7},{7,6},{8,9},{9,8},{10,11... | collective-permute-start | bytes 786440 | tf_op jit(solution)/shard_map/ppermute | solution.py:365

commit v10 on v9

--- a/solution.py
+++ b/solution.py
@@ -239,34 +239,53 @@
     )(var_order, *arrays)
 
 
-def attend_kernel(*refs, spots):
-    count = len(spots)
-    weight_refs = refs[6 : 6 + count]
-    mine_ref, other_ref, query_s, key_s, value_s, weight_s, sems = refs[6 + count :]
+def assemble_kernel(*refs, spots):
+    weight_refs, out_ref, sems = refs[:-2], refs[-2], refs[-1]
     index, plane = lax.axis_index("space"), lax.axis_index("groups")
-    side = index % 2
     moves = []
     for ref, (step, share) in zip(weight_refs, spots):
         rows = ref.shape[0]
         if share == "ring":
             start = pl.multiple_of(plane * (rows // 2), 32)
-            moves.append((ref, weight_s.at[chip_at(index, step), pl.ds(start, rows), :]))
+            moves.append((ref, out_ref.at[chip_at(index, step), pl.ds(start, rows), :]))
         elif share == "swap":
             rows = rows // len(step)
             start = pl.multiple_of((1 - plane) * (2 * rows), 32)
             for i, one in enumerate(step):
-                place = weight_s.at[chip_at(index, one), pl.ds(start, rows), :]
+                place = out_ref.at[chip_at(index, one), pl.ds(start, rows), :]
                 moves.append((ref.at[pl.ds(i * rows, rows), :], place))
         else:
-            moves.append((ref, weight_s.at[chip_at(index, step)]))
+            moves.append((ref, out_ref.at[chip_at(index, step)]))
     for wait in fetch(moves, sems):
         wait()
-    flip = index // 2 % 2 if spots[0][0] is not None else 0
+
+
+def assemble(weights):
+    spots = tuple(spot for _, spot in weights)
+    weights = [piece for piece, _ in weights]
+    blocks = 1 if len(weights) == 1 else len(RING)
+    return pl.pallas_call(
+        functools.partial(assemble_kernel, spots=spots),
+        out_shape=jax.ShapeDtypeStruct((blocks,) + weights[0].shape, BF16),
+        in_specs=[HBM] * len(weights),
+        out_specs=VMEM,
+        scratch_shapes=[pltpu.SemaphoreType.DMA((32,))],
+        compiler_params=pltpu.CompilerParams(vmem_limit_bytes=PART_VMEM),
+        cost_estimate=cost(1, 6),
+        name="assemble",
+    )(*weights)
+
+
+def attend_kernel(*refs, flipped):
+    weight_ref, mine_ref, other_ref, query_s, key_s, value_s = refs[6:]
+    index = lax.axis_index("space")
+    side = index % 2
+    flip = index // 2 % 2 if flipped else 0
     near, far = 4 - 4 * flip, 4 * flip
     tokens, width = refs[0].shape
     pairs = mine_ref.shape[0]
     cols = pairs * LANES
-    weight = weight_s[...].reshape(3 * cols, width)
+    weight = weight_ref[...].reshape(3 * cols, width)
     head_size = LANES // 2
     scale = 1.0 / math.sqrt(head_size)
     pieces = (2 + side, 3 - side, near + side, near + 1 - side, far + side, far + 1 - side)
@@ -308,30 +327,25 @@
     lax.fori_loop(0, pairs, attend, 0, unroll=True)
 
 
-def attend(pieces, weights):
+def attend(pieces, weight):
     tokens, width = pieces[0].shape
-    spots = tuple(spot for _, spot in weights)
-    weights = [piece for piece, _ in weights]
-    rows = weights[0].shape[0]
-    blocks = 1 if len(weights) == 1 else len(RING)
+    blocks, rows, _ = weight.shape
     cols = rows * blocks // 3
     pairs = cols // LANES
     return pl.pallas_call(
-        functools.partial(attend_kernel, spots=spots),
+        functools.partial(attend_kernel, flipped=blocks > 1),
         out_shape=[jax.ShapeDtypeStruct((pairs, tokens, LANES), BF16)] * 2,
-        in_specs=[VMEM] * 6 + [HBM] * len(weights),
+        in_specs=[VMEM] * 7,
         out_specs=[VMEM, VMEM],
         scratch_shapes=[
             pltpu.VMEM((2, pairs, tokens, LANES), BF16),
             pltpu.VMEM((pairs, 6 * tokens, LANES), BF16),
             pltpu.VMEM((pairs, 6 * tokens, 2 * LANES), BF16),
-            pltpu.VMEM((blocks, rows, width), BF16),
-            pltpu.SemaphoreType.DMA((32,)),
         ],
         compiler_params=pltpu.CompilerParams(vmem_limit_bytes=PART_VMEM),
         cost_estimate=cost(10, 8, 5 << 20),
         name="attend",
-    )(*pieces, *weights)
+    )(*pieces, weight)
 
 
 def finish_kernel(tokens_ref, mine_ref, other_ref, weight_ref, out_ref):
@@ -460,16 +474,16 @@
         swap = swapped(early)
         place = ring_place(lax.axis_index("space"))
         near = crossed(normed, 2)
-        pair = crossed(jnp.where(place % 2 == 0, early[2], early[3]), 4)
         low = place % 4 < 2
         opposite = crossed(jnp.where(low, early[2], early[3]), 8)
-        near, pair, opposite = together(near, pair, opposite)
+        pair = crossed(jnp.where(place % 2 == 0, early[2], early[3]), 4)
+        near, opposite, pair = together(near, opposite, pair)
         far, near_sib = onward(near), sibling(near)
         beside = crossed(jnp.where(low, early[3], early[2]), 2)
         first = swapped([pair, opposite])
         swap, near_sib, beside = together(swap, near_sib, beside)
         second = swapped([beside])
-        first, second, far = together(first, second, far)
+        _, _, far = together(first, second, far)
         weights += [(pair, ("pair", "ring")), (opposite, (4, "ring")), (beside, ("beside", "ring"))]
         weights += [(swap, ((-1, 1, -2, 2), "swap"))]
         weights += [(first, (("pair", 4), "swap")), (second, (("beside",), "swap"))]
@@ -477,7 +491,7 @@
         near, far = from_chip(normed, 1), from_chip(normed, -1)
         near_sib = sibling(near)
     pieces = (normed, sibling(normed), near, near_sib, far, sibling(far))
-    mine, other = attend(pieces, weights)
+    mine, other = attend(pieces, assemble(weights))
     return finish(tokens_zero, mine, sibling(other), attn_out)
 
 

time: 73.4 us -> 71.1 us (0.969)
  waiting for transfers between devices: 22.3 us -> 18.7 us
  starting transfers between devices: 20.9 us -> 22.2 us
    ppermute x5, waiting for transfers between devices: 4.3 us -> 2.16 us  [sibling(): return lax.ppermute(value, 'space', [(i, i ^ 1) for i in range(length)])]
    ppermute x4, waiting for transfers between devices: 13.5 us -> 12.5 us  [crossed(): lax.ppermute(value, 'space', [(i, i ^ bits) for i in range(2 * len(RING))])]
    ppermute x1, starting transfers between devices: 0.95 us -> 1.73 us  [onward(): return lax.ppermute(value, 'space', pairs)]
    pallas_call x1 -> x2, Pallas kernels: 12.5 us -> 12.4 us  [the longest x1 10.4 us: attend(): pl.pallas_call(functools.partial(attend_kernel, flipped=blocks > 1), out_...]
  transfers between devices with their start and end apart: 17 -> 17, of which waited for: 8 -> 5; matrix products, arithmetic and copies ran while one was open for 0% -> 0% of each run, Pallas kernels for 20% -> 23%
where the time goes in v10:
time: 71.1 us; the launch traced here: 71 us
  Pallas kernels  28.5 us (40%)
  starting transfers between devices  22.2 us (31%)
  waiting for transfers between devices  18.7 us (26%)
  local copies, waits for them, and re-layouts  1.17 us (2%)
    pallas_call x1, Pallas kernels, aggregate(): pl.pallas_call(aggregate_kernel, out_shape=[jax.ShapeDtypeStruct((tokens,...  14.6 us
    ppermute x4, waiting for transfers between devices, crossed(): lax.ppermute(value, 'space', [(i, i ^ bits) for i in range(2 * len(RING))])  12.5 us
    pallas_call x1, Pallas kernels, attend(): pl.pallas_call(functools.partial(attend_kernel, flipped=blocks > 1), out_...  10.4 us
    ppermute x4, starting transfers between devices, crossed(): lax.ppermute(value, 'space', [(i, i ^ bits) for i in range(2 * len(RING))])  8.65 us
    ppermute x4, starting transfers between devices, around(): return lax.ppermute(value, 'space', pairs)  6.03 us
    ppermute x3, starting transfers between devices, across(): return lax.ppermute(value, 'groups', [(0, 1), (1, 0)])  4.66 us
    ppermute x1, waiting for transfers between devices, onward(): return lax.ppermute(value, 'space', pairs)  4.04 us
    ppermute x5, waiting for transfers between devices, sibling(): return lax.ppermute(value, 'space', [(i, i ^ 1) for i in range(length)])  2.16 us
  transfers between devices with their start and end apart: 17, of which 5 were waited for; matrix products, arithmetic and copies ran while one was open for 0% of the time, Pallas kernels for 23%

profile of v10, /device:TPU:0, one launch (start us, length us, event | category | flops | bytes accessed | tf_op | source)
XLA Modules:
  0.0 71.0 jit_solution(6728547147214481321)
XLA Ops:
  0.0 1.1 %fusion = (bf16[64,1024]{1,0:T(8,128)(2,1)S(1)}, bf16[64,1024]{1,0:T(8,128)(2,1)S(1)}, bf16[64,1024]{1,0:T(8,128)(2,1)S(1)}) fusion(bf16[192,1024]{1,0:T(8,128)(2,1)} %bitcast.4), kind=kLoop, calls=%fused_computation.14 | loop fusion | bytes 786432 | tf_op jit(solution)/shard_map/slice | solution.py:416
  1.1 0.5 collective-permute-start
  1.6 1.0 %collective-permute-done = bf16[64,1024]{1,0:T(8,128)(2,1)S(1)} collective-permute-done((bf16[64,1024]{1,0:T(8,128)(2,1)S(1)}, bf16[64,1024]{1,0:T(8,128)(2,1)S(1)}, u32[]{:S(2)}, u32[]{:S(2)}) %collective-permute-start) | collective-permute-done | bytes 131104 | tf_op jit(solution)/shard_map/ppermute | solution.py:379
  2.6 0.1 maximum_select_fusion.refs_0_
  2.7 3.0 %collective-permute-start.1 = (bf16[128,1024]{1,0:T(8,128)(2,1)S(1)}, bf16[128,1024]{1,0:T(8,128)(2,1)S(1)}, u32[]{:S(2)}, u32[]{:S(2)}) collective-permute-start(bf16[128,1024]{1,0:T(8,128)(2,1)S(1)} %constant_dynamic-slice_fusion.7), channel_id=1, source_target_pairs={{0,4},{1,5},{4,8},{5,9},{8,12},{9,13},{12,14},{13,15},{14,10},{15,... | collective-permute-start | bytes 786440 | tf_op jit(solution)/shard_map/ppermute | solution.py:393
  5.7 0.0 collective-permute-start.2
  5.7 3.0 %collective-permute-start.3 = (bf16[128,1024]{1,0:T(8,128)(2,1)S(1)}, bf16[128,1024]{1,0:T(8,128)(2,1)S(1)}, u32[]{:S(2)}, u32[]{:S(2)}) collective-permute-start(bf16[128,1024]{1,0:T(8,128)(2,1)S(1)} %constant_dynamic-slice_fusion.7), channel_id=1, source_target_pairs={{0,8},{1,9},{4,12},{5,13},{8,14},{9,15},{12,10},{13,11},{14,6},{15... | collective-permute-start | bytes 786440 | tf_op jit(solution)/shard_map/ppermute | solution.py:393
  8.7 0.0 collective-permute-start.4
  8.7 14.6 %aggregate.1 = (bf16[256,1024]{1,0:T(8,128)(2,1)}, bf16[256,1024]{1,0:T(8,128)(2,1)}) custom-call(s32[64]{0:T(128)} %order_ref.1, bf16[64,1024]{1,0:T(8,128)(2,1)} %var_embed_hbm.1, bf16[16,1024]{1,0:T(8,128)(2,1)} %keys_hbm.1, bf16[64,16,1024]{2,1,0:T(8,128)(2,1)} %embed_hbm, bf16[256,1024]{1,0:T(8,128)(2,1)} %patches_hbm.1, bf16[1024,1024]{1,0:T(8,128)(2,1)} %value_hbm.1, ...), custom_call_target="tpu_custom_call" | custom-call | flops 16000000000 | bytes 8388608 | tf_op jit(solution)/shard_map/aggregate/pallas_call | solution.py:227
  23.3 1.9 %collective-permute-start.6 = (bf16[256,1024]{1,0:T(8,128)(2,1)}, bf16[256,1024]{1,0:T(8,128)(2,1)S(1)}, u32[]{:S(2)}, u32[]{:S(2)}) collective-permute-start(bf16[256,1024]{1,0:T(8,128)(2,1)} %get-tuple-element.27.refs_0_), channel_id=1, source_target_pairs={{0,2},{1,3},{2,0},{3,1},{4,6},{5,7},{6,4},{7,5},{8,10},{9,11},{10,... | collective-permute-start | bytes 1572872 | tf_op jit(solution)/shard_map/ppermute | solution.py:397
  25.2 0.0 collective-permute-done.1.refs_1_
  25.2 0.0 collective-permute-done.2.refs_2_
  25.2 0.0 collective-permute-done.3.refs_3_
  25.2 0.0 collective-permute-done.4.refs_4_
  25.3 0.0 copy-start.1
  25.3 0.1 broadcast_select_fusion.1
  25.3 2.7 %collective-permute-start.7 = (bf16[128,1024]{1,0:T(8,128)(2,1)S(1)}, bf16[128,1024]{1,0:T(8,128)(2,1)S(1)}, u32[]{:S(2)}, u32[]{:S(2)}) collective-permute-start(bf16[128,1024]{1,0:T(8,128)(2,1)S(1)} %get-tuple-element.43), channel_id=1, source_target_pairs={{0,8},{1,9},{2,10},{3,11},{4,12},{5,13},{6,14},{7,15},{8,0},{9,1},... | collective-permute-start | bytes 786440 | tf_op jit(solution)/shard_map/ppermute | solution.py:397
  28.0 1.6 %collective-permute-start.8 = (bf16[128,1024]{1,0:T(8,128)(2,1)S(1)}, bf16[128,1024]{1,0:T(8,128)(2,1)S(1)}, u32[]{:S(2)}, u32[]{:S(2)}) collective-permute-start(bf16[128,1024]{1,0:T(8,128)(2,1)S(1)} %get-tuple-element.42), channel_id=1, source_target_pairs={{0,4},{1,5},{2,6},{3,7},{4,0},{5,1},{6,2},{7,3},{8,12},{9,13},{10,... | collective-permute-start | bytes 786440 | tf_op jit(solution)/shard_map/ppermute | solution.py:397
  29.7 1.6 %collective-permute-start.9 = (bf16[256,1024]{1,0:T(8,128)(2,1)S(1)}, bf16[256,1024]{1,0:T(8,128)(2,1)S(1)}, u32[]{:S(2)}, u32[]{:S(2)}) collective-permute-start(bf16[256,1024]{1,0:T(8,128)(2,1)S(1)} %pad_maximum_fusion), channel_id=1, source_target_pairs={{0,16},{16,0},{1,17},{17,1},{2,18},{18,2},{3,19},{19,3},{4,20},{20... | collective-permute-start | bytes 1572872 | tf_op jit(solution)/shard_map/ppermute | solution.py:407
  31.2 7.7 %collective-permute-done.7.refs_6_ = bf16[128,1024]{1,0:T(8,128)(2,1)S(1)} collective-permute-done((bf16[128,1024]{1,0:T(8,128)(2,1)S(1)}, bf16[128,1024]{1,0:T(8,128)(2,1)S(1)}, u32[]{:S(2)}, u32[]{:S(2)}) %collective-permute-start.7) | collective-permute-done | bytes 262176 | tf_op jit(solution)/shard_map/ppermute | solution.py:397
  38.9 0.0 collective-permute-done.8.refs_5_
  38.9 0.0 collective-permute-done.6.refs_2_
  38.9 0.0 collective-permute-start.10
  38.9 1.7 %collective-permute-start.14 = (bf16[256,1024]{1,0:T(8,128)(2,1)S(1)}, bf16[256,1024]{1,0:T(8,128)(2,1)S(1)}, u32[]{:S(2)}, u32[]{:S(2)}) collective-permute-start(bf16[256,1024]{1,0:T(8,128)(2,1)S(1)} %collective-permute-done.6.refs_2_), channel_id=1, source_target_pairs={{0,4},{1,5},{2,14},{3,15},{4,8},{5,9},{6,2},{7,3},{8,12},{9,13},{1... | collective-permute-start | bytes 1572872 | tf_op jit(solution)/shard_map/ppermute | solution.py:403
  40.6 2.5 %collective-permute-start.11 = (bf16[128,1024]{1,0:T(8,128)(2,1)S(1)}, bf16[128,1024]{1,0:T(8,128)(2,1)S(1)}, u32[]{:S(2)}, u32[]{:S(2)}) collective-permute-start(bf16[128,1024]{1,0:T(8,128)(2,1)S(1)} %get-tuple-element.41), channel_id=1, source_target_pairs={{0,2},{1,3},{2,0},{3,1},{4,6},{5,7},{6,4},{7,5},{8,10},{9,11},{10,... | collective-permute-start | bytes 786440 | tf_op jit(solution)/shard_map/ppermute | solution.py:397
  43.2 1.6 %collective-permute-start.12 = (bf16[128,1024]{1,0:T(8,128)(2,1)S(1)}, bf16[128,1024]{1,0:T(8,128)(2,1)S(1)}, u32[]{:S(2)}, u32[]{:S(2)}) collective-permute-start(bf16[128,1024]{1,0:T(8,128)(2,1)S(1)} %pad_maximum_fusion.1), channel_id=1, source_target_pairs={{0,16},{16,0},{1,17},{17,1},{2,18},{18,2},{3,19},{19,3},{4,20},{20... | collective-permute-start | bytes 786440 | tf_op jit(solution)/shard_map/ppermute | solution.py:407
  44.7 4.9 %collective-permute-done.11.refs_7_ = bf16[128,1024]{1,0:T(8,128)(2,1)S(1)} collective-permute-done((bf16[128,1024]{1,0:T(8,128)(2,1)S(1)}, bf16[128,1024]{1,0:T(8,128)(2,1)S(1)}, u32[]{:S(2)}, u32[]{:S(2)}) %collective-permute-start.11) | collective-permute-done | bytes 262176 | tf_op jit(solution)/shard_map/ppermute | solution.py:397
  49.6 0.0 collective-permute-done.9.refs_8_
  49.6 0.0 collective-permute-done.10.refs_3_
  49.6 1.6 %collective-permute-start.13 = (bf16[64,1024]{1,0:T(8,128)(2,1)S(1)}, bf16[64,1024]{1,0:T(8,128)(2,1)S(1)}, u32[]{:S(2)}, u32[]{:S(2)}) collective-permute-start(bf16[64,1024]{1,0:T(8,128)(2,1)S(1)} %constant_dynamic-slice_fusion), channel_id=1, source_target_pairs={{0,16},{16,0},{1,17},{17,1},{2,18},{18,2},{3,19},{19,3},{4,20},{20... | collective-permute-start | bytes 393224 | tf_op jit(solution)/shard_map/ppermute | solution.py:407
  51.2 0.0 copy-done.1
  51.2 0.0 collective-permute-start.5
  51.2 0.0 collective-permute-done.12.refs_9_
  51.2 4.0 %collective-permute-done.14.refs_4_ = bf16[256,1024]{1,0:T(8,128)(2,1)S(1)} collective-permute-done((bf16[256,1024]{1,0:T(8,128)(2,1)S(1)}, bf16[256,1024]{1,0:T(8,128)(2,1)S(1)}, u32[]{:S(2)}, u32[]{:S(2)}) %collective-permute-start.14) | collective-permute-done | bytes 524320 | tf_op jit(solution)/shard_map/ppermute | solution.py:403
  55.2 0.0 collective-permute-done.13.refs_10_
  55.2 0.0 collective-permute-start.15
  55.2 2.1 %assemble.1.refs_6_ = bf16[8,192,1024]{2,1,0:T(8,128)(2,1)S(1)} custom-call(bf16[192,1024]{1,0:T(8,128)(2,1)S(1)} %maximum_select_fusion.refs_0_, bf16[128,1024]{1,0:T(8,128)(2,1)S(1)} %collective-permute-done.1.refs_1_, bf16[128,1024]{1,0:T(8,128)(2,1)S(1)} %collective-permute-done.2.refs_2_, bf16[128,1024]{1,0:T(8,128)(2,1)S(1)} %collective-permute-done.3.refs_3_, ...), custom_call_target="tpu_custom_call" | custom-call | flops 1000000000 | bytes 6291456 | tf_op jit(solution)/shard_map/assemble/pallas_call | solution.py:267
  57.3 0.0 copy-start
  57.3 0.0 copy-start.2
  57.3 0.0 collective-permute-done.5.refs_1_
  57.3 0.0 collective-permute-done.15.refs_5_
  57.3 10.4 %attend.1 = (bf16[4,256,128]{2,1,0:T(8,128)(2,1)S(1)}, bf16[4,256,128]{2,1,0:T(8,128)(2,1)S(1)}) custom-call(bf16[256,1024]{1,0:T(8,128)(2,1)S(1)} %copy-done.1, bf16[256,1024]{1,0:T(8,128)(2,1)S(1)} %collective-permute-done.5.refs_1_, bf16[256,1024]{1,0:T(8,128)(2,1)S(1)} %collective-permute-done.6.refs_2_, ...), custom_call_target="tpu_custom_call" | custom-call | flops 10000000000 | bytes 8388608 | tf_op jit(solution)/shard_map/attend/pallas_call | solution.py:335
  67.7 0.6 collective-permute-start.16
  68.3 1.2 %collective-permute-done.16.other_ref = bf16[4,256,128]{2,1,0:T(8,128)(2,1)S(1)} collective-permute-done((bf16[4,256,128]{2,1,0:T(8,128)(2,1)S(1)}, bf16[4,256,128]{2,1,0:T(8,128)(2,1)S(1)}, u32[]{:S(2)}, u32[]{:S(2)}) %collective-permute-start.16) | collective-permute-done | bytes 262176 | tf_op jit(solution)/shard_map/ppermute | solution.py:379
  69.4 0.0 copy-done
  69.4 0.0 copy-done.2
  69.4 1.5 %finish.1 = bf16[256,1024]{1,0:T(8,128)(2,1)} custom-call(bf16[256,1024]{1,0:T(8,128)(2,1)S(1)} %copy-done.2, bf16[4,256,128]{2,1,0:T(8,128)(2,1)S(1)} %get-tuple-element.39.mine_ref, bf16[4,256,128]{2,1,0:T(8,128)(2,1)S(1)} %collective-permute-done.16.other_ref, bf16[8,2,64,1024]{3,2,1,0:T(8,128)(2,1)S(1)} %bitcast.3), custom_call_target="tpu_custom_call" | custom-call | flops 1000000000 | bytes 4194304 | tf_op jit(solution)/shard_map/finish/pallas_call | solution.py:366
  (7 shorter events, 0.2 us)
Async XLA Ops:
  1.1 1.5 %collective-permute-start = (bf16[64,1024]{1,0:T(8,128)(2,1)S(1)}, bf16[64,1024]{1,0:T(8,128)(2,1)S(1)}, u32[]{:S(2)}, u32[]{:S(2)}) collective-permute-start(bf16[64,1024]{1,0:T(8,128)(2,1)S(1)} %get-tuple-element.45), channel_id=1, source_target_pairs={{0,1},{1,0},{2,3},{3,2},{4,5},{5,4},{6,7},{7,6},{8,9},{9,8},{10,11... | collective-permute-start | bytes 393224 | tf_op jit(solution)/shard_map/ppermute | solution.py:379
  2.7 22.5 %collective-permute-start.1 = (bf16[128,1024]{1,0:T(8,128)(2,1)S(1)}, bf16[128,1024]{1,0:T(8,128)(2,1)S(1)}, u32[]{:S(2)}, u32[]{:S(2)}) collective-permute-start(bf16[128,1024]{1,0:T(8,128)(2,1)S(1)} %constant_dynamic-slice_fusion.7), channel_id=1, source_target_pairs={{0,4},{1,5},{4,8},{5,9},{8,12},{9,13},{12,14},{13,15},{14,10},{15,... | collective-permute-start | bytes 786440 | tf_op jit(solution)/shard_map/ppermute | solution.py:393
  5.7 19.6 %collective-permute-start.2 = (bf16[128,1024]{1,0:T(8,128)(2,1)S(1)}, bf16[128,1024]{1,0:T(8,128)(2,1)S(1)}, u32[]{:S(2)}, u32[]{:S(2)}) collective-permute-start(bf16[128,1024]{1,0:T(8,128)(2,1)S(1)} %constant_dynamic-slice_fusion.7), channel_id=1, source_target_pairs={{0,2},{1,3},{4,0},{5,1},{8,4},{9,5},{12,8},{13,9},{14,12},{15,13},... | collective-permute-start | bytes 786440 | tf_op jit(solution)/shard_map/ppermute | solution.py:393
  5.7 19.6 %collective-permute-start.3 = (bf16[128,1024]{1,0:T(8,128)(2,1)S(1)}, bf16[128,1024]{1,0:T(8,128)(2,1)S(1)}, u32[]{:S(2)}, u32[]{:S(2)}) collective-permute-start(bf16[128,1024]{1,0:T(8,128)(2,1)S(1)} %constant_dynamic-slice_fusion.7), channel_id=1, source_target_pairs={{0,8},{1,9},{4,12},{5,13},{8,14},{9,15},{12,10},{13,11},{14,6},{15... | collective-permute-start | bytes 786440 | tf_op jit(solution)/shard_map/ppermute | solution.py:393
  8.7 16.5 %collective-permute-start.4 = (bf16[128,1024]{1,0:T(8,128)(2,1)S(1)}, bf16[128,1024]{1,0:T(8,128)(2,1)S(1)}, u32[]{:S(2)}, u32[]{:S(2)}) collective-permute-start(bf16[128,1024]{1,0:T(8,128)(2,1)S(1)} %constant_dynamic-slice_fusion.7), channel_id=1, source_target_pairs={{0,6},{1,7},{4,2},{5,3},{8,0},{9,1},{12,4},{13,5},{14,8},{15,9},{1... | collective-permute-start | bytes 786440 | tf_op jit(solution)/shard_map/ppermute | solution.py:393
  23.3 15.6 %collective-permute-start.6 = (bf16[256,1024]{1,0:T(8,128)(2,1)}, bf16[256,1024]{1,0:T(8,128)(2,1)S(1)}, u32[]{:S(2)}, u32[]{:S(2)}) collective-permute-start(bf16[256,1024]{1,0:T(8,128)(2,1)} %get-tuple-element.27.refs_0_), channel_id=1, source_target_pairs={{0,2},{1,3},{2,0},{3,1},{4,6},{5,7},{6,4},{7,5},{8,10},{9,11},{10,... | collective-permute-start | bytes 1572872 | tf_op jit(solution)/shard_map/ppermute | solution.py:397
  25.3 25.9 %copy-start.1 = (bf16[256,1024]{1,0:T(8,128)(2,1)S(1)}, bf16[256,1024]{1,0:T(8,128)(2,1)}, u32[]{:S(2)}) copy-start(bf16[256,1024]{1,0:T(8,128)(2,1)} %get-tuple-element.27.refs_0_) | copy-start | bytes 1572868
  25.3 13.5 %collective-permute-start.7 = (bf16[128,1024]{1,0:T(8,128)(2,1)S(1)}, bf16[128,1024]{1,0:T(8,128)(2,1)S(1)}, u32[]{:S(2)}, u32[]{:S(2)}) collective-permute-start(bf16[128,1024]{1,0:T(8,128)(2,1)S(1)} %get-tuple-element.43), channel_id=1, source_target_pairs={{0,8},{1,9},{2,10},{3,11},{4,12},{5,13},{6,14},{7,15},{8,0},{9,1},... | collective-permute-start | bytes 786440 | tf_op jit(solution)/shard_map/ppermute | solution.py:397
  28.0 10.9 %collective-permute-start.8 = (bf16[128,1024]{1,0:T(8,128)(2,1)S(1)}, bf16[128,1024]{1,0:T(8,128)(2,1)S(1)}, u32[]{:S(2)}, u32[]{:S(2)}) collective-permute-start(bf16[128,1024]{1,0:T(8,128)(2,1)S(1)} %get-tuple-element.42), channel_id=1, source_target_pairs={{0,4},{1,5},{2,6},{3,7},{4,0},{5,1},{6,2},{7,3},{8,12},{9,13},{10,... | collective-permute-start | bytes 786440 | tf_op jit(solution)/shard_map/ppermute | solution.py:397
  29.7 19.9 %collective-permute-start.9 = (bf16[256,1024]{1,0:T(8,128)(2,1)S(1)}, bf16[256,1024]{1,0:T(8,128)(2,1)S(1)}, u32[]{:S(2)}, u32[]{:S(2)}) collective-permute-start(bf16[256,1024]{1,0:T(8,128)(2,1)S(1)} %pad_maximum_fusion), channel_id=1, source_target_pairs={{0,16},{16,0},{1,17},{17,1},{2,18},{18,2},{3,19},{19,3},{4,20},{20... | collective-permute-start | bytes 1572872 | tf_op jit(solution)/shard_map/ppermute | solution.py:407
  38.9 10.7 %collective-permute-start.10 = (bf16[256,1024]{1,0:T(8,128)(2,1)S(1)}, bf16[256,1024]{1,0:T(8,128)(2,1)S(1)}, u32[]{:S(2)}, u32[]{:S(2)}) collective-permute-start(bf16[256,1024]{1,0:T(8,128)(2,1)S(1)} %collective-permute-done.6.refs_2_), channel_id=1, source_target_pairs={{0,1},{1,0},{2,3},{3,2},{4,5},{5,4},{6,7},{7,6},{8,9},{9,8},{10,11... | collective-permute-start | bytes 1572872 | tf_op jit(solution)/shard_map/ppermute | solution.py:379
  38.9 16.3 %collective-permute-start.14 = (bf16[256,1024]{1,0:T(8,128)(2,1)S(1)}, bf16[256,1024]{1,0:T(8,128)(2,1)S(1)}, u32[]{:S(2)}, u32[]{:S(2)}) collective-permute-start(bf16[256,1024]{1,0:T(8,128)(2,1)S(1)} %collective-permute-done.6.refs_2_), channel_id=1, source_target_pairs={{0,4},{1,5},{2,14},{3,15},{4,8},{5,9},{6,2},{7,3},{8,12},{9,13},{1... | collective-permute-start | bytes 1572872 | tf_op jit(solution)/shard_map/ppermute | solution.py:403
  40.6 9.0 %collective-permute-start.11 = (bf16[128,1024]{1,0:T(8,128)(2,1)S(1)}, bf16[128,1024]{1,0:T(8,128)(2,1)S(1)}, u32[]{:S(2)}, u32[]{:S(2)}) collective-permute-start(bf16[128,1024]{1,0:T(8,128)(2,1)S(1)} %get-tuple-element.41), channel_id=1, source_target_pairs={{0,2},{1,3},{2,0},{3,1},{4,6},{5,7},{6,4},{7,5},{8,10},{9,11},{10,... | collective-permute-start | bytes 786440 | tf_op jit(solution)/shard_map/ppermute | solution.py:397
  43.2 8.0 %collective-permute-start.12 = (bf16[128,1024]{1,0:T(8,128)(2,1)S(1)}, bf16[128,1024]{1,0:T(8,128)(2,1)S(1)}, u32[]{:S(2)}, u32[]{:S(2)}) collective-permute-start(bf16[128,1024]{1,0:T(8,128)(2,1)S(1)} %pad_maximum_fusion.1), channel_id=1, source_target_pairs={{0,16},{16,0},{1,17},{17,1},{2,18},{18,2},{3,19},{19,3},{4,20},{20... | collective-permute-start | bytes 786440 | tf_op jit(solution)/shard_map/ppermute | solution.py:407
  49.6 5.6 %collective-permute-start.13 = (bf16[64,1024]{1,0:T(8,128)(2,1)S(1)}, bf16[64,1024]{1,0:T(8,128)(2,1)S(1)}, u32[]{:S(2)}, u32[]{:S(2)}) collective-permute-start(bf16[64,1024]{1,0:T(8,128)(2,1)S(1)} %constant_dynamic-slice_fusion), channel_id=1, source_target_pairs={{0,16},{16,0},{1,17},{17,1},{2,18},{18,2},{3,19},{19,3},{4,20},{20... | collective-permute-start | bytes 393224 | tf_op jit(solution)/shard_map/ppermute | solution.py:407
  51.2 6.2 %collective-permute-start.5 = (bf16[256,1024]{1,0:T(8,128)(2,1)S(1)}, bf16[256,1024]{1,0:T(8,128)(2,1)S(1)}, u32[]{:S(2)}, u32[]{:S(2)}) collective-permute-start(bf16[256,1024]{1,0:T(8,128)(2,1)S(1)} %copy-done.1), channel_id=1, source_target_pairs={{0,1},{1,0},{2,3},{3,2},{4,5},{5,4},{6,7},{7,6},{8,9},{9,8},{10,11... | collective-permute-start | bytes 1572872 | tf_op jit(solution)/shard_map/ppermute | solution.py:379
  55.2 2.1 %collective-permute-start.15 = (bf16[256,1024]{1,0:T(8,128)(2,1)S(1)}, bf16[256,1024]{1,0:T(8,128)(2,1)S(1)}, u32[]{:S(2)}, u32[]{:S(2)}) collective-permute-start(bf16[256,1024]{1,0:T(8,128)(2,1)S(1)} %collective-permute-done.14.refs_4_), channel_id=1, source_target_pairs={{0,1},{1,0},{2,3},{3,2},{4,5},{5,4},{6,7},{7,6},{8,9},{9,8},{10,11... | collective-permute-start | bytes 1572872 | tf_op jit(solution)/shard_map/ppermute | solution.py:379
  57.3 12.1 %copy-start = (bf16[1024,1024]{1,0:T(8,128)(2,1)S(1)}, bf16[1024,1024]{1,0:T(8,128)(2,1)}, u32[]{:S(2)}) copy-start(bf16[1024,1024]{1,0:T(8,128)(2,1)} %param.21) | copy-start | bytes 6291460
  57.3 12.1 %copy-start.2 = (bf16[256,1024]{1,0:T(8,128)(2,1)S(1)}, bf16[256,1024]{1,0:T(8,128)(2,1)}, u32[]{:S(2)}) copy-start(bf16[256,1024]{1,0:T(8,128)(2,1)} %get-tuple-element.26.tokens_ref) | copy-start | bytes 1572868
  67.7 1.7 %collective-permute-start.16 = (bf16[4,256,128]{2,1,0:T(8,128)(2,1)S(1)}, bf16[4,256,128]{2,1,0:T(8,128)(2,1)S(1)}, u32[]{:S(2)}, u32[]{:S(2)}) collective-permute-start(bf16[4,256,128]{2,1,0:T(8,128)(2,1)S(1)} %get-tuple-element.40), channel_id=1, source_target_pairs={{0,1},{1,0},{2,3},{3,2},{4,5},{5,4},{6,7},{7,6},{8,9},{9,8},{10,11... | collective-permute-start | bytes 786440 | tf_op jit(solution)/shard_map/ppermute | solution.py:379

commit v11 on v10

--- a/solution.py
+++ b/solution.py
@@ -243,19 +243,11 @@
     weight_refs, out_ref, sems = refs[:-2], refs[-2], refs[-1]
     index, plane = lax.axis_index("space"), lax.axis_index("groups")
     moves = []
-    for ref, (step, share) in zip(weight_refs, spots):
-        rows = ref.shape[0]
-        if share == "ring":
-            start = pl.multiple_of(plane * (rows // 2), 32)
-            moves.append((ref, out_ref.at[chip_at(index, step), pl.ds(start, rows), :]))
-        elif share == "swap":
-            rows = rows // len(step)
-            start = pl.multiple_of((1 - plane) * (2 * rows), 32)
-            for i, one in enumerate(step):
-                place = out_ref.at[chip_at(index, one), pl.ds(start, rows), :]
-                moves.append((ref.at[pl.ds(i * rows, rows), :], place))
-        else:
-            moves.append((ref, out_ref.at[chip_at(index, step)]))
+    for ref, parts in zip(weight_refs, spots):
+        for first, rows, step, start0, start1 in parts:
+            start = pl.multiple_of(jnp.where(plane == 0, start0, start1), 32)
+            place = out_ref.at[chip_at(index, step), pl.ds(start, rows), :]
+            moves.append((ref.at[pl.ds(first, rows), :], place))
     for wait in fetch(moves, sems):
         wait()
 
@@ -426,7 +418,8 @@
     rows = lax.all_gather(qkv_weight.T, "space", axis=0, tiled=True)
     blocks = rows.reshape(-1, 2, head_size, rows.shape[1])
     picked = lax.dynamic_index_in_dim(blocks, side, 1, keepdims=False)
-    return [(picked.reshape(-1, rows.shape[1]), (None, None))]
+    picked = picked.reshape(-1, rows.shape[1])
+    return [(picked, ((0, picked.shape[0], None, 0, 0),))]
 
 
 def per_device(
@@ -457,7 +450,7 @@
         plane = lax.axis_index("groups")
         share = lax.dynamic_slice_in_dim(block, plane * third, 2 * third, 0)
         early = [around(share, step) for step in (1, -1, 2, -2)]
-        weights = [(block, (0, None))]
+        weights = [(block, ((0, 3 * third, 0, 0, 0),))]
     else:
         weights = parity_weight(qkv_weight, side, head_size)
     tokens_zero, normed = aggregate(
@@ -465,28 +458,34 @@
     )
     if ringed:
 
-        def swapped(blocks):
+        def swapped(blocks, *whole):
             parts = [lax.dynamic_slice_in_dim(b, plane * third, third, 0) for b in blocks]
+            parts += whole
             return across(jnp.concatenate(parts, axis=0))
 
         tokens_zero, *early = together(tokens_zero, *early)
-        weights += [(b, (-step, "ring")) for b, step in zip(early, (1, -1, 2, -2))]
+        ring = [((0, 2 * third, step, 0, third),) for step in (-1, 1, -2, 2, "pair", "beside")]
+        weights += list(zip(early, ring))
         swap = swapped(early)
         place = ring_place(lax.axis_index("space"))
         near = crossed(normed, 2)
         low = place % 4 < 2
-        opposite = crossed(jnp.where(low, early[2], early[3]), 8)
+        opposite = jnp.where(low, early[2], early[3])
+        opposite = lax.dynamic_slice_in_dim(opposite, plane * (third // 2), 3 * third // 2, 0)
+        opposite = crossed(opposite, 8)
         pair = crossed(jnp.where(place % 2 == 0, early[2], early[3]), 4)
         near, opposite, pair = together(near, opposite, pair)
         far, near_sib = onward(near), sibling(near)
         beside = crossed(jnp.where(low, early[3], early[2]), 2)
-        first = swapped([pair, opposite])
+        first = swapped([pair], opposite)
         swap, near_sib, beside = together(swap, near_sib, beside)
         second = swapped([beside])
         _, _, far = together(first, second, far)
-        weights += [(pair, ("pair", "ring")), (opposite, (4, "ring")), (beside, ("beside", "ring"))]
-        weights += [(swap, ((-1, 1, -2, 2), "swap"))]
-        weights += [(first, (("pair", 4), "swap")), (second, (("beside",), "swap"))]
+        half = 3 * third // 2
+        swaps = [(i * third, third, step, 2 * third, 0) for i, step in enumerate((-1, 1, -2, 2))]
+        weights += [(pair, ring[4]), (beside, ring[5]), (opposite, ((0, half, 4, 0, half),))]
+        weights += [(swap, tuple(swaps)), (second, ((0, third, "beside", 2 * third, 0),))]
+        weights += [(first, ((0, third, "pair", 2 * third, 0), (third, half, 4, half, 0)))]
     else:
         near, far = from_chip(normed, 1), from_chip(normed, -1)
         near_sib = sibling(near)

time: 71.1 us -> 70.5 us (level)
  starting transfers between devices: 22.2 us -> 20.5 us
    ppermute x3, waiting for transfers between devices: 0.01 us -> 2.89 us  [across(): return lax.ppermute(value, 'groups', [(0, 1), (1, 0)])]
    ppermute x4, waiting for transfers between devices: 12.5 us -> 10.7 us  [crossed(): lax.ppermute(value, 'space', [(i, i ^ bits) for i in range(2 * len(RING))])]
    ppermute x4, starting transfers between devices: 8.65 us -> 7.13 us  [crossed(): lax.ppermute(value, 'space', [(i, i ^ bits) for i in range(2 * len(RING))])]
  transfers between devices with their start and end apart: 17 -> 17, of which waited for: 5 -> 7; matrix products, arithmetic and copies ran while one was open for 0% -> 0% of each run, Pallas kernels for 23% -> 24%
where the time goes in v11:
time: 70.5 us; the launch traced here: 70.4 us
  Pallas kernels  28.9 us (41%)
  starting transfers between devices  20.5 us (29%)
  waiting for transfers between devices  19.4 us (28%)
  local copies, waits for them, and re-layouts  1.16 us (2%)
    pallas_call x1, Pallas kernels, aggregate(): pl.pallas_call(aggregate_kernel, out_shape=[jax.ShapeDtypeStruct((tokens,...  14.6 us
    ppermute x4, waiting for transfers between devices, crossed(): lax.ppermute(value, 'space', [(i, i ^ bits) for i in range(2 * len(RING))])  10.7 us
    pallas_call x1, Pallas kernels, attend(): pl.pallas_call(functools.partial(attend_kernel, flipped=blocks > 1), out_...  10.4 us
    ppermute x4, starting transfers between devices, crossed(): lax.ppermute(value, 'space', [(i, i ^ bits) for i in range(2 * len(RING))])  7.13 us
    ppermute x4, starting transfers between devices, around(): return lax.ppermute(value, 'space', pairs)  6.03 us
    ppermute x3, starting transfers between devices, across(): return lax.ppermute(value, 'groups', [(0, 1), (1, 0)])  4.66 us
    ppermute x1, waiting for transfers between devices, onward(): return lax.ppermute(value, 'space', pairs)  3.65 us
    ppermute x3, waiting for transfers between devices, across(): return lax.ppermute(value, 'groups', [(0, 1), (1, 0)])  2.89 us
  transfers between devices with their start and end apart: 17, of which 7 were waited for; matrix products, arithmetic and copies ran while one was open for 0% of the time, Pallas kernels for 24%

profile of v11, /device:TPU:0, one launch (start us, length us, event | category | flops | bytes accessed | tf_op | source)
XLA Modules:
  0.0 70.4 jit_solution(14802471816454856021)
XLA Ops:
  0.0 1.1 %fusion = (bf16[64,1024]{1,0:T(8,128)(2,1)S(1)}, bf16[64,1024]{1,0:T(8,128)(2,1)S(1)}, bf16[64,1024]{1,0:T(8,128)(2,1)S(1)}) fusion(bf16[192,1024]{1,0:T(8,128)(2,1)} %bitcast.4), kind=kLoop, calls=%fused_computation.13 | loop fusion | bytes 786432 | tf_op jit(solution)/shard_map/slice | solution.py:408
  1.1 0.5 collective-permute-start
  1.6 1.0 %collective-permute-done = bf16[64,1024]{1,0:T(8,128)(2,1)S(1)} collective-permute-done((bf16[64,1024]{1,0:T(8,128)(2,1)S(1)}, bf16[64,1024]{1,0:T(8,128)(2,1)S(1)}, u32[]{:S(2)}, u32[]{:S(2)}) %collective-permute-start) | collective-permute-done | bytes 131104 | tf_op jit(solution)/shard_map/ppermute | solution.py:371
  2.6 0.1 maximum_select_fusion.refs_0_
  2.7 3.0 %collective-permute-start.1 = (bf16[128,1024]{1,0:T(8,128)(2,1)S(1)}, bf16[128,1024]{1,0:T(8,128)(2,1)S(1)}, u32[]{:S(2)}, u32[]{:S(2)}) collective-permute-start(bf16[128,1024]{1,0:T(8,128)(2,1)S(1)} %constant_dynamic-slice_fusion.6), channel_id=1, source_target_pairs={{0,4},{1,5},{4,8},{5,9},{8,12},{9,13},{12,14},{13,15},{14,10},{15,... | collective-permute-start | bytes 786440 | tf_op jit(solution)/shard_map/ppermute | solution.py:385
  5.7 0.0 collective-permute-start.2
  5.7 3.0 %collective-permute-start.3 = (bf16[128,1024]{1,0:T(8,128)(2,1)S(1)}, bf16[128,1024]{1,0:T(8,128)(2,1)S(1)}, u32[]{:S(2)}, u32[]{:S(2)}) collective-permute-start(bf16[128,1024]{1,0:T(8,128)(2,1)S(1)} %constant_dynamic-slice_fusion.6), channel_id=1, source_target_pairs={{0,8},{1,9},{4,12},{5,13},{8,14},{9,15},{12,10},{13,11},{14,6},{15... | collective-permute-start | bytes 786440 | tf_op jit(solution)/shard_map/ppermute | solution.py:385
  8.7 0.0 collective-permute-start.4
  8.7 14.6 %aggregate.1 = (bf16[256,1024]{1,0:T(8,128)(2,1)}, bf16[256,1024]{1,0:T(8,128)(2,1)}) custom-call(s32[64]{0:T(128)} %order_ref.1, bf16[64,1024]{1,0:T(8,128)(2,1)} %var_embed_hbm.1, bf16[16,1024]{1,0:T(8,128)(2,1)} %keys_hbm.1, bf16[64,16,1024]{2,1,0:T(8,128)(2,1)} %embed_hbm, bf16[256,1024]{1,0:T(8,128)(2,1)} %patches_hbm.1, bf16[1024,1024]{1,0:T(8,128)(2,1)} %value_hbm.1, ...), custom_call_target="tpu_custom_call" | custom-call | flops 16000000000 | bytes 8388608 | tf_op jit(solution)/shard_map/aggregate/pallas_call | solution.py:227
  23.3 1.9 %collective-permute-start.6 = (bf16[256,1024]{1,0:T(8,128)(2,1)}, bf16[256,1024]{1,0:T(8,128)(2,1)S(1)}, u32[]{:S(2)}, u32[]{:S(2)}) collective-permute-start(bf16[256,1024]{1,0:T(8,128)(2,1)} %get-tuple-element.27.refs_0_), channel_id=1, source_target_pairs={{0,2},{1,3},{2,0},{3,1},{4,6},{5,7},{6,4},{7,5},{8,10},{9,11},{10,... | collective-permute-start | bytes 1572872 | tf_op jit(solution)/shard_map/ppermute | solution.py:389
  25.2 0.0 collective-permute-done.1.refs_1_
  25.2 0.0 collective-permute-done.2.refs_2_
  25.2 0.0 collective-permute-done.3.refs_3_
  25.2 0.0 collective-permute-done.4.refs_4_
  25.3 0.0 copy-start.1
  25.3 2.4 %collective-permute-start.8 = (bf16[128,1024]{1,0:T(8,128)(2,1)S(1)}, bf16[128,1024]{1,0:T(8,128)(2,1)S(1)}, u32[]{:S(2)}, u32[]{:S(2)}) collective-permute-start(bf16[128,1024]{1,0:T(8,128)(2,1)S(1)} %get-tuple-element.42), channel_id=1, source_target_pairs={{0,4},{1,5},{2,6},{3,7},{4,0},{5,1},{6,2},{7,3},{8,12},{9,13},{10,... | collective-permute-start | bytes 786440 | tf_op jit(solution)/shard_map/ppermute | solution.py:389
  27.7 0.1 dynamic-slice_select_fusion
  27.8 1.9 %collective-permute-start.7 = (bf16[96,1024]{1,0:T(8,128)(2,1)S(1)}, bf16[96,1024]{1,0:T(8,128)(2,1)S(1)}, u32[]{:S(2)}, u32[]{:S(2)}) collective-permute-start(bf16[96,1024]{1,0:T(8,128)(2,1)S(1)} %dynamic-slice_select_fusion), channel_id=1, source_target_pairs={{0,8},{1,9},{2,10},{3,11},{4,12},{5,13},{6,14},{7,15},{8,0},{9,1},... | collective-permute-start | bytes 589832 | tf_op jit(solution)/shard_map/ppermute | solution.py:389
  29.8 1.6 %collective-permute-start.9 = (bf16[256,1024]{1,0:T(8,128)(2,1)S(1)}, bf16[256,1024]{1,0:T(8,128)(2,1)S(1)}, u32[]{:S(2)}, u32[]{:S(2)}) collective-permute-start(bf16[256,1024]{1,0:T(8,128)(2,1)S(1)} %pad_maximum_fusion), channel_id=1, source_target_pairs={{0,16},{16,0},{1,17},{17,1},{2,18},{18,2},{3,19},{19,3},{4,20},{20... | collective-permute-start | bytes 1572872 | tf_op jit(solution)/shard_map/ppermute | solution.py:399
  31.3 5.3 %collective-permute-done.7.refs_7_ = bf16[96,1024]{1,0:T(8,128)(2,1)S(1)} collective-permute-done((bf16[96,1024]{1,0:T(8,128)(2,1)S(1)}, bf16[96,1024]{1,0:T(8,128)(2,1)S(1)}, u32[]{:S(2)}, u32[]{:S(2)}) %collective-permute-start.7) | collective-permute-done | bytes 196640 | tf_op jit(solution)/shard_map/ppermute | solution.py:389
  36.6 0.7 %collective-permute-done.8.refs_5_ = bf16[128,1024]{1,0:T(8,128)(2,1)S(1)} collective-permute-done((bf16[128,1024]{1,0:T(8,128)(2,1)S(1)}, bf16[128,1024]{1,0:T(8,128)(2,1)S(1)}, u32[]{:S(2)}, u32[]{:S(2)}) %collective-permute-start.8) | collective-permute-done | bytes 262176 | tf_op jit(solution)/shard_map/ppermute | solution.py:389
  37.4 0.0 collective-permute-done.6.refs_2_
  37.4 0.0 collective-permute-start.10
  37.4 0.9 %collective-permute-start.11 = (bf16[128,1024]{1,0:T(8,128)(2,1)S(1)}, bf16[128,1024]{1,0:T(8,128)(2,1)S(1)}, u32[]{:S(2)}, u32[]{:S(2)}) collective-permute-start(bf16[128,1024]{1,0:T(8,128)(2,1)S(1)} %get-tuple-element.41), channel_id=1, source_target_pairs={{0,2},{1,3},{2,0},{3,1},{4,6},{5,7},{6,4},{7,5},{8,10},{9,11},{10,... | collective-permute-start | bytes 786440 | tf_op jit(solution)/shard_map/ppermute | solution.py:389
  38.3 1.6 %collective-permute-start.14 = (bf16[256,1024]{1,0:T(8,128)(2,1)S(1)}, bf16[256,1024]{1,0:T(8,128)(2,1)S(1)}, u32[]{:S(2)}, u32[]{:S(2)}) collective-permute-start(bf16[256,1024]{1,0:T(8,128)(2,1)S(1)} %collective-permute-done.6.refs_2_), channel_id=1, source_target_pairs={{0,4},{1,5},{2,14},{3,15},{4,8},{5,9},{6,2},{7,3},{8,12},{9,13},{1... | collective-permute-start | bytes 1572872 | tf_op jit(solution)/shard_map/ppermute | solution.py:395
  39.9 1.6 %collective-permute-start.12 = (bf16[160,1024]{1,0:T(8,128)(2,1)S(1)}, bf16[160,1024]{1,0:T(8,128)(2,1)S(1)}, u32[]{:S(2)}, u32[]{:S(2)}) collective-permute-start(bf16[160,1024]{1,0:T(8,128)(2,1)S(1)} %pad_maximum_fusion.1), channel_id=1, source_target_pairs={{0,16},{16,0},{1,17},{17,1},{2,18},{18,2},{3,19},{19,3},{4,20},{20... | collective-permute-start | bytes 983048 | tf_op jit(solution)/shard_map/ppermute | solution.py:399
  41.5 4.6 %collective-permute-done.11.refs_6_ = bf16[128,1024]{1,0:T(8,128)(2,1)S(1)} collective-permute-done((bf16[128,1024]{1,0:T(8,128)(2,1)S(1)}, bf16[128,1024]{1,0:T(8,128)(2,1)S(1)}, u32[]{:S(2)}, u32[]{:S(2)}) %collective-permute-start.11) | collective-permute-done | bytes 262176 | tf_op jit(solution)/shard_map/ppermute | solution.py:389
  46.1 0.0 collective-permute-done.9.refs_8_
  46.1 0.0 collective-permute-done.10.refs_3_
  46.1 1.6 %collective-permute-start.13 = (bf16[64,1024]{1,0:T(8,128)(2,1)S(1)}, bf16[64,1024]{1,0:T(8,128)(2,1)S(1)}, u32[]{:S(2)}, u32[]{:S(2)}) collective-permute-start(bf16[64,1024]{1,0:T(8,128)(2,1)S(1)} %constant_dynamic-slice_fusion), channel_id=1, source_target_pairs={{0,16},{16,0},{1,17},{17,1},{2,18},{18,2},{3,19},{19,3},{4,20},{20... | collective-permute-start | bytes 393224 | tf_op jit(solution)/shard_map/ppermute | solution.py:399
  47.7 0.0 copy-done.1
  47.7 0.0 collective-permute-start.5
  47.7 2.9 %collective-permute-done.12.refs_10_ = bf16[160,1024]{1,0:T(8,128)(2,1)S(1)} collective-permute-done((bf16[160,1024]{1,0:T(8,128)(2,1)S(1)}, bf16[160,1024]{1,0:T(8,128)(2,1)S(1)}, u32[]{:S(2)}, u32[]{:S(2)}) %collective-permute-start.12) | collective-permute-done | bytes 327712 | tf_op jit(solution)/shard_map/ppermute | solution.py:399
  50.6 3.6 %collective-permute-done.14.refs_4_ = bf16[256,1024]{1,0:T(8,128)(2,1)S(1)} collective-permute-done((bf16[256,1024]{1,0:T(8,128)(2,1)S(1)}, bf16[256,1024]{1,0:T(8,128)(2,1)S(1)}, u32[]{:S(2)}, u32[]{:S(2)}) %collective-permute-start.14) | collective-permute-done | bytes 524320 | tf_op jit(solution)/shard_map/ppermute | solution.py:395
  54.2 0.0 collective-permute-done.13.refs_9_
  54.2 0.0 collective-permute-start.15
  54.2 2.5 %assemble.1.refs_6_ = bf16[8,192,1024]{2,1,0:T(8,128)(2,1)S(1)} custom-call(bf16[192,1024]{1,0:T(8,128)(2,1)S(1)} %maximum_select_fusion.refs_0_, bf16[128,1024]{1,0:T(8,128)(2,1)S(1)} %collective-permute-done.1.refs_1_, bf16[128,1024]{1,0:T(8,128)(2,1)S(1)} %collective-permute-done.2.refs_2_, bf16[128,1024]{1,0:T(8,128)(2,1)S(1)} %collective-permute-done.3.refs_3_, ...), custom_call_target="tpu_custom_call" | custom-call | flops 1000000000 | bytes 6291456 | tf_op jit(solution)/shard_map/assemble/pallas_call | solution.py:259
  56.7 0.0 copy-start
  56.7 0.0 copy-start.2
  56.7 0.0 collective-permute-done.5.refs_1_
  56.7 0.0 collective-permute-done.15.refs_5_
  56.7 10.4 %attend.1 = (bf16[4,256,128]{2,1,0:T(8,128)(2,1)S(1)}, bf16[4,256,128]{2,1,0:T(8,128)(2,1)S(1)}) custom-call(bf16[256,1024]{1,0:T(8,128)(2,1)S(1)} %copy-done.1, bf16[256,1024]{1,0:T(8,128)(2,1)S(1)} %collective-permute-done.5.refs_1_, bf16[256,1024]{1,0:T(8,128)(2,1)S(1)} %collective-permute-done.6.refs_2_, ...), custom_call_target="tpu_custom_call" | custom-call | flops 10000000000 | bytes 8388608 | tf_op jit(solution)/shard_map/attend/pallas_call | solution.py:327
  67.1 0.6 collective-permute-start.16
  67.7 1.2 %collective-permute-done.16.other_ref = bf16[4,256,128]{2,1,0:T(8,128)(2,1)S(1)} collective-permute-done((bf16[4,256,128]{2,1,0:T(8,128)(2,1)S(1)}, bf16[4,256,128]{2,1,0:T(8,128)(2,1)S(1)}, u32[]{:S(2)}, u32[]{:S(2)}) %collective-permute-start.16) | collective-permute-done | bytes 262176 | tf_op jit(solution)/shard_map/ppermute | solution.py:371
  68.8 0.0 copy-done
  68.8 0.0 copy-done.2
  68.9 1.5 %finish.1 = bf16[256,1024]{1,0:T(8,128)(2,1)} custom-call(bf16[256,1024]{1,0:T(8,128)(2,1)S(1)} %copy-done.2, bf16[4,256,128]{2,1,0:T(8,128)(2,1)S(1)} %get-tuple-element.39.mine_ref, bf16[4,256,128]{2,1,0:T(8,128)(2,1)S(1)} %collective-permute-done.16.other_ref, bf16[8,2,64,1024]{3,2,1,0:T(8,128)(2,1)S(1)} %bitcast.3), custom_call_target="tpu_custom_call" | custom-call | flops 1000000000 | bytes 4194304 | tf_op jit(solution)/shard_map/finish/pallas_call | solution.py:358
  (8 shorter events, 0.2 us)
Async XLA Ops:
  1.1 1.5 %collective-permute-start = (bf16[64,1024]{1,0:T(8,128)(2,1)S(1)}, bf16[64,1024]{1,0:T(8,128)(2,1)S(1)}, u32[]{:S(2)}, u32[]{:S(2)}) collective-permute-start(bf16[64,1024]{1,0:T(8,128)(2,1)S(1)} %get-tuple-element.44), channel_id=1, source_target_pairs={{0,1},{1,0},{2,3},{3,2},{4,5},{5,4},{6,7},{7,6},{8,9},{9,8},{10,11... | collective-permute-start | bytes 393224 | tf_op jit(solution)/shard_map/ppermute | solution.py:371
  2.7 22.6 %collective-permute-start.1 = (bf16[128,1024]{1,0:T(8,128)(2,1)S(1)}, bf16[128,1024]{1,0:T(8,128)(2,1)S(1)}, u32[]{:S(2)}, u32[]{:S(2)}) collective-permute-start(bf16[128,1024]{1,0:T(8,128)(2,1)S(1)} %constant_dynamic-slice_fusion.6), channel_id=1, source_target_pairs={{0,4},{1,5},{4,8},{5,9},{8,12},{9,13},{12,14},{13,15},{14,10},{15,... | collective-permute-start | bytes 786440 | tf_op jit(solution)/shard_map/ppermute | solution.py:385
  5.7 19.6 %collective-permute-start.2 = (bf16[128,1024]{1,0:T(8,128)(2,1)S(1)}, bf16[128,1024]{1,0:T(8,128)(2,1)S(1)}, u32[]{:S(2)}, u32[]{:S(2)}) collective-permute-start(bf16[128,1024]{1,0:T(8,128)(2,1)S(1)} %constant_dynamic-slice_fusion.6), channel_id=1, source_target_pairs={{0,2},{1,3},{4,0},{5,1},{8,4},{9,5},{12,8},{13,9},{14,12},{15,13},... | collective-permute-start | bytes 786440 | tf_op jit(solution)/shard_map/ppermute | solution.py:385
  5.7 19.6 %collective-permute-start.3 = (bf16[128,1024]{1,0:T(8,128)(2,1)S(1)}, bf16[128,1024]{1,0:T(8,128)(2,1)S(1)}, u32[]{:S(2)}, u32[]{:S(2)}) collective-permute-start(bf16[128,1024]{1,0:T(8,128)(2,1)S(1)} %constant_dynamic-slice_fusion.6), channel_id=1, source_target_pairs={{0,8},{1,9},{4,12},{5,13},{8,14},{9,15},{12,10},{13,11},{14,6},{15... | collective-permute-start | bytes 786440 | tf_op jit(solution)/shard_map/ppermute | solution.py:385
  8.7 16.5 %collective-permute-start.4 = (bf16[128,1024]{1,0:T(8,128)(2,1)S(1)}, bf16[128,1024]{1,0:T(8,128)(2,1)S(1)}, u32[]{:S(2)}, u32[]{:S(2)}) collective-permute-start(bf16[128,1024]{1,0:T(8,128)(2,1)S(1)} %constant_dynamic-slice_fusion.6), channel_id=1, source_target_pairs={{0,6},{1,7},{4,2},{5,3},{8,0},{9,1},{12,4},{13,5},{14,8},{15,9},{1... | collective-permute-start | bytes 786440 | tf_op jit(solution)/shard_map/ppermute | solution.py:385
  23.3 14.1 %collective-permute-start.6 = (bf16[256,1024]{1,0:T(8,128)(2,1)}, bf16[256,1024]{1,0:T(8,128)(2,1)S(1)}, u32[]{:S(2)}, u32[]{:S(2)}) collective-permute-start(bf16[256,1024]{1,0:T(8,128)(2,1)} %get-tuple-element.27.refs_0_), channel_id=1, source_target_pairs={{0,2},{1,3},{2,0},{3,1},{4,6},{5,7},{6,4},{7,5},{8,10},{9,11},{10,... | collective-permute-start | bytes 1572872 | tf_op jit(solution)/shard_map/ppermute | solution.py:389
  25.3 22.4 %copy-start.1 = (bf16[256,1024]{1,0:T(8,128)(2,1)S(1)}, bf16[256,1024]{1,0:T(8,128)(2,1)}, u32[]{:S(2)}) copy-start(bf16[256,1024]{1,0:T(8,128)(2,1)} %get-tuple-element.27.refs_0_) | copy-start | bytes 1572868
  25.3 12.1 %collective-permute-start.8 = (bf16[128,1024]{1,0:T(8,128)(2,1)S(1)}, bf16[128,1024]{1,0:T(8,128)(2,1)S(1)}, u32[]{:S(2)}, u32[]{:S(2)}) collective-permute-start(bf16[128,1024]{1,0:T(8,128)(2,1)S(1)} %get-tuple-element.42), channel_id=1, source_target_pairs={{0,4},{1,5},{2,6},{3,7},{4,0},{5,1},{6,2},{7,3},{8,12},{9,13},{10,... | collective-permute-start | bytes 786440 | tf_op jit(solution)/shard_map/ppermute | solution.py:389
  27.8 8.9 %collective-permute-start.7 = (bf16[96,1024]{1,0:T(8,128)(2,1)S(1)}, bf16[96,1024]{1,0:T(8,128)(2,1)S(1)}, u32[]{:S(2)}, u32[]{:S(2)}) collective-permute-start(bf16[96,1024]{1,0:T(8,128)(2,1)S(1)} %dynamic-slice_select_fusion), channel_id=1, source_target_pairs={{0,8},{1,9},{2,10},{3,11},{4,12},{5,13},{6,14},{7,15},{8,0},{9,1},... | collective-permute-start | bytes 589832 | tf_op jit(solution)/shard_map/ppermute | solution.py:389
  29.8 16.3 %collective-permute-start.9 = (bf16[256,1024]{1,0:T(8,128)(2,1)S(1)}, bf16[256,1024]{1,0:T(8,128)(2,1)S(1)}, u32[]{:S(2)}, u32[]{:S(2)}) collective-permute-start(bf16[256,1024]{1,0:T(8,128)(2,1)S(1)} %pad_maximum_fusion), channel_id=1, source_target_pairs={{0,16},{16,0},{1,17},{17,1},{2,18},{18,2},{3,19},{19,3},{4,20},{20... | collective-permute-start | bytes 1572872 | tf_op jit(solution)/shard_map/ppermute | solution.py:399
  37.4 8.7 %collective-permute-start.10 = (bf16[256,1024]{1,0:T(8,128)(2,1)S(1)}, bf16[256,1024]{1,0:T(8,128)(2,1)S(1)}, u32[]{:S(2)}, u32[]{:S(2)}) collective-permute-start(bf16[256,1024]{1,0:T(8,128)(2,1)S(1)} %collective-permute-done.6.refs_2_), channel_id=1, source_target_pairs={{0,1},{1,0},{2,3},{3,2},{4,5},{5,4},{6,7},{7,6},{8,9},{9,8},{10,11... | collective-permute-start | bytes 1572872 | tf_op jit(solution)/shard_map/ppermute | solution.py:371
  37.4 8.7 %collective-permute-start.11 = (bf16[128,1024]{1,0:T(8,128)(2,1)S(1)}, bf16[128,1024]{1,0:T(8,128)(2,1)S(1)}, u32[]{:S(2)}, u32[]{:S(2)}) collective-permute-start(bf16[128,1024]{1,0:T(8,128)(2,1)S(1)} %get-tuple-element.41), channel_id=1, source_target_pairs={{0,2},{1,3},{2,0},{3,1},{4,6},{5,7},{6,4},{7,5},{8,10},{9,11},{10,... | collective-permute-start | bytes 786440 | tf_op jit(solution)/shard_map/ppermute | solution.py:389
  38.3 15.9 %collective-permute-start.14 = (bf16[256,1024]{1,0:T(8,128)(2,1)S(1)}, bf16[256,1024]{1,0:T(8,128)(2,1)S(1)}, u32[]{:S(2)}, u32[]{:S(2)}) collective-permute-start(bf16[256,1024]{1,0:T(8,128)(2,1)S(1)} %collective-permute-done.6.refs_2_), channel_id=1, source_target_pairs={{0,4},{1,5},{2,14},{3,15},{4,8},{5,9},{6,2},{7,3},{8,12},{9,13},{1... | collective-permute-start | bytes 1572872 | tf_op jit(solution)/shard_map/ppermute | solution.py:395
  39.9 10.6 %collective-permute-start.12 = (bf16[160,1024]{1,0:T(8,128)(2,1)S(1)}, bf16[160,1024]{1,0:T(8,128)(2,1)S(1)}, u32[]{:S(2)}, u32[]{:S(2)}) collective-permute-start(bf16[160,1024]{1,0:T(8,128)(2,1)S(1)} %pad_maximum_fusion.1), channel_id=1, source_target_pairs={{0,16},{16,0},{1,17},{17,1},{2,18},{18,2},{3,19},{19,3},{4,20},{20... | collective-permute-start | bytes 983048 | tf_op jit(solution)/shard_map/ppermute | solution.py:399
  46.1 8.1 %collective-permute-start.13 = (bf16[64,1024]{1,0:T(8,128)(2,1)S(1)}, bf16[64,1024]{1,0:T(8,128)(2,1)S(1)}, u32[]{:S(2)}, u32[]{:S(2)}) collective-permute-start(bf16[64,1024]{1,0:T(8,128)(2,1)S(1)} %constant_dynamic-slice_fusion), channel_id=1, source_target_pairs={{0,16},{16,0},{1,17},{17,1},{2,18},{18,2},{3,19},{19,3},{4,20},{20... | collective-permute-start | bytes 393224 | tf_op jit(solution)/shard_map/ppermute | solution.py:399
  47.7 9.0 %collective-permute-start.5 = (bf16[256,1024]{1,0:T(8,128)(2,1)S(1)}, bf16[256,1024]{1,0:T(8,128)(2,1)S(1)}, u32[]{:S(2)}, u32[]{:S(2)}) collective-permute-start(bf16[256,1024]{1,0:T(8,128)(2,1)S(1)} %copy-done.1), channel_id=1, source_target_pairs={{0,1},{1,0},{2,3},{3,2},{4,5},{5,4},{6,7},{7,6},{8,9},{9,8},{10,11... | collective-permute-start | bytes 1572872 | tf_op jit(solution)/shard_map/ppermute | solution.py:371
  54.2 2.5 %collective-permute-start.15 = (bf16[256,1024]{1,0:T(8,128)(2,1)S(1)}, bf16[256,1024]{1,0:T(8,128)(2,1)S(1)}, u32[]{:S(2)}, u32[]{:S(2)}) collective-permute-start(bf16[256,1024]{1,0:T(8,128)(2,1)S(1)} %collective-permute-done.14.refs_4_), channel_id=1, source_target_pairs={{0,1},{1,0},{2,3},{3,2},{4,5},{5,4},{6,7},{7,6},{8,9},{9,8},{10,11... | collective-permute-start | bytes 1572872 | tf_op jit(solution)/shard_map/ppermute | solution.py:371
  56.7 12.1 %copy-start = (bf16[1024,1024]{1,0:T(8,128)(2,1)S(1)}, bf16[1024,1024]{1,0:T(8,128)(2,1)}, u32[]{:S(2)}) copy-start(bf16[1024,1024]{1,0:T(8,128)(2,1)} %param.21) | copy-start | bytes 6291460
  56.7 12.1 %copy-start.2 = (bf16[256,1024]{1,0:T(8,128)(2,1)S(1)}, bf16[256,1024]{1,0:T(8,128)(2,1)}, u32[]{:S(2)}) copy-start(bf16[256,1024]{1,0:T(8,128)(2,1)} %get-tuple-element.26.tokens_ref) | copy-start | bytes 1572868
  67.1 1.7 %collective-permute-start.16 = (bf16[4,256,128]{2,1,0:T(8,128)(2,1)S(1)}, bf16[4,256,128]{2,1,0:T(8,128)(2,1)S(1)}, u32[]{:S(2)}, u32[]{:S(2)}) collective-permute-start(bf16[4,256,128]{2,1,0:T(8,128)(2,1)S(1)} %get-tuple-element.40), channel_id=1, source_target_pairs={{0,1},{1,0},{2,3},{3,2},{4,5},{5,4},{6,7},{7,6},{8,9},{9,8},{10,11... | collective-permute-start | bytes 786440 | tf_op jit(solution)/shard_map/ppermute | solution.py:371

commit v12 on v11

--- a/solution.py
+++ b/solution.py
@@ -474,9 +474,9 @@
         opposite = lax.dynamic_slice_in_dim(opposite, plane * (third // 2), 3 * third // 2, 0)
         opposite = crossed(opposite, 8)
         pair = crossed(jnp.where(place % 2 == 0, early[2], early[3]), 4)
-        near, opposite, pair = together(near, opposite, pair)
-        far, near_sib = onward(near), sibling(near)
-        beside = crossed(jnp.where(low, early[3], early[2]), 2)
+        beside = jnp.where(low, early[3], early[2])
+        near, opposite, pair, beside = together(near, opposite, pair, beside)
+        far, near_sib, beside = onward(near), sibling(near), crossed(beside, 2)
         first = swapped([pair], opposite)
         swap, near_sib, beside = together(swap, near_sib, beside)
         second = swapped([beside])

time: 70.5 us -> 70.7 us (level)
  starting transfers between devices: 20.5 us -> 22.5 us
  waiting for transfers between devices: 19.4 us -> 17.5 us
    ppermute x1, waiting for transfers between devices: 3.65 us -> 1.43 us  [onward(): return lax.ppermute(value, 'space', pairs)]
    ppermute x4, starting transfers between devices: 7.13 us -> 8.73 us  [crossed(): lax.ppermute(value, 'space', [(i, i ^ bits) for i in range(2 * len(RING))])]
  transfers between devices with their start and end apart: 17 -> 17, of which waited for: 7 -> 8; matrix products, arithmetic and copies ran while one was open for 0% -> 0% of each run, Pallas kernels for 24% -> 24%
where the time goes in v12:
time: 70.7 us; the launch traced here: 70.5 us
  Pallas kernels  28.9 us (41%)
  starting transfers between devices  22.5 us (32%)
  waiting for transfers between devices  17.5 us (25%)
  local copies, waits for them, and re-layouts  1.16 us (2%)
    pallas_call x1, Pallas kernels, aggregate(): pl.pallas_call(aggregate_kernel, out_shape=[jax.ShapeDtypeStruct((tokens,...  14.6 us
    ppermute x4, waiting for transfers between devices, crossed(): lax.ppermute(value, 'space', [(i, i ^ bits) for i in range(2 * len(RING))])  11.1 us
    pallas_call x1, Pallas kernels, attend(): pl.pallas_call(functools.partial(attend_kernel, flipped=blocks > 1), out_...  10.4 us
    ppermute x4, starting transfers between devices, crossed(): lax.ppermute(value, 'space', [(i, i ^ bits) for i in range(2 * len(RING))])  8.73 us
    ppermute x4, starting transfers between devices, around(): return lax.ppermute(value, 'space', pairs)  6.03 us
    ppermute x3, starting transfers between devices, across(): return lax.ppermute(value, 'groups', [(0, 1), (1, 0)])  4.66 us
    ppermute x3, waiting for transfers between devices, across(): return lax.ppermute(value, 'groups', [(0, 1), (1, 0)])  2.78 us
    pallas_call x1, Pallas kernels, assemble(): pl.pallas_call(functools.partial(assemble_kernel, spots=spots), out_shape...  2.46 us
  transfers between devices with their start and end apart: 17, of which 8 were waited for; matrix products, arithmetic and copies ran while one was open for 0% of the time, Pallas kernels for 24%

profile of v12, /device:TPU:0, one launch (start us, length us, event | category | flops | bytes accessed | tf_op | source)
XLA Modules:
  0.0 70.5 jit_solution(10212715104631912841)
XLA Ops:
  0.0 1.1 %fusion = (bf16[64,1024]{1,0:T(8,128)(2,1)S(1)}, bf16[64,1024]{1,0:T(8,128)(2,1)S(1)}, bf16[64,1024]{1,0:T(8,128)(2,1)S(1)}) fusion(bf16[192,1024]{1,0:T(8,128)(2,1)} %bitcast.4), kind=kLoop, calls=%fused_computation.13 | loop fusion | bytes 786432 | tf_op jit(solution)/shard_map/slice | solution.py:408
  1.1 0.5 collective-permute-start
  1.6 1.0 %collective-permute-done = bf16[64,1024]{1,0:T(8,128)(2,1)S(1)} collective-permute-done((bf16[64,1024]{1,0:T(8,128)(2,1)S(1)}, bf16[64,1024]{1,0:T(8,128)(2,1)S(1)}, u32[]{:S(2)}, u32[]{:S(2)}) %collective-permute-start) | collective-permute-done | bytes 131104 | tf_op jit(solution)/shard_map/ppermute | solution.py:371
  2.6 0.1 maximum_select_fusion.refs_0_
  2.7 3.0 %collective-permute-start.1 = (bf16[128,1024]{1,0:T(8,128)(2,1)S(1)}, bf16[128,1024]{1,0:T(8,128)(2,1)S(1)}, u32[]{:S(2)}, u32[]{:S(2)}) collective-permute-start(bf16[128,1024]{1,0:T(8,128)(2,1)S(1)} %constant_dynamic-slice_fusion.6), channel_id=1, source_target_pairs={{0,4},{1,5},{4,8},{5,9},{8,12},{9,13},{12,14},{13,15},{14,10},{15,... | collective-permute-start | bytes 786440 | tf_op jit(solution)/shard_map/ppermute | solution.py:385
  5.7 0.0 collective-permute-start.2
  5.7 3.0 %collective-permute-start.3 = (bf16[128,1024]{1,0:T(8,128)(2,1)S(1)}, bf16[128,1024]{1,0:T(8,128)(2,1)S(1)}, u32[]{:S(2)}, u32[]{:S(2)}) collective-permute-start(bf16[128,1024]{1,0:T(8,128)(2,1)S(1)} %constant_dynamic-slice_fusion.6), channel_id=1, source_target_pairs={{0,8},{1,9},{4,12},{5,13},{8,14},{9,15},{12,10},{13,11},{14,6},{15... | collective-permute-start | bytes 786440 | tf_op jit(solution)/shard_map/ppermute | solution.py:385
  8.7 0.0 collective-permute-start.4
  8.7 14.6 %aggregate.1 = (bf16[256,1024]{1,0:T(8,128)(2,1)}, bf16[256,1024]{1,0:T(8,128)(2,1)}) custom-call(s32[64]{0:T(128)} %order_ref.1, bf16[64,1024]{1,0:T(8,128)(2,1)} %var_embed_hbm.1, bf16[16,1024]{1,0:T(8,128)(2,1)} %keys_hbm.1, bf16[64,16,1024]{2,1,0:T(8,128)(2,1)} %embed_hbm, bf16[256,1024]{1,0:T(8,128)(2,1)} %patches_hbm.1, bf16[1024,1024]{1,0:T(8,128)(2,1)} %value_hbm.1, ...), custom_call_target="tpu_custom_call" | custom-call | flops 16000000000 | bytes 8388608 | tf_op jit(solution)/shard_map/aggregate/pallas_call | solution.py:227
  23.3 1.9 %collective-permute-start.6 = (bf16[256,1024]{1,0:T(8,128)(2,1)}, bf16[256,1024]{1,0:T(8,128)(2,1)S(1)}, u32[]{:S(2)}, u32[]{:S(2)}) collective-permute-start(bf16[256,1024]{1,0:T(8,128)(2,1)} %get-tuple-element.28.refs_0_), channel_id=1, source_target_pairs={{0,2},{1,3},{2,0},{3,1},{4,6},{5,7},{6,4},{7,5},{8,10},{9,11},{10,... | collective-permute-start | bytes 1572872 | tf_op jit(solution)/shard_map/ppermute | solution.py:389
  25.2 0.0 collective-permute-done.1.refs_1_
  25.2 0.0 collective-permute-done.2.refs_2_
  25.2 0.0 collective-permute-done.3.refs_3_
  25.2 0.0 collective-permute-done.4.refs_4_
  25.3 0.0 copy-start.1
  25.3 2.4 %collective-permute-start.8 = (bf16[128,1024]{1,0:T(8,128)(2,1)S(1)}, bf16[128,1024]{1,0:T(8,128)(2,1)S(1)}, u32[]{:S(2)}, u32[]{:S(2)}) collective-permute-start(bf16[128,1024]{1,0:T(8,128)(2,1)S(1)} %get-tuple-element.44), channel_id=1, source_target_pairs={{0,4},{1,5},{2,6},{3,7},{4,0},{5,1},{6,2},{7,3},{8,12},{9,13},{10,... | collective-permute-start | bytes 786440 | tf_op jit(solution)/shard_map/ppermute | solution.py:389
  27.7 0.1 dynamic-slice_select_fusion
  27.8 1.9 %collective-permute-start.7 = (bf16[96,1024]{1,0:T(8,128)(2,1)S(1)}, bf16[96,1024]{1,0:T(8,128)(2,1)S(1)}, u32[]{:S(2)}, u32[]{:S(2)}) collective-permute-start(bf16[96,1024]{1,0:T(8,128)(2,1)S(1)} %dynamic-slice_select_fusion), channel_id=1, source_target_pairs={{0,8},{1,9},{2,10},{3,11},{4,12},{5,13},{6,14},{7,15},{8,0},{9,1},... | collective-permute-start | bytes 589832 | tf_op jit(solution)/shard_map/ppermute | solution.py:389
  29.8 1.6 %collective-permute-start.9 = (bf16[256,1024]{1,0:T(8,128)(2,1)S(1)}, bf16[256,1024]{1,0:T(8,128)(2,1)S(1)}, u32[]{:S(2)}, u32[]{:S(2)}) collective-permute-start(bf16[256,1024]{1,0:T(8,128)(2,1)S(1)} %pad_maximum_fusion), channel_id=1, source_target_pairs={{0,16},{16,0},{1,17},{17,1},{2,18},{18,2},{3,19},{19,3},{4,20},{20... | collective-permute-start | bytes 1572872 | tf_op jit(solution)/shard_map/ppermute | solution.py:399
  31.3 5.3 %collective-permute-done.7.refs_7_ = bf16[96,1024]{1,0:T(8,128)(2,1)S(1)} collective-permute-done((bf16[96,1024]{1,0:T(8,128)(2,1)S(1)}, bf16[96,1024]{1,0:T(8,128)(2,1)S(1)}, u32[]{:S(2)}, u32[]{:S(2)}) %collective-permute-start.7) | collective-permute-done | bytes 196640 | tf_op jit(solution)/shard_map/ppermute | solution.py:389
  36.6 0.7 %collective-permute-done.8.refs_5_ = bf16[128,1024]{1,0:T(8,128)(2,1)S(1)} collective-permute-done((bf16[128,1024]{1,0:T(8,128)(2,1)S(1)}, bf16[128,1024]{1,0:T(8,128)(2,1)S(1)}, u32[]{:S(2)}, u32[]{:S(2)}) %collective-permute-start.8) | collective-permute-done | bytes 262176 | tf_op jit(solution)/shard_map/ppermute | solution.py:389
  37.4 0.0 collective-permute-done.6.refs_2_
  37.4 0.0 collective-permute-start.10
  37.4 2.0 %collective-permute-start.14 = (bf16[256,1024]{1,0:T(8,128)(2,1)S(1)}, bf16[256,1024]{1,0:T(8,128)(2,1)S(1)}, u32[]{:S(2)}, u32[]{:S(2)}) collective-permute-start(bf16[256,1024]{1,0:T(8,128)(2,1)S(1)} %collective-permute-done.6.refs_2_), channel_id=1, source_target_pairs={{0,4},{1,5},{2,14},{3,15},{4,8},{5,9},{6,2},{7,3},{8,12},{9,13},{1... | collective-permute-start | bytes 1572872 | tf_op jit(solution)/shard_map/ppermute | solution.py:395
  39.4 2.5 %collective-permute-start.11 = (bf16[128,1024]{1,0:T(8,128)(2,1)S(1)}, bf16[128,1024]{1,0:T(8,128)(2,1)S(1)}, u32[]{:S(2)}, u32[]{:S(2)}) collective-permute-start(bf16[128,1024]{1,0:T(8,128)(2,1)S(1)} %get-tuple-element.34), channel_id=1, source_target_pairs={{0,2},{1,3},{2,0},{3,1},{4,6},{5,7},{6,4},{7,5},{8,10},{9,11},{10,... | collective-permute-start | bytes 786440 | tf_op jit(solution)/shard_map/ppermute | solution.py:389
  42.0 1.6 %collective-permute-start.12 = (bf16[160,1024]{1,0:T(8,128)(2,1)S(1)}, bf16[160,1024]{1,0:T(8,128)(2,1)S(1)}, u32[]{:S(2)}, u32[]{:S(2)}) collective-permute-start(bf16[160,1024]{1,0:T(8,128)(2,1)S(1)} %pad_maximum_fusion.1), channel_id=1, source_target_pairs={{0,16},{16,0},{1,17},{17,1},{2,18},{18,2},{3,19},{19,3},{4,20},{20... | collective-permute-start | bytes 983048 | tf_op jit(solution)/shard_map/ppermute | solution.py:399
  43.5 0.0 collective-permute-done.9.refs_8_
  43.5 5.1 %collective-permute-done.11.refs_6_ = bf16[128,1024]{1,0:T(8,128)(2,1)S(1)} collective-permute-done((bf16[128,1024]{1,0:T(8,128)(2,1)S(1)}, bf16[128,1024]{1,0:T(8,128)(2,1)S(1)}, u32[]{:S(2)}, u32[]{:S(2)}) %collective-permute-start.11) | collective-permute-done | bytes 262176 | tf_op jit(solution)/shard_map/ppermute | solution.py:389
  48.6 0.0 collective-permute-done.10.refs_3_
  48.6 1.6 %collective-permute-start.13 = (bf16[64,1024]{1,0:T(8,128)(2,1)S(1)}, bf16[64,1024]{1,0:T(8,128)(2,1)S(1)}, u32[]{:S(2)}, u32[]{:S(2)}) collective-permute-start(bf16[64,1024]{1,0:T(8,128)(2,1)S(1)} %constant_dynamic-slice_fusion), channel_id=1, source_target_pairs={{0,16},{16,0},{1,17},{17,1},{2,18},{18,2},{3,19},{19,3},{4,20},{20... | collective-permute-start | bytes 393224 | tf_op jit(solution)/shard_map/ppermute | solution.py:399
  50.2 0.0 copy-done.1
  50.2 0.0 collective-permute-start.5
  50.2 1.9 %collective-permute-done.12.refs_10_ = bf16[160,1024]{1,0:T(8,128)(2,1)S(1)} collective-permute-done((bf16[160,1024]{1,0:T(8,128)(2,1)S(1)}, bf16[160,1024]{1,0:T(8,128)(2,1)S(1)}, u32[]{:S(2)}, u32[]{:S(2)}) %collective-permute-start.12) | collective-permute-done | bytes 327712 | tf_op jit(solution)/shard_map/ppermute | solution.py:399
  52.1 1.4 %collective-permute-done.14.refs_4_ = bf16[256,1024]{1,0:T(8,128)(2,1)S(1)} collective-permute-done((bf16[256,1024]{1,0:T(8,128)(2,1)S(1)}, bf16[256,1024]{1,0:T(8,128)(2,1)S(1)}, u32[]{:S(2)}, u32[]{:S(2)}) %collective-permute-start.14) | collective-permute-done | bytes 524320 | tf_op jit(solution)/shard_map/ppermute | solution.py:395
  53.5 0.9 %collective-permute-done.13.refs_9_ = bf16[64,1024]{1,0:T(8,128)(2,1)S(1)} collective-permute-done((bf16[64,1024]{1,0:T(8,128)(2,1)S(1)}, bf16[64,1024]{1,0:T(8,128)(2,1)S(1)}, u32[]{:S(2)}, u32[]{:S(2)}) %collective-permute-start.13) | collective-permute-done | bytes 131104 | tf_op jit(solution)/shard_map/ppermute | solution.py:399
  54.4 0.0 collective-permute-start.15
  54.4 2.5 %assemble.1.refs_6_ = bf16[8,192,1024]{2,1,0:T(8,128)(2,1)S(1)} custom-call(bf16[192,1024]{1,0:T(8,128)(2,1)S(1)} %maximum_select_fusion.refs_0_, bf16[128,1024]{1,0:T(8,128)(2,1)S(1)} %collective-permute-done.1.refs_1_, bf16[128,1024]{1,0:T(8,128)(2,1)S(1)} %collective-permute-done.2.refs_2_, bf16[128,1024]{1,0:T(8,128)(2,1)S(1)} %collective-permute-done.3.refs_3_, ...), custom_call_target="tpu_custom_call" | custom-call | flops 1000000000 | bytes 6291456 | tf_op jit(solution)/shard_map/assemble/pallas_call | solution.py:259
  56.9 0.0 copy-start
  56.9 0.0 copy-start.2
  56.9 0.0 collective-permute-done.5.refs_1_
  56.9 0.0 collective-permute-done.15.refs_5_
  56.9 10.4 %attend.1 = (bf16[4,256,128]{2,1,0:T(8,128)(2,1)S(1)}, bf16[4,256,128]{2,1,0:T(8,128)(2,1)S(1)}) custom-call(bf16[256,1024]{1,0:T(8,128)(2,1)S(1)} %copy-done.1, bf16[256,1024]{1,0:T(8,128)(2,1)S(1)} %collective-permute-done.5.refs_1_, bf16[256,1024]{1,0:T(8,128)(2,1)S(1)} %collective-permute-done.6.refs_2_, ...), custom_call_target="tpu_custom_call" | custom-call | flops 10000000000 | bytes 8388608 | tf_op jit(solution)/shard_map/attend/pallas_call | solution.py:327
  67.3 0.6 collective-permute-start.16
  67.8 1.2 %collective-permute-done.16.other_ref = bf16[4,256,128]{2,1,0:T(8,128)(2,1)S(1)} collective-permute-done((bf16[4,256,128]{2,1,0:T(8,128)(2,1)S(1)}, bf16[4,256,128]{2,1,0:T(8,128)(2,1)S(1)}, u32[]{:S(2)}, u32[]{:S(2)}) %collective-permute-start.16) | collective-permute-done | bytes 262176 | tf_op jit(solution)/shard_map/ppermute | solution.py:371
  69.0 0.0 copy-done
  69.0 0.0 copy-done.2
  69.0 1.5 %finish.1 = bf16[256,1024]{1,0:T(8,128)(2,1)} custom-call(bf16[256,1024]{1,0:T(8,128)(2,1)S(1)} %copy-done.2, bf16[4,256,128]{2,1,0:T(8,128)(2,1)S(1)} %get-tuple-element.41.mine_ref, bf16[4,256,128]{2,1,0:T(8,128)(2,1)S(1)} %collective-permute-done.16.other_ref, bf16[8,2,64,1024]{3,2,1,0:T(8,128)(2,1)S(1)} %bitcast.3), custom_call_target="tpu_custom_call" | custom-call | flops 1000000000 | bytes 4194304 | tf_op jit(solution)/shard_map/finish/pallas_call | solution.py:358
  (8 shorter events, 0.2 us)
Async XLA Ops:
  1.1 1.5 %collective-permute-start = (bf16[64,1024]{1,0:T(8,128)(2,1)S(1)}, bf16[64,1024]{1,0:T(8,128)(2,1)S(1)}, u32[]{:S(2)}, u32[]{:S(2)}) collective-permute-start(bf16[64,1024]{1,0:T(8,128)(2,1)S(1)} %get-tuple-element.46), channel_id=1, source_target_pairs={{0,1},{1,0},{2,3},{3,2},{4,5},{5,4},{6,7},{7,6},{8,9},{9,8},{10,11... | collective-permute-start | bytes 393224 | tf_op jit(solution)/shard_map/ppermute | solution.py:371
  2.7 22.6 %collective-permute-start.1 = (bf16[128,1024]{1,0:T(8,128)(2,1)S(1)}, bf16[128,1024]{1,0:T(8,128)(2,1)S(1)}, u32[]{:S(2)}, u32[]{:S(2)}) collective-permute-start(bf16[128,1024]{1,0:T(8,128)(2,1)S(1)} %constant_dynamic-slice_fusion.6), channel_id=1, source_target_pairs={{0,4},{1,5},{4,8},{5,9},{8,12},{9,13},{12,14},{13,15},{14,10},{15,... | collective-permute-start | bytes 786440 | tf_op jit(solution)/shard_map/ppermute | solution.py:385
  5.7 19.6 %collective-permute-start.2 = (bf16[128,1024]{1,0:T(8,128)(2,1)S(1)}, bf16[128,1024]{1,0:T(8,128)(2,1)S(1)}, u32[]{:S(2)}, u32[]{:S(2)}) collective-permute-start(bf16[128,1024]{1,0:T(8,128)(2,1)S(1)} %constant_dynamic-slice_fusion.6), channel_id=1, source_target_pairs={{0,2},{1,3},{4,0},{5,1},{8,4},{9,5},{12,8},{13,9},{14,12},{15,13},... | collective-permute-start | bytes 786440 | tf_op jit(solution)/shard_map/ppermute | solution.py:385
  5.7 19.6 %collective-permute-start.3 = (bf16[128,1024]{1,0:T(8,128)(2,1)S(1)}, bf16[128,1024]{1,0:T(8,128)(2,1)S(1)}, u32[]{:S(2)}, u32[]{:S(2)}) collective-permute-start(bf16[128,1024]{1,0:T(8,128)(2,1)S(1)} %constant_dynamic-slice_fusion.6), channel_id=1, source_target_pairs={{0,8},{1,9},{4,12},{5,13},{8,14},{9,15},{12,10},{13,11},{14,6},{15... | collective-permute-start | bytes 786440 | tf_op jit(solution)/shard_map/ppermute | solution.py:385
  8.7 16.5 %collective-permute-start.4 = (bf16[128,1024]{1,0:T(8,128)(2,1)S(1)}, bf16[128,1024]{1,0:T(8,128)(2,1)S(1)}, u32[]{:S(2)}, u32[]{:S(2)}) collective-permute-start(bf16[128,1024]{1,0:T(8,128)(2,1)S(1)} %constant_dynamic-slice_fusion.6), channel_id=1, source_target_pairs={{0,6},{1,7},{4,2},{5,3},{8,0},{9,1},{12,4},{13,5},{14,8},{15,9},{1... | collective-permute-start | bytes 786440 | tf_op jit(solution)/shard_map/ppermute | solution.py:385
  23.3 14.1 %collective-permute-start.6 = (bf16[256,1024]{1,0:T(8,128)(2,1)}, bf16[256,1024]{1,0:T(8,128)(2,1)S(1)}, u32[]{:S(2)}, u32[]{:S(2)}) collective-permute-start(bf16[256,1024]{1,0:T(8,128)(2,1)} %get-tuple-element.28.refs_0_), channel_id=1, source_target_pairs={{0,2},{1,3},{2,0},{3,1},{4,6},{5,7},{6,4},{7,5},{8,10},{9,11},{10,... | collective-permute-start | bytes 1572872 | tf_op jit(solution)/shard_map/ppermute | solution.py:389
  25.3 24.9 %copy-start.1 = (bf16[256,1024]{1,0:T(8,128)(2,1)S(1)}, bf16[256,1024]{1,0:T(8,128)(2,1)}, u32[]{:S(2)}) copy-start(bf16[256,1024]{1,0:T(8,128)(2,1)} %get-tuple-element.28.refs_0_) | copy-start | bytes 1572868
  25.3 12.1 %collective-permute-start.8 = (bf16[128,1024]{1,0:T(8,128)(2,1)S(1)}, bf16[128,1024]{1,0:T(8,128)(2,1)S(1)}, u32[]{:S(2)}, u32[]{:S(2)}) collective-permute-start(bf16[128,1024]{1,0:T(8,128)(2,1)S(1)} %get-tuple-element.44), channel_id=1, source_target_pairs={{0,4},{1,5},{2,6},{3,7},{4,0},{5,1},{6,2},{7,3},{8,12},{9,13},{10,... | collective-permute-start | bytes 786440 | tf_op jit(solution)/shard_map/ppermute | solution.py:389
  27.8 8.9 %collective-permute-start.7 = (bf16[96,1024]{1,0:T(8,128)(2,1)S(1)}, bf16[96,1024]{1,0:T(8,128)(2,1)S(1)}, u32[]{:S(2)}, u32[]{:S(2)}) collective-permute-start(bf16[96,1024]{1,0:T(8,128)(2,1)S(1)} %dynamic-slice_select_fusion), channel_id=1, source_target_pairs={{0,8},{1,9},{2,10},{3,11},{4,12},{5,13},{6,14},{7,15},{8,0},{9,1},... | collective-permute-start | bytes 589832 | tf_op jit(solution)/shard_map/ppermute | solution.py:389
  29.8 13.7 %collective-permute-start.9 = (bf16[256,1024]{1,0:T(8,128)(2,1)S(1)}, bf16[256,1024]{1,0:T(8,128)(2,1)S(1)}, u32[]{:S(2)}, u32[]{:S(2)}) collective-permute-start(bf16[256,1024]{1,0:T(8,128)(2,1)S(1)} %pad_maximum_fusion), channel_id=1, source_target_pairs={{0,16},{16,0},{1,17},{17,1},{2,18},{18,2},{3,19},{19,3},{4,20},{20... | collective-permute-start | bytes 1572872 | tf_op jit(solution)/shard_map/ppermute | solution.py:399
  37.4 11.2 %collective-permute-start.10 = (bf16[256,1024]{1,0:T(8,128)(2,1)S(1)}, bf16[256,1024]{1,0:T(8,128)(2,1)S(1)}, u32[]{:S(2)}, u32[]{:S(2)}) collective-permute-start(bf16[256,1024]{1,0:T(8,128)(2,1)S(1)} %collective-permute-done.6.refs_2_), channel_id=1, source_target_pairs={{0,1},{1,0},{2,3},{3,2},{4,5},{5,4},{6,7},{7,6},{8,9},{9,8},{10,11... | collective-permute-start | bytes 1572872 | tf_op jit(solution)/shard_map/ppermute | solution.py:371
  37.4 16.1 %collective-permute-start.14 = (bf16[256,1024]{1,0:T(8,128)(2,1)S(1)}, bf16[256,1024]{1,0:T(8,128)(2,1)S(1)}, u32[]{:S(2)}, u32[]{:S(2)}) collective-permute-start(bf16[256,1024]{1,0:T(8,128)(2,1)S(1)} %collective-permute-done.6.refs_2_), channel_id=1, source_target_pairs={{0,4},{1,5},{2,14},{3,15},{4,8},{5,9},{6,2},{7,3},{8,12},{9,13},{1... | collective-permute-start | bytes 1572872 | tf_op jit(solution)/shard_map/ppermute | solution.py:395
  39.4 9.2 %collective-permute-start.11 = (bf16[128,1024]{1,0:T(8,128)(2,1)S(1)}, bf16[128,1024]{1,0:T(8,128)(2,1)S(1)}, u32[]{:S(2)}, u32[]{:S(2)}) collective-permute-start(bf16[128,1024]{1,0:T(8,128)(2,1)S(1)} %get-tuple-element.34), channel_id=1, source_target_pairs={{0,2},{1,3},{2,0},{3,1},{4,6},{5,7},{6,4},{7,5},{8,10},{9,11},{10,... | collective-permute-start | bytes 786440 | tf_op jit(solution)/shard_map/ppermute | solution.py:389
  42.0 10.1 %collective-permute-start.12 = (bf16[160,1024]{1,0:T(8,128)(2,1)S(1)}, bf16[160,1024]{1,0:T(8,128)(2,1)S(1)}, u32[]{:S(2)}, u32[]{:S(2)}) collective-permute-start(bf16[160,1024]{1,0:T(8,128)(2,1)S(1)} %pad_maximum_fusion.1), channel_id=1, source_target_pairs={{0,16},{16,0},{1,17},{17,1},{2,18},{18,2},{3,19},{19,3},{4,20},{20... | collective-permute-start | bytes 983048 | tf_op jit(solution)/shard_map/ppermute | solution.py:399
  48.6 5.8 %collective-permute-start.13 = (bf16[64,1024]{1,0:T(8,128)(2,1)S(1)}, bf16[64,1024]{1,0:T(8,128)(2,1)S(1)}, u32[]{:S(2)}, u32[]{:S(2)}) collective-permute-start(bf16[64,1024]{1,0:T(8,128)(2,1)S(1)} %constant_dynamic-slice_fusion), channel_id=1, source_target_pairs={{0,16},{16,0},{1,17},{17,1},{2,18},{18,2},{3,19},{19,3},{4,20},{20... | collective-permute-start | bytes 393224 | tf_op jit(solution)/shard_map/ppermute | solution.py:399
  50.2 6.7 %collective-permute-start.5 = (bf16[256,1024]{1,0:T(8,128)(2,1)S(1)}, bf16[256,1024]{1,0:T(8,128)(2,1)S(1)}, u32[]{:S(2)}, u32[]{:S(2)}) collective-permute-start(bf16[256,1024]{1,0:T(8,128)(2,1)S(1)} %copy-done.1), channel_id=1, source_target_pairs={{0,1},{1,0},{2,3},{3,2},{4,5},{5,4},{6,7},{7,6},{8,9},{9,8},{10,11... | collective-permute-start | bytes 1572872 | tf_op jit(solution)/shard_map/ppermute | solution.py:371
  54.4 2.5 %collective-permute-start.15 = (bf16[256,1024]{1,0:T(8,128)(2,1)S(1)}, bf16[256,1024]{1,0:T(8,128)(2,1)S(1)}, u32[]{:S(2)}, u32[]{:S(2)}) collective-permute-start(bf16[256,1024]{1,0:T(8,128)(2,1)S(1)} %collective-permute-done.14.refs_4_), channel_id=1, source_target_pairs={{0,1},{1,0},{2,3},{3,2},{4,5},{5,4},{6,7},{7,6},{8,9},{9,8},{10,11... | collective-permute-start | bytes 1572872 | tf_op jit(solution)/shard_map/ppermute | solution.py:371
  56.9 12.2 %copy-start = (bf16[1024,1024]{1,0:T(8,128)(2,1)S(1)}, bf16[1024,1024]{1,0:T(8,128)(2,1)}, u32[]{:S(2)}) copy-start(bf16[1024,1024]{1,0:T(8,128)(2,1)} %param.21) | copy-start | bytes 6291460
  56.9 12.1 %copy-start.2 = (bf16[256,1024]{1,0:T(8,128)(2,1)S(1)}, bf16[256,1024]{1,0:T(8,128)(2,1)}, u32[]{:S(2)}) copy-start(bf16[256,1024]{1,0:T(8,128)(2,1)} %get-tuple-element.27.tokens_ref) | copy-start | bytes 1572868
  67.3 1.7 %collective-permute-start.16 = (bf16[4,256,128]{2,1,0:T(8,128)(2,1)S(1)}, bf16[4,256,128]{2,1,0:T(8,128)(2,1)S(1)}, u32[]{:S(2)}, u32[]{:S(2)}) collective-permute-start(bf16[4,256,128]{2,1,0:T(8,128)(2,1)S(1)} %get-tuple-element.42), channel_id=1, source_target_pairs={{0,1},{1,0},{2,3},{3,2},{4,5},{5,4},{6,7},{7,6},{8,9},{9,8},{10,11... | collective-permute-start | bytes 786440 | tf_op jit(solution)/shard_map/ppermute | solution.py:371
